TPU v7x, 32 devices: a whole 2x2x4 slice. The times are simulated.
32 devices in a mesh: clip: 8 (over z, y), win: 4 (over x, core).
Axes of the slice: x: 2, y: 2, z: 4, core: 2. Of those that a mesh axis runs over, the one named last changes fastest.
Arguments:
- tokens: bfloat16 [2, 8, 4, 4, 5, 4, 8, 1024], P(None, 'clip', 'win'), may hold values from -6 to 6
- cond: bfloat16 [2, 8, 1024], P(None, 'clip'), may hold values from -6 to 6
- lengths: int32 [2, 8], P(None, 'clip'), may hold values from 2 to 9, as said below
- ada_w: bfloat16 [1024, 6144], P(('clip', 'win')), may hold values from -0.1875 to 0.1875
- ada_b: bfloat16 [6144], P(('clip', 'win')), may hold values from -3 to 3
- w_qkv: bfloat16 [1024, 3072], P(('clip', 'win')), may hold values from -0.1875 to 0.1875
- w_out: bfloat16 [1024, 1024], P(('clip', 'win')), may hold values from -3.5 to 3.5
- w_up: bfloat16 [1024, 4096], P(('clip', 'win')), may hold values from -0.1875 to 0.1875
- b_up: bfloat16 [4096], P(('clip', 'win')), may hold values from -3 to 3
- w_down: bfloat16 [4096, 1024], P(('clip', 'win')), may hold values from -0.09375 to 0.09375
- b_down: bfloat16 [1024], P(('clip', 'win')), may hold values from -3 to 3
- rel_table: bfloat16 [512, 16], P(('clip', 'win')), may hold values from -4 to 4
- bucket: int32 [2025], replicated, may hold values from 0 to 511
- cotangent: bfloat16 [2, 8, 4, 4, 5, 4, 8, 1024], P(None, 'clip', 'win'), may hold values from -6 to 6
Outputs:
- output: bfloat16 [2, 8, 4, 4, 5, 4, 8, 1024], P(None, 'clip', 'win')
- grad_tokens: bfloat16 [2, 8, 4, 4, 5, 4, 8, 1024], P(None, 'clip', 'win')
- grad_ada_w: float32 [1024, 6144], P(('clip', 'win'))
- grad_ada_b: float32 [6144], P(('clip', 'win'))
- grad_w_qkv: float32 [1024, 3072], P(('clip', 'win'))
- grad_w_out: float32 [1024, 1024], P(('clip', 'win'))
- grad_w_up: float32 [1024, 4096], P(('clip', 'win'))
- grad_b_up: float32 [4096], P(('clip', 'win'))
- grad_w_down: float32 [4096, 1024], P(('clip', 'win'))
- grad_b_down: float32 [1024], P(('clip', 'win'))
- grad_rel_table: float32 [512, 16], P(('clip', 'win'))
Inputs may be any that keep to these rules, and one draw needn't show every extreme that they name: `lengths`: in each micro-batch some clip has 9 frames.
All inputs are finite; a program needn't handle non-finite values.
Results may differ from a plain program's by a relative error of at most 0.013.
The roundings to bfloat16 on the way count: a program that leaves them out, or rounds other values in their place, can miss the bound.
Values may be sent and summed in bfloat16 or wider, within the bound.
No kernel may reach another device: no remote copies, remote signals or barrier semaphores. Data moves between devices by JAX's collectives and lax.ppermute only.
A program may use at most 448 MiB of HBM per device.

v0:
```python
import math

import jax
import jax.numpy as jnp
from jax import lax
from jax.sharding import PartitionSpec as P

HEADS = 16


EPSILON = 1e-06
MASKED = -1000000000.0
HIGHEST = lax.Precision.HIGHEST


def relative_index(frames, strip_rows, window_side):
    position = jnp.arange(frames * window_side * window_side, dtype=jnp.int32)
    column = position % window_side
    row_in = position // window_side % strip_rows
    frame_pos = position // (window_side * strip_rows) % frames
    half_idx = position // (window_side * strip_rows * frames)
    row_pos = half_idx * strip_rows + row_in
    span_len = 2 * window_side - 1
    delta_t = frame_pos[:, None] - frame_pos[None, :] + frames - 1
    delta_y = row_pos[:, None] - row_pos[None, :] + window_side - 1
    delta_x = column[:, None] - column[None, :] + window_side - 1
    return (delta_t * span_len + delta_y) * span_len + delta_x


def normalize(values):
    centered = values - jnp.mean(values, axis=-1, keepdims=True)
    inv_std = lax.rsqrt(jnp.mean(centered * centered, axis=-1, keepdims=True) + EPSILON)
    return (centered * inv_std, inv_std)


def norm_back(grad_in, normed, inv_std):
    return inv_std * (
        grad_in
        - jnp.mean(grad_in, axis=-1, keepdims=True)
        - normed * jnp.mean(grad_in * normed, axis=-1, keepdims=True)
    )


def smooth_gate(values):
    return jax.nn.gelu(values, approximate=True)


def contract_rows(left_mat, right_mat):
    return lax.dot_general(
        left_mat, right_mat, (((0,), (0,)), ((), ())), preferred_element_type=jnp.float32
    )


def contract_cols(left_mat, right_mat):
    return lax.dot_general(
        left_mat, right_mat, (((1,), (1,)), ((), ())), preferred_element_type=jnp.float32
    )


def pack_rows(arrays, devices):
    return jnp.concatenate([element.reshape(devices, -1) for element in arrays], axis=1).reshape(-1)


def unpack_rows(vector, shard_shapes):
    pieces = []
    offset = 0
    for shape_one in shard_shapes:
        length_one = math.prod(shape_one)
        pieces.append(vector[offset : offset + length_one].reshape(shape_one))
        offset = offset + length_one
    return tuple(pieces)


def make_bias(rel_table, pair_bucket, groups):
    window_len = pair_bucket.shape[0]
    buckets, head_count = rel_table.shape
    grouped = pair_bucket.reshape(groups, -1)
    table_t = rel_table.T

    def one_group(bucket_row):
        onehot = (jnp.arange(buckets, dtype=jnp.int32)[:, None] == bucket_row[None, :]).astype(
            jnp.bfloat16
        )
        return jnp.dot(table_t, onehot, preferred_element_type=jnp.float32)

    pieces = lax.map(one_group, grouped)
    pieces = pieces.reshape(groups, head_count, window_len // groups, window_len)
    return pieces.transpose(1, 0, 2, 3).reshape(head_count, window_len, window_len)


def table_back(grad_bias, pair_bucket, groups, buckets):
    head_count = grad_bias.shape[0]
    grouped = pair_bucket.reshape(groups, -1)
    spread = grad_bias.reshape(head_count, groups, -1)

    def add_group(group_step, running):
        bucket_row = lax.dynamic_index_in_dim(grouped, group_step, 0, keepdims=False)
        onehot = (jnp.arange(buckets, dtype=jnp.int32)[:, None] == bucket_row[None, :]).astype(
            jnp.bfloat16
        )
        grad_part = lax.dynamic_index_in_dim(spread, group_step, 1, keepdims=False)
        grad_high = grad_part.astype(jnp.bfloat16)
        grad_rest = (grad_part - grad_high.astype(jnp.float32)).astype(jnp.bfloat16)
        dims = (((1,), (1,)), ((), ()))
        return (
            running
            + lax.dot_general(onehot, grad_high, dims, preferred_element_type=jnp.float32)
            + lax.dot_general(onehot, grad_rest, dims, preferred_element_type=jnp.float32)
        )

    return lax.fori_loop(0, groups, add_group, jnp.zeros((buckets, head_count), jnp.float32))


def scores_of(query_rows, key_rows, rel_bias, key_ok, score_scale):
    raw_scores = (
        jnp.einsum("wphd,wqhd->whpq", query_rows, key_rows, preferred_element_type=jnp.float32)
        * score_scale
        + rel_bias[None]
    )
    return jnp.where(key_ok, raw_scores, MASKED)


def body(
    tokens,
    cond,
    lengths,
    ada_w,
    ada_b,
    w_qkv,
    w_out,
    w_up,
    b_up,
    w_down,
    b_down,
    rel_table,
    bucket,
    cotangent,
):
    micro_count, _, _, blocks, frames, strip_rows, window_side, model_width = tokens.shape
    halves = window_side // strip_rows
    side_wins = blocks // halves
    piece_rows = frames * strip_rows * window_side
    window_len = halves * piece_rows
    tokens_dev = blocks * piece_rows
    head_size = model_width // HEADS
    score_scale = 1.0 / math.sqrt(head_size)
    groups = 8
    devices = lax.axis_size(("clip", "win"))
    time_win = lax.axis_index("win") // side_wins
    pair_bucket = jnp.take(
        bucket, relative_index(frames, strip_rows, window_side).reshape(-1)
    ).reshape(window_len, window_len)
    block_ids = jnp.arange(blocks, dtype=jnp.int32)
    tok_frame = (block_ids // side_wins)[:, None] * frames + jnp.arange(frames, dtype=jnp.int32)[
        None, :
    ]
    tok_frame = jnp.broadcast_to(
        tok_frame[:, :, None], (blocks, frames, strip_rows * window_side)
    ).reshape(tokens_dev)
    win_frame = (
        time_win * frames
        + jnp.arange(window_len, dtype=jnp.int32) // (strip_rows * window_side) % frames
    )
    shards = (w_qkv, w_out, w_up, b_up, w_down, b_down, rel_table)
    shard_shapes = [shard_arr.shape for shard_arr in shards]
    full_shapes = [(shard_arr.shape[0] * devices,) + shard_arr.shape[1:] for shard_arr in shards]
    buckets_all = rel_table.shape[0] * devices

    def fresh():
        zeros_list = [jnp.zeros(shape_one, jnp.float32) for shape_one in full_shapes[:6]]
        return tuple(zeros_list) + (jnp.zeros((HEADS, window_len, window_len), jnp.float32),)

    cond_local = jax.nn.silu(cond[:, 0].astype(jnp.float32)).astype(jnp.bfloat16)
    full_ada_w, full_ada_b = (
        lax.all_gather(ada_w, ("clip", "win"), axis=0, tiled=True),
        lax.all_gather(ada_b, ("clip", "win"), axis=0, tiled=True),
    )
    mod_all = (
        jnp.dot(cond_local, full_ada_w, preferred_element_type=jnp.float32)
        + full_ada_b.astype(jnp.float32)[None, :]
    )
    local_sums = fresh()
    summed = None
    outputs = []
    input_grads = []
    mod_grads = []
    for micro_step in range(micro_count):
        weights = (
            lax.all_gather(w_qkv, ("clip", "win"), axis=0, tiled=True),
            lax.all_gather(w_out, ("clip", "win"), axis=0, tiled=True),
            lax.all_gather(w_up, ("clip", "win"), axis=0, tiled=True),
            lax.all_gather(b_up, ("clip", "win"), axis=0, tiled=True),
            lax.all_gather(w_down, ("clip", "win"), axis=0, tiled=True),
            lax.all_gather(b_down, ("clip", "win"), axis=0, tiled=True),
            lax.all_gather(rel_table, ("clip", "win"), axis=0, tiled=True),
        )
        full_qkv, full_out, full_up, full_bup, full_down, full_bdown, full_table = weights
        rel_bias = make_bias(full_table, pair_bucket, groups)
        length = lengths[micro_step, 0]
        tok_mask = (tok_frame < length).astype(jnp.float32)[:, None]
        win_valid = (win_frame < length).astype(jnp.float32)
        query_mask = jnp.tile(win_valid, side_wins)[:, None]
        key_ok = win_valid[None, None, None, :] > 0
        layer_in = tokens[micro_step, 0, 0].reshape(tokens_dev, model_width).astype(jnp.float32)
        modulation = mod_all[micro_step]
        shift_one, scale_one, gate_one, shift_two, scale_two, gate_two = jnp.split(modulation, 6)
        normed_one, inv_one = normalize(layer_in)
        hidden_one = (normed_one * (1.0 + scale_one) + shift_one).astype(jnp.bfloat16)
        window_h = lax.all_to_all(
            hidden_one.reshape(blocks, piece_rows, model_width),
            "win",
            split_axis=0,
            concat_axis=0,
            tiled=True,
        )
        window_h = window_h.reshape(side_wins * window_len, model_width)
        qkv_rows = jnp.dot(window_h, full_qkv, preferred_element_type=jnp.float32).astype(
            jnp.bfloat16
        )
        qkv_rows = qkv_rows.reshape(side_wins, window_len, 3, HEADS, head_size)
        query_rows = qkv_rows[:, :, 0]
        key_rows = qkv_rows[:, :, 1]
        value_rows = qkv_rows[:, :, 2]
        scores = scores_of(query_rows, key_rows, rel_bias, key_ok, score_scale)
        row_max = jnp.max(scores, axis=-1, keepdims=True)
        log_total = row_max + jnp.log(jnp.sum(jnp.exp(scores - row_max), axis=-1, keepdims=True))
        probabilities = jnp.exp(scores - log_total).astype(jnp.bfloat16)
        attended = jnp.einsum(
            "whpq,wqhd->wphd", probabilities, value_rows, preferred_element_type=jnp.float32
        ).astype(jnp.bfloat16)
        attended = attended.reshape(side_wins * window_len, model_width)
        branch = (
            jnp.dot(attended, full_out, preferred_element_type=jnp.float32) * query_mask
        ).astype(jnp.bfloat16)
        back_rows = lax.all_to_all(
            branch.reshape(blocks, piece_rows, model_width),
            "win",
            split_axis=0,
            concat_axis=0,
            tiled=True,
        )
        back_rows = back_rows.reshape(tokens_dev, model_width).astype(jnp.float32)
        middle = layer_in + gate_one * back_rows
        normed_two, inv_two = normalize(middle)
        hidden_two = (normed_two * (1.0 + scale_two) + shift_two).astype(jnp.bfloat16)
        pre_act = jnp.dot(
            hidden_two, full_up, preferred_element_type=jnp.float32
        ) + full_bup.astype(jnp.float32)
        activated, gate_back = jax.vjp(smooth_gate, pre_act)
        act_low = activated.astype(jnp.bfloat16)
        mlp_out = jnp.dot(
            act_low, full_down, preferred_element_type=jnp.float32
        ) + full_bdown.astype(jnp.float32)
        outputs.append(
            (middle + tok_mask * gate_two * mlp_out).astype(jnp.bfloat16).reshape(tokens.shape[3:])
        )
        grad_out = cotangent[micro_step, 0, 0].reshape(tokens_dev, model_width).astype(jnp.float32)
        grad_mlp = (grad_out * tok_mask * gate_two).astype(jnp.bfloat16)
        grad_gate_two = jnp.sum(grad_out * tok_mask * mlp_out, axis=0)
        grad_act = contract_cols(grad_mlp, full_down)
        grad_pre = gate_back(grad_act)[0].astype(jnp.bfloat16)
        grad_two = contract_cols(grad_pre, full_up)
        grad_shift_two = jnp.sum(grad_two, axis=0)
        grad_scale_two = jnp.sum(grad_two * normed_two, axis=0)
        grad_middle = grad_out + norm_back(grad_two * (1.0 + scale_two), normed_two, inv_two)
        grad_gate_one = jnp.sum(grad_middle * back_rows, axis=0)
        grad_back = (grad_middle * gate_one).astype(jnp.bfloat16)
        grad_branch = lax.all_to_all(
            grad_back.reshape(blocks, piece_rows, model_width),
            "win",
            split_axis=0,
            concat_axis=0,
            tiled=True,
        )
        grad_branch = grad_branch.reshape(side_wins * window_len, model_width) * query_mask.astype(
            jnp.bfloat16
        )
        grad_attended = (
            contract_cols(grad_branch, full_out)
            .astype(jnp.bfloat16)
            .reshape(side_wins, window_len, HEADS, head_size)
        )
        scores = scores_of(query_rows, key_rows, rel_bias, key_ok, score_scale)
        probs_full = jnp.exp(scores - log_total)
        probs_low = probs_full.astype(jnp.bfloat16)
        grad_probs = jnp.einsum(
            "wphd,wqhd->whpq", grad_attended, value_rows, preferred_element_type=jnp.float32
        )
        grad_values = jnp.einsum(
            "whpq,wphd->wqhd", probs_low, grad_attended, preferred_element_type=jnp.float32
        )
        grad_scores = probs_full * (
            grad_probs - jnp.sum(probs_full * grad_probs, axis=-1, keepdims=True)
        )
        grad_scores = jnp.where(key_ok, grad_scores, 0.0).astype(jnp.bfloat16)
        grad_query = (
            jnp.einsum("whpq,wqhd->wphd", grad_scores, key_rows, preferred_element_type=jnp.float32)
            * score_scale
        )
        grad_keys = (
            jnp.einsum(
                "whpq,wphd->wqhd", grad_scores, query_rows, preferred_element_type=jnp.float32
            )
            * score_scale
        )
        grad_qkv = jnp.stack([grad_query, grad_keys, grad_values], axis=2).astype(jnp.bfloat16)
        grad_qkv = grad_qkv.reshape(side_wins * window_len, 3 * model_width)
        grad_window = contract_cols(grad_qkv, full_qkv).astype(jnp.bfloat16)
        grad_one = lax.all_to_all(
            grad_window.reshape(blocks, piece_rows, model_width),
            "win",
            split_axis=0,
            concat_axis=0,
            tiled=True,
        )
        grad_one = grad_one.reshape(tokens_dev, model_width).astype(jnp.float32)
        grad_shift_one = jnp.sum(grad_one, axis=0)
        grad_scale_one = jnp.sum(grad_one * normed_one, axis=0)
        grad_input = grad_middle + norm_back(grad_one * (1.0 + scale_one), normed_one, inv_one)
        input_grads.append(grad_input.astype(jnp.bfloat16).reshape(tokens.shape[3:]))
        mod_grads.append(
            jnp.concatenate(
                [
                    grad_shift_one,
                    grad_scale_one,
                    grad_gate_one,
                    grad_shift_two,
                    grad_scale_two,
                    grad_gate_two,
                ]
            )
        )
        updates = (
            contract_rows(window_h, grad_qkv),
            contract_rows(attended, grad_branch),
            contract_rows(hidden_two, grad_pre),
            jnp.sum(grad_pre.astype(jnp.float32), axis=0),
            contract_rows(act_low, grad_mlp),
            jnp.sum(grad_mlp.astype(jnp.float32), axis=0),
            jnp.sum(grad_scores.astype(jnp.float32), axis=0),
        )
        local_sums = tuple((addend for addend in updates))
        packed = pack_rows(
            local_sums[:6] + (table_back(local_sums[6], pair_bucket, groups, buckets_all),), devices
        )
        part_sums = lax.psum_scatter(packed, ("clip", "win"), scatter_dimension=0, tiled=True)
        if summed is None:
            summed = part_sums
        else:
            summed = summed + part_sums
        local_sums = fresh()
    weight_grads = unpack_rows(summed, shard_shapes)
    mod_stack = jnp.stack(mod_grads)
    ada_term_w = lax.dot_general(
        cond_local.astype(jnp.float32),
        mod_stack,
        (((0,), (0,)), ((), ())),
        precision=HIGHEST,
        preferred_element_type=jnp.float32,
    )
    ada_term_b = jnp.sum(mod_stack, axis=0)
    ada_packed = pack_rows((ada_term_w, ada_term_b), devices)
    ada_summed = lax.psum_scatter(ada_packed, ("clip", "win"), scatter_dimension=0, tiled=True)
    grad_ada_w, grad_ada_b = unpack_rows(ada_summed, (ada_w.shape, ada_b.shape))
    out_tokens = jnp.stack(outputs)[:, None, None]
    out_grads = jnp.stack(input_grads)[:, None, None]
    return (out_tokens, out_grads, grad_ada_w, grad_ada_b) + tuple(weight_grads)


def solution(mesh):
    placed = (
        P(None, "clip", "win", None, None, None, None, None),
        P(None, "clip", None),
        P(None, "clip"),
        P(("clip", "win"), None),
        P(("clip", "win")),
        P(("clip", "win"), None),
        P(("clip", "win"), None),
        P(("clip", "win"), None),
        P(("clip", "win")),
        P(("clip", "win"), None),
        P(("clip", "win")),
        P(("clip", "win"), None),
        P(),
        P(None, "clip", "win", None, None, None, None, None),
    )
    return jax.shard_map(
        body,
        mesh=mesh,
        in_specs=placed,
        out_specs=(
            P(None, "clip", "win", None, None, None, None, None),
            P(None, "clip", "win", None, None, None, None, None),
            P(("clip", "win"), None),
            P(("clip", "win")),
            P(("clip", "win"), None),
            P(("clip", "win"), None),
            P(("clip", "win"), None),
            P(("clip", "win")),
            P(("clip", "win"), None),
            P(("clip", "win")),
            P(("clip", "win"), None),
        ),
        check_vma=False,
    )
```

profile of v0, /device:TPU:0, one launch (start us, length us, event | category | flops | bytes accessed | tf_op | source)
XLA Modules:
  0.0 3116.5 jit_solution(8477251402224630834)
XLA Ops:
  19.3 43.1 %all-reduce.5 = (bf16[6144]{0:T(1024)(128)(2,1)S(1)}, bf16[1024]{0:T(1024)(128)(2,1)}) all-reduce(bf16[6144]{0:T(1024)(128)(2,1)S(1)} %dynamic-update-slice, bf16[1024]{0:T(1024)(128)(2,1)S(1)} %dynamic-update-slice.1), channel_id=1, replica_groups=mesh['clip'=8,'win'=4] {'clip','win'}, use_global_device_ids=true, to_apply=%add | all-reduce | flops 7168 | bytes 28672
  64.3 566.4 %gather_fusion = s32[102400]{0:T(1024)S(1)} fusion(s32[2025]{0:T(1024)S(1)} %copy-done, s32[102400]{0:T(1024)S(1)} %broadcast_clamp_fusion), kind=kCustom, calls=%fused_computation | custom fusion | bytes 1228800 | tf_op jit(solution)/shard_map/jit(_take)/gather | solution.py:150
  632.0 41.4 %all_gather.37 = bf16[512,16]{1,0:T(8,128)(2,1)S(1)} all-gather(bf16[16,16]{1,0:T(8,128)(2,1)S(1)} %copy-done.91), channel_id=1, replica_groups=mesh['clip'=8,'win'=4] {'clip','win'}, dimensions={0}, use_global_device_ids=true | all-gather | bytes 16896 | tf_op jit(solution)/shard_map/all_gather | solution.py:195
  673.7 40.0 %while.42 = (s32[]{:T(128)}, f32[8,16,12800]{2,1,0:T(8,128)}, s32[8,12800]{1,0:T(8,128)S(1)}, bf16[16,512]{1,0:T(8,128)(2,1)S(1)}, s32[]{:T(128)}) while((s32[]{:T(128)}, f32[8,16,12800]{2,1,0:T(8,128)}, s32[8,12800]{1,0:T(8,128)S(1)}, bf16[16,512]{1,0:T(8,128)(2,1)S(1)}, s32[]{:T(128)}) %tuple.145), condition=%wide.region_3.4_spmd, body=%wide.region_2.3_spmd.sunk | while | flops 216268800 | bytes 989261 | solution.py:86
  740.3 36.4 %all-gather = bf16[32,1,128]{2,1,0:T(2,128)(2,1)S(1)} all-gather(bf16[1,1,128]{2,1,0:T(2,128)(2,1)S(1)} %bitcast.439), channel_id=1, replica_groups=mesh['clip'=8,'win'=4] {'clip','win'}, dimensions={0}, use_global_device_ids=true | all-gather | bytes 8448 | tf_op jit(solution)/shard_map/all_gather | solution.py:192
  890.7 14.1 fusion.38
  904.9 16.4 exponential_reduce_fusion.1
  1019.3 14.8 fusion.187
  1042.3 14.5 fusion.185
  1056.8 24.9 convert_reduce_fusion.3
  1116.8 17.8 fusion.75
  1134.6 15.9 fusion.81
  1238.9 29.9 convert_reduce_fusion.1
  1312.2 30.1 convert_reduce_fusion
  1468.6 104.6 %while.43 = (s32[]{:T(128)}, f32[512,16]{0,1:T(8,128)S(1)}, s32[8,12800]{1,0:T(8,128)}, f32[16,8,12800]{2,1,0:T(8,128)}, s32[]{:T(128)}, /*index=5*/s32[]{:T(128)}) while((s32[]{:T(128)}, f32[512,16]{0,1:T(8,128)S(1)}, s32[8,12800]{1,0:T(8,128)}, f32[16,8,12800]{2,1,0:T(8,128)}, s32[]{:T(128)}, /*index=5*/s32[]{:T(128)}) %tuple.170), condition=%wide.region_41.42_spmd.clone, body=%wide.region_40.41_spmd.clone.sunk | while | flops 433381376 | bytes 3612767 | solution.py:111
  1631.0 104.4 %while.44 = (s32[]{:T(128)}, f32[512,16]{0,1:T(8,128)S(1)}, s32[8,12800]{1,0:T(8,128)}, f32[16,8,12800]{2,1,0:T(8,128)}, s32[]{:T(128)}, /*index=5*/s32[]{:T(128)}) while((s32[]{:T(128)}, f32[512,16]{0,1:T(8,128)S(1)}, s32[8,12800]{1,0:T(8,128)}, f32[16,8,12800]{2,1,0:T(8,128)}, s32[]{:T(128)}, /*index=5*/s32[]{:T(128)}) %tuple.169), condition=%wide.region_47.48_spmd.clone, body=%wide.region_46.47_spmd.clone.sunk | while | flops 433381376 | bytes 3612767 | solution.py:111
  1740.1 13.2 constant_dynamic-update-slice_fusion.4
  1804.4 49.0 %add.724 = f32[32,393632]{1,0:T(8,128)} add(f32[32,393632]{1,0:T(8,128)} %dynamic-update-slice.15, f32[32,393632]{1,0:T(8,128)} %dynamic-update-slice.8) | non-fusion elementwise | flops 12596224 | bytes 151154688 | tf_op jit(solution)/shard_map/add | solution.py:350
  1853.5 64.9 %reshape.1121 = f32[12596224]{0:T(1024)} reshape(f32[32,393632]{1,0:T(8,128)} %add.724) | data formatting | bytes 100769792 | tf_op jit(solution)/shard_map/add | solution.py:350
  1925.1 13.8 fusion.140
  1938.8 26.3 reshape.1072
  1965.1 19.0 pad_maximum_fusion
  1984.1 30.3 reshape.1073
  2026.0 1068.6 %all-reduce.8.cloned.1.call-done = (f32[6297600]{0:T(1024)}, f32[12596224]{0:T(1024)}) async-done(((f32[6297600]{0:T(1024)}, f32[12596224]{0:T(1024)}), (f32[6297600]{0:T(1024)}, f32[12596224]{0:T(1024)})) %all-reduce.8.cloned.1.call-update) | async-done | bytes 75575312
  (589 shorter events, 949.4 us)
Async XLA Ops:
  7.2 57.2 %copy-start = (s32[2025]{0:T(1024)S(1)}, s32[2025]{0:T(1024)}, u32[]{:S(2)}) copy-start(s32[2025]{0:T(1024)} %param.32) | copy-start | bytes 24304
  7.2 769.6 %all-gather.7.cloned.1.call-start = ((), (), s32[]{:S(2)}) async-start(), calls=%async_computation.8 | async-start | bytes 12976128 | tf_op jit(solution)/shard_map/all_gather | solution.py:175
  7.9 804.3 %all-gather.9.cloned.1.call-start = ((), (), s32[]{:S(2)}) async-start(), calls=%async_computation.9 | async-start | bytes 6488064 | tf_op jit(solution)/shard_map/all_gather | solution.py:189
  8.7 928.3 %all-gather.11.cloned.1.call-start = ((), (), s32[]{:S(2)}) async-start(), calls=%async_computation.10 | async-start | bytes 2162688 | tf_op jit(solution)/shard_map/all_gather | solution.py:190
  9.4 969.1 %all-gather.15.cloned.1.call-start = ((), (), s32[]{:S(2)}) async-start(), calls=%async_computation.12 | async-start | bytes 8650752 | tf_op jit(solution)/shard_map/all_gather | solution.py:193
  10.0 997.5 %all-gather.13.cloned.1.call-start = ((), (), s32[]{:S(2)}) async-start(), calls=%async_computation.11 | async-start | bytes 8650752 | tf_op jit(solution)/shard_map/all_gather | solution.py:191
  16.0 48.2 %copy-start.45 = (f32[4,5,4,8]{3,2,1,0:T(4,128)}, f32[4,5,4,8]{3,2,1,0:T(4,128)S(1)}, u32[]{:S(2)}) copy-start(f32[4,5,4,8]{3,2,1,0:T(4,128)S(1)} %get-tuple-element.357) | copy-start | bytes 7684
  62.6 720.8 %copy-start.71 = (f32[4,160]{1,0:T(4,128)}, f32[4,160]{1,0:T(4,128)S(1)}, u32[]{:S(2)}) copy-start(f32[4,160]{1,0:T(4,128)S(1)} %rsqrt.57) | copy-start | bytes 7684
  738.7 57.3 %copy-start.73 = (f32[4,160]{1,0:T(4,128)}, f32[4,160]{1,0:T(4,128)S(1)}, u32[]{:S(2)}) copy-start(f32[4,160]{1,0:T(4,128)S(1)} %rsqrt.53) | copy-start | bytes 7684
  739.4 181.9 %copy-start.63 = (pred[320]{0:T(512)(128)(4,1)}, pred[320]{0:T(512)(128)(4,1)S(1)}, u32[]{:S(2)}) copy-start(pred[320]{0:T(512)(128)(4,1)S(1)} %get-tuple-element.362) | copy-start | bytes 964
  740.1 215.0 %copy-start.75 = (pred[320]{0:T(512)(128)(4,1)}, pred[320]{0:T(512)(128)(4,1)S(1)}, u32[]{:S(2)}) copy-start(pred[320]{0:T(512)(128)(4,1)S(1)} %get-tuple-element.366) | copy-start | bytes 964
  783.3 206.9 %copy-start.65 = (f32[1,1024]{1,0:T(1,128)}, f32[1,1024]{1,0:T(1,128)S(1)}, u32[]{:S(2)}) copy-start(f32[1,1024]{1,0:T(1,128)S(1)} %get-tuple-element.330) | copy-start | bytes 12292
  785.5 21.9 all-to-all-start.2
  807.4 34.9 %all-to-all-start = ((bf16[4,160,1024]{2,1,0:T(8,128)(2,1)}), bf16[4,160,1024]{2,1,0:T(8,128)(2,1)}, u32[]{:S(2)}, u32[]{:S(2)}) async-start(bf16[4,160,1024]{2,1,0:T(8,128)(2,1)} %add_convert_fusion.5), calls=%async_computation | async-start | bytes 2621440 | tf_op jit(solution)/shard_map/all_to_all | solution.py:209
  941.7 31.8 %all-to-all-start.1 = ((bf16[4,160,1024]{2,1,0:T(8,128)(2,1)}), bf16[4,160,1024]{2,1,0:T(8,128)(2,1)S(1)}, u32[]{:S(2)}, u32[]{:S(2)}) async-start(bf16[4,160,1024]{2,1,0:T(8,128)(2,1)} %bitcast.394), calls=%async_computation.1 | async-start | bytes 2621440 | tf_op jit(solution)/shard_map/all_to_all | solution.py:235
  973.5 22.4 all-to-all-start.3
  1153.3 68.3 %all-to-all-start.4 = ((bf16[4,160,1024]{2,1,0:T(8,128)(2,1)}), bf16[4,160,1024]{2,1,0:T(8,128)(2,1)S(1)}, u32[]{:S(2)}, u32[]{:S(2)}) async-start(bf16[4,160,1024]{2,1,0:T(8,128)(2,1)} %bitcast.48), calls=%async_computation.4 | async-start | bytes 2621440 | tf_op jit(solution)/shard_map/all_to_all | solution.py:268
  1221.7 68.5 %all-to-all-start.6 = ((bf16[4,160,1024]{2,1,0:T(8,128)(2,1)}), bf16[4,160,1024]{2,1,0:T(8,128)(2,1)S(1)}, u32[]{:S(2)}, u32[]{:S(2)}) async-start(bf16[4,160,1024]{2,1,0:T(8,128)(2,1)} %bitcast.386), calls=%async_computation.6 | async-start | bytes 2621440 | tf_op jit(solution)/shard_map/all_to_all | solution.py:268
  1393.2 389.0 %all-to-all-start.5 = ((bf16[4,160,1024]{2,1,0:T(8,128)(2,1)}), bf16[4,160,1024]{2,1,0:T(8,128)(2,1)}, u32[]{:S(2)}, u32[]{:S(2)}) async-start(bf16[4,160,1024]{2,1,0:T(8,128)(2,1)} %bitcast.392), calls=%async_computation.5 | async-start | bytes 2621440 | tf_op jit(solution)/shard_map/all_to_all | solution.py:309
  1782.2 139.9 %all-to-all-start.7 = ((bf16[4,160,1024]{2,1,0:T(8,128)(2,1)}), bf16[4,160,1024]{2,1,0:T(8,128)(2,1)}, u32[]{:S(2)}, u32[]{:S(2)}) async-start(bf16[4,160,1024]{2,1,0:T(8,128)(2,1)} %bitcast.68), calls=%async_computation.7 | async-start | bytes 2621440 | tf_op jit(solution)/shard_map/all_to_all | solution.py:309
  1786.6 1308.1 %all-reduce.8.cloned.1.call-start = ((), (), s32[]{:S(2)}) async-start(), calls=%async_computation.13 | async-start | bytes 151150592
  1853.4 64.9 %copy-start.62 = (f32[1,1024]{1,0:T(1,128)S(1)}, f32[1,1024]{1,0:T(1,128)}, u32[]{:S(2)}) copy-start(f32[1,1024]{1,0:T(1,128)} %copy-done.61) | copy-start | bytes 12292
  1853.4 64.9 %copy-start.70 = (f32[4,160]{1,0:T(4,128)S(1)}, f32[4,160]{1,0:T(4,128)}, u32[]{:S(2)}) copy-start(f32[4,160]{1,0:T(4,128)} %div.141) | copy-start | bytes 7684
  1853.4 64.9 %copy-start.74 = (f32[4,160]{1,0:T(4,128)S(1)}, f32[4,160]{1,0:T(4,128)}, u32[]{:S(2)}) copy-start(f32[4,160]{1,0:T(4,128)} %copy-done.73) | copy-start | bytes 7684
  (113 other events, 1068.1 us)
Sparse Core Ops, SparseCore 0:
  10.9 98.8 all-gather.6
  112.7 67.8 all-gather.8
  183.4 54.8 all-gather.10
  241.0 76.3 all-gather.14
  320.1 76.0 all-gather.12
  2014.6 1080.0 all-reduce.7
where the time goes:
time: 3130 us; the launch traced here: 3120 us
  local copies, waits for them, and re-layouts  1140 us (36%)
  waiting for transfers between devices  1080 us (35%)
  matrix products  588 us (19%)
  other arithmetic  140 us (4%)
  blocking collectives  121 us (4%)
  starting transfers between devices  35.1 us (1%)
    unnamed x7, waiting for transfers between devices  1070 us
    gather x2, local copies, waits for them, and re-layouts, body(): jnp.take(bucket, relative_index(frames, strip_rows, window_side).reshape(...  567 us
    unnamed x278, local copies, waits for them, and re-layouts  117 us
    reshape x13, local copies, waits for them, and re-layouts, pack_rows(): element.reshape(devices, -1)  107 us
    dot_general x8, matrix products, contract_rows(): lax.dot_general(left_mat, right_mat, (((0,), (0,)), ((), ())), preferred_...  81 us
    dot_general x8, matrix products, contract_cols(): lax.dot_general(left_mat, right_mat, (((1,), (1,)), ((), ())), preferred_...  76.7 us
    dot_general x16, matrix products, add_group(): lax.dot_general(onehot, grad_rest, dims, preferred_element_type=jnp.float32)  67.8 us
    dot_general x16, matrix products, add_group(): lax.dot_general(onehot, grad_high, dims, preferred_element_type=jnp.float32)  67.6 us
  transfers between devices with their start and end apart: 14, of which 2 were waited for; matrix products, arithmetic and copies ran while one was open for 48% of the time, Pallas kernels for 0%

commit v1 on v0

v1 whole, which is shorter than its diff:
```python
import functools
import math

import jax
import jax.numpy as jnp
from jax import lax
from jax.experimental import pallas as pl
from jax.experimental.pallas import tpu as pltpu
from jax.sharding import PartitionSpec as P

HEADS = 16
EPSILON = 1e-06
MASKED = -1000000000.0
F32 = jnp.float32
BF16 = jnp.bfloat16
VMEM_LIMIT = 58 * 1024 * 1024
HIGHEST = lax.Precision.HIGHEST


def dot_nn(a, b):
    return lax.dot_general(a, b, (((1,), (0,)), ((), ())), preferred_element_type=F32)


def dot_nt(a, b):
    return lax.dot_general(a, b, (((1,), (1,)), ((), ())), preferred_element_type=F32)


def dot_tn(a, b):
    return lax.dot_general(a, b, (((0,), (0,)), ((), ())), preferred_element_type=F32)


def params(count):
    return pltpu.CompilerParams(
        dimension_semantics=("arbitrary",) * count, vmem_limit_bytes=VMEM_LIMIT
    )


def cost(flops, size):
    return pl.CostEstimate(flops=flops, bytes_accessed=size, transcendentals=0)


def once(shape, index_map):
    return pl.BlockSpec(shape, index_map, pipeline_mode=pl.Buffered(1))


def normalize(values):
    centered = values - jnp.mean(values, axis=-1, keepdims=True)
    inv = lax.rsqrt(jnp.mean(centered * centered, axis=-1, keepdims=True) + EPSILON)
    return centered * inv, inv


def norm_back(grad, normed, inv):
    return inv * (
        grad
        - jnp.mean(grad, axis=-1, keepdims=True)
        - normed * jnp.mean(grad * normed, axis=-1, keepdims=True)
    )


class Sizes:
    def __init__(self, tokens):
        self.micro, _, _, self.blocks, self.frames, rows, side, self.width = tokens.shape
        self.half = rows * side
        self.cols = self.blocks // 2
        self.strip_rows, self.side = rows, side
        self.used = 2 * self.frames - 1
        self.frame = 2 * self.half
        self.win_rows = self.used * self.frame
        self.rows = self.micro * self.win_rows
        self.lens = (self.frames * self.frame, (self.frames - 1) * self.frame)
        self.head = self.width // HEADS
        self.group = 4
        self.gcols = self.group * self.head
        self.groups = HEADS // self.group


def frame_rows(value):
    return value.reshape(-1, value.shape[-1])


def first_norm(tok, mod, core, sz):
    def kernel(sc_ref, x_ref, mod_ref, own_ref, far_ref):
        shift = mod_ref[0, 0:1, :]
        scale = 1.0 + mod_ref[0, 1:2, :]
        for slot, out_ref in enumerate((own_ref, far_ref)):
            column = sc_ref[0] ^ slot
            for tw in range(2):
                count = sz.frames - tw
                rows = frame_rows(x_ref[0, tw, column, :count].astype(F32))
                normed, _ = normalize(rows)
                hidden = (normed * scale + shift).astype(BF16)
                out_ref[0, tw * sz.frames : tw * sz.frames + count] = hidden.reshape(
                    count, sz.half, sz.width
                )

    strip = (1, 2, 2, sz.frames, sz.half, sz.width)
    piece = (1, sz.used, sz.half, sz.width)
    shape = jax.ShapeDtypeStruct((sz.micro,) + piece[1:], BF16)
    return pl.pallas_call(
        kernel,
        grid_spec=pltpu.PrefetchScalarGridSpec(
            num_scalar_prefetch=1,
            grid=(sz.micro,),
            in_specs=[
                pl.BlockSpec(strip, lambda m, s: (m, 0, 0, 0, 0, 0)),
                pl.BlockSpec((1, 6, sz.width), lambda m, s: (m, 0, 0)),
            ],
            out_specs=[pl.BlockSpec(piece, lambda m, s: (m, 0, 0, 0))] * 2,
        ),
        out_shape=[shape, shape],
        compiler_params=params(1),
        name="first_norm",
    )(core, tok, mod)


def valid_rows(tw, count, length, sz):
    frame = tw * sz.frames + lax.broadcasted_iota(jnp.int32, (count * sz.half, 1), 0) // sz.half
    return (frame < length).astype(F32)


def second_norm(tok, cot, branch_own, branch_far, mod, scalars, sz):
    def kernel(sc_ref, x_ref, c_ref, bo_ref, bf_ref, mod_ref, h_ref, g_ref):
        length = sc_ref[1 + pl.program_id(0)]
        gate1 = mod_ref[0, 2:3, :]
        shift = mod_ref[0, 3:4, :]
        scale = 1.0 + mod_ref[0, 4:5, :]
        gate2 = mod_ref[0, 5:6, :]
        for slot, b_ref in enumerate((bo_ref, bf_ref)):
            column = sc_ref[0] ^ slot
            for tw in range(2):
                count = sz.frames - tw
                span = slice(tw * sz.frames, tw * sz.frames + count)
                rows = frame_rows(x_ref[0, tw, column, :count].astype(F32))
                branch = frame_rows(b_ref[0, span].astype(F32))
                normed, _ = normalize(rows + gate1 * branch)
                h_ref[slot, 0, span] = (
                    (normed * scale + shift).astype(BF16).reshape(count, sz.half, sz.width)
                )
                grad = frame_rows(c_ref[0, tw, column, :count].astype(F32))
                grad = grad * valid_rows(tw, count, length, sz) * gate2
                g_ref[slot, 0, span] = grad.astype(BF16).reshape(count, sz.half, sz.width)

    strip = (1, 2, 2, sz.frames, sz.half, sz.width)
    piece = (1, sz.used, sz.half, sz.width)
    both = (2, 1, sz.used, sz.half, sz.width)
    shape = jax.ShapeDtypeStruct((2, sz.micro, sz.used, sz.half, sz.width), BF16)
    return pl.pallas_call(
        kernel,
        grid_spec=pltpu.PrefetchScalarGridSpec(
            num_scalar_prefetch=1,
            grid=(sz.micro,),
            in_specs=[
                pl.BlockSpec(strip, lambda m, s: (m, 0, 0, 0, 0, 0)),
                pl.BlockSpec(strip, lambda m, s: (m, 0, 0, 0, 0, 0)),
                pl.BlockSpec(piece, lambda m, s: (m, 0, 0, 0)),
                pl.BlockSpec(piece, lambda m, s: (m, 0, 0, 0)),
                pl.BlockSpec((1, 6, sz.width), lambda m, s: (m, 0, 0)),
            ],
            out_specs=[pl.BlockSpec(both, lambda m, s: (0, m, 0, 0, 0))] * 2,
        ),
        out_shape=[shape, shape],
        compiler_params=params(1),
        name="second_norm",
    )(scalars, tok, cot, branch_own, branch_far, mod)


def after_mlp(tok, cot, branch_own, branch_far, mlps, grads, mod, b_down, scalars, sz):
    def kernel(
        sc_ref, x_ref, c_ref, bo_ref, bf_ref, y0_ref, y1_ref, t0_ref, t1_ref, mod_ref, bd_ref,
        out_ref, gm_ref, go_ref, gf_ref, sum_ref,
    ):
        length = sc_ref[1 + pl.program_id(0)]
        gate1 = mod_ref[0, 2:3, :]
        scale = 1.0 + mod_ref[0, 4:5, :]
        gate2 = mod_ref[0, 5:6, :]
        sums = [jnp.zeros((1, sz.width), F32) for _ in range(4)]
        for slot, (b_ref, g_ref) in enumerate(((bo_ref, go_ref), (bf_ref, gf_ref))):
            column = sc_ref[0] ^ slot
            for tw in range(2):
                count = sz.frames - tw
                span = slice(tw * sz.frames, tw * sz.frames + count)
                shape = (count, sz.half, sz.width)
                valid = valid_rows(tw, count, length, sz)
                branch = frame_rows(b_ref[0, span].astype(F32))
                middle = frame_rows(x_ref[0, tw, column, :count].astype(F32)) + gate1 * branch
                normed, inv = normalize(middle)
                y = frame_rows(y0_ref[slot, 0, span] + y1_ref[slot, 0, span]) + bd_ref[0:1, :]
                grad = frame_rows(c_ref[0, tw, column, :count].astype(F32))
                out_ref[0, tw, column, :count] = (
                    (middle + valid * gate2 * y).astype(BF16).reshape(shape)
                )
                two = frame_rows(t0_ref[slot, 0, span] + t1_ref[slot, 0, span])
                gm = grad + norm_back(two * scale, normed, inv)
                gm_ref[slot, 0, span] = gm.reshape(shape)
                g_ref[0, span] = (valid * (gm * gate1)).astype(BF16).reshape(shape)
                for n, term in enumerate((two, two * normed, grad * valid * y, gm * branch)):
                    sums[n] = sums[n] + jnp.sum(term, axis=0, keepdims=True)
            out_ref[0, 1, column, sz.frames - 1] = x_ref[0, 1, column, sz.frames - 1]
        for n in range(4):
            sum_ref[0, n : n + 1, :] = sums[n]

    strip = (1, 2, 2, sz.frames, sz.half, sz.width)
    piece = (1, sz.used, sz.half, sz.width)
    both = (2, 1, sz.used, sz.half, sz.width)
    full = (sz.micro,) + piece[1:]
    at_strip = lambda m, s: (m, 0, 0, 0, 0, 0)
    at_piece = lambda m, s: (m, 0, 0, 0)
    at_both = lambda m, s: (0, m, 0, 0, 0)
    return pl.pallas_call(
        kernel,
        grid_spec=pltpu.PrefetchScalarGridSpec(
            num_scalar_prefetch=1,
            grid=(sz.micro,),
            in_specs=[
                pl.BlockSpec(strip, at_strip),
                pl.BlockSpec(strip, at_strip),
                pl.BlockSpec(piece, at_piece),
                pl.BlockSpec(piece, at_piece),
                pl.BlockSpec(both, at_both),
                pl.BlockSpec(both, at_both),
                pl.BlockSpec(both, at_both),
                pl.BlockSpec(both, at_both),
                pl.BlockSpec((1, 6, sz.width), lambda m, s: (m, 0, 0)),
                pl.BlockSpec((1, sz.width), lambda m, s: (0, 0)),
            ],
            out_specs=[
                pl.BlockSpec(strip, at_strip),
                pl.BlockSpec(both, at_both),
                pl.BlockSpec(piece, at_piece),
                pl.BlockSpec(piece, at_piece),
                pl.BlockSpec((1, 4, sz.width), lambda m, s: (m, 0, 0)),
            ],
        ),
        out_shape=[
            jax.ShapeDtypeStruct(tok.shape, BF16),
            jax.ShapeDtypeStruct((2,) + full, F32),
            jax.ShapeDtypeStruct(full, BF16),
            jax.ShapeDtypeStruct(full, BF16),
            jax.ShapeDtypeStruct((sz.micro, 4, sz.width), F32),
        ],
        compiler_params=params(1),
        name="after_mlp",
    )(scalars, tok, cot, branch_own, branch_far, *mlps, *grads, mod, b_down)


def last_norm(tok, cot, grad_mid, grad_own, grad_far, mod, scalars, sz):
    def kernel(sc_ref, x_ref, c_ref, gm_ref, go_ref, gf_ref, mod_ref, out_ref, sum_ref):
        scale = 1.0 + mod_ref[0, 1:2, :]
        sums = [jnp.zeros((1, sz.width), F32) for _ in range(2)]
        for slot, g_ref in enumerate((go_ref, gf_ref)):
            column = sc_ref[0] ^ slot
            for tw in range(2):
                count = sz.frames - tw
                span = slice(tw * sz.frames, tw * sz.frames + count)
                normed, inv = normalize(frame_rows(x_ref[0, tw, column, :count].astype(F32)))
                one = frame_rows(g_ref[0, span].astype(F32))
                grad = frame_rows(gm_ref[slot, 0, span]) + norm_back(one * scale, normed, inv)
                out_ref[0, tw, column, :count] = grad.astype(BF16).reshape(
                    count, sz.half, sz.width
                )
                for n, term in enumerate((one, one * normed)):
                    sums[n] = sums[n] + jnp.sum(term, axis=0, keepdims=True)
        for slot in range(2):
            out_ref[0, 1, slot, sz.frames - 1] = c_ref[0, 0, slot, 0]
        for n in range(2):
            sum_ref[0, n : n + 1, :] = sums[n]

    strip = (1, 2, 2, sz.frames, sz.half, sz.width)
    tail = (1, 1, 2, 1, sz.half, sz.width)
    piece = (1, sz.used, sz.half, sz.width)
    both = (2, 1, sz.used, sz.half, sz.width)
    return pl.pallas_call(
        kernel,
        grid_spec=pltpu.PrefetchScalarGridSpec(
            num_scalar_prefetch=1,
            grid=(sz.micro,),
            in_specs=[
                pl.BlockSpec(strip, lambda m, s: (m, 0, 0, 0, 0, 0)),
                pl.BlockSpec(tail, lambda m, s: (m, 1, 0, sz.frames - 1, 0, 0)),
                pl.BlockSpec(both, lambda m, s: (0, m, 0, 0, 0)),
                pl.BlockSpec(piece, lambda m, s: (m, 0, 0, 0)),
                pl.BlockSpec(piece, lambda m, s: (m, 0, 0, 0)),
                pl.BlockSpec((1, 6, sz.width), lambda m, s: (m, 0, 0)),
            ],
            out_specs=[
                pl.BlockSpec(strip, lambda m, s: (m, 0, 0, 0, 0, 0)),
                pl.BlockSpec((1, 2, sz.width), lambda m, s: (m, 0, 0)),
            ],
        ),
        out_shape=[
            jax.ShapeDtypeStruct(tok.shape, BF16),
            jax.ShapeDtypeStruct((sz.micro, 2, sz.width), F32),
        ],
        compiler_params=params(1),
        name="last_norm",
    )(scalars, tok, cot, grad_mid, grad_own, grad_far, mod)


class Pieces:
    def __init__(self, arrays):
        self.arrays = arrays
        self.whole = len(arrays) == 1

    def specs(self, columns, index_map):
        if self.whole:
            at = lambda *g: (0, index_map(*g))
            return [pl.BlockSpec((self.arrays[0].shape[0], columns), at)]
        at = lambda *g: (0, 0, 0, 0, index_map(*g))
        shape = self.arrays[0].shape[:-1] + (columns,)
        return [pl.BlockSpec(shape, at)] * 4

    def row_specs(self, columns, row_map, block):
        shape = self.arrays[0].shape[:2] + (1,) + self.arrays[0].shape[3:4] + (columns,)
        return [pl.BlockSpec(shape, lambda *g: (0, 0, row_map(*g), 0, block))] * 4


def place(refs, key, out_ref, columns, pitch=None, offset=0):
    depth, cut = refs[0].shape[2:4]
    pitch = 2 * cut if pitch is None else pitch
    for n, ref in enumerate(refs):
        half, far = n // 2, n % 2
        for i in range(2):
            for j in range(2):
                away = (i * 4 + j * 2 if half == 0 else j * 4 + i * 2) + far
                at = (key ^ away) * pitch + offset + half * cut
                for z in range(depth):
                    rows = pl.ds(pl.multiple_of(z * 8 * pitch + at, cut), cut)
                    out_ref[rows, columns] = ref[i, j, z]


def hand_out(value, start, rows, core, keep_ref, send_ref):
    for parity in range(2):
        for own, ref in ((0, keep_ref), (1, send_ref)):

            @pl.when(core == parity ^ own)
            def _(parity=parity, ref=ref):
                for low in range(parity * rows, value.shape[0], 2 * rows):
                    ref[(start + low) // (2 * rows)] = value[low : low + rows].astype(BF16)


def join_frames(own_ref, far_ref, joined_ref, sz):
    for m in range(sz.micro):
        for f in range(sz.used):
            at = m * sz.win_rows + f * sz.frame
            joined_ref[at : at + sz.half] = own_ref[m, f]
            joined_ref[at + sz.half : at + sz.frame] = far_ref[m, f]


def spread_bias(block_ref, head, bias_ref, sz):
    full = sz.lens[0]
    for t in range(sz.frames):
        low = (sz.frames - 1 - t) * sz.frame
        bias_ref[t * sz.frame : (t + 1) * sz.frame, :] = block_ref[head, :, low : low + full]


def window_rows(m, tw, sz):
    start = pl.multiple_of(m * sz.win_rows + tw * sz.lens[0], sz.frame)
    return pl.ds(start, sz.lens[tw])


def attention(half, own, far, w_qkv, bias, scalars, sz, att_first=None, w_out=None):
    scale = 1.0 / math.sqrt(sz.head)
    last = w_out is not None
    steps = sz.groups // 2
    direct = not w_qkv.whole
    gcols = sz.gcols

    def kernel(sc_ref, own_ref, far_ref, bias_ref, *refs):
        refs = list(refs)
        take = lambda count: [refs.pop(0) for _ in range(count)]
        w_refs = take(len(w_qkv.arrays))
        if last:
            (first_ref,) = take(1)
            out_refs = take(8 if direct else 1)
        qkv_ref, att_ref, w_ref = take(3)
        if last:
            wo_ref, bo_ref, bf_ref = take(3)
        joined, spread = take(2)
        step = pl.program_id(0)
        key = sc_ref[1 + sz.micro]

        @pl.when(step == 0)
        def _():
            join_frames(own_ref, far_ref, joined, sz)

        if direct:
            place(w_refs, key, w_ref, slice(None))
        else:
            w_ref[...] = w_refs[0][...]
        for n in range(3):
            part = dot_nn(joined[...], w_ref[:, n * gcols : (n + 1) * gcols]).astype(BF16)
            qkv_ref[n] = part * scale if n == 0 else part
        for head in range(sz.group):
            lanes = slice(head * sz.head, (head + 1) * sz.head)
            spread_bias(bias_ref, head, spread, sz)

            def one_micro(m, carry, lanes=lanes):
                for tw in range(2):
                    size = sz.lens[tw]
                    rows = window_rows(m, tw, sz)
                    keys_ok = (sc_ref[1 + m] - tw * sz.frames) * sz.frame

                    @pl.when(keys_ok > 0)
                    def _(rows=rows, size=size, keys_ok=keys_ok):
                        scores = dot_nt(qkv_ref[0, rows, lanes], qkv_ref[1, rows, lanes])
                        scores = scores + spread[:size, :size].astype(F32)
                        column = lax.broadcasted_iota(jnp.int32, (1, size), 1)
                        scores = jnp.where(column < keys_ok, scores, MASKED)
                        top = jnp.max(scores, axis=-1, keepdims=True)
                        weight = jnp.exp(scores - top)
                        share = 1.0 / jnp.sum(weight, axis=-1, keepdims=True)
                        probs = (weight * share).astype(BF16)
                        att_ref[rows, lanes] = dot_nn(probs, qkv_ref[2, rows, lanes]).astype(BF16)

                    @pl.when(keys_ok <= 0)
                    def _(rows=rows, size=size):
                        att_ref[rows, lanes] = jnp.zeros((size, sz.head), BF16)

                return carry

            lax.fori_loop(0, sz.micro, one_micro, 0)
        if not last:
            return
        kept, total = take(2)
        for n in range(steps):

            @pl.when(step == n)
            def _(n=n):
                kept[:, n * gcols : (n + 1) * gcols] = att_ref[...]

        @pl.when(step == steps - 1)
        def _():
            if direct:
                place(out_refs[:4], key, wo_ref, slice(0, 2 * gcols))
                place(out_refs[4:], key, wo_ref, slice(2 * gcols, 4 * gcols))
            else:
                wo_ref[...] = out_refs[0][...]
            middle = first_ref.shape[1]
            total[...] = dot_nn(first_ref[...], wo_ref[:middle]) + dot_nn(
                kept[...], wo_ref[middle:]
            )
            for m in range(sz.micro):
                for f in range(sz.used):
                    at = m * sz.win_rows + f * sz.frame
                    valid = (f < sc_ref[1 + m]).astype(F32)
                    bo_ref[m, f] = (total[at : at + sz.half] * valid).astype(BF16)
                    bf_ref[m, f] = (total[at + sz.half : at + sz.frame] * valid).astype(BF16)

    piece = (sz.micro, sz.used, sz.half, sz.width)
    fixed = lambda g, s: (0, 0, 0, 0)
    flat = lambda g, s: (0, 0)
    width, cols = sz.width, sz.width // 2
    in_specs = [
        once(piece, fixed),
        once(piece, fixed),
        pl.BlockSpec((sz.group,) + bias.shape[1:], lambda g, s: (half * steps + g, 0, 0)),
    ] + w_qkv.specs(3 * gcols, lambda g, s: g)
    out_specs = [
        pl.BlockSpec((3, sz.rows, gcols), lambda g, s: (0, 0, g)),
        pl.BlockSpec((sz.rows, gcols), lambda g, s: (0, g)),
        pl.BlockSpec((width, 3 * gcols), lambda g, s: (0, g)),
    ]
    out_shape = [
        jax.ShapeDtypeStruct((3, sz.rows, cols), BF16),
        jax.ShapeDtypeStruct((sz.rows, cols), BF16),
        jax.ShapeDtypeStruct((width, 3 * cols), BF16),
    ]
    scratch = [
        pltpu.VMEM((sz.rows, width), BF16),
        pltpu.VMEM((sz.lens[0], sz.lens[0]), BF16),
    ]
    args = [scalars, own, far, bias, *w_qkv.arrays]
    flops = 6 * sz.rows * width * cols + 4 * sz.rows * sz.lens[0] * cols
    if last:
        in_specs += [once((sz.rows, cols), flat)]
        if direct:
            low = w_out.arrays[0].shape[-1] // (2 * gcols) - 2
            in_specs += w_out.specs(2 * gcols, lambda g, s: low)
            in_specs += w_out.specs(2 * gcols, lambda g, s: low + 1)
            out_args = w_out.arrays * 2
        else:
            in_specs += w_out.specs(width, lambda g, s: 0)
            out_args = w_out.arrays
        out_specs += [pl.BlockSpec((width, width), flat)] + [pl.BlockSpec(piece, fixed)] * 2
        out_shape += [jax.ShapeDtypeStruct((width, width), BF16)]
        out_shape += [jax.ShapeDtypeStruct(piece, BF16)] * 2
        scratch += [pltpu.VMEM((sz.rows, cols), BF16), pltpu.VMEM((sz.rows, width), F32)]
        args += [att_first, *out_args]
        flops += 2 * sz.rows * width * width
    return pl.pallas_call(
        kernel,
        grid_spec=pltpu.PrefetchScalarGridSpec(
            num_scalar_prefetch=1,
            grid=(steps,),
            in_specs=in_specs,
            out_specs=out_specs,
            scratch_shapes=scratch,
        ),
        out_shape=out_shape,
        compiler_params=params(1),
        cost_estimate=cost(3 * flops, 16 * sz.rows * width),
        name="attention" + "_last" * last,
    )(*args)


def grad_shapes(direct, rows, width, columns, sz):
    if not direct:
        return [jax.ShapeDtypeStruct((width, columns), BF16)]
    return [jax.ShapeDtypeStruct((width // (2 * rows), rows, columns), BF16)] * 2


def grad_specs(direct, rows, width, columns, at_row, at_column):
    if not direct:
        return [pl.BlockSpec((width, columns), lambda *g: (at_row(*g), at_column(*g)))]
    shape = (width // (2 * rows), rows, columns)
    return [pl.BlockSpec(shape, lambda *g: (at_row(*g), 0, at_column(*g)))] * 2


def attention_back(half, grad_own, grad_far, own, far, qkv, atts, w_qkv, w_out, bias_t, scalars, sz, shard, carry=None):
    scale = 1.0 / math.sqrt(sz.head)
    last = carry is not None
    steps = sz.groups // 2
    direct = shard is not None
    outs = 2 if direct else 1
    gcols, width = sz.gcols, sz.width
    quarter = width // 4

    def kernel(
        sc_ref, go_ref, gf_ref, own_ref, far_ref, qkv_ref, w_ref, wo_ref, bias_ref, *refs
    ):
        refs = list(refs)
        take = lambda count: [refs.pop(0) for _ in range(count)]
        if last:
            (carry_ref,) = take(1)
        else:
            att_refs = take(2)
        gw_refs = take(outs)
        (fold_ref,) = take(1)
        if last:
            ho_ref, hf_ref = take(2)
        else:
            gwo_refs = take(outs)
            (total,) = take(1)
        grad, hidden_t, grad_att, parts, spread, pair_sum = take(6)
        if last:
            (total,) = take(1)
        step = pl.program_id(0)

        def give(value, start, refs):
            if direct:
                hand_out(value, start, shard, sc_ref[0], *refs)
            else:
                refs[0][start : start + value.shape[0]] = value.astype(BF16)

        @pl.when(step == 0)
        def _():
            join_frames(own_ref, far_ref, grad, sz)
            hidden_t[...] = grad[...].T
            join_frames(go_ref, gf_ref, grad, sz)
            if last:
                total[...] = carry_ref[...]
            else:
                total[...] = jnp.zeros_like(total)

        grad_att[...] = dot_nt(grad[...], wo_ref[...]).astype(BF16)
        full = sz.lens[0]
        for head in range(sz.group):
            lanes = slice(head * sz.head, (head + 1) * sz.head)
            spread_bias(bias_ref, head, spread, sz)
            pair_sum[...] = jnp.zeros((full, full), F32)

            def one_micro(m, carry, head=head, lanes=lanes):
                for tw in range(2):
                    size = sz.lens[tw]
                    rows = window_rows(m, tw, sz)
                    keys_ok = (sc_ref[1 + m] - tw * sz.frames) * sz.frame
                    spot = [
                        slice(n * gcols + head * sz.head, n * gcols + (head + 1) * sz.head)
                        for n in range(3)
                    ]

                    @pl.when(keys_ok > 0)
                    def _(rows=rows, size=size, keys_ok=keys_ok, spot=spot):
                        query = qkv_ref[0, rows, lanes]
                        key = qkv_ref[1, rows, lanes]
                        value = qkv_ref[2, rows, lanes]
                        grad_out = grad_att[rows, lanes]
                        scores = dot_nt(key, query) + spread[:size, :size].astype(F32)
                        row = lax.broadcasted_iota(jnp.int32, (size, 1), 0)
                        scores = jnp.where(row < keys_ok, scores, MASKED)
                        weight = jnp.exp(scores - jnp.max(scores, axis=0, keepdims=True))
                        probs = weight * (1.0 / jnp.sum(weight, axis=0, keepdims=True))
                        grad_probs = dot_nt(value, grad_out)
                        inner = jnp.sum(probs * grad_probs, axis=0, keepdims=True)
                        grad_scores = (probs * (grad_probs - inner)).astype(BF16)
                        pair_sum[:size, :size] += grad_scores.astype(F32)
                        parts[rows, spot[2]] = dot_nn(probs.astype(BF16), grad_out).astype(BF16)
                        parts[rows, spot[1]] = dot_nn(grad_scores, query).astype(BF16)
                        parts[rows, spot[0]] = (dot_tn(grad_scores, key) * scale).astype(BF16)

                    @pl.when(keys_ok <= 0)
                    def _(rows=rows, size=size, spot=spot):
                        for n in range(3):
                            parts[rows, spot[n]] = jnp.zeros((size, sz.head), BF16)

                return carry

            lax.fori_loop(0, sz.micro, one_micro, 0)
            fold_ref[head] = jnp.zeros(fold_ref.shape[1:], F32)
            for t in range(sz.frames):
                low = (sz.frames - 1 - t) * sz.frame
                fold_ref[head, :, low : low + full] += pair_sum[
                    t * sz.frame : (t + 1) * sz.frame, :
                ]
        for n in range(4):
            rows = slice(n * quarter, (n + 1) * quarter)
            give(dot_nn(hidden_t[rows, :], parts[...]), n * quarter, gw_refs)
        total[...] += dot_nt(parts[...], w_ref[...])
        if not last:
            for n, a_ref in enumerate(att_refs):

                @pl.when(step == n)
                def _(a_ref=a_ref):
                    for k in range(2):
                        columns = slice(k * quarter, (k + 1) * quarter)
                        give(dot_tn(a_ref[:, columns], grad[...]), k * quarter, gwo_refs)

            return

        @pl.when(step == steps - 1)
        def _():
            for m in range(sz.micro):
                for f in range(sz.used):
                    at = m * sz.win_rows + f * sz.frame
                    ho_ref[m, f] = total[at : at + sz.half].astype(BF16)
                    hf_ref[m, f] = total[at + sz.half : at + sz.frame].astype(BF16)

    piece = (sz.micro, sz.used, sz.half, width)
    fixed = lambda g, s: (0, 0, 0, 0)
    flat = lambda g, s: (0, 0)
    cols = width // 2
    block_bias = (sz.group,) + bias_t.shape[1:]
    in_specs = [
        once(piece, fixed),
        once(piece, fixed),
        once(piece, fixed),
        once(piece, fixed),
        pl.BlockSpec((3, sz.rows, gcols), lambda g, s: (0, 0, g)),
        pl.BlockSpec((width, 3 * gcols), lambda g, s: (0, g)),
        pl.BlockSpec((gcols, width), lambda g, s: (half * steps + g, 0)),
        pl.BlockSpec(block_bias, lambda g, s: (half * steps + g, 0, 0)),
    ]
    zero = lambda g, s: 0
    along = lambda g, s: g
    out_specs = grad_specs(direct, shard, width, 3 * gcols, zero, along)
    out_specs += [pl.BlockSpec(block_bias, lambda g, s: (g, 0, 0))]
    out_shape = grad_shapes(direct, shard, width, 3 * cols, sz)
    out_shape += [jax.ShapeDtypeStruct((HEADS // 2,) + bias_t.shape[1:], F32)]
    scratch = [
        pltpu.VMEM((sz.rows, width), BF16),
        pltpu.VMEM((width, sz.rows), BF16),
        pltpu.VMEM((sz.rows, gcols), BF16),
        pltpu.VMEM((sz.rows, 3 * gcols), BF16),
        pltpu.VMEM((sz.lens[0], sz.lens[0]), BF16),
        pltpu.VMEM((sz.lens[0], sz.lens[0]), F32),
    ]
    args = [scalars, grad_own, grad_far, own, far, qkv, w_qkv, w_out, bias_t]
    flops = 14 * sz.rows * width * cols + 10 * sz.rows * sz.lens[0] * cols
    if last:
        in_specs += [once((sz.rows, width), flat)]
        out_specs += [pl.BlockSpec(piece, fixed)] * 2
        out_shape += [jax.ShapeDtypeStruct(piece, BF16)] * 2
        scratch += [pltpu.VMEM((sz.rows, width), F32)]
        args += [carry]
    else:
        in_specs += [once((sz.rows, cols), flat)] * 2
        out_specs += grad_specs(direct, shard, cols, width, along, zero)
        out_specs += [once((sz.rows, width), flat)]
        out_shape += grad_shapes(direct, shard, width, width, sz)
        out_shape += [jax.ShapeDtypeStruct((sz.rows, width), F32)]
        args += list(atts)
        flops += 2 * sz.rows * width * width
    return pl.pallas_call(
        kernel,
        grid_spec=pltpu.PrefetchScalarGridSpec(
            num_scalar_prefetch=1,
            grid=(steps,),
            in_specs=in_specs,
            out_specs=out_specs,
            scratch_shapes=scratch,
        ),
        out_shape=out_shape,
        compiler_params=params(1),
        cost_estimate=cost(3 * flops, 24 * sz.rows * width),
        name="attention_back" + "_last" * last,
    )(*args)


GELU_A = math.sqrt(2.0 / math.pi)
GELU_B = 0.044715


def mlp(hidden, grad, w_up, b_up, w_down, scalars, sz, shards):
    chunk = 512
    tiles = 3
    tile = sz.rows // tiles
    inner = b_up.shape[1]
    steps = inner // chunk
    direct = shards is not None
    outs = 2 if direct else 1
    rows, width = sz.rows, sz.width
    quarter = width // 4

    def kernel(sc_ref, h_ref, g_ref, bu_ref, *refs):
        refs = list(refs)
        take = lambda count: [refs.pop(0) for _ in range(count)]
        up_refs = take(4 if direct else 1)
        down_refs = take(8 if direct else 1)
        y_ref, t_ref, gbu_ref, gbd_ref = take(4)
        gwu_refs, gwd_refs = take(outs), take(outs)
        hidden_t, act_s, gpre_s = take(3)
        if direct:
            wu_ref, wd_ref = take(2)
        else:
            wu_ref, wd_ref = up_refs[0], down_refs[0]
        step = pl.program_id(0)

        def give(value, start, shard, refs):
            if direct:
                hand_out(value, start, shard, sc_ref[0], *refs)
            else:
                refs[0][start : start + value.shape[0]] = value.astype(BF16)

        @pl.when(step == 0)
        def _():
            hidden_t[...] = h_ref[...].T
            gbd_ref[...] = jnp.sum(g_ref[...].astype(F32), axis=0, keepdims=True)
            y_ref[...] = jnp.zeros_like(y_ref)
            t_ref[...] = jnp.zeros_like(t_ref)

        if direct:
            key = sc_ref[1 + sz.micro]
            place(up_refs, key, wu_ref, slice(None))
            for part in range(2):
                refs_part = down_refs[4 * part : 4 * part + 4]
                place(refs_part, key, wd_ref, slice(None), shards[1], part * shards[0])
        bias_sum = jnp.zeros((1, chunk), F32)
        for n in range(tiles):
            span = slice(n * tile, (n + 1) * tile)
            pre = dot_nn(h_ref[span], wu_ref[...]) + bu_ref[...]
            grad_act = dot_nt(g_ref[span], wd_ref[...])
            square = pre * pre
            tanh = jnp.tanh(GELU_A * pre * (1.0 + GELU_B * square))
            half = 0.5 * (1.0 + tanh)
            act = (pre * half).astype(BF16)
            slope = half + (0.5 * GELU_A) * pre * (1.0 - tanh * tanh) * (
                1.0 + (3.0 * GELU_B) * square
            )
            grad_pre = (grad_act * slope).astype(BF16)
            act_s[span] = act
            gpre_s[span] = grad_pre
            bias_sum = bias_sum + jnp.sum(grad_pre.astype(F32), axis=0, keepdims=True)
            y_ref[span] += dot_nn(act, wd_ref[...])
            t_ref[span] += dot_nt(grad_pre, wu_ref[...])
        gbu_ref[...] = bias_sum
        for n in range(4):
            span = slice(n * quarter, (n + 1) * quarter)
            give(dot_nn(hidden_t[span, :], gpre_s[...]), n * quarter, shards and shards[0], gwu_refs)
        for n in range(2):
            span = slice(n * quarter, (n + 1) * quarter)
            give(dot_tn(act_s[:, span], g_ref[...]), n * quarter, shards and shards[1], gwd_refs)

    fixed = lambda j, s: (0, 0)
    zero = lambda j, s: 0
    along = lambda j, s: j
    in_specs = [
        once((rows, width), fixed),
        once((rows, width), fixed),
        pl.BlockSpec((1, chunk), lambda j, s: (0, j)),
    ] + w_up.specs(chunk, along)
    args = [scalars, hidden, grad, b_up, *w_up.arrays]
    if direct:
        low = w_down.arrays[0].shape[-1] // width - 2
        for part in range(2):
            in_specs += w_down.row_specs(width, along, low + part)
            args += w_down.arrays
    else:
        in_specs += [pl.BlockSpec((chunk, width), lambda j, s: (j, 0))]
        args += w_down.arrays
    out_specs = [
        pl.BlockSpec((rows, width), fixed),
        pl.BlockSpec((rows, width), fixed),
        pl.BlockSpec((1, chunk), lambda j, s: (0, j)),
        pl.BlockSpec((1, width), fixed),
    ]
    out_specs += grad_specs(direct, shards and shards[0], width, chunk, zero, along)
    out_specs += grad_specs(direct, shards and shards[1], chunk, width, along, zero)
    out_shape = [
        jax.ShapeDtypeStruct((rows, width), F32),
        jax.ShapeDtypeStruct((rows, width), F32),
        jax.ShapeDtypeStruct((1, inner), F32),
        jax.ShapeDtypeStruct((1, width), F32),
    ]
    out_shape += grad_shapes(direct, shards and shards[0], width, inner, sz)
    out_shape += grad_shapes(direct, shards and shards[1], inner, width, sz)
    scratch = [
        pltpu.VMEM((width, rows), BF16),
        pltpu.VMEM((rows, chunk), BF16),
        pltpu.VMEM((rows, chunk), BF16),
    ]
    if direct:
        scratch += [pltpu.VMEM((width, chunk), BF16), pltpu.VMEM((chunk, width), BF16)]
    return pl.pallas_call(
        kernel,
        grid_spec=pltpu.PrefetchScalarGridSpec(
            num_scalar_prefetch=1,
            grid=(steps,),
            in_specs=in_specs,
            out_specs=out_specs,
            scratch_shapes=scratch,
        ),
        out_shape=out_shape,
        compiler_params=params(1),
        cost_estimate=cost(14 * rows * width * inner, 16 * rows * width),
        name="mlp",
    )(*args)


def offset_onehot(core, sz):
    span = 2 * sz.side - 1
    place = jnp.arange(sz.frame, dtype=jnp.int32)
    row = ((place // sz.half) ^ core) * sz.strip_rows + place // sz.side % sz.strip_rows
    column = place % sz.side
    index = (row[:, None] - row[None, :] + sz.side - 1) * span
    index = index + column[:, None] - column[None, :] + sz.side - 1
    return (jnp.arange(span * span, dtype=jnp.int32)[:, None, None] == index[None]).astype(BF16)


def bucket_onehot(bucket, count):
    return (jnp.arange(count, dtype=jnp.int32)[:, None] == bucket[None, :]).astype(BF16)


def bias_blocks(table, bucket, places, sz):
    steps = 2 * sz.frames - 1
    by_offset = dot_tn(table, bucket_onehot(bucket, table.shape[0])).astype(BF16)
    by_offset = by_offset.reshape(HEADS, steps, -1)
    shape = (HEADS, sz.frame, steps * sz.frame)
    forward = jnp.einsum("hkj,jpq->hpkq", by_offset[:, ::-1], places, preferred_element_type=F32)
    backward = jnp.einsum("hkj,jpq->hqkp", by_offset, places, preferred_element_type=F32)
    return forward.astype(BF16).reshape(shape), backward.astype(BF16).reshape(shape)


def split_low(value):
    high = value.astype(BF16)
    return high, (value - high.astype(F32)).astype(BF16)


def table_grad(fold, bucket, places, buckets, sz):
    steps = 2 * sz.frames - 1
    fold = fold.reshape(HEADS, sz.frame, steps, sz.frame)
    by_offset = sum(
        jnp.einsum("hqkp,jpq->hkj", part, places, preferred_element_type=F32)
        for part in split_low(fold)
    ).reshape(HEADS, -1)
    onehot = bucket_onehot(bucket, buckets)
    return sum(dot_nt(onehot, part) for part in split_low(by_offset))


class Net:
    AXES = ("clip", "win")
    X, Y, CORE = 2, 4, 1

    def __init__(self):
        self.count = lax.axis_size(self.AXES)
        self.direct = lax.axis_size("win") == 4 and self.count == 32
        self.deep = self.count // 8
        self.index = lax.axis_index(self.AXES)
        self.z = self.index // 8

    def bit(self, which):
        return self.index // which % 2

    def swap(self, value, which):
        return lax.ppermute(value, self.AXES, [(n, n ^ which) for n in range(self.count)])

    def from_z(self, value, step):
        move = lambda n: (n // 8 - step) % self.deep * 8 + n % 8
        return lax.ppermute(value, self.AXES, [(n, move(n)) for n in range(self.count)])

    def swap_sum(self, value, which):
        return value + self.swap(value, which)


    def gather_clips(self, value):
        along = jnp.stack([value] + [self.from_z(value, k) for k in range(1, self.deep)])
        return jnp.stack([along, self.swap(along, self.Y)], axis=1)

    def scatter_clips(self, value):
        kept = value[:, 0] + self.swap(value[:, 1], self.Y)
        return kept[0] + sum(
            self.from_z(kept[self.deep - k], k) for k in range(1, self.deep)
        )

    def sum_all(self, value):
        for which in (self.CORE, self.X, self.Y):
            value = self.swap_sum(value, which)
        return value + sum(self.from_z(value, k) for k in range(1, self.deep))

    def gather_small(self, value):
        parts = self.gather_clips(value)
        for which in (self.X, self.CORE):
            parts = jnp.stack([parts, self.swap(parts, which)], axis=2 if which == self.X else 3)
        parts = parts.reshape(self.count, -1)
        place = jnp.arange(self.count, dtype=jnp.int32)
        holder = (self.z + place // 8) % self.deep * 8 + (place % 8 ^ self.index % 8)
        pick = (place[:, None] == holder[None, :]).astype(BF16)
        return dot_nn(pick, parts).astype(BF16)


    def gather_rows(self, shard):
        along = [shard] + [self.from_z(shard, k) for k in range(1, self.deep)]
        ready = along[-1]
        along = jnp.concatenate([a[None] for a in along + along[:-1]])
        along = lax.dynamic_slice_in_dim(along, (self.deep - self.z) % self.deep, self.deep, 0)
        cut = shard.shape[0] // 2
        arrays = []
        for half, order in enumerate(((self.X, self.Y), (self.Y, self.X))):
            here = along[:, half * cut : (half + 1) * cut]
            for which in order:
                here = jnp.stack([here, self.swap(here, which)])
            arrays += [here, self.swap(here, self.CORE)]
        return Pieces(arrays), ready


class Scatter:
    def __init__(self, net):
        self.net = net

    @staticmethod
    def add(one, two):
        return (one.astype(F32) + two.astype(F32)).astype(BF16)

    @staticmethod
    def pick(value, at, axis):
        return lax.dynamic_index_in_dim(value, at, axis, keepdims=False)

    def core(self, keep, send):
        got = self.net.swap(send, self.net.CORE)
        total = self.add(keep, got)
        return total.reshape((self.net.deep, 2, 2) + total.shape[1:])

    def second(self, value):
        net = self.net
        cut = value.shape[3] // 2
        first, last = value[..., :cut, :], value[..., cut:, :]
        y, x = net.bit(net.Y), net.bit(net.X)
        got = net.swap(self.pick(first, 1 - y, 1), net.Y), net.swap(self.pick(last, 1 - x, 2), net.X)
        return self.add(self.pick(first, y, 1), got[0]), self.add(self.pick(last, x, 2), got[1])

    def third(self, value):
        net = self.net
        first, last = value
        y, x = net.bit(net.Y), net.bit(net.X)
        got = net.swap(self.pick(first, 1 - x, 1), net.X), net.swap(self.pick(last, 1 - y, 1), net.Y)
        first = self.add(self.pick(first, x, 1), got[0])
        return jnp.concatenate([first, self.add(self.pick(last, y, 1), got[1])], axis=1)

    def fourth(self, value):
        net = self.net
        total = self.pick(value, net.z, 0).astype(F32)
        for k in range(1, net.deep):
            send = self.pick(value, (net.z + net.deep - k) % net.deep, 0)
            total = total + net.from_z(send, k).astype(F32)
        return total


def tie(value, *others):
    return lax.optimization_barrier((value,) + others)[0]


def body(
    tokens, cond, lengths, ada_w, ada_b, w_qkv, w_out, w_up, b_up, w_down, b_down,
    rel_table, bucket, cotangent,
):
    axes = ("clip", "win")
    sz = Sizes(tokens)
    net = Net()
    devices, index = net.count, net.index
    clips = lax.axis_size("clip")
    width = sz.width
    core = lax.axis_index("win") % 2
    swap = [(n, n ^ 1) for n in range(lax.axis_size("win"))]
    scalars = jnp.stack([core] + [lengths[n, 0] for n in range(sz.micro)] + [index % 8])
    strip = (sz.micro, 2, 2, sz.frames, sz.half, width)
    tok = tokens.reshape(strip)
    cot = cotangent.reshape(strip)

    cond_act = jax.nn.silu(cond[:, 0].astype(F32)).astype(BF16)
    rows = ada_w.shape[0]
    if net.direct:
        cond_all = net.gather_clips(cond_act)
    else:
        cond_all = lax.all_gather(cond_act, "clip", axis=0)
    cond_mine = lax.dynamic_slice_in_dim(cond_all, index * rows, rows, cond_all.ndim - 1)
    lead = cond_mine.shape[:-1]
    cond_mine = cond_mine.reshape(clips * sz.micro, rows)
    mod_part = dot_nn(cond_mine, ada_w)
    spread_b = jnp.zeros((mod_part.shape[1],), F32)
    spread_b = lax.dynamic_update_slice(spread_b, ada_b.astype(F32), (index * ada_b.shape[0],))
    mod_part = (mod_part + spread_b[None, :]).reshape(lead + (6 * width,))
    if net.direct:
        mod = net.scatter_clips(mod_part)
        mod = net.swap_sum(net.swap_sum(mod, net.CORE), net.X)
    else:
        mod = lax.psum_scatter(mod_part, "clip", scatter_dimension=0, tiled=False)
        mod = lax.psum(mod, "win")
    mod = mod.reshape(sz.micro, 6, width)

    cols = width // 2
    half_groups = sz.groups // 2
    by_group = w_qkv.reshape(rows, 3, sz.groups, sz.gcols).transpose(0, 2, 1, 3)
    by_group = by_group.reshape(rows, 2, 3 * cols)
    shard_q = [by_group[:, n] for n in range(2)]
    inner = w_up.shape[1]
    per = w_down.shape[0] // 2
    shard_u = w_up.reshape(rows, devices, 2, per)
    shard_u = [shard_u[:, :, n].reshape(rows, inner // 2) for n in range(2)]
    shard_d = [w_down[:per], w_down[per:]]
    small = jnp.concatenate([b_up, b_down, rel_table.reshape(-1)])
    if net.direct:
        fold_d = [d.reshape(2, rows, width) for d in shard_d]
        packs = [
            shard_q[0],
            jnp.concatenate([shard_q[1], w_out], axis=1),
            jnp.concatenate([shard_u[0], fold_d[0][0], fold_d[0][1]], axis=1),
            jnp.concatenate([shard_u[1], fold_d[1][0], fold_d[1][1]], axis=1),
        ]
        small = jnp.pad(small, (0, -small.shape[0] % 128))
        small = net.gather_small(small)
        q_0, ready = net.gather_rows(packs[0])
        q_1, ready = net.gather_rows(tie(packs[1], ready))
        full_q, full_out = [q_0, q_1], q_1
        u_0, ready = net.gather_rows(tie(packs[2], ready, mod))
        u_1, ready = net.gather_rows(tie(packs[3], ready))
        full_u = full_d = [u_0, u_1]
    else:
        gather = lambda v: lax.all_gather(v, axes, axis=0, tiled=True)
        full_q = [Pieces([gather(v)]) for v in shard_q]
        full_out = Pieces([gather(w_out)])
        full_u = [Pieces([gather(v)]) for v in shard_u]
        full_d = [Pieces([gather(v)]) for v in shard_d]
        small = gather(small[None])
    n_up, n_down = b_up.shape[0], b_down.shape[0]
    n_small = n_up + n_down + rel_table.size
    full_bup = small[:, :n_up].astype(F32).reshape(devices, 2, per)
    full_bup = [full_bup[:, n].reshape(1, inner // 2) for n in range(2)]
    full_bdown = small[:, n_up : n_up + n_down].astype(F32).reshape(1, width)
    table = small[:, n_up + n_down : n_small].reshape(-1, HEADS)
    places = offset_onehot(core, sz)
    bias, bias_t = bias_blocks(table, bucket, places, sz)

    own, send = first_norm(tok, mod, scalars, sz)
    far = lax.ppermute(send, "win", swap)
    qkv_0, att_0, wide_0 = attention(0, own, far, full_q[0], bias, scalars, sz)
    qkv_1, att_1, wide_1, wide_out, branch_own, branch_send = attention(
        1, own, far, full_q[1], bias, scalars, sz, att_0, full_out
    )
    branch_far = lax.ppermute(branch_send, "win", swap)
    hidden_two, grad_mlp = second_norm(tok, cot, branch_own, branch_far, mod, scalars, sz)
    flat = (sz.rows, width)
    both = (2, sz.micro, sz.used, sz.half, width)
    hidden_two, grad_mlp = hidden_two.reshape(flat), grad_mlp.reshape(flat)
    shards = (rows, per) if net.direct else None
    mlps = [
        mlp(hidden_two, grad_mlp, full_u[n], full_bup[n], full_d[n], scalars, sz, shards)
        for n in range(2)
    ]

    scat = Scatter(net)
    output, grad_mid, grad_own, grad_send, sums_two = after_mlp(
        tok, cot, branch_own, branch_far, [v[0].reshape(both) for v in mlps],
        [v[1].reshape(both) for v in mlps], mod, full_bdown, scalars, sz,
    )
    grad_far = lax.ppermute(grad_send, "win", swap)
    if net.direct:
        inner_terms = []
        for v in mlps:
            up, down = scat.core(*v[4:6]), scat.core(*v[6:8])
            inner_terms += [up, down[..., :rows, :], down[..., rows:, :]]
        terms = jnp.concatenate(inner_terms, axis=-1)
        grad_far = tie(grad_far, terms)
    g_q0, fold_0, g_out, carry = unpack(
        attention_back(
            0, grad_own, grad_far, own, far, qkv_0, (att_0, att_1), wide_0, wide_out, bias_t,
            scalars, sz, rows if net.direct else None,
        ),
        net.direct,
    )
    if net.direct:
        terms = scat.second(terms)
        carry = tie(carry, *terms)
    g_q1, fold_1, hid_own, hid_send = unpack(
        attention_back(
            1, grad_own, grad_far, own, far, qkv_1, None, wide_1, wide_out, bias_t, scalars, sz,
            rows if net.direct else None, carry,
        ),
        net.direct,
    )
    hid_far = lax.ppermute(hid_send, "win", swap)
    if net.direct:
        terms = scat.third(terms)
        hid_far = tie(hid_far, terms)
    grad_in, sums_one = last_norm(tok, cot, grad_mid, hid_own, hid_far, mod, scalars, sz)

    grad_mod = jnp.concatenate(
        [sums_one, sums_two[:, 3:4], sums_two[:, 0:3]], axis=1
    ).reshape(sz.micro, 6 * width)
    if net.direct:
        grad_mod = net.swap_sum(net.swap_sum(grad_mod, net.CORE), net.X)
        mod_all = net.gather_clips(grad_mod)
    else:
        mod_all = lax.all_gather(lax.psum(grad_mod, "win"), "clip", axis=0)
    mod_all = mod_all.reshape(clips * sz.micro, -1)
    grad_ada_w = lax.dot_general(
        cond_mine.astype(F32), mod_all, (((0,), (0,)), ((), ())),
        precision=HIGHEST, preferred_element_type=F32,
    )
    grad_ada_b = lax.dynamic_slice_in_dim(
        jnp.sum(mod_all, axis=0), index * ada_b.shape[0], ada_b.shape[0]
    )
    g_table = table_grad(
        jnp.concatenate([fold_0, fold_1]), bucket, places, table.shape[0], sz
    ).reshape(devices, -1)
    g_bup = jnp.stack([v[2].reshape(devices, per) for v in mlps], axis=1).reshape(devices, -1)
    g_bdown = mlps[0][3].reshape(devices, -1)
    g_small = jnp.concatenate([g_bup, g_bdown, g_table], axis=1)
    if net.direct:
        g_small = lax.dynamic_index_in_dim(net.sum_all(g_small), index, 0, keepdims=False)
        terms_att = jnp.concatenate([scat.core(*v) for v in (g_q0, g_q1, g_out)], axis=-1)
        terms_att = scat.third(scat.second(terms_att))
        terms = scat.fourth(terms)
        terms_att = scat.fourth(terms_att)
        r_u, r_d = [], []
        for n in range(2):
            mine = terms[:, n * inner : (n + 1) * inner]
            r_u.append(mine[:, : inner // 2])
            r_d += [mine[:, inner // 2 : inner // 2 + width], mine[:, inner // 2 + width :]]
        r_q = [terms_att[:, n * 3 * cols : (n + 1) * 3 * cols] for n in range(2)]
        r_out = terms_att[:, 6 * cols :]
    else:
        scatter = lambda v: lax.psum_scatter(
            v[0].astype(F32), axes, scatter_dimension=0, tiled=True
        )
        g_small = lax.psum_scatter(g_small, axes, scatter_dimension=0, tiled=False)
        r_u = [scatter(v[4:5]) for v in mlps]
        r_d = [scatter(v[5:6]) for v in mlps]
        r_q, r_out = [scatter(v) for v in (g_q0, g_q1)], scatter(g_out)
    r_up = jnp.stack([v.reshape(rows, devices, per) for v in r_u], axis=2).reshape(rows, inner)
    r_down = jnp.concatenate(r_d)
    r_qkv = jnp.stack([v.reshape(rows, half_groups, 3, sz.gcols) for v in r_q], axis=1)
    r_qkv = r_qkv.reshape(rows, sz.groups, 3, sz.gcols).transpose(0, 2, 1, 3)
    r_qkv = r_qkv.reshape(rows, 3 * width)
    return (
        output.reshape(tokens.shape), grad_in.reshape(tokens.shape), grad_ada_w, grad_ada_b,
        r_qkv, r_out, r_up, g_small[:n_up], r_down, g_small[n_up : n_up + n_down],
        g_small[n_up + n_down :].reshape(rel_table.shape),
    )


def unpack(results, direct):
    results = list(results)
    count = 2 if direct else 1
    out = [results[:count], results[count]]
    results = results[count + 1 :]
    if len(results) == count + 1:
        if results[0].ndim == (3 if direct else 2):
            return out + [results[:count], results[count]]
    return out + results


def solution(mesh):
    weights = P(("clip", "win"), None)
    vector = P(("clip", "win"))
    strips = P(None, "clip", "win", None, None, None, None, None)
    return jax.shard_map(
        body,
        mesh=mesh,
        in_specs=(
            strips, P(None, "clip", None), P(None, "clip"), weights, vector, weights, weights,
            weights, vector, weights, vector, weights, P(), strips,
        ),
        out_specs=(
            strips, strips, weights, vector, weights, weights, weights, vector, weights, vector,
            weights,
        ),
        check_vma=False,
    )
```

time: 3130 us -> 723 us (0.23)
  local copies, waits for them, and re-layouts: 1140 us -> 76.4 us
  waiting for transfers between devices: 1080 us -> 156 us
  matrix products: 588 us -> 15 us
  Pallas kernels: 0 us -> 300 us
  blocking collectives: 121 us -> 0 us
  other arithmetic: 140 us -> 69.4 us
  starting transfers between devices: 35.1 us -> 93 us
    unnamed x7 -> x0, waiting for transfers between devices: 1070 us -> none
    gather x2 -> x0, local copies, waits for them, and re-layouts: 567 us -> none  [body(): jnp.take(bucket, relative_index(frames, strip_rows, window_side).reshape(...]
    dot_general x76 -> x10, matrix products: 528 us -> 15 us  [the longest x2 6.47 us: table_grad(): jnp.einsum('hqkp,jpq->hkj', part, places, preferred_element_type=F32)]
    pallas_call x0 -> x10, Pallas kernels: none -> 300 us  [the longest x2 98.6 us: attention_back(): pl.pallas_call(kernel, grid_spec=pltpu.PrefetchScalarGridSpec(num_scalar_...]
    reshape x31 -> x22, local copies, waits for them, and re-layouts: 214 us -> 20.6 us  [the longest x1 4.8 us: table_grad(): fold = fold.reshape(HEADS, sz.frame, steps, sz.frame)]
    ppermute x0 -> x89, waiting for transfers between devices: none -> 156 us  [the longest x33 84.5 us: from_z(): lax.ppermute(value, self.AXES, [(n, move(n)) for n in range(self.count)])]
    ppermute x0 -> x89, starting transfers between devices: none -> 93 us  [the longest x33 48.1 us: from_z(): lax.ppermute(value, self.AXES, [(n, move(n)) for n in range(self.count)])]
    unnamed x278 -> x124, local copies, waits for them, and re-layouts: 117 us -> 24.3 us
  transfers between devices with their start and end apart: 14 -> 89, of which waited for: 2 -> 28; matrix products, arithmetic and copies ran while one was open for 48% -> 21% of each run, Pallas kernels for 0% -> 42%
where the time goes in v1:
time: 723 us; the launch traced here: 712 us
  Pallas kernels  300 us (41%)
  waiting for transfers between devices  156 us (22%)
  starting transfers between devices  93 us (13%)
  local copies, waits for them, and re-layouts  76.4 us (11%)
  other arithmetic  69.4 us (10%)
  matrix products  15 us (2%)
    pallas_call x2, Pallas kernels, attention_back(): pl.pallas_call(kernel, grid_spec=pltpu.PrefetchScalarGridSpec(num_scalar_...  98.6 us
    pallas_call x2, Pallas kernels, mlp(): pl.pallas_call(kernel, grid_spec=pltpu.PrefetchScalarGridSpec(num_scalar_...  98.6 us
    ppermute x33, waiting for transfers between devices, from_z(): lax.ppermute(value, self.AXES, [(n, move(n)) for n in range(self.count)])  84.5 us
    ppermute x52, waiting for transfers between devices, swap(): lax.ppermute(value, self.AXES, [(n, n ^ which) for n in range(self.count)])  71.9 us
    pallas_call x2, Pallas kernels, attention(): pl.pallas_call(kernel, grid_spec=pltpu.PrefetchScalarGridSpec(num_scalar_...  67.3 us
    ppermute x33, starting transfers between devices, from_z(): lax.ppermute(value, self.AXES, [(n, move(n)) for n in range(self.count)])  48.1 us
    ppermute x52, starting transfers between devices, swap(): lax.ppermute(value, self.AXES, [(n, n ^ which) for n in range(self.count)])  44.6 us
    convert_element_type x15, other arithmetic, add(): return (one.astype(F32) + two.astype(F32)).astype(BF16)  31.3 us
  transfers between devices with their start and end apart: 89, of which 28 were waited for; matrix products, arithmetic and copies ran while one was open for 21% of the time, Pallas kernels for 42%

profile of v1, /device:TPU:0, one launch (start us, length us, event | category | flops | bytes accessed | tf_op | source)
XLA Modules:
  0.0 712.3 jit_solution(15899564568192226386)
XLA Ops:
  1.5 5.1 collective-permute-start
  85.9 9.7 %collective-permute-done.9 = f32[2,6144]{1,0:T(2,128)S(1)} collective-permute-done((f32[2,6144]{1,0:T(2,128)S(1)}, f32[2,6144]{1,0:T(2,128)S(1)}, u32[]{:S(2)}, u32[]{:S(2)}) %collective-permute-start.9) | collective-permute-done | bytes 49184 | tf_op jit(solution)/shard_map/ppermute | solution.py:884
  97.4 4.6 first_norm.1
  114.5 7.6 %collective-permute-done.37 = bf16[32,4096]{1,0:T(8,128)(2,1)S(1)} collective-permute-done((bf16[32,4096]{1,0:T(8,128)(2,1)S(1)}, bf16[32,4096]{1,0:T(8,128)(2,1)S(1)}, u32[]{:S(2)}, u32[]{:S(2)}) %collective-permute-start.37) | collective-permute-done | bytes 262176 | tf_op jit(solution)/shard_map/ppermute | solution.py:888
  133.3 5.3 collective-permute-done.45
  138.8 14.4 %collective-permute-done.46 = bf16[32,4096]{1,0:T(8,128)(2,1)S(1)} collective-permute-done((bf16[32,4096]{1,0:T(8,128)(2,1)S(1)}, bf16[32,4096]{1,0:T(8,128)(2,1)S(1)}, u32[]{:S(2)}, u32[]{:S(2)}) %collective-permute-start.46) | collective-permute-done | bytes 262176 | tf_op jit(solution)/shard_map/ppermute | solution.py:888
  155.6 10.3 %collective-permute-done.42 = bf16[4,16,4096]{2,1,0:T(8,128)(2,1)S(1)} collective-permute-done((bf16[4,16,4096]{2,1,0:T(8,128)(2,1)S(1)}, bf16[4,16,4096]{2,1,0:T(8,128)(2,1)S(1)}, u32[]{:S(2)}, u32[]{:S(2)}) %collective-permute-start.42) | collective-permute-done | bytes 524320 | tf_op jit(solution)/shard_map/ppermute | solution.py:884
  172.3 10.4 %collective-permute-done.51 = bf16[4,16,4096]{2,1,0:T(8,128)(2,1)S(1)} collective-permute-done((bf16[4,16,4096]{2,1,0:T(8,128)(2,1)S(1)}, bf16[4,16,4096]{2,1,0:T(8,128)(2,1)S(1)}, u32[]{:S(2)}, u32[]{:S(2)}) %collective-permute-start.51) | collective-permute-done | bytes 524320 | tf_op jit(solution)/shard_map/ppermute | solution.py:884
  189.1 31.0 %attention.1 = (bf16[3,1152,512]{2,1,0:T(8,128)(2,1)}, bf16[1152,512]{1,0:T(8,128)(2,1)}, bf16[1024,1536]{1,0:T(8,128)(2,1)}) custom-call(s32[4]{0:T(128)} %pad_add_fusion.sc_ref, bf16[2,9,32,1024]{3,2,1,0:T(8,128)(2,1)} %get-tuple-element.63.own_ref, bf16[2,9,32,1024]{3,2,1,0:T(8,128)(2,1)} %collective-permute-done.10.far_ref, ...), custom_call_target="tpu_custom_call" | custom-call | flops 13136560128 | bytes 18874368 | tf_op jit(solution)/shard_map/attention/pallas_call | solution.py:490
  227.7 36.3 %attention_last.1 = (bf16[3,1152,512]{2,1,0:T(8,128)(2,1)}, bf16[1152,512]{1,0:T(8,128)(2,1)}, bf16[1024,1536]{1,0:T(8,128)(2,1)}, bf16[1024,1024]{1,0:T(8,128)(...) custom-call(s32[4]{0:T(128)} %pad_add_fusion.sc_ref, ...), custom_call_target="tpu_custom_call" | custom-call | flops 20384317440 | bytes 18874368 | tf_op jit(solution)/shard_map/attention_last/pallas_call | solution.py:490
  271.3 7.1 second_norm.1
  278.4 49.3 %mlp.2 = (f32[1152,1024]{1,0:T(8,128)}, f32[1152,1024]{1,0:T(8,128)}, f32[1,2048]{1,0:T(1,128)}, f32[1,1024]{1,0:T(1,128)}, bf16[16,32,2048]{2,1,0:T(8,128)(2,1)...) custom-call(s32[4]{0:T(128)} %pad_add_fusion.sc_ref, ...), custom_call_target="tpu_custom_call" | custom-call | flops 33822867456 | bytes 18874368 | tf_op jit(solution)/shard_map/mlp/pallas_call | solution.py:813
  328.3 49.3 %mlp.3 = (f32[1152,1024]{1,0:T(8,128)}, f32[1152,1024]{1,0:T(8,128)}, f32[1,2048]{1,0:T(1,128)}, f32[1,1024]{1,0:T(1,128)}, bf16[16,32,2048]{2,1,0:T(8,128)(2,1)...) custom-call(s32[4]{0:T(128)} %pad_add_fusion.sc_ref, ...), custom_call_target="tpu_custom_call" | custom-call | flops 33822867456 | bytes 18874368 | tf_op jit(solution)/shard_map/mlp/pallas_call | solution.py:813
  385.7 15.5 %after_mlp.1 = (bf16[2,2,2,5,32,1024]{5,4,3,2,1,0:T(8,128)(2,1)}, f32[2,2,9,32,1024]{4,3,2,1,0:T(8,128)}, bf16[2,9,32,1024]{3,2,1,0:T(8,128)(2,1)}, bf16[2,9,32,1024]{3,2,1,0:T(8,128)(2,1)}, f32[2,4,1024]{2,1,0:T(4,128)}) custom-call(s32[4]{0:T(128)} %pad_add_fusion.sc_ref, bf16[2,2,2,5,32,1024]{5,4,3,2,1,0:T(8,128)(2,1)} %bitcast.320, ...), custom_call_target="tpu_custom_call" | custom-call | tf_op jit(solution)/shard_map/after_mlp/pallas_call | solution.py:209
  425.0 51.4 %attention_back.1 = (bf16[16,32,1536]{2,1,0:T(8,128)(2,1)}, bf16[16,32,1536]{2,1,0:T(8,128)(2,1)}, f32[8,64,576]{2,1,0:T(8,128)}, bf16[16,32,1024]{2,1,0:T(8,128...) custom-call(s32[4]{0:T(128)} %pad_add_fusion.sc_ref, bf16[2,9,32,1024]{3,2,1,0:T(8,128)(2,1)} %get-tuple-element.79.go_ref, ...), custom_call_target="tpu_custom_call" | custom-call | flops 38277218304 | bytes 28311552 | tf_op jit(solution)/shard_map/attention_back/pallas_call | solution.py:683
  484.6 47.1 %attention_back_last.1 = (bf16[16,32,1536]{2,1,0:T(8,128)(2,1)}, bf16[16,32,1536]{2,1,0:T(8,128)(2,1)}, f32[8,64,576]{2,1,0:T(8,128)}, bf16[2,9,32,1024]{3,2,1,0:T(8,128)(2,1)}, bf16[2,9,32,1024]{3,2,1,0:T(8,128)(2,1)}) custom-call(s32[4]{0:T(128)} %pad_add_fusion.sc_ref, bf16[2,9,32,1024]{3,2,1,0:T(8,128)(2,1)} %get-tuple-element.79.go_ref, ...), custom_call_target="tpu_custom_call" | custom-call | flops 31029460992 | bytes 28311552 | tf_op jit(solution)/shard_map/attention_back_last/pallas_call | solution.py:683
  533.2 4.8 copy.208
  538.0 5.3 fusion.33
  568.4 8.0 %last_norm.1 = (bf16[2,2,2,5,32,1024]{5,4,3,2,1,0:T(8,128)(2,1)}, f32[2,2,1024]{2,1,0:T(2,128)}) custom-call(s32[4]{0:T(128)} %pad_add_fusion.sc_ref, bf16[2,2,2,5,32,1024]{5,4,3,2,1,0:T(8,128)(2,1)} %bitcast.321, bf16[2,2,2,5,32,1024]{5,4,3,2,1,0:T(8,128)(2,1)} %bitcast.324, f32[2,2,9,32,1024]{4,3,2,1,0:T(8,128)} %get-tuple-element.78.gm_ref, ...), custom_call_target="tpu_custom_call" | custom-call | tf_op jit(solution)/shard_map/last_norm/pallas_call | solution.py:272
  582.4 4.6 collective-permute-done.65
  611.7 28.4 %collective-permute-done.81 = bf16[32,8192]{1,0:T(8,128)(2,1)} collective-permute-done((bf16[32,8192]{1,0:T(8,128)(2,1)}, bf16[32,8192]{1,0:T(8,128)(2,1)}, u32[]{:S(2)}, u32[]{:S(2)}) %collective-permute-start.81) | collective-permute-done | bytes 524320 | tf_op jit(solution)/shard_map/ppermute | solution.py:888
  652.0 20.8 %collective-permute-done.73 = bf16[4,2,16,4096]{3,2,0,1:T(8,128)(2,1)S(1)} collective-permute-done((bf16[4,2,16,4096]{3,2,0,1:T(8,128)(2,1)S(1)}, bf16[4,2,16,4096]{3,2,0,1:T(8,128)(2,1)S(1)}, u32[]{:S(2)}, u32[]{:S(2)}) %collective-permute-start.73) | collective-permute-done | bytes 1048608 | tf_op jit(solution)/shard_map/ppermute | solution.py:884
  682.7 6.3 collective-permute-start.78
  692.5 16.9 %collective-permute-done.78 = bf16[32,4096]{1,0:T(8,128)(2,1)S(1)} collective-permute-done((bf16[32,4096]{1,0:T(8,128)(2,1)S(1)}, bf16[32,4096]{1,0:T(8,128)(2,1)S(1)}, u32[]{:S(2)}, u32[]{:S(2)}) %collective-permute-start.78) | collective-permute-done | bytes 262176 | tf_op jit(solution)/shard_map/ppermute | solution.py:888
  (473 shorter events, 260.3 us)
Async XLA Ops:
  81.4 47.0 %collective-permute-start.33 = (bf16[2,4,16,1536]{3,2,1,0:T(8,128)(2,1)}, bf16[2,4,16,1536]{3,2,1,0:T(8,128)(2,1)S(1)}, u32[]{:S(2)}, u32[]{:S(2)}) collective-permute-start(bf16[2,4,16,1536]{3,2,1,0:T(8,128)(2,1)} %get-tuple-element.206), channel_id=1, source_target_pairs={{0,2},{1,3},{2,0},{3,1},{4,6},{5,7},{6,4},{7,5},{8,10},{9,11},{10,... | collective-permute-start | bytes 1179656 | tf_op jit(solution)/shard_map/ppermute | solution.py:884
  84.4 47.6 %collective-permute-start.30 = (bf16[2,4,16,1536]{3,2,1,0:T(8,128)(2,1)}, bf16[2,4,16,1536]{3,2,1,0:T(8,128)(2,1)}, u32[]{:S(2)}, u32[]{:S(2)}) collective-permute-start(bf16[2,4,16,1536]{3,2,1,0:T(8,128)(2,1)} %get-tuple-element.208), channel_id=1, source_target_pairs={{0,4},{1,5},{2,6},{3,7},{4,0},{5,1},{6,2},{7,3},{8,12},{9,13},{10,... | collective-permute-start | bytes 1179656 | tf_op jit(solution)/shard_map/ppermute | solution.py:884
  107.8 80.2 %collective-permute-start.10 = (bf16[2,9,32,1024]{3,2,1,0:T(8,128)(2,1)S(1)}, bf16[2,9,32,1024]{3,2,1,0:T(8,128)(2,1)}, u32[]{:S(2)}, u32[]{:S(2)}) collective-permute-start(bf16[2,9,32,1024]{3,2,1,0:T(8,128)(2,1)S(1)} %copy-done.39), channel_id=1, source_target_pairs={{0,1},{1,0},{2,3},{3,2},{4,5},{5,4},{6,7},{7,6},{8,9},{9,8},{10,11... | collective-permute-start | bytes 3538952 | tf_op jit(solution)/shard_map/ppermute | solution.py:1063
  112.3 56.5 %collective-permute-start.25 = (bf16[2,4,16,2560]{3,2,1,0:T(8,128)(2,1)S(1)}, bf16[2,4,16,2560]{3,2,1,0:T(8,128)(2,1)S(1)}, u32[]{:S(2)}, u32[]{:S(2)}) collective-permute-start(bf16[2,4,16,2560]{3,2,1,0:T(8,128)(2,1)S(1)} %get-tuple-element.200), channel_id=1, source_target_pairs={{0,2},{1,3},{2,0},{3,1},{4,6},{5,7},{6,4},{7,5},{8,10},{9,11},{10,... | collective-permute-start | bytes 1966088 | tf_op jit(solution)/shard_map/ppermute | solution.py:884
  122.1 47.4 %collective-permute-start.22 = (bf16[2,4,16,2560]{3,2,1,0:T(8,128)(2,1)S(1)}, bf16[2,4,16,2560]{3,2,1,0:T(8,128)(2,1)S(1)}, u32[]{:S(2)}, u32[]{:S(2)}) collective-permute-start(bf16[2,4,16,2560]{3,2,1,0:T(8,128)(2,1)S(1)} %get-tuple-element.202), channel_id=1, source_target_pairs={{0,4},{1,5},{2,6},{3,7},{4,0},{5,1},{6,2},{7,3},{8,12},{9,13},{10,... | collective-permute-start | bytes 1966088 | tf_op jit(solution)/shard_map/ppermute | solution.py:884
  185.3 39.1 %collective-permute-start.40 = (bf16[2,4,16,4096]{3,2,1,0:T(8,128)(2,1)}, bf16[2,4,16,4096]{3,2,1,0:T(8,128)(2,1)}, u32[]{:S(2)}, u32[]{:S(2)}) collective-permute-start(bf16[2,4,16,4096]{3,2,1,0:T(8,128)(2,1)} %get-tuple-element.196), channel_id=1, source_target_pairs={{0,4},{1,5},{2,6},{3,7},{4,0},{5,1},{6,2},{7,3},{8,12},{9,13},{10,... | collective-permute-start | bytes 3145736 | tf_op jit(solution)/shard_map/ppermute | solution.py:884
  187.4 39.8 %collective-permute-start.26 = (bf16[2,2,4,16,2560]{4,3,2,1,0:T(8,128)(2,1)S(1)}, bf16[2,2,4,16,2560]{4,3,2,1,0:T(8,128)(2,1)}, u32[]{:S(2)}, u32[]{:S(2)}) collective-permute-start(bf16[2,2,4,16,2560]{4,3,2,1,0:T(8,128)(2,1)S(1)} %pad_maximum_fusion.8.refs_2_.refs_7_.refs_11_), channel_id=1, source_target_pairs={{0,1},{1,0},{2,3},{3,2},{4,5},{5,4},{6,7},{7,6},{8,9},{9,8},{10,11... | collective-permute-start | bytes 3932168 | tf_op jit(solution)/shard_map/ppermute | solution.py:884
  187.5 40.2 %collective-permute-start.23 = (bf16[2,2,4,16,2560]{4,3,2,1,0:T(8,128)(2,1)}, bf16[2,2,4,16,2560]{4,3,2,1,0:T(8,128)(2,1)}, u32[]{:S(2)}, u32[]{:S(2)}) collective-permute-start(bf16[2,2,4,16,2560]{4,3,2,1,0:T(8,128)(2,1)} %pad_maximum_fusion.7.refs_0_.refs_5_.refs_9_), channel_id=1, source_target_pairs={{0,1},{1,0},{2,3},{3,2},{4,5},{5,4},{6,7},{7,6},{8,9},{9,8},{10,11... | collective-permute-start | bytes 3932168 | tf_op jit(solution)/shard_map/ppermute | solution.py:884
  188.6 76.2 %collective-permute-start.52 = (bf16[2,4,16,4096]{3,2,1,0:T(8,128)(2,1)}, bf16[2,4,16,4096]{3,2,1,0:T(8,128)(2,1)}, u32[]{:S(2)}, u32[]{:S(2)}) collective-permute-start(bf16[2,4,16,4096]{3,2,1,0:T(8,128)(2,1)} %get-tuple-element.190), channel_id=1, source_target_pairs={{0,2},{1,3},{2,0},{3,1},{4,6},{5,7},{6,4},{7,5},{8,10},{9,11},{10,... | collective-permute-start | bytes 3145736 | tf_op jit(solution)/shard_map/ppermute | solution.py:884
  220.1 46.7 %collective-permute-start.49 = (bf16[2,4,16,4096]{3,2,1,0:T(8,128)(2,1)}, bf16[2,4,16,4096]{3,2,1,0:T(8,128)(2,1)}, u32[]{:S(2)}, u32[]{:S(2)}) collective-permute-start(bf16[2,4,16,4096]{3,2,1,0:T(8,128)(2,1)} %get-tuple-element.192), channel_id=1, source_target_pairs={{0,4},{1,5},{2,6},{3,7},{4,0},{5,1},{6,2},{7,3},{8,12},{9,13},{10,... | collective-permute-start | bytes 3145736 | tf_op jit(solution)/shard_map/ppermute | solution.py:884
  224.4 54.0 %collective-permute-start.44 = (bf16[2,2,4,16,4096]{4,3,2,1,0:T(8,128)(2,1)}, bf16[2,2,4,16,4096]{4,3,2,1,0:T(8,128)(2,1)}, u32[]{:S(2)}, u32[]{:S(2)}) collective-permute-start(bf16[2,2,4,16,4096]{4,3,2,1,0:T(8,128)(2,1)} %pad_maximum_fusion.4.refs_2_.refs_6_.refs_10_), channel_id=1, source_target_pairs={{0,1},{1,0},{2,3},{3,2},{4,5},{5,4},{6,7},{7,6},{8,9},{9,8},{10,11... | collective-permute-start | bytes 6291464 | tf_op jit(solution)/shard_map/ppermute | solution.py:884
  227.2 51.2 %collective-permute-start.41 = (bf16[2,2,4,16,4096]{4,3,2,1,0:T(8,128)(2,1)}, bf16[2,2,4,16,4096]{4,3,2,1,0:T(8,128)(2,1)}, u32[]{:S(2)}, u32[]{:S(2)}) collective-permute-start(bf16[2,2,4,16,4096]{4,3,2,1,0:T(8,128)(2,1)} %pad_maximum_fusion.3.refs_0_.refs_4_.refs_8_), channel_id=1, source_target_pairs={{0,1},{1,0},{2,3},{3,2},{4,5},{5,4},{6,7},{7,6},{8,9},{9,8},{10,11... | collective-permute-start | bytes 6291464 | tf_op jit(solution)/shard_map/ppermute | solution.py:884
  266.3 62.0 %collective-permute-start.53 = (bf16[2,2,4,16,4096]{4,3,2,1,0:T(8,128)(2,1)S(1)}, bf16[2,2,4,16,4096]{4,3,2,1,0:T(8,128)(2,1)}, u32[]{:S(2)}, u32[]{:S(2)}) collective-permute-start(bf16[2,2,4,16,4096]{4,3,2,1,0:T(8,128)(2,1)S(1)} %pad_maximum_fusion.6.refs_2_.refs_6_.refs_10_), channel_id=1, source_target_pairs={{0,1},{1,0},{2,3},{3,2},{4,5},{5,4},{6,7},{7,6},{8,9},{9,8},{10,11... | collective-permute-start | bytes 6291464 | tf_op jit(solution)/shard_map/ppermute | solution.py:884
  269.7 58.6 %collective-permute-start.50 = (bf16[2,2,4,16,4096]{4,3,2,1,0:T(8,128)(2,1)}, bf16[2,2,4,16,4096]{4,3,2,1,0:T(8,128)(2,1)}, u32[]{:S(2)}, u32[]{:S(2)}) collective-permute-start(bf16[2,2,4,16,4096]{4,3,2,1,0:T(8,128)(2,1)} %pad_maximum_fusion.5.refs_0_.refs_4_.refs_8_), channel_id=1, source_target_pairs={{0,1},{1,0},{2,3},{3,2},{4,5},{5,4},{6,7},{7,6},{8,9},{9,8},{10,11... | collective-permute-start | bytes 6291464 | tf_op jit(solution)/shard_map/ppermute | solution.py:884
  327.7 77.8 %collective-permute-start.56 = (bf16[16,64,1024]{2,1,0:T(8,128)(2,1)}, bf16[16,64,1024]{2,1,0:T(8,128)(2,1)}, u32[]{:S(2)}, u32[]{:S(2)}) collective-permute-start(bf16[16,64,1024]{2,1,0:T(8,128)(2,1)} %get-tuple-element.84), channel_id=1, source_target_pairs={{0,1},{1,0},{2,3},{3,2},{4,5},{5,4},{6,7},{7,6},{8,9},{9,8},{10,11... | collective-permute-start | bytes 6291464 | tf_op jit(solution)/shard_map/ppermute | solution.py:884
  327.8 75.2 %collective-permute-start.55 = (bf16[16,32,2048]{2,1,0:T(8,128)(2,1)}, bf16[16,32,2048]{2,1,0:T(8,128)(2,1)}, u32[]{:S(2)}, u32[]{:S(2)}) collective-permute-start(bf16[16,32,2048]{2,1,0:T(8,128)(2,1)} %get-tuple-element.82), channel_id=1, source_target_pairs={{0,1},{1,0},{2,3},{3,2},{4,5},{5,4},{6,7},{7,6},{8,9},{9,8},{10,11... | collective-permute-start | bytes 6291464 | tf_op jit(solution)/shard_map/ppermute | solution.py:884
  421.3 55.7 %collective-permute-start.60 = (bf16[4,2,16,8192]{3,2,0,1:T(8,128)(2,1)}, bf16[4,2,16,8192]{3,2,0,1:T(8,128)(2,1)}, u32[]{:S(2)}, u32[]{:S(2)}) collective-permute-start(bf16[4,2,16,8192]{3,2,0,1:T(8,128)(2,1)} %dynamic-slice_bitcast_fusion), channel_id=1, source_target_pairs={{0,2},{1,3},{2,0},{3,1},{4,6},{5,7},{6,4},{7,5},{8,10},{9,11},{10,... | collective-permute-start | bytes 6291464 | tf_op jit(solution)/shard_map/ppermute | solution.py:884
  424.3 56.7 %collective-permute-start.59 = (bf16[4,2,16,8192]{3,2,0,1:T(8,128)(2,1)}, bf16[4,2,16,8192]{3,2,0,1:T(8,128)(2,1)}, u32[]{:S(2)}, u32[]{:S(2)}) collective-permute-start(bf16[4,2,16,8192]{3,2,0,1:T(8,128)(2,1)} %dynamic-slice_bitcast_fusion.1), channel_id=1, source_target_pairs={{0,4},{1,5},{2,6},{3,7},{4,0},{5,1},{6,2},{7,3},{8,12},{9,13},{10,... | collective-permute-start | bytes 6291464 | tf_op jit(solution)/shard_map/ppermute | solution.py:884
  476.4 73.7 %collective-permute-start.70 = (bf16[16,32,1536]{2,1,0:T(8,128)(2,1)}, bf16[16,32,1536]{2,1,0:T(8,128)(2,1)}, u32[]{:S(2)}, u32[]{:S(2)}) collective-permute-start(bf16[16,32,1536]{2,1,0:T(8,128)(2,1)} %get-tuple-element.105), channel_id=1, source_target_pairs={{0,1},{1,0},{2,3},{3,2},{4,5},{5,4},{6,7},{7,6},{8,9},{9,8},{10,11... | collective-permute-start | bytes 4718600 | tf_op jit(solution)/shard_map/ppermute | solution.py:884
  476.5 70.3 %collective-permute-start.72 = (bf16[16,32,1024]{2,1,0:T(8,128)(2,1)}, bf16[16,32,1024]{2,1,0:T(8,128)(2,1)}, u32[]{:S(2)}, u32[]{:S(2)}) collective-permute-start(bf16[16,32,1024]{2,1,0:T(8,128)(2,1)} %get-tuple-element.109), channel_id=1, source_target_pairs={{0,1},{1,0},{2,3},{3,2},{4,5},{5,4},{6,7},{7,6},{8,9},{9,8},{10,11... | collective-permute-start | bytes 3145736 | tf_op jit(solution)/shard_map/ppermute | solution.py:884
  565.7 37.6 %collective-permute-start.71 = (bf16[16,32,1536]{2,1,0:T(8,128)(2,1)}, bf16[16,32,1536]{2,1,0:T(8,128)(2,1)}, u32[]{:S(2)}, u32[]{:S(2)}) collective-permute-start(bf16[16,32,1536]{2,1,0:T(8,128)(2,1)} %get-tuple-element.107), channel_id=1, source_target_pairs={{0,1},{1,0},{2,3},{3,2},{4,5},{5,4},{6,7},{7,6},{8,9},{9,8},{10,11... | collective-permute-start | bytes 4718600 | tf_op jit(solution)/shard_map/ppermute | solution.py:884
  599.0 41.1 %collective-permute-start.81 = (bf16[32,8192]{1,0:T(8,128)(2,1)}, bf16[32,8192]{1,0:T(8,128)(2,1)}, u32[]{:S(2)}, u32[]{:S(2)}) collective-permute-start(bf16[32,8192]{1,0:T(8,128)(2,1)} %get-tuple-element.168), channel_id=1, source_target_pairs={{0,16},{1,17},{2,18},{3,19},{4,20},{5,21},{6,22},{7,23},{8,24},{9,... | collective-permute-start | bytes 1572872 | tf_op jit(solution)/shard_map/ppermute | solution.py:888
  599.3 40.8 %collective-permute-start.82 = (bf16[32,8192]{1,0:T(8,128)(2,1)}, bf16[32,8192]{1,0:T(8,128)(2,1)}, u32[]{:S(2)}, u32[]{:S(2)}) collective-permute-start(bf16[32,8192]{1,0:T(8,128)(2,1)} %get-tuple-element.169), channel_id=1, source_target_pairs={{0,8},{1,9},{2,10},{3,11},{4,12},{5,13},{6,14},{7,15},{8,16},{9,17... | collective-permute-start | bytes 1572872 | tf_op jit(solution)/shard_map/ppermute | solution.py:888
  609.6 39.8 %collective-permute-start.75 = (bf16[4,2,16,4096]{3,2,0,1:T(8,128)(2,1)}, bf16[4,2,16,4096]{3,2,0,1:T(8,128)(2,1)}, u32[]{:S(2)}, u32[]{:S(2)}) collective-permute-start(bf16[4,2,16,4096]{3,2,0,1:T(8,128)(2,1)} %bitcast.312), channel_id=1, source_target_pairs={{0,2},{1,3},{2,0},{3,1},{4,6},{5,7},{6,4},{7,5},{8,10},{9,11},{10,... | collective-permute-start | bytes 3145736 | tf_op jit(solution)/shard_map/ppermute | solution.py:884
  (110 other events, 1425.4 us)

commit v2 on v1

--- a/solution.py
+++ b/solution.py
@@ -309,33 +309,81 @@
         shape = self.arrays[0].shape[:-1] + (columns,)
         return [pl.BlockSpec(shape, at)] * 4
 
-    def row_specs(self, columns, row_map, block):
-        shape = self.arrays[0].shape[:2] + (1,) + self.arrays[0].shape[3:4] + (columns,)
-        return [pl.BlockSpec(shape, lambda *g: (0, 0, row_map(*g), 0, block))] * 4
-
-
-def place(refs, key, out_ref, columns, pitch=None, offset=0):
-    depth, cut = refs[0].shape[2:4]
-    pitch = 2 * cut if pitch is None else pitch
-    for n, ref in enumerate(refs):
-        half, far = n // 2, n % 2
-        for i in range(2):
-            for j in range(2):
-                away = (i * 4 + j * 2 if half == 0 else j * 4 + i * 2) + far
-                at = (key ^ away) * pitch + offset + half * cut
-                for z in range(depth):
-                    rows = pl.ds(pl.multiple_of(z * 8 * pitch + at, cut), cut)
-                    out_ref[rows, columns] = ref[i, j, z]
-
-
-def hand_out(value, start, rows, core, keep_ref, send_ref):
-    for parity in range(2):
-        for own, ref in ((0, keep_ref), (1, send_ref)):
-
-            @pl.when(core == parity ^ own)
-            def _(parity=parity, ref=ref):
-                for low in range(parity * rows, value.shape[0], 2 * rows):
-                    ref[(start + low) // (2 * rows)] = value[low : low + rows].astype(BF16)
+
+def pieces_of(refs, key, z_here):
+    depth = refs[0].shape[2]
+    for z in range(depth):
+        for n in range(4):
+            half, far = n // 2, n % 2
+            for i in range(2):
+                for j in range(2):
+                    away = (i * 4 + j * 2 if half == 0 else j * 4 + i * 2) + far
+                    yield (z_here + z) % depth, key ^ away, half, refs[n].at[i, j, z]
+
+
+def place(refs, key, z_here, out_ref, columns=slice(None), source=slice(None)):
+    if len(refs) == 1:
+        out_ref[:, columns] = refs[0][:, source]
+        return
+    for z, at, half, piece in pieces_of(refs, key, z_here):
+        cut = piece.shape[0]
+        row = pl.multiple_of((z * 8 + at) * (2 * cut) + half * cut, cut)
+        out_ref[pl.ds(row, cut), columns] = piece[:, source]
+
+
+def place_inner(refs, key, z_here, out_ref, source):
+    size = source.stop - source.start
+    if len(refs) == 1:
+        cut = out_ref.shape[0] // 32
+        for n in range(64):
+            at, half = n // 2, n % 2
+            to = (at % 2) * (16 * cut) + at // 2 * cut
+            out_ref[to : to + cut, half * size : (half + 1) * size] = refs[0][
+                n * cut : (n + 1) * cut, source
+            ]
+        return
+    for z, at, half, piece in pieces_of(refs, key, z_here):
+        cut = piece.shape[0]
+        row = pl.multiple_of((at % 2) * (16 * cut) + (z * 4 + at // 2) * cut, cut)
+        out_ref[pl.ds(row, cut), half * size : (half + 1) * size] = piece[:, source]
+
+
+def turn(value, out_ref, core, shard, start=0):
+    turned = value.T
+    if shard is None:
+        out_ref[start : start + turned.shape[0]] = turned
+        return
+    height = out_ref.shape[0]
+    for n in range(turned.shape[0] // shard):
+        at = start // shard + n
+        at = (core ^ (at % 2)) * (height // 2) + at // 2 * shard
+        out_ref[pl.ds(pl.multiple_of(at, shard), shard), :] = turned[n * shard : (n + 1) * shard]
+
+
+def give(refs, half, low, value, start=0):
+    value = value.astype(BF16)
+    columns = slice(start, start + value.shape[1])
+    if len(refs) == 1:
+        low = half * (refs[0].shape[0] // 2) + low
+        refs[0][low : low + value.shape[0], columns] = value
+        return
+    rows = refs[half].shape[1]
+    refs[half][low // rows : (low + value.shape[0]) // rows, :, columns] = value.reshape(
+        value.shape[0] // rows, rows, value.shape[1]
+    )
+
+
+def grad_shapes(direct, rows, height, columns):
+    if not direct:
+        return [jax.ShapeDtypeStruct((height, columns), BF16)]
+    return [jax.ShapeDtypeStruct((height // (2 * rows), rows, columns), BF16)] * 2
+
+
+def grad_specs(direct, rows, height, columns, at_column):
+    if not direct:
+        return [pl.BlockSpec((height, columns), lambda *g: (0, at_column(*g)))]
+    shape = (height // (2 * rows), rows, columns)
+    return [pl.BlockSpec(shape, lambda *g: (0, 0, at_column(*g)))] * 2
 
 
 def join_frames(own_ref, far_ref, joined_ref, sz):
@@ -362,8 +410,9 @@
     scale = 1.0 / math.sqrt(sz.head)
     last = w_out is not None
     steps = sz.groups // 2
-    direct = not w_qkv.whole
     gcols = sz.gcols
+    joint = w_out is w_qkv
+    n_out = 2 * len(w_qkv.arrays) if joint else 1
 
     def kernel(sc_ref, own_ref, far_ref, bias_ref, *refs):
         refs = list(refs)
@@ -371,40 +420,38 @@
         w_refs = take(len(w_qkv.arrays))
         if last:
             (first_ref,) = take(1)
-            out_refs = take(8 if direct else 1)
+            out_refs = take(n_out)
         qkv_ref, att_ref, w_ref = take(3)
         if last:
             wo_ref, bo_ref, bf_ref = take(3)
         joined, spread = take(2)
         step = pl.program_id(0)
-        key = sc_ref[1 + sz.micro]
+        key, z_here = sc_ref[1 + sz.micro], sc_ref[2 + sz.micro]
 
         @pl.when(step == 0)
         def _():
             join_frames(own_ref, far_ref, joined, sz)
 
-        if direct:
-            place(w_refs, key, w_ref, slice(None))
-        else:
-            w_ref[...] = w_refs[0][...]
+        place(w_refs, key, z_here, w_ref)
         for n in range(3):
             part = dot_nn(joined[...], w_ref[:, n * gcols : (n + 1) * gcols]).astype(BF16)
             qkv_ref[n] = part * scale if n == 0 else part
         for head in range(sz.group):
-            lanes = slice(head * sz.head, (head + 1) * sz.head)
-            spread_bias(bias_ref, head, spread, sz)
-
-            def one_micro(m, carry, lanes=lanes):
-                for tw in range(2):
-                    size = sz.lens[tw]
-                    rows = window_rows(m, tw, sz)
-                    keys_ok = (sc_ref[1 + m] - tw * sz.frames) * sz.frame
-
-                    @pl.when(keys_ok > 0)
-                    def _(rows=rows, size=size, keys_ok=keys_ok):
+            spread_bias(bias_ref, head, spread.at[head], sz)
+
+        def one_micro(m, carry):
+            for tw in range(2):
+                size = sz.lens[tw]
+                rows = window_rows(m, tw, sz)
+                keys_ok = (sc_ref[1 + m] - tw * sz.frames) * sz.frame
+
+                @pl.when(keys_ok > 0)
+                def _(rows=rows, size=size, keys_ok=keys_ok):
+                    column = lax.broadcasted_iota(jnp.int32, (1, size), 1)
+                    for head in range(sz.group):
+                        lanes = slice(head * sz.head, (head + 1) * sz.head)
                         scores = dot_nt(qkv_ref[0, rows, lanes], qkv_ref[1, rows, lanes])
-                        scores = scores + spread[:size, :size].astype(F32)
-                        column = lax.broadcasted_iota(jnp.int32, (1, size), 1)
+                        scores = scores + spread[head, :size, :size].astype(F32)
                         scores = jnp.where(column < keys_ok, scores, MASKED)
                         top = jnp.max(scores, axis=-1, keepdims=True)
                         weight = jnp.exp(scores - top)
@@ -412,13 +459,13 @@
                         probs = (weight * share).astype(BF16)
                         att_ref[rows, lanes] = dot_nn(probs, qkv_ref[2, rows, lanes]).astype(BF16)
 
-                    @pl.when(keys_ok <= 0)
-                    def _(rows=rows, size=size):
-                        att_ref[rows, lanes] = jnp.zeros((size, sz.head), BF16)
-
-                return carry
-
-            lax.fori_loop(0, sz.micro, one_micro, 0)
+                @pl.when(keys_ok <= 0)
+                def _(rows=rows, size=size):
+                    att_ref[rows, :] = jnp.zeros((size, gcols), BF16)
+
+            return carry
+
+        lax.fori_loop(0, sz.micro, one_micro, 0)
         if not last:
             return
         kept, total = take(2)
@@ -430,11 +477,11 @@
 
         @pl.when(step == steps - 1)
         def _():
-            if direct:
-                place(out_refs[:4], key, wo_ref, slice(0, 2 * gcols))
-                place(out_refs[4:], key, wo_ref, slice(2 * gcols, 4 * gcols))
+            if joint:
+                place(out_refs[: n_out // 2], key, z_here, wo_ref, slice(0, 2 * gcols))
+                place(out_refs[n_out // 2 :], key, z_here, wo_ref, slice(2 * gcols, 4 * gcols))
             else:
-                wo_ref[...] = out_refs[0][...]
+                place(out_refs, key, z_here, wo_ref)
             middle = first_ref.shape[1]
             total[...] = dot_nn(first_ref[...], wo_ref[:middle]) + dot_nn(
                 kept[...], wo_ref[middle:]
@@ -467,13 +514,13 @@
     ]
     scratch = [
         pltpu.VMEM((sz.rows, width), BF16),
-        pltpu.VMEM((sz.lens[0], sz.lens[0]), BF16),
+        pltpu.VMEM((sz.group, sz.lens[0], sz.lens[0]), BF16),
     ]
     args = [scalars, own, far, bias, *w_qkv.arrays]
     flops = 6 * sz.rows * width * cols + 4 * sz.rows * sz.lens[0] * cols
     if last:
         in_specs += [once((sz.rows, cols), flat)]
-        if direct:
+        if joint:
             low = w_out.arrays[0].shape[-1] // (2 * gcols) - 2
             in_specs += w_out.specs(2 * gcols, lambda g, s: low)
             in_specs += w_out.specs(2 * gcols, lambda g, s: low + 1)
@@ -503,19 +550,6 @@
     )(*args)
 
 
-def grad_shapes(direct, rows, width, columns, sz):
-    if not direct:
-        return [jax.ShapeDtypeStruct((width, columns), BF16)]
-    return [jax.ShapeDtypeStruct((width // (2 * rows), rows, columns), BF16)] * 2
-
-
-def grad_specs(direct, rows, width, columns, at_row, at_column):
-    if not direct:
-        return [pl.BlockSpec((width, columns), lambda *g: (at_row(*g), at_column(*g)))]
-    shape = (width // (2 * rows), rows, columns)
-    return [pl.BlockSpec(shape, lambda *g: (at_row(*g), 0, at_column(*g)))] * 2
-
-
 def attention_back(half, grad_own, grad_far, own, far, qkv, atts, w_qkv, w_out, bias_t, scalars, sz, shard, carry=None):
     scale = 1.0 / math.sqrt(sz.head)
     last = carry is not None
@@ -539,92 +573,85 @@
         if last:
             ho_ref, hf_ref = take(2)
         else:
-            gwo_refs = take(outs)
+            gwo_refs = gw_refs if direct else take(1)
             (total,) = take(1)
         grad, hidden_t, grad_att, parts, spread, pair_sum = take(6)
         if last:
             (total,) = take(1)
+        else:
+            (turned,) = take(1)
         step = pl.program_id(0)
-
-        def give(value, start, refs):
-            if direct:
-                hand_out(value, start, shard, sc_ref[0], *refs)
-            else:
-                refs[0][start : start + value.shape[0]] = value.astype(BF16)
 
         @pl.when(step == 0)
         def _():
             join_frames(own_ref, far_ref, grad, sz)
-            hidden_t[...] = grad[...].T
+            turn(grad[...], hidden_t, sc_ref[0], shard)
             join_frames(go_ref, gf_ref, grad, sz)
             if last:
                 total[...] = carry_ref[...]
             else:
                 total[...] = jnp.zeros_like(total)
+                for n, a_ref in enumerate(att_refs):
+                    turn(a_ref[...], turned, sc_ref[0], shard, n * a_ref.shape[1])
 
         grad_att[...] = dot_nt(grad[...], wo_ref[...]).astype(BF16)
         full = sz.lens[0]
         for head in range(sz.group):
-            lanes = slice(head * sz.head, (head + 1) * sz.head)
-            spread_bias(bias_ref, head, spread, sz)
-            pair_sum[...] = jnp.zeros((full, full), F32)
-
-            def one_micro(m, carry, head=head, lanes=lanes):
-                for tw in range(2):
-                    size = sz.lens[tw]
-                    rows = window_rows(m, tw, sz)
-                    keys_ok = (sc_ref[1 + m] - tw * sz.frames) * sz.frame
-                    spot = [
-                        slice(n * gcols + head * sz.head, n * gcols + (head + 1) * sz.head)
-                        for n in range(3)
-                    ]
-
-                    @pl.when(keys_ok > 0)
-                    def _(rows=rows, size=size, keys_ok=keys_ok, spot=spot):
+            spread_bias(bias_ref, head, spread.at[head], sz)
+            pair_sum[head] = jnp.zeros((full, full), F32)
+
+        def one_micro(m, carry):
+            for tw in range(2):
+                size = sz.lens[tw]
+                rows = window_rows(m, tw, sz)
+                keys_ok = (sc_ref[1 + m] - tw * sz.frames) * sz.frame
+
+                @pl.when(keys_ok > 0)
+                def _(rows=rows, size=size, keys_ok=keys_ok):
+                    row = lax.broadcasted_iota(jnp.int32, (size, 1), 0)
+                    for head in range(sz.group):
+                        lanes = slice(head * sz.head, (head + 1) * sz.head)
+                        spot = [slice(n * gcols + lanes.start, n * gcols + lanes.stop) for n in range(3)]
                         query = qkv_ref[0, rows, lanes]
                         key = qkv_ref[1, rows, lanes]
                         value = qkv_ref[2, rows, lanes]
                         grad_out = grad_att[rows, lanes]
-                        scores = dot_nt(key, query) + spread[:size, :size].astype(F32)
-                        row = lax.broadcasted_iota(jnp.int32, (size, 1), 0)
+                        scores = dot_nt(key, query) + spread[head, :size, :size].astype(F32)
                         scores = jnp.where(row < keys_ok, scores, MASKED)
                         weight = jnp.exp(scores - jnp.max(scores, axis=0, keepdims=True))
                         probs = weight * (1.0 / jnp.sum(weight, axis=0, keepdims=True))
                         grad_probs = dot_nt(value, grad_out)
                         inner = jnp.sum(probs * grad_probs, axis=0, keepdims=True)
                         grad_scores = (probs * (grad_probs - inner)).astype(BF16)
-                        pair_sum[:size, :size] += grad_scores.astype(F32)
+                        pair_sum[head, :size, :size] += grad_scores.astype(F32)
                         parts[rows, spot[2]] = dot_nn(probs.astype(BF16), grad_out).astype(BF16)
                         parts[rows, spot[1]] = dot_nn(grad_scores, query).astype(BF16)
                         parts[rows, spot[0]] = (dot_tn(grad_scores, key) * scale).astype(BF16)
 
-                    @pl.when(keys_ok <= 0)
-                    def _(rows=rows, size=size, spot=spot):
-                        for n in range(3):
-                            parts[rows, spot[n]] = jnp.zeros((size, sz.head), BF16)
-
-                return carry
-
-            lax.fori_loop(0, sz.micro, one_micro, 0)
+                @pl.when(keys_ok <= 0)
+                def _(rows=rows, size=size):
+                    parts[rows, :] = jnp.zeros((size, 3 * gcols), BF16)
+
+            return carry
+
+        lax.fori_loop(0, sz.micro, one_micro, 0)
+        for head in range(sz.group):
             fold_ref[head] = jnp.zeros(fold_ref.shape[1:], F32)
             for t in range(sz.frames):
                 low = (sz.frames - 1 - t) * sz.frame
                 fold_ref[head, :, low : low + full] += pair_sum[
-                    t * sz.frame : (t + 1) * sz.frame, :
+                    head, t * sz.frame : (t + 1) * sz.frame, :
                 ]
         for n in range(4):
             rows = slice(n * quarter, (n + 1) * quarter)
-            give(dot_nn(hidden_t[rows, :], parts[...]), n * quarter, gw_refs)
+            give(gw_refs, n // 2, n % 2 * quarter, dot_nn(hidden_t[rows, :], parts[...]))
         total[...] += dot_nt(parts[...], w_ref[...])
         if not last:
-            for n, a_ref in enumerate(att_refs):
-
-                @pl.when(step == n)
-                def _(a_ref=a_ref):
-                    for k in range(2):
-                        columns = slice(k * quarter, (k + 1) * quarter)
-                        give(dot_tn(a_ref[:, columns], grad[...]), k * quarter, gwo_refs)
-
+            columns = pl.ds(pl.multiple_of(step * 2 * gcols, 2 * gcols), 2 * gcols)
+            for n in range(4):
+                rows = slice(n * quarter, (n + 1) * quarter)
+                value = dot_nn(turned[rows, :], grad[:, columns])
+                give(gwo_refs, n // 2, n % 2 * quarter, value, 3 * gcols if direct else 0)
             return
 
         @pl.when(step == steps - 1)
@@ -650,19 +677,19 @@
         pl.BlockSpec((gcols, width), lambda g, s: (half * steps + g, 0)),
         pl.BlockSpec(block_bias, lambda g, s: (half * steps + g, 0, 0)),
     ]
-    zero = lambda g, s: 0
     along = lambda g, s: g
-    out_specs = grad_specs(direct, shard, width, 3 * gcols, zero, along)
+    wide = 3 * gcols if last or not direct else 5 * gcols
+    out_specs = grad_specs(direct, shard, width, wide, along)
     out_specs += [pl.BlockSpec(block_bias, lambda g, s: (g, 0, 0))]
-    out_shape = grad_shapes(direct, shard, width, 3 * cols, sz)
+    out_shape = grad_shapes(direct, shard, width, steps * wide)
     out_shape += [jax.ShapeDtypeStruct((HEADS // 2,) + bias_t.shape[1:], F32)]
     scratch = [
         pltpu.VMEM((sz.rows, width), BF16),
         pltpu.VMEM((width, sz.rows), BF16),
         pltpu.VMEM((sz.rows, gcols), BF16),
         pltpu.VMEM((sz.rows, 3 * gcols), BF16),
-        pltpu.VMEM((sz.lens[0], sz.lens[0]), BF16),
-        pltpu.VMEM((sz.lens[0], sz.lens[0]), F32),
+        pltpu.VMEM((sz.group, sz.lens[0], sz.lens[0]), BF16),
+        pltpu.VMEM((sz.group, sz.lens[0], sz.lens[0]), F32),
     ]
     args = [scalars, grad_own, grad_far, own, far, qkv, w_qkv, w_out, bias_t]
     flops = 14 * sz.rows * width * cols + 10 * sz.rows * sz.lens[0] * cols
@@ -674,10 +701,12 @@
         args += [carry]
     else:
         in_specs += [once((sz.rows, cols), flat)] * 2
-        out_specs += grad_specs(direct, shard, cols, width, along, zero)
+        if not direct:
+            out_specs += grad_specs(direct, shard, width, 2 * gcols, along)
+            out_shape += grad_shapes(direct, shard, width, width)
         out_specs += [once((sz.rows, width), flat)]
-        out_shape += grad_shapes(direct, shard, width, width, sz)
         out_shape += [jax.ShapeDtypeStruct((sz.rows, width), F32)]
+        scratch += [pltpu.VMEM((width, sz.rows), BF16)]
         args += list(atts)
         flops += 2 * sz.rows * width * width
     return pl.pallas_call(
@@ -698,56 +727,59 @@
 
 GELU_A = math.sqrt(2.0 / math.pi)
 GELU_B = 0.044715
-
-
-def mlp(hidden, grad, w_up, b_up, w_down, scalars, sz, shards):
-    chunk = 512
-    tiles = 3
+MLP_TILES = 3
+CHUNK = 512
+
+
+def mlp(hidden, grad, weights, b_up, scalars, sz, shard, inner_first):
+    chunk = CHUNK
+    tiles = MLP_TILES
     tile = sz.rows // tiles
     inner = b_up.shape[1]
     steps = inner // chunk
-    direct = shards is not None
-    outs = 2 if direct else 1
+    packed = len(weights) == 1
+    direct = shard is not None
     rows, width = sz.rows, sz.width
     quarter = width // 4
+    n_up = len(weights[0].arrays)
+    copied = n_up == 4
 
     def kernel(sc_ref, h_ref, g_ref, bu_ref, *refs):
         refs = list(refs)
         take = lambda count: [refs.pop(0) for _ in range(count)]
-        up_refs = take(4 if direct else 1)
-        down_refs = take(8 if direct else 1)
-        y_ref, t_ref, gbu_ref, gbd_ref = take(4)
-        gwu_refs, gwd_refs = take(outs), take(outs)
+        up_refs = take(n_up)
+        down_refs = up_refs if packed else take(1)
+        y_ref, t_ref, gbu_ref = take(3)
+        if inner_first:
+            (gbd_ref,) = take(1)
+        gw_refs = take(2 if direct else 1)
+        gwd_refs = gw_refs if packed else take(1)
         hidden_t, act_s, gpre_s = take(3)
-        if direct:
-            wu_ref, wd_ref = take(2)
-        else:
-            wu_ref, wd_ref = up_refs[0], down_refs[0]
         step = pl.program_id(0)
-
-        def give(value, start, shard, refs):
-            if direct:
-                hand_out(value, start, shard, sc_ref[0], *refs)
-            else:
-                refs[0][start : start + value.shape[0]] = value.astype(BF16)
+        key, z_here = sc_ref[1 + sz.micro], sc_ref[2 + sz.micro]
 
         @pl.when(step == 0)
         def _():
-            hidden_t[...] = h_ref[...].T
-            gbd_ref[...] = jnp.sum(g_ref[...].astype(F32), axis=0, keepdims=True)
+            turn(h_ref[...], hidden_t, sc_ref[0], shard)
+            if inner_first:
+                gbd_ref[...] = jnp.sum(g_ref[...].astype(F32), axis=0, keepdims=True)
             y_ref[...] = jnp.zeros_like(y_ref)
             t_ref[...] = jnp.zeros_like(t_ref)
 
-        if direct:
-            key = sc_ref[1 + sz.micro]
-            place(up_refs, key, wu_ref, slice(None))
-            for part in range(2):
-                refs_part = down_refs[4 * part : 4 * part + 4]
-                place(refs_part, key, wd_ref, slice(None), shards[1], part * shards[0])
+        if packed:
+            (wd_ref,) = take(1)
+            place_inner(down_refs, key, z_here, wd_ref, slice(chunk, chunk + width // 2))
+        else:
+            wd_ref = down_refs[0]
+        if copied:
+            (wu_ref,) = take(1)
+            place(up_refs, key, z_here, wu_ref, source=slice(0, chunk))
+        else:
+            wu_ref = up_refs[0]
         bias_sum = jnp.zeros((1, chunk), F32)
         for n in range(tiles):
             span = slice(n * tile, (n + 1) * tile)
-            pre = dot_nn(h_ref[span], wu_ref[...]) + bu_ref[...]
+            pre = dot_nn(h_ref[span], wu_ref[:, :chunk]) + bu_ref[...]
             grad_act = dot_nt(g_ref[span], wd_ref[...])
             square = pre * pre
             tanh = jnp.tanh(GELU_A * pre * (1.0 + GELU_B * square))
@@ -757,59 +789,79 @@
                 1.0 + (3.0 * GELU_B) * square
             )
             grad_pre = (grad_act * slope).astype(BF16)
-            act_s[span] = act
+            act_s[0, span] = act[:, : chunk // 2]
+            act_s[1, span] = act[:, chunk // 2 :]
             gpre_s[span] = grad_pre
             bias_sum = bias_sum + jnp.sum(grad_pre.astype(F32), axis=0, keepdims=True)
             y_ref[span] += dot_nn(act, wd_ref[...])
-            t_ref[span] += dot_nt(grad_pre, wu_ref[...])
+            t_ref[span] += dot_nt(grad_pre, wu_ref[:, :chunk])
         gbu_ref[...] = bias_sum
         for n in range(4):
             span = slice(n * quarter, (n + 1) * quarter)
-            give(dot_nn(hidden_t[span, :], gpre_s[...]), n * quarter, shards and shards[0], gwu_refs)
+            give(gw_refs, n // 2, n % 2 * quarter, dot_nn(hidden_t[span, :], gpre_s[...]))
         for n in range(2):
-            span = slice(n * quarter, (n + 1) * quarter)
-            give(dot_tn(act_s[:, span], g_ref[...]), n * quarter, shards and shards[1], gwd_refs)
+            source = sc_ref[0] ^ n if direct else n
+            value = dot_tn(act_s[source], g_ref[...])
+            if not packed:
+                give(gwd_refs, n, 0, value)
+                continue
+            value = value.astype(BF16)
+            cut = chunk // 32
+            for half in range(2):
+                part = value[:, half * width // 2 : (half + 1) * width // 2]
+                if direct:
+                    gw_refs[n][:, half * cut : (half + 1) * cut, chunk:] = part.reshape(
+                        16, cut, width // 2
+                    )
+                    continue
+                for k in range(16):
+                    to = (2 * k + n) * 2 * cut + half * cut
+                    gw_refs[0][to : to + cut, chunk:] = part[k * cut : (k + 1) * cut]
 
     fixed = lambda j, s: (0, 0)
-    zero = lambda j, s: 0
     along = lambda j, s: j
     in_specs = [
         once((rows, width), fixed),
         once((rows, width), fixed),
         pl.BlockSpec((1, chunk), lambda j, s: (0, j)),
-    ] + w_up.specs(chunk, along)
-    args = [scalars, hidden, grad, b_up, *w_up.arrays]
-    if direct:
-        low = w_down.arrays[0].shape[-1] // width - 2
-        for part in range(2):
-            in_specs += w_down.row_specs(width, along, low + part)
-            args += w_down.arrays
-    else:
-        in_specs += [pl.BlockSpec((chunk, width), lambda j, s: (j, 0))]
-        args += w_down.arrays
+    ]
+    args = [scalars, hidden, grad, b_up]
     out_specs = [
         pl.BlockSpec((rows, width), fixed),
         pl.BlockSpec((rows, width), fixed),
         pl.BlockSpec((1, chunk), lambda j, s: (0, j)),
-        pl.BlockSpec((1, width), fixed),
     ]
-    out_specs += grad_specs(direct, shards and shards[0], width, chunk, zero, along)
-    out_specs += grad_specs(direct, shards and shards[1], chunk, width, along, zero)
     out_shape = [
         jax.ShapeDtypeStruct((rows, width), F32),
         jax.ShapeDtypeStruct((rows, width), F32),
         jax.ShapeDtypeStruct((1, inner), F32),
-        jax.ShapeDtypeStruct((1, width), F32),
     ]
-    out_shape += grad_shapes(direct, shards and shards[0], width, inner, sz)
-    out_shape += grad_shapes(direct, shards and shards[1], inner, width, sz)
+    if inner_first:
+        out_specs += [pl.BlockSpec((1, width), fixed)]
+        out_shape += [jax.ShapeDtypeStruct((1, width), F32)]
+    if packed:
+        wide = chunk + width // 2
+        in_specs += weights[0].specs(wide, along)
+        args += weights[0].arrays
+        out_specs += grad_specs(direct, shard, width, wide, along)
+        out_shape += grad_shapes(direct, shard, width, steps * wide)
+    else:
+        in_specs += weights[0].specs(chunk, along)
+        in_specs += [pl.BlockSpec((chunk, width), lambda j, s: (j, 0))]
+        args += [weights[0].arrays[0], weights[1].arrays[0]]
+        out_specs += grad_specs(False, None, width, chunk, along)
+        out_specs += [pl.BlockSpec((chunk, width), lambda j, s: (j, 0))]
+        out_shape += grad_shapes(False, None, width, inner)
+        out_shape += grad_shapes(False, None, inner, width)
     scratch = [
         pltpu.VMEM((width, rows), BF16),
-        pltpu.VMEM((rows, chunk), BF16),
+        pltpu.VMEM((2, rows, chunk // 2), BF16),
         pltpu.VMEM((rows, chunk), BF16),
     ]
-    if direct:
-        scratch += [pltpu.VMEM((width, chunk), BF16), pltpu.VMEM((chunk, width), BF16)]
+    if packed:
+        scratch += [pltpu.VMEM((chunk, width), BF16)]
+    if copied:
+        scratch += [pltpu.VMEM((width, chunk), BF16)]
     return pl.pallas_call(
         kernel,
         grid_spec=pltpu.PrefetchScalarGridSpec(
@@ -855,13 +907,16 @@
     return high, (value - high.astype(F32)).astype(BF16)
 
 
-def table_grad(fold, bucket, places, buckets, sz):
+def offset_grad(fold, places, sz):
     steps = 2 * sz.frames - 1
-    fold = fold.reshape(HEADS, sz.frame, steps, sz.frame)
-    by_offset = sum(
+    fold = fold.reshape(-1, sz.frame, steps, sz.frame)
+    return sum(
         jnp.einsum("hqkp,jpq->hkj", part, places, preferred_element_type=F32)
         for part in split_low(fold)
-    ).reshape(HEADS, -1)
+    ).reshape(fold.shape[0], -1)
+
+
+def table_grad(by_offset, bucket, buckets):
     onehot = bucket_onehot(bucket, buckets)
     return sum(dot_nt(onehot, part) for part in split_low(by_offset))
 
@@ -895,19 +950,16 @@
         along = jnp.stack([value] + [self.from_z(value, k) for k in range(1, self.deep)])
         return jnp.stack([along, self.swap(along, self.Y)], axis=1)
 
-    def scatter_clips(self, value):
-        kept = value[:, 0] + self.swap(value[:, 1], self.Y)
-        return kept[0] + sum(
-            self.from_z(kept[self.deep - k], k) for k in range(1, self.deep)
-        )
-
-    def sum_all(self, value):
-        for which in (self.CORE, self.X, self.Y):
-            value = self.swap_sum(value, which)
-        return value + sum(self.from_z(value, k) for k in range(1, self.deep))
-
-    def gather_small(self, value):
-        parts = self.gather_clips(value)
+    def scatter_clips(self, value, notes):
+        got = self.swap(value[:, 1], self.Y)
+        notes.append(got)
+        kept = value[:, 0] + got
+        got = [self.from_z(kept[self.deep - k], k) for k in range(1, self.deep)]
+        notes.append(got[-1])
+        return kept[0] + sum(got)
+
+    def gather_pairs(self, value):
+        parts = value
         for which in (self.X, self.CORE):
             parts = jnp.stack([parts, self.swap(parts, which)], axis=2 if which == self.X else 3)
         parts = parts.reshape(self.count, -1)
@@ -917,65 +969,164 @@
         return dot_nn(pick, parts).astype(BF16)
 
 
-    def gather_rows(self, shard):
-        along = [shard] + [self.from_z(shard, k) for k in range(1, self.deep)]
-        ready = along[-1]
-        along = jnp.concatenate([a[None] for a in along + along[:-1]])
-        along = lax.dynamic_slice_in_dim(along, (self.deep - self.z) % self.deep, self.deep, 0)
-        cut = shard.shape[0] // 2
-        arrays = []
-        for half, order in enumerate(((self.X, self.Y), (self.Y, self.X))):
-            here = along[:, half * cut : (half + 1) * cut]
-            for which in order:
-                here = jnp.stack([here, self.swap(here, which)])
-            arrays += [here, self.swap(here, self.CORE)]
-        return Pieces(arrays), ready
+def cut_rows(parts):
+    rows, columns = parts[0].shape
+    half = rows // 2
+
+    def kernel(*refs):
+        ins, outs = refs[:-2], refs[-2:]
+        for n, ref in enumerate(ins):
+            for k, out in enumerate(outs):
+                out[n] = ref[k * half : (k + 1) * half]
+
+    return pl.pallas_call(
+        kernel,
+        out_shape=[jax.ShapeDtypeStruct((len(parts), half, columns), BF16)] * 2,
+        compiler_params=pltpu.CompilerParams(vmem_limit_bytes=VMEM_LIMIT),
+        cost_estimate=cost(0, 4 * len(parts) * rows * columns),
+        name="cut_rows",
+    )(*parts)
+
+
+class Gather:
+    def __init__(self, net, shard):
+        self.net = net
+        self.got = [net.from_z(shard, k) for k in range(1, net.deep)]
+        self.shard = shard
+        self.halves = None
+
+    def along_z(self):
+        self.halves = cut_rows([self.shard] + list(self.got))
+
+    def start(self, first):
+        net = self.net
+        order = (net.X, net.Y) if first else (net.Y, net.X)
+        self.got = [net.swap(v, which) for v, which in zip(self.halves, order)]
+
+    def join(self):
+        self.halves = [jnp.stack(pair) for pair in zip(self.halves, self.got)]
+
+    def tie(self, *others):
+        self.got = list(lax.optimization_barrier((*self.got, *others))[: len(self.got)])
+
+    def core(self):
+        net = self.net
+        self.got = [net.swap(v, net.CORE) for v in self.halves]
+
+    def pieces(self):
+        return Pieces([self.halves[0], self.got[0], self.halves[1], self.got[1]])
+
+
+def add_bf16(one, two):
+    return (one.astype(F32) + two.astype(F32)).astype(BF16)
 
 
 class Scatter:
-    def __init__(self, net):
+    def __init__(self, net, pair):
         self.net = net
-
-    @staticmethod
-    def add(one, two):
-        return (one.astype(F32) + two.astype(F32)).astype(BF16)
-
-    @staticmethod
-    def pick(value, at, axis):
-        return lax.dynamic_index_in_dim(value, at, axis, keepdims=False)
-
-    def core(self, keep, send):
-        got = self.net.swap(send, self.net.CORE)
-        total = self.add(keep, got)
-        return total.reshape((self.net.deep, 2, 2) + total.shape[1:])
-
-    def second(self, value):
-        net = self.net
-        cut = value.shape[3] // 2
-        first, last = value[..., :cut, :], value[..., cut:, :]
-        y, x = net.bit(net.Y), net.bit(net.X)
-        got = net.swap(self.pick(first, 1 - y, 1), net.Y), net.swap(self.pick(last, 1 - x, 2), net.X)
-        return self.add(self.pick(first, y, 1), got[0]), self.add(self.pick(last, x, 2), got[1])
-
-    def third(self, value):
-        net = self.net
-        first, last = value
-        y, x = net.bit(net.Y), net.bit(net.X)
-        got = net.swap(self.pick(first, 1 - x, 1), net.X), net.swap(self.pick(last, 1 - y, 1), net.Y)
-        first = self.add(self.pick(first, x, 1), got[0])
-        return jnp.concatenate([first, self.add(self.pick(last, y, 1), got[1])], axis=1)
-
-    def fourth(self, value):
-        net = self.net
-        total = self.pick(value, net.z, 0).astype(F32)
-        for k in range(1, net.deep):
-            send = self.pick(value, (net.z + net.deep - k) % net.deep, 0)
-            total = total + net.from_z(send, k).astype(F32)
-        return total
+        keep, send = [v.reshape((net.deep, 4) + v.shape[1:]) for v in pair]
+        self.keep = [keep]
+        self.got = [net.swap(send, net.CORE)]
+        self.bits = jnp.stack([net.bit(net.Y), net.bit(net.X), net.z])
+        self.rows, self.columns = keep.shape[2:]
+
+    def tie(self, *others):
+        self.got = list(lax.optimization_barrier((*self.got, *others))[: len(self.got)])
+
+    def tie_keep(self, *others):
+        self.keep = list(lax.optimization_barrier((*self.keep, *others))[: len(self.keep)])
+
+    def second(self):
+        net, cut = self.net, self.rows // 2
+
+        def kernel(sc_ref, keep, got, *outs):
+            for half in range(2):
+                span = slice(half * cut, (half + 1) * cut)
+                for role in range(2):
+                    for other in range(2):
+                        near = sc_ref[half] ^ role
+                        at = near * 2 + other if half == 0 else other * 2 + near
+                        outs[2 * half + role][0, other] = add_bf16(keep[0, at, span], got[0, at, span])
+
+        block = (1,) + self.keep[0].shape[1:]
+        out = (2, cut, self.columns)
+        made = pl.pallas_call(
+            kernel,
+            grid_spec=pltpu.PrefetchScalarGridSpec(
+                num_scalar_prefetch=1,
+                grid=(net.deep,),
+                in_specs=[pl.BlockSpec(block, lambda z, s: (z, 0, 0, 0))] * 2,
+                out_specs=[pl.BlockSpec((1,) + out, lambda z, s: (z, 0, 0, 0))] * 4,
+            ),
+            out_shape=[jax.ShapeDtypeStruct((net.deep,) + out, BF16)] * 4,
+            compiler_params=params(1),
+            cost_estimate=cost(0, 6 * self.keep[0].size),
+            name="add_cores",
+        )(self.bits, *self.keep, *self.got)
+        self.keep = [made[0], made[2]]
+        self.got = [net.swap(made[1], net.Y), net.swap(made[3], net.X)]
+
+    def third(self):
+        net, cut = self.net, self.rows // 2
+
+        def kernel(sc_ref, k0, k1, g0, g1, *outs):
+            for half, (keep, got) in enumerate(((k0, g0), (k1, g1))):
+                for role in range(2):
+                    at = sc_ref[1 - half] ^ role
+                    outs[2 * half + role][...] = add_bf16(keep[:, at], got[:, at])
+
+        out = jax.ShapeDtypeStruct((net.deep, cut, self.columns), BF16)
+        made = self.call(kernel, [*self.keep, *self.got], [out] * 4, "add_second")
+        self.keep = [made[0], made[2]]
+        self.got = [net.swap(made[1], net.X), net.swap(made[3], net.Y)]
+
+    def fourth(self, *joined):
+        net, rows, cut = self.net, self.rows, self.rows // 2
+        group = (self,) + joined
+        widths = [v.columns for v in group]
+
+        def kernel(sc_ref, *refs):
+            ins, outs = refs[: 4 * len(group)], refs[4 * len(group) :]
+            for away, out in enumerate(outs):
+                at = (sc_ref[2] + net.deep - away) % net.deep
+                low = 0
+                for n, size in enumerate(widths):
+                    k0, k1, g0, g1 = ins[4 * n : 4 * n + 4]
+                    out[:cut, low : low + size] = add_bf16(k0[at], g0[at])
+                    out[cut:, low : low + size] = add_bf16(k1[at], g1[at])
+                    low += size
+
+        out = jax.ShapeDtypeStruct((rows, sum(widths)), BF16)
+        args = [v for one in group for v in (*one.keep, *one.got)]
+        made = self.call(kernel, args, [out] * net.deep, "add_third")
+        self.keep = [made[0]]
+        self.got = [net.from_z(made[k], k) for k in range(1, net.deep)]
+
+    def total(self):
+        return self.keep[0].astype(F32) + sum(v.astype(F32) for v in self.got)
+
+    def call(self, kernel, args, outs, name):
+        return pl.pallas_call(
+            kernel,
+            grid_spec=pltpu.PrefetchScalarGridSpec(
+                num_scalar_prefetch=1,
+                grid=(1,),
+                in_specs=[pl.BlockSpec(memory_space=pltpu.VMEM)] * len(args),
+                out_specs=[pl.BlockSpec(memory_space=pltpu.VMEM)] * len(outs),
+            ),
+            out_shape=outs,
+            compiler_params=params(1),
+            cost_estimate=cost(0, 6 * sum(v.size for v in args)),
+            name=name,
+        )(self.bits, *args)
 
 
 def tie(value, *others):
     return lax.optimization_barrier((value,) + others)[0]
+
+
+def tie2(values, others):
+    return lax.optimization_barrier((*values, *others))[: len(values)]
 
 
 def body(
@@ -990,15 +1141,20 @@
     width = sz.width
     core = lax.axis_index("win") % 2
     swap = [(n, n ^ 1) for n in range(lax.axis_size("win"))]
-    scalars = jnp.stack([core] + [lengths[n, 0] for n in range(sz.micro)] + [index % 8])
+    flags = [core] + [lengths[n, 0] for n in range(sz.micro)]
+    scalars = jnp.stack(flags + [index % 8, index // 8])
     strip = (sz.micro, 2, 2, sz.frames, sz.half, width)
     tok = tokens.reshape(strip)
     cot = cotangent.reshape(strip)
 
     cond_act = jax.nn.silu(cond[:, 0].astype(F32)).astype(BF16)
     rows = ada_w.shape[0]
+    small = jnp.concatenate([b_up, b_down, rel_table.reshape(-1)])
+    n_cond = cond_act.size
     if net.direct:
-        cond_all = net.gather_clips(cond_act)
+        early = jnp.concatenate([cond_act.reshape(-1), small])
+        early = net.gather_clips(jnp.pad(early, (0, -early.size % 128)))
+        cond_all = early[:, :, :n_cond].reshape(early.shape[:2] + cond_act.shape)
     else:
         cond_all = lax.all_gather(cond_act, "clip", axis=0)
     cond_mine = lax.dynamic_slice_in_dim(cond_all, index * rows, rows, cond_all.ndim - 1)
@@ -1008,8 +1164,9 @@
     spread_b = jnp.zeros((mod_part.shape[1],), F32)
     spread_b = lax.dynamic_update_slice(spread_b, ada_b.astype(F32), (index * ada_b.shape[0],))
     mod_part = (mod_part + spread_b[None, :]).reshape(lead + (6 * width,))
+    notes = []
     if net.direct:
-        mod = net.scatter_clips(mod_part)
+        mod = net.scatter_clips(mod_part, notes)
         mod = net.swap_sum(net.swap_sum(mod, net.CORE), net.X)
     else:
         mod = lax.psum_scatter(mod_part, "clip", scatter_dimension=0, tiled=False)
@@ -1023,45 +1180,86 @@
     shard_q = [by_group[:, n] for n in range(2)]
     inner = w_up.shape[1]
     per = w_down.shape[0] // 2
-    shard_u = w_up.reshape(rows, devices, 2, per)
-    shard_u = [shard_u[:, :, n].reshape(rows, inner // 2) for n in range(2)]
+    thin = CHUNK // devices
+
+    def inner_order(value):
+        if not net.direct:
+            value = value.reshape(-1, devices, 2, per).transpose(2, 0, 1, 3)
+        else:
+            value = value.reshape(-1, devices // 2, 2, 2, per // thin, thin)
+            value = value.transpose(3, 0, 4, 2, 1, 5)
+        return value.reshape(2, -1, inner // 2)
+
+    def inner_back(halves):
+        value = jnp.stack(halves)
+        if not net.direct:
+            value = value.reshape(2, -1, devices, per).transpose(1, 2, 0, 3)
+        else:
+            value = value.reshape(2, -1, per // thin, 2, devices // 2, thin)
+            value = value.transpose(1, 4, 3, 0, 2, 5)
+        return value.reshape(-1, inner)
+
+    def pack_inner(up, down):
+        down = down.reshape(per // thin, thin, 2, width // 2).transpose(2, 1, 0, 3)
+        down = down.reshape(rows, per // thin, width // 2)
+        return jnp.concatenate([up.reshape(rows, -1, CHUNK), down], axis=2).reshape(rows, -1)
+
+    def unpack_inner(value):
+        value = value.reshape(rows, per // thin, -1)
+        down = value[:, :, CHUNK:].reshape(2, thin, per // thin, width // 2)
+        return value[:, :, :CHUNK].reshape(rows, -1), down.transpose(2, 1, 0, 3).reshape(per, width)
+
+    shard_u = inner_order(w_up)
     shard_d = [w_down[:per], w_down[per:]]
-    small = jnp.concatenate([b_up, b_down, rel_table.reshape(-1)])
+    gather = lambda v: lax.all_gather(v, axes, axis=0, tiled=True)
     if net.direct:
-        fold_d = [d.reshape(2, rows, width) for d in shard_d]
         packs = [
             shard_q[0],
             jnp.concatenate([shard_q[1], w_out], axis=1),
-            jnp.concatenate([shard_u[0], fold_d[0][0], fold_d[0][1]], axis=1),
-            jnp.concatenate([shard_u[1], fold_d[1][0], fold_d[1][1]], axis=1),
+            pack_inner(shard_u[0], shard_d[0]),
+            pack_inner(shard_u[1], shard_d[1]),
         ]
-        small = jnp.pad(small, (0, -small.shape[0] % 128))
-        small = net.gather_small(small)
-        q_0, ready = net.gather_rows(packs[0])
-        q_1, ready = net.gather_rows(tie(packs[1], ready))
-        full_q, full_out = [q_0, q_1], q_1
-        u_0, ready = net.gather_rows(tie(packs[2], ready, mod))
-        u_1, ready = net.gather_rows(tie(packs[3], ready))
-        full_u = full_d = [u_0, u_1]
+        rest_q = gather(packs[1])
+        one = Gather(net, packs[0])
+        one.along_z()
+        one.halves = tie2(one.halves, [mod_part])
+        one.start(True)
+        one.join()
+        one.halves = tie2(one.halves, notes[:1])
+        one.start(False)
+        one.join()
+        one.halves = tie2(one.halves, notes[1:])
+        one.core()
+        small = net.gather_pairs(tie(early[:, :, n_cond:], *notes))
+        three = Gather(net, tie(packs[2], *notes))
+        full_q = [one.pieces(), Pieces([rest_q])]
+        full_out = full_q[1]
+        rest = gather(tie(packs[3], early))
     else:
-        gather = lambda v: lax.all_gather(v, axes, axis=0, tiled=True)
         full_q = [Pieces([gather(v)]) for v in shard_q]
         full_out = Pieces([gather(w_out)])
-        full_u = [Pieces([gather(v)]) for v in shard_u]
-        full_d = [Pieces([gather(v)]) for v in shard_d]
+        full_i = [[Pieces([gather(u)]), Pieces([gather(d)])] for u, d in zip(shard_u, shard_d)]
         small = gather(small[None])
     n_up, n_down = b_up.shape[0], b_down.shape[0]
     n_small = n_up + n_down + rel_table.size
-    full_bup = small[:, :n_up].astype(F32).reshape(devices, 2, per)
-    full_bup = [full_bup[:, n].reshape(1, inner // 2) for n in range(2)]
+    full_bup = inner_order(small[:, :n_up].astype(F32).reshape(1, inner))
     full_bdown = small[:, n_up : n_up + n_down].astype(F32).reshape(1, width)
     table = small[:, n_up + n_down : n_small].reshape(-1, HEADS)
     places = offset_onehot(core, sz)
-    bias, bias_t = bias_blocks(table, bucket, places, sz)
+    bias, bias_t = lax.optimization_barrier(bias_blocks(table, bucket, places, sz))
 
     own, send = first_norm(tok, mod, scalars, sz)
     far = lax.ppermute(send, "win", swap)
+    if net.direct:
+        three.along_z()
+        three.start(True)
+        far = tie(far, *three.halves)
     qkv_0, att_0, wide_0 = attention(0, own, far, full_q[0], bias, scalars, sz)
+    if net.direct:
+        three.tie(att_0)
+        three.join()
+        three.start(False)
+        att_0 = tie(att_0, *three.halves)
     qkv_1, att_1, wide_1, wide_out, branch_own, branch_send = attention(
         1, own, far, full_q[1], bias, scalars, sz, att_0, full_out
     )
@@ -1070,56 +1268,87 @@
     flat = (sz.rows, width)
     both = (2, sz.micro, sz.used, sz.half, width)
     hidden_two, grad_mlp = hidden_two.reshape(flat), grad_mlp.reshape(flat)
-    shards = (rows, per) if net.direct else None
-    mlps = [
-        mlp(hidden_two, grad_mlp, full_u[n], full_bup[n], full_d[n], scalars, sz, shards)
-        for n in range(2)
-    ]
-
-    scat = Scatter(net)
+    if net.direct:
+        three.tie(branch_own)
+        three.join()
+        three.core()
+        full_i = [[three.pieces()], [Pieces([rest])]]
+    mlps = []
+    for n in range(2):
+        shard = rows if net.direct and n == 1 else None
+        mlps.append(
+            mlp(hidden_two, grad_mlp, full_i[n], full_bup[n], scalars, sz, shard, n == 0)
+        )
+        if net.direct and n == 0:
+            pack, hidden_two = lax.optimization_barrier((mlps[0][4], hidden_two))
+            r_first = lax.psum_scatter(pack, axes, scatter_dimension=0, tiled=True).astype(F32)
+
+    if net.direct:
+        second = Scatter(net, mlps[1][3:5])
     output, grad_mid, grad_own, grad_send, sums_two = after_mlp(
         tok, cot, branch_own, branch_far, [v[0].reshape(both) for v in mlps],
         [v[1].reshape(both) for v in mlps], mod, full_bdown, scalars, sz,
     )
     grad_far = lax.ppermute(grad_send, "win", swap)
     if net.direct:
-        inner_terms = []
-        for v in mlps:
-            up, down = scat.core(*v[4:6]), scat.core(*v[6:8])
-            inner_terms += [up, down[..., :rows, :], down[..., rows:, :]]
-        terms = jnp.concatenate(inner_terms, axis=-1)
-        grad_far = tie(grad_far, terms)
-    g_q0, fold_0, g_out, carry = unpack(
-        attention_back(
-            0, grad_own, grad_far, own, far, qkv_0, (att_0, att_1), wide_0, wide_out, bias_t,
-            scalars, sz, rows if net.direct else None,
-        ),
-        net.direct,
+        second.tie(grad_own)
+        second.second()
+        grad_own = tie(grad_own, *second.keep)
+    shard = rows if net.direct else None
+    *g_0, carry = attention_back(
+        0, grad_own, grad_far, own, far, qkv_0, (att_0, att_1), wide_0, wide_out, bias_t,
+        scalars, sz, shard,
     )
     if net.direct:
-        terms = scat.second(terms)
-        carry = tie(carry, *terms)
-    g_q1, fold_1, hid_own, hid_send = unpack(
-        attention_back(
-            1, grad_own, grad_far, own, far, qkv_1, None, wide_1, wide_out, bias_t, scalars, sz,
-            rows if net.direct else None, carry,
-        ),
-        net.direct,
+        second.tie(carry)
+        second.third()
+        g_0 = lax.optimization_barrier((*g_0, *second.keep))[: len(g_0)]
+        heads_0 = Scatter(net, g_0[:2])
+        heads_0.second()
+        carry = tie(carry, *heads_0.keep)
+        fold_0 = g_0[2]
+    else:
+        fold_0 = g_0[1]
+    *g_1, fold_1, hid_own, hid_send = attention_back(
+        1, grad_own, grad_far, own, far, qkv_1, None, wide_1, wide_out, bias_t, scalars, sz,
+        shard, carry,
     )
-    hid_far = lax.ppermute(hid_send, "win", swap)
     if net.direct:
-        terms = scat.third(terms)
-        hid_far = tie(hid_far, terms)
+        second.tie(hid_own)
+        second.fourth()
+        heads_0.tie(hid_own)
+        heads_0.third()
+        g_1 = tie2(g_1, second.keep + heads_0.keep)
+        hid_send = tie(hid_send, *second.keep, *heads_0.keep)
+        heads_1 = Scatter(net, g_1)
+        hid_far = lax.ppermute(hid_send, "win", swap)
+        heads_1.second()
+        hid_far = tie(hid_far, *heads_1.keep)
+    else:
+        hid_far = lax.ppermute(hid_send, "win", swap)
     grad_in, sums_one = last_norm(tok, cot, grad_mid, hid_own, hid_far, mod, scalars, sz)
+    if net.direct:
+        heads_1.tie(sums_one)
+        heads_1.third()
+        sums_one = tie(sums_one, *heads_1.keep)
 
     grad_mod = jnp.concatenate(
         [sums_one, sums_two[:, 3:4], sums_two[:, 0:3]], axis=1
     ).reshape(sz.micro, 6 * width)
+    by_offset = jnp.concatenate([offset_grad(fold, places, sz) for fold in (fold_0, fold_1)])
+    g_table = table_grad(by_offset, bucket, table.shape[0]).reshape(devices, -1)
+    g_bup = inner_back([v[2] for v in mlps]).reshape(devices, -1)
+    g_bdown = mlps[0][3].reshape(devices, -1)
+    g_small = jnp.concatenate([g_bup, g_bdown, g_table], axis=1)
     if net.direct:
-        grad_mod = net.swap_sum(net.swap_sum(grad_mod, net.CORE), net.X)
-        mod_all = net.gather_clips(grad_mod)
+        every = jnp.concatenate([grad_mod.reshape(-1), g_small.reshape(-1)])
+        every = net.gather_clips(net.swap_sum(net.swap_sum(every, net.CORE), net.X))
+        mod_all = every[:, :, : grad_mod.size]
+        g_small = jnp.sum(every[:, :, grad_mod.size :], axis=(0, 1)).reshape(g_small.shape)
+        g_small = lax.dynamic_index_in_dim(g_small, index, 0, keepdims=False)
     else:
         mod_all = lax.all_gather(lax.psum(grad_mod, "win"), "clip", axis=0)
+        g_small = lax.psum_scatter(g_small, axes, scatter_dimension=0, tiled=False)
     mod_all = mod_all.reshape(clips * sz.micro, -1)
     grad_ada_w = lax.dot_general(
         cond_mine.astype(F32), mod_all, (((0,), (0,)), ((), ())),
@@ -1128,34 +1357,21 @@
     grad_ada_b = lax.dynamic_slice_in_dim(
         jnp.sum(mod_all, axis=0), index * ada_b.shape[0], ada_b.shape[0]
     )
-    g_table = table_grad(
-        jnp.concatenate([fold_0, fold_1]), bucket, places, table.shape[0], sz
-    ).reshape(devices, -1)
-    g_bup = jnp.stack([v[2].reshape(devices, per) for v in mlps], axis=1).reshape(devices, -1)
-    g_bdown = mlps[0][3].reshape(devices, -1)
-    g_small = jnp.concatenate([g_bup, g_bdown, g_table], axis=1)
     if net.direct:
-        g_small = lax.dynamic_index_in_dim(net.sum_all(g_small), index, 0, keepdims=False)
-        terms_att = jnp.concatenate([scat.core(*v) for v in (g_q0, g_q1, g_out)], axis=-1)
-        terms_att = scat.third(scat.second(terms_att))
-        terms = scat.fourth(terms)
-        terms_att = scat.fourth(terms_att)
-        r_u, r_d = [], []
-        for n in range(2):
-            mine = terms[:, n * inner : (n + 1) * inner]
-            r_u.append(mine[:, : inner // 2])
-            r_d += [mine[:, inner // 2 : inner // 2 + width], mine[:, inner // 2 + width :]]
-        r_q = [terms_att[:, n * 3 * cols : (n + 1) * 3 * cols] for n in range(2)]
-        r_out = terms_att[:, 6 * cols :]
+        heads_1.fourth(heads_0)
+        r_u, r_d = zip(unpack_inner(r_first), unpack_inner(second.total()))
+        mine = heads_1.total()
+        r_q = [mine[:, 3 * cols :].reshape(rows, half_groups, -1), mine[:, : 3 * cols]]
+        r_out = r_q[0][:, :, 3 * sz.gcols :].reshape(rows, width)
+        r_q[0] = r_q[0][:, :, : 3 * sz.gcols]
     else:
         scatter = lambda v: lax.psum_scatter(
-            v[0].astype(F32), axes, scatter_dimension=0, tiled=True
+            v.astype(F32), axes, scatter_dimension=0, tiled=True
         )
-        g_small = lax.psum_scatter(g_small, axes, scatter_dimension=0, tiled=False)
-        r_u = [scatter(v[4:5]) for v in mlps]
-        r_d = [scatter(v[5:6]) for v in mlps]
-        r_q, r_out = [scatter(v) for v in (g_q0, g_q1)], scatter(g_out)
-    r_up = jnp.stack([v.reshape(rows, devices, per) for v in r_u], axis=2).reshape(rows, inner)
+        r_u = [scatter(v[-2]) for v in mlps]
+        r_d = [scatter(v[-1]) for v in mlps]
+        r_q, r_out = [scatter(g_0[0]), scatter(g_1[0])], scatter(g_0[2])
+    r_up = inner_back(r_u)
     r_down = jnp.concatenate(r_d)
     r_qkv = jnp.stack([v.reshape(rows, half_groups, 3, sz.gcols) for v in r_q], axis=1)
     r_qkv = r_qkv.reshape(rows, sz.groups, 3, sz.gcols).transpose(0, 2, 1, 3)
@@ -1165,17 +1381,6 @@
         r_qkv, r_out, r_up, g_small[:n_up], r_down, g_small[n_up : n_up + n_down],
         g_small[n_up + n_down :].reshape(rel_table.shape),
     )
-
-
-def unpack(results, direct):
-    results = list(results)
-    count = 2 if direct else 1
-    out = [results[:count], results[count]]
-    results = results[count + 1 :]
-    if len(results) == count + 1:
-        if results[0].ndim == (3 if direct else 2):
-            return out + [results[:count], results[count]]
-    return out + results
 
 
 def solution(mesh):

time: 723 us -> 546 us (0.76)
  waiting for transfers between devices: 156 us -> 94.4 us
  other arithmetic: 69.4 us -> 21.9 us
  Pallas kernels: 300 us -> 259 us
  local copies, waits for them, and re-layouts: 76.4 us -> 49.3 us
  between operations: 2.43 us -> 15.8 us
  starting transfers between devices: 93 us -> 83.6 us
    ppermute x33 -> x21, waiting for transfers between devices: 84.5 us -> 30.7 us  [from_z(): lax.ppermute(value, self.AXES, [(n, move(n)) for n in range(self.count)])]
    pallas_call x0 -> x10, Pallas kernels: none -> 38.4 us  [the longest x5 18.1 us: call(): pl.pallas_call(kernel, grid_spec=pltpu.PrefetchScalarGridSpec(num_scalar_...]
    pallas_call x2, Pallas kernels: 98.6 us -> 63 us  [attention_back(): pl.pallas_call(kernel, grid_spec=pltpu.PrefetchScalarGridSpec(num_scalar_...]
    convert_element_type x15 -> x2, other arithmetic: 31.3 us -> 1.23 us  [split_low(): return (high, (value - high.astype(F32)).astype(BF16))]
    pallas_call x2, Pallas kernels: 67.3 us -> 40 us  [attention(): pl.pallas_call(kernel, grid_spec=pltpu.PrefetchScalarGridSpec(num_scalar_...]
    pallas_call x2, Pallas kernels: 98.6 us -> 82.5 us  [mlp(): pl.pallas_call(kernel, grid_spec=pltpu.PrefetchScalarGridSpec(num_scalar_...]
    ppermute x52 -> x36, waiting for transfers between devices: 71.9 us -> 58.8 us  [swap(): lax.ppermute(value, self.AXES, [(n, n ^ which) for n in range(self.count)])]
    unnamed x124 -> x115, local copies, waits for them, and re-layouts: 24.3 us -> 11.5 us
  transfers between devices with their start and end apart: 89 -> 64, of which waited for: 28 -> 17; matrix products, arithmetic and copies ran while one was open for 21% -> 13% of each run, Pallas kernels for 42% -> 40%
where the time goes in v2:
time: 546 us; the launch traced here: 539 us
  Pallas kernels  259 us (47%)
  waiting for transfers between devices  94.4 us (17%)
  starting transfers between devices  83.6 us (15%)
  local copies, waits for them, and re-layouts  49.3 us (9%)
  other arithmetic  21.9 us (4%)
  between operations  15.8 us (3%)
  matrix products  15.6 us (3%)
    pallas_call x2, Pallas kernels, mlp(): pl.pallas_call(kernel, grid_spec=pltpu.PrefetchScalarGridSpec(num_scalar_...  82.5 us
    pallas_call x2, Pallas kernels, attention_back(): pl.pallas_call(kernel, grid_spec=pltpu.PrefetchScalarGridSpec(num_scalar_...  63 us
    ppermute x36, waiting for transfers between devices, swap(): lax.ppermute(value, self.AXES, [(n, n ^ which) for n in range(self.count)])  58.8 us
    ppermute x21, starting transfers between devices, from_z(): lax.ppermute(value, self.AXES, [(n, move(n)) for n in range(self.count)])  42.6 us
    ppermute x36, starting transfers between devices, swap(): lax.ppermute(value, self.AXES, [(n, n ^ which) for n in range(self.count)])  40.3 us
    pallas_call x2, Pallas kernels, attention(): pl.pallas_call(kernel, grid_spec=pltpu.PrefetchScalarGridSpec(num_scalar_...  40 us
    ppermute x21, waiting for transfers between devices, from_z(): lax.ppermute(value, self.AXES, [(n, move(n)) for n in range(self.count)])  30.7 us
    pallas_call x5, Pallas kernels, call(): pl.pallas_call(kernel, grid_spec=pltpu.PrefetchScalarGridSpec(num_scalar_...  18.1 us
  transfers between devices with their start and end apart: 64, of which 17 were waited for; matrix products, arithmetic and copies ran while one was open for 13% of the time, Pallas kernels for 40%

profile of v2, /device:TPU:0, one launch (start us, length us, event | category | flops | bytes accessed | tf_op | source)
XLA Modules:
  0.0 539.4 jit_solution(3082600247498086575)
XLA Ops:
  62.5 10.3 %collective-permute-done.9 = f32[2,6144]{1,0:T(2,128)S(1)} collective-permute-done((f32[2,6144]{1,0:T(2,128)S(1)}, f32[2,6144]{1,0:T(2,128)S(1)}, u32[]{:S(2)}, u32[]{:S(2)}) %collective-permute-start.9) | collective-permute-done | bytes 49184 | tf_op jit(solution)/shard_map/ppermute | solution.py:939
  95.9 9.4 %collective-permute-done.11.refs_1_ = bf16[32,4096]{1,0:T(8,128)(2,1)S(1)} collective-permute-done((bf16[32,4096]{1,0:T(8,128)(2,1)S(1)}, bf16[32,4096]{1,0:T(8,128)(2,1)S(1)}, u32[]{:S(2)}, u32[]{:S(2)}) %collective-permute-start.11) | collective-permute-done | bytes 262176 | tf_op jit(solution)/shard_map/ppermute | solution.py:943
  111.0 17.7 %attention.1 = (bf16[3,1152,512]{2,1,0:T(8,128)(2,1)}, bf16[1152,512]{1,0:T(8,128)(2,1)}, bf16[1024,1536]{1,0:T(8,128)(2,1)}) custom-call(s32[5]{0:T(128)} %stack.190.sc_ref, bf16[2,9,32,1024]{3,2,1,0:T(8,128)(2,1)} %get-tuple-element.124.own_ref, bf16[2,9,32,1024]{3,2,1,0:T(8,128)(2,1)} %collective-permute-done.10.far_ref, ...), custom_call_target="tpu_custom_call" | custom-call | flops 13136560128 | bytes 18874368 | tf_op jit(solution)/shard_map/attention/pallas_call | solution.py:537
  130.2 6.1 %collective-permute-start.28 = (bf16[2,4,16,4096]{3,2,1,0:T(8,128)(2,1)}, bf16[2,4,16,4096]{3,2,1,0:T(8,128)(2,1)}, u32[]{:S(2)}, u32[]{:S(2)}) collective-permute-start(bf16[2,4,16,4096]{3,2,1,0:T(8,128)(2,1)} %get-tuple-element.312), channel_id=1, source_target_pairs={{0,4},{1,5},{2,6},{3,7},{4,0},{5,1},{6,2},{7,3},{8,12},{9,13},{10,... | collective-permute-start | bytes 3145736 | tf_op jit(solution)/shard_map/ppermute | solution.py:939
  137.9 22.3 %attention_last.1 = (bf16[3,1152,512]{2,1,0:T(8,128)(2,1)}, bf16[1152,512]{1,0:T(8,128)(2,1)}, bf16[1024,1536]{1,0:T(8,128)(2,1)}, bf16[1024,1024]{1,0:T(8,128)(...) custom-call(s32[5]{0:T(128)} %stack.190.sc_ref, ...), custom_call_target="tpu_custom_call" | custom-call | flops 20384317440 | bytes 18874368 | tf_op jit(solution)/shard_map/attention_last/pallas_call | solution.py:537
  160.2 8.0 %collective-permute-done.28 = bf16[2,4,16,4096]{3,2,1,0:T(8,128)(2,1)} collective-permute-done((bf16[2,4,16,4096]{3,2,1,0:T(8,128)(2,1)}, bf16[2,4,16,4096]{3,2,1,0:T(8,128)(2,1)}, u32[]{:S(2)}, u32[]{:S(2)}) %collective-permute-start.28) | collective-permute-done | bytes 1048608 | tf_op jit(solution)/shard_map/ppermute | solution.py:939
  168.2 5.5 %collective-permute-done.29 = bf16[2,4,16,4096]{3,2,1,0:T(8,128)(2,1)} collective-permute-done((bf16[2,4,16,4096]{3,2,1,0:T(8,128)(2,1)}, bf16[2,4,16,4096]{3,2,1,0:T(8,128)(2,1)}, u32[]{:S(2)}, u32[]{:S(2)}) %collective-permute-start.29) | collective-permute-done | bytes 1048608 | tf_op jit(solution)/shard_map/ppermute | solution.py:939
  181.8 4.8 collective-permute-done.27.bf_ref
  186.6 7.2 %second_norm.1 = (bf16[2,2,9,32,1024]{4,3,2,1,0:T(8,128)(2,1)}, bf16[2,2,9,32,1024]{4,3,2,1,0:T(8,128)(2,1)}) custom-call(s32[5]{0:T(128)} %stack.190.sc_ref, bf16[2,2,2,5,32,1024]{5,4,3,2,1,0:T(8,128)(2,1)} %bitcast.218, bf16[2,2,2,5,32,1024]{5,4,3,2,1,0:T(8,128)(2,1)} %bitcast.221, bf16[2,9,32,1024]{3,2,1,0:T(8,128)(2,1)} %get-tuple-element.144.bo_ref, ...), custom_call_target="tpu_custom_call" | custom-call | tf_op jit(solution)/shard_map/second_norm/pallas_call | solution.py:147
  193.9 41.1 %mlp.2 = (f32[1152,1024]{1,0:T(8,128)}, f32[1152,1024]{1,0:T(8,128)}, f32[1,2048]{1,0:T(1,128)}, f32[1,1024]{1,0:T(1,128)}, bf16[1024,4096]{1,0:T(8,128)(2,1)}) custom-call(s32[5]{0:T(128)} %stack.190.sc_ref, bf16[1152,1024]{1,0:T(8,128)(2,1)} %bitcast.290, bf16[1152,1024]{1,0:T(8,128)(2,1)} %bitcast.292, f32[1,2048]{1,0:T(1,128)} %squeeze.41.bu_ref, ...), custom_call_target="tpu_custom_call" | custom-call | flops 33822867456 | bytes 18874368 | tf_op jit(solution)/shard_map/mlp/pallas_call | solution.py:865
  235.0 41.4 %mlp.3 = (f32[1152,1024]{1,0:T(8,128)}, f32[1152,1024]{1,0:T(8,128)}, f32[1,2048]{1,0:T(1,128)}, bf16[16,32,4096]{2,1,0:T(8,128)(2,1)}, bf16[16,32,4096]{2,1,0:T(8,128)(2,1)}) custom-call(s32[5]{0:T(128)} %stack.190.sc_ref, bf16[1152,1024]{1,0:T(8,128)(2,1)} %bitcast.291, bf16[1152,1024]{1,0:T(8,128)(2,1)} %bitcast.293, f32[1,2048]{1,0:T(1,128)} %squeeze.42.bu_ref, ...), custom_call_target="tpu_custom_call" | custom-call | flops 33822867456 | bytes 18874368 | tf_op jit(solution)/shard_map/mlp/pallas_call | solution.py:865
  277.1 14.9 %after_mlp.1 = (bf16[2,2,2,5,32,1024]{5,4,3,2,1,0:T(8,128)(2,1)}, f32[2,2,9,32,1024]{4,3,2,1,0:T(8,128)}, bf16[2,9,32,1024]{3,2,1,0:T(8,128)(2,1)}, bf16[2,9,32,1024]{3,2,1,0:T(8,128)(2,1)}, f32[2,4,1024]{2,1,0:T(4,128)}) custom-call(s32[5]{0:T(128)} %stack.190.sc_ref, bf16[2,2,2,5,32,1024]{5,4,3,2,1,0:T(8,128)(2,1)} %bitcast.219, ...), custom_call_target="tpu_custom_call" | custom-call | tf_op jit(solution)/shard_map/after_mlp/pallas_call | solution.py:209
  296.7 6.6 %add_cores.3 = (bf16[4,2,16,4096]{3,2,1,0:T(8,128)(2,1)}, bf16[4,2,16,4096]{3,2,1,0:T(8,128)(2,1)}, bf16[4,2,16,4096]{3,2,1,0:T(8,128)(2,1)}, bf16[4,2,16,4096]{3,2,1,0:T(8,128)(2,1)}) custom-call(s32[3]{0:T(128)} %pad_add_fusion.sc_ref, bf16[4,4,32,4096]{3,2,1,0:T(8,128)(2,1)} %bitcast.236, bf16[4,4,32,4096]{3,2,1,0:T(8,128)(2,1)} %collective-permute-done.32.got), custom_call_target="tpu_custom_call" | custom-call | bytes 12582912 | tf_op jit(solution)/shard_map/add_cores/pallas_call | solution.py:1053
  303.4 32.5 %attention_back.1 = (bf16[16,32,2560]{2,1,0:T(8,128)(2,1)}, bf16[16,32,2560]{2,1,0:T(8,128)(2,1)}, f32[8,64,576]{2,1,0:T(8,128)}, f32[1152,1024]{1,0:T(8,128)}) custom-call(s32[5]{0:T(128)} %stack.190.sc_ref, bf16[2,9,32,1024]{3,2,1,0:T(8,128)(2,1)} %get-tuple-element.165.go_ref, bf16[2,9,32,1024]{3,2,1,0:T(8,128)(2,1)} %collective-permute-done.33.gf_ref, ...), custom_call_target="tpu_custom_call" | custom-call | flops 38277218304 | bytes 28311552 | tf_op jit(solution)/shard_map/attention_back/pallas_call | solution.py:712
  335.9 10.2 %collective-permute-done.35.g1 = bf16[4,2,16,4096]{3,2,1,0:T(8,128)(2,1)S(1)} collective-permute-done((bf16[4,2,16,4096]{3,2,1,0:T(8,128)(2,1)}, bf16[4,2,16,4096]{3,2,1,0:T(8,128)(2,1)S(1)}, u32[]{:S(2)}, u32[]{:S(2)}) %collective-permute-start.35) | collective-permute-done | bytes 1048608 | tf_op jit(solution)/shard_map/ppermute | solution.py:939
  362.1 5.2 add_cores.4
  369.3 30.5 %attention_back_last.1 = (bf16[16,32,1536]{2,1,0:T(8,128)(2,1)}, bf16[16,32,1536]{2,1,0:T(8,128)(2,1)}, f32[8,64,576]{2,1,0:T(8,128)}, bf16[2,9,32,1024]{3,2,1,0:T(8,128)(2,1)}, bf16[2,9,32,1024]{3,2,1,0:T(8,128)(2,1)}) custom-call(s32[5]{0:T(128)} %stack.190.sc_ref, bf16[2,9,32,1024]{3,2,1,0:T(8,128)(2,1)} %get-tuple-element.165.go_ref, ...), custom_call_target="tpu_custom_call" | custom-call | flops 31029460992 | bytes 28311552 | tf_op jit(solution)/shard_map/attention_back_last/pallas_call | solution.py:712
  404.0 7.4 %collective-permute-done.40.g1 = bf16[4,2,16,2560]{3,2,1,0:T(8,128)(2,1)S(1)} collective-permute-done((bf16[4,2,16,2560]{3,2,1,0:T(8,128)(2,1)}, bf16[4,2,16,2560]{3,2,1,0:T(8,128)(2,1)S(1)}, u32[]{:S(2)}, u32[]{:S(2)}) %collective-permute-start.40) | collective-permute-done | bytes 655392 | tf_op jit(solution)/shard_map/ppermute | solution.py:939
  417.7 7.7 %collective-permute-start.58 = (bf16[32,4096]{1,0:T(8,128)(2,1)}, bf16[32,4096]{1,0:T(8,128)(2,1)S(1)}, u32[]{:S(2)}, u32[]{:S(2)}) collective-permute-start(bf16[32,4096]{1,0:T(8,128)(2,1)} %get-tuple-element.234), channel_id=1, source_target_pairs={{0,24},{1,25},{2,26},{3,27},{4,28},{5,29},{6,30},{7,31},{8,0},{9,1... | collective-permute-start | bytes 786440 | tf_op jit(solution)/shard_map/ppermute | solution.py:943
  425.4 8.1 %collective-permute-start.59 = (bf16[32,4096]{1,0:T(8,128)(2,1)}, bf16[32,4096]{1,0:T(8,128)(2,1)S(1)}, u32[]{:S(2)}, u32[]{:S(2)}) collective-permute-start(bf16[32,4096]{1,0:T(8,128)(2,1)} %get-tuple-element.235), channel_id=1, source_target_pairs={{0,16},{1,17},{2,18},{3,19},{4,20},{5,21},{6,22},{7,23},{8,24},{9,... | collective-permute-start | bytes 786440 | tf_op jit(solution)/shard_map/ppermute | solution.py:943
  444.3 5.5 %collective-permute-start.43 = (bf16[4,2,16,1536]{3,2,1,0:T(8,128)(2,1)}, bf16[4,2,16,1536]{3,2,1,0:T(8,128)(2,1)S(1)}, u32[]{:S(2)}, u32[]{:S(2)}) collective-permute-start(bf16[4,2,16,1536]{3,2,1,0:T(8,128)(2,1)} %get-tuple-element.212), channel_id=1, source_target_pairs={{0,4},{1,5},{2,6},{3,7},{4,0},{5,1},{6,2},{7,3},{8,12},{9,13},{10,... | collective-permute-start | bytes 1179656 | tf_op jit(solution)/shard_map/ppermute | solution.py:939
  453.0 8.2 %last_norm.1 = (bf16[2,2,2,5,32,1024]{5,4,3,2,1,0:T(8,128)(2,1)}, f32[2,2,1024]{2,1,0:T(2,128)}) custom-call(s32[5]{0:T(128)} %stack.190.sc_ref, bf16[2,2,2,5,32,1024]{5,4,3,2,1,0:T(8,128)(2,1)} %bitcast.220, bf16[2,2,2,5,32,1024]{5,4,3,2,1,0:T(8,128)(2,1)} %bitcast.223, f32[2,2,9,32,1024]{4,3,2,1,0:T(8,128)} %get-tuple-element.158.gm_ref, ...), custom_call_target="tpu_custom_call" | custom-call | tf_op jit(solution)/shard_map/last_norm/pallas_call | solution.py:272
  476.8 6.2 %collective-permute-done.46 = f32[25600]{0:T(1024)S(1)} collective-permute-done((f32[25600]{0:T(1024)S(1)}, f32[25600]{0:T(1024)S(1)}, u32[]{:S(2)}, u32[]{:S(2)}) %collective-permute-start.46) | collective-permute-done | bytes 102432 | tf_op jit(solution)/shard_map/ppermute | solution.py:939
  502.0 16.4 %collective-permute-done.56 = bf16[32,4096]{1,0:T(8,128)(2,1)S(1)} collective-permute-done((bf16[32,4096]{1,0:T(8,128)(2,1)}, bf16[32,4096]{1,0:T(8,128)(2,1)S(1)}, u32[]{:S(2)}, u32[]{:S(2)}) %collective-permute-start.56) | collective-permute-done | bytes 262176 | tf_op jit(solution)/shard_map/ppermute | solution.py:943
  (395 shorter events, 190.5 us)
Async XLA Ops:
  7.3 130.6 %all-gather.3.cloned.1.call-start = ((), (), s32[]{:S(2)}) async-start(), calls=%async_computation.1 | async-start | bytes 5406720 | tf_op jit(solution)/shard_map/all_gather | solution.py:1214
  9.8 225.2 %all-gather.5.cloned.1.call-start = ((), (), s32[]{:S(2)}) async-start(), calls=%async_computation.2 | async-start | bytes 8650752 | tf_op jit(solution)/shard_map/all_gather | solution.py:1214
  20.6 507.1 %reduce-scatter.2.cloned.1.call-start = ((), (), s32[]{:S(2)}) async-start(), calls=%async_computation.3 | async-start | bytes 8650752 | tf_op jit(solution)/shard_map/reduce_scatter | solution.py:1284
  49.6 34.7 %collective-permute-start.13 = (bf16[32,4096]{1,0:T(8,128)(2,1)S(1)}, bf16[32,4096]{1,0:T(8,128)(2,1)S(1)}, u32[]{:S(2)}, u32[]{:S(2)}) collective-permute-start(bf16[32,4096]{1,0:T(8,128)(2,1)S(1)} %copy.298.refs_0_), channel_id=1, source_target_pairs={{0,8},{1,9},{2,10},{3,11},{4,12},{5,13},{6,14},{7,15},{8,16},{9,17... | collective-permute-start | bytes 786440 | tf_op jit(solution)/shard_map/ppermute | solution.py:943
  50.5 45.4 %collective-permute-start.12 = (bf16[32,4096]{1,0:T(8,128)(2,1)S(1)}, bf16[32,4096]{1,0:T(8,128)(2,1)S(1)}, u32[]{:S(2)}, u32[]{:S(2)}) collective-permute-start(bf16[32,4096]{1,0:T(8,128)(2,1)S(1)} %copy.298.refs_0_), channel_id=1, source_target_pairs={{0,16},{1,17},{2,18},{3,19},{4,20},{5,21},{6,22},{7,23},{8,24},{9,... | collective-permute-start | bytes 786440 | tf_op jit(solution)/shard_map/ppermute | solution.py:943
  78.0 32.9 %collective-permute-start.10 = (bf16[2,9,32,1024]{3,2,1,0:T(8,128)(2,1)}, bf16[2,9,32,1024]{3,2,1,0:T(8,128)(2,1)}, u32[]{:S(2)}, u32[]{:S(2)}) collective-permute-start(bf16[2,9,32,1024]{3,2,1,0:T(8,128)(2,1)} %get-tuple-element.125), channel_id=1, source_target_pairs={{0,1},{1,0},{2,3},{3,2},{4,5},{5,4},{6,7},{7,6},{8,9},{9,8},{10,11... | collective-permute-start | bytes 3538952 | tf_op jit(solution)/shard_map/ppermute | solution.py:1252
  80.0 31.0 %collective-permute-start.23 = (bf16[2,2,4,16,1536]{4,3,2,1,0:T(8,128)(2,1)}, bf16[2,2,4,16,1536]{4,3,2,1,0:T(8,128)(2,1)}, u32[]{:S(2)}, u32[]{:S(2)}) collective-permute-start(bf16[2,2,4,16,1536]{4,3,2,1,0:T(8,128)(2,1)} %pad_maximum_fusion.6.refs_0_), channel_id=1, source_target_pairs={{0,1},{1,0},{2,3},{3,2},{4,5},{5,4},{6,7},{7,6},{8,9},{9,8},{10,11... | collective-permute-start | bytes 2359304 | tf_op jit(solution)/shard_map/ppermute | solution.py:939
  80.5 30.5 %collective-permute-start.24 = (bf16[2,2,4,16,1536]{4,3,2,1,0:T(8,128)(2,1)}, bf16[2,2,4,16,1536]{4,3,2,1,0:T(8,128)(2,1)}, u32[]{:S(2)}, u32[]{:S(2)}) collective-permute-start(bf16[2,2,4,16,1536]{4,3,2,1,0:T(8,128)(2,1)} %pad_maximum_fusion.7.refs_2_), channel_id=1, source_target_pairs={{0,1},{1,0},{2,3},{3,2},{4,5},{5,4},{6,7},{7,6},{8,9},{9,8},{10,11... | collective-permute-start | bytes 2359304 | tf_op jit(solution)/shard_map/ppermute | solution.py:939
  84.3 21.1 %collective-permute-start.11 = (bf16[32,4096]{1,0:T(8,128)(2,1)S(1)}, bf16[32,4096]{1,0:T(8,128)(2,1)S(1)}, u32[]{:S(2)}, u32[]{:S(2)}) collective-permute-start(bf16[32,4096]{1,0:T(8,128)(2,1)S(1)} %copy.298.refs_0_), channel_id=1, source_target_pairs={{0,24},{1,25},{2,26},{3,27},{4,28},{5,29},{6,30},{7,31},{8,0},{9,1... | collective-permute-start | bytes 786440 | tf_op jit(solution)/shard_map/ppermute | solution.py:943
  130.2 38.0 %collective-permute-start.28 = (bf16[2,4,16,4096]{3,2,1,0:T(8,128)(2,1)}, bf16[2,4,16,4096]{3,2,1,0:T(8,128)(2,1)}, u32[]{:S(2)}, u32[]{:S(2)}) collective-permute-start(bf16[2,4,16,4096]{3,2,1,0:T(8,128)(2,1)} %get-tuple-element.312), channel_id=1, source_target_pairs={{0,4},{1,5},{2,6},{3,7},{4,0},{5,1},{6,2},{7,3},{8,12},{9,13},{10,... | collective-permute-start | bytes 3145736 | tf_op jit(solution)/shard_map/ppermute | solution.py:939
  137.8 35.9 %collective-permute-start.29 = (bf16[2,4,16,4096]{3,2,1,0:T(8,128)(2,1)}, bf16[2,4,16,4096]{3,2,1,0:T(8,128)(2,1)}, u32[]{:S(2)}, u32[]{:S(2)}) collective-permute-start(bf16[2,4,16,4096]{3,2,1,0:T(8,128)(2,1)} %get-tuple-element.310), channel_id=1, source_target_pairs={{0,2},{1,3},{2,0},{3,1},{4,6},{5,7},{6,4},{7,5},{8,10},{9,11},{10,... | collective-permute-start | bytes 3145736 | tf_op jit(solution)/shard_map/ppermute | solution.py:939
  303.2 32.6 %collective-permute-start.34 = (bf16[4,2,16,4096]{3,2,1,0:T(8,128)(2,1)}, bf16[4,2,16,4096]{3,2,1,0:T(8,128)(2,1)S(1)}, u32[]{:S(2)}, u32[]{:S(2)}) collective-permute-start(bf16[4,2,16,4096]{3,2,1,0:T(8,128)(2,1)} %get-tuple-element.178), channel_id=1, source_target_pairs={{0,4},{1,5},{2,6},{3,7},{4,0},{5,1},{6,2},{7,3},{8,12},{9,13},{10,... | collective-permute-start | bytes 3145736 | tf_op jit(solution)/shard_map/ppermute | solution.py:939
  303.2 42.9 %collective-permute-start.35 = (bf16[4,2,16,4096]{3,2,1,0:T(8,128)(2,1)}, bf16[4,2,16,4096]{3,2,1,0:T(8,128)(2,1)S(1)}, u32[]{:S(2)}, u32[]{:S(2)}) collective-permute-start(bf16[4,2,16,4096]{3,2,1,0:T(8,128)(2,1)} %get-tuple-element.179), channel_id=1, source_target_pairs={{0,2},{1,3},{2,0},{3,1},{4,6},{5,7},{6,4},{7,5},{8,10},{9,11},{10,... | collective-permute-start | bytes 3145736 | tf_op jit(solution)/shard_map/ppermute | solution.py:939
  354.9 44.9 %collective-permute-start.37 = (bf16[4,16,4096]{2,1,0:T(8,128)(2,1)}, bf16[4,16,4096]{2,1,0:T(8,128)(2,1)S(1)}, u32[]{:S(2)}, u32[]{:S(2)}) collective-permute-start(bf16[4,16,4096]{2,1,0:T(8,128)(2,1)} %get-tuple-element.191), channel_id=1, source_target_pairs={{0,2},{1,3},{2,0},{3,1},{4,6},{5,7},{6,4},{7,5},{8,10},{9,11},{10,... | collective-permute-start | bytes 1572872 | tf_op jit(solution)/shard_map/ppermute | solution.py:939
  357.1 42.7 %collective-permute-start.38 = (bf16[4,16,4096]{2,1,0:T(8,128)(2,1)}, bf16[4,16,4096]{2,1,0:T(8,128)(2,1)}, u32[]{:S(2)}, u32[]{:S(2)}) collective-permute-start(bf16[4,16,4096]{2,1,0:T(8,128)(2,1)} %get-tuple-element.192), channel_id=1, source_target_pairs={{0,4},{1,5},{2,6},{3,7},{4,0},{5,1},{6,2},{7,3},{8,12},{9,13},{10,... | collective-permute-start | bytes 1572872 | tf_op jit(solution)/shard_map/ppermute | solution.py:939
  367.3 36.6 %collective-permute-start.39 = (bf16[4,2,16,2560]{3,2,1,0:T(8,128)(2,1)}, bf16[4,2,16,2560]{3,2,1,0:T(8,128)(2,1)S(1)}, u32[]{:S(2)}, u32[]{:S(2)}) collective-permute-start(bf16[4,2,16,2560]{3,2,1,0:T(8,128)(2,1)} %get-tuple-element.196), channel_id=1, source_target_pairs={{0,4},{1,5},{2,6},{3,7},{4,0},{5,1},{6,2},{7,3},{8,12},{9,13},{10,... | collective-permute-start | bytes 1966088 | tf_op jit(solution)/shard_map/ppermute | solution.py:939
  368.7 42.6 %collective-permute-start.40 = (bf16[4,2,16,2560]{3,2,1,0:T(8,128)(2,1)}, bf16[4,2,16,2560]{3,2,1,0:T(8,128)(2,1)S(1)}, u32[]{:S(2)}, u32[]{:S(2)}) collective-permute-start(bf16[4,2,16,2560]{3,2,1,0:T(8,128)(2,1)} %get-tuple-element.197), channel_id=1, source_target_pairs={{0,2},{1,3},{2,0},{3,1},{4,6},{5,7},{6,4},{7,5},{8,10},{9,11},{10,... | collective-permute-start | bytes 1966088 | tf_op jit(solution)/shard_map/ppermute | solution.py:939
  415.8 24.0 %collective-permute-start.42 = (bf16[4,4,32,1536]{3,2,1,0:T(8,128)(2,1)}, bf16[4,4,32,1536]{3,2,1,0:T(8,128)(2,1)}, u32[]{:S(2)}, u32[]{:S(2)}) collective-permute-start(bf16[4,4,32,1536]{3,2,1,0:T(8,128)(2,1)} %bitcast.75), channel_id=1, source_target_pairs={{0,1},{1,0},{2,3},{3,2},{4,5},{5,4},{6,7},{7,6},{8,9},{9,8},{10,11... | collective-permute-start | bytes 4718600 | tf_op jit(solution)/shard_map/ppermute | solution.py:939
  417.7 55.9 %collective-permute-start.58 = (bf16[32,4096]{1,0:T(8,128)(2,1)}, bf16[32,4096]{1,0:T(8,128)(2,1)S(1)}, u32[]{:S(2)}, u32[]{:S(2)}) collective-permute-start(bf16[32,4096]{1,0:T(8,128)(2,1)} %get-tuple-element.234), channel_id=1, source_target_pairs={{0,24},{1,25},{2,26},{3,27},{4,28},{5,29},{6,30},{7,31},{8,0},{9,1... | collective-permute-start | bytes 786440 | tf_op jit(solution)/shard_map/ppermute | solution.py:943
  425.4 49.1 %collective-permute-start.59 = (bf16[32,4096]{1,0:T(8,128)(2,1)}, bf16[32,4096]{1,0:T(8,128)(2,1)S(1)}, u32[]{:S(2)}, u32[]{:S(2)}) collective-permute-start(bf16[32,4096]{1,0:T(8,128)(2,1)} %get-tuple-element.235), channel_id=1, source_target_pairs={{0,16},{1,17},{2,18},{3,19},{4,20},{5,21},{6,22},{7,23},{8,24},{9,... | collective-permute-start | bytes 786440 | tf_op jit(solution)/shard_map/ppermute | solution.py:943
  452.0 22.6 %collective-permute-start.60 = (bf16[32,4096]{1,0:T(8,128)(2,1)}, bf16[32,4096]{1,0:T(8,128)(2,1)S(1)}, u32[]{:S(2)}, u32[]{:S(2)}) collective-permute-start(bf16[32,4096]{1,0:T(8,128)(2,1)} %get-tuple-element.236), channel_id=1, source_target_pairs={{0,8},{1,9},{2,10},{3,11},{4,12},{5,13},{6,14},{7,15},{8,16},{9,17... | collective-permute-start | bytes 786440 | tf_op jit(solution)/shard_map/ppermute | solution.py:943
  494.9 23.5 %collective-permute-start.56 = (bf16[32,4096]{1,0:T(8,128)(2,1)}, bf16[32,4096]{1,0:T(8,128)(2,1)S(1)}, u32[]{:S(2)}, u32[]{:S(2)}) collective-permute-start(bf16[32,4096]{1,0:T(8,128)(2,1)} %get-tuple-element.231), channel_id=1, source_target_pairs={{0,16},{1,17},{2,18},{3,19},{4,20},{5,21},{6,22},{7,23},{8,24},{9,... | collective-permute-start | bytes 786440 | tf_op jit(solution)/shard_map/ppermute | solution.py:943
  495.1 23.2 %collective-permute-start.57 = (bf16[32,4096]{1,0:T(8,128)(2,1)}, bf16[32,4096]{1,0:T(8,128)(2,1)S(1)}, u32[]{:S(2)}, u32[]{:S(2)}) collective-permute-start(bf16[32,4096]{1,0:T(8,128)(2,1)} %get-tuple-element.232), channel_id=1, source_target_pairs={{0,8},{1,9},{2,10},{3,11},{4,12},{5,13},{6,14},{7,15},{8,16},{9,17... | collective-permute-start | bytes 786440 | tf_op jit(solution)/shard_map/ppermute | solution.py:943
  498.8 22.4 %collective-permute-start.50 = (f32[4,25600]{1,0:T(4,128)S(1)}, f32[4,25600]{1,0:T(4,128)}, u32[]{:S(2)}, u32[]{:S(2)}) collective-permute-start(f32[4,25600]{1,0:T(4,128)S(1)} %get-tuple-element.318), channel_id=1, source_target_pairs={{0,4},{1,5},{2,6},{3,7},{4,0},{5,1},{6,2},{7,3},{8,12},{9,13},{10,... | collective-permute-start | bytes 1228808 | tf_op jit(solution)/shard_map/ppermute | solution.py:939
  (91 other events, 833.9 us)
Sparse Core Ops, SparseCore 0:
  11.0 85.3 all-gather.2
  99.2 94.6 all-gather.4
  296.8 170.8 reduce-scatter.1

commit v3 on v2

--- a/solution.py
+++ b/solution.py
@@ -305,20 +305,19 @@
         if self.whole:
             at = lambda *g: (0, index_map(*g))
             return [pl.BlockSpec((self.arrays[0].shape[0], columns), at)]
-        at = lambda *g: (0, 0, 0, 0, index_map(*g))
+        at = lambda *g: (0, 0, 0, index_map(*g))
         shape = self.arrays[0].shape[:-1] + (columns,)
-        return [pl.BlockSpec(shape, at)] * 4
+        return [pl.BlockSpec(shape, at)] * 8
 
 
 def pieces_of(refs, key, z_here):
-    depth = refs[0].shape[2]
+    depth = refs[0].shape[1]
     for z in range(depth):
-        for n in range(4):
-            half, far = n // 2, n % 2
-            for i in range(2):
-                for j in range(2):
-                    away = (i * 4 + j * 2 if half == 0 else j * 4 + i * 2) + far
-                    yield (z_here + z) % depth, key ^ away, half, refs[n].at[i, j, z]
+        for n in range(8):
+            half, far, i = n // 4, n // 2 % 2, n % 2
+            for j in range(2):
+                away = (i * 4 + j * 2 if half == 0 else i * 2 + j * 4) + far
+                yield (z_here + z) % depth, key ^ away, half, refs[n].at[j, z]
 
 
 def place(refs, key, z_here, out_ref, columns=slice(None), source=slice(None)):
@@ -394,11 +393,17 @@
             joined_ref[at + sz.half : at + sz.frame] = far_ref[m, f]
 
 
-def spread_bias(block_ref, head, bias_ref, sz):
-    full = sz.lens[0]
-    for t in range(sz.frames):
-        low = (sz.frames - 1 - t) * sz.frame
-        bias_ref[t * sz.frame : (t + 1) * sz.frame, :] = block_ref[head, :, low : low + full]
+def spread_bias(block_ref, head, bias_ref, sz, turned=False):
+    size = sz.frame
+    for step in range(2 * sz.frames - 1):
+        block = block_ref[head, step]
+        if turned:
+            block = block.T
+        for key in range(sz.frames):
+            query = key + step - (sz.frames - 1)
+            if 0 <= query < sz.frames:
+                row, column = (key, query) if turned else (query, key)
+                bias_ref[row * size : (row + 1) * size, column * size : (column + 1) * size] = block
 
 
 def window_rows(m, tw, sz):
@@ -406,7 +411,7 @@
     return pl.ds(start, sz.lens[tw])
 
 
-def attention(half, own, far, w_qkv, bias, scalars, sz, att_first=None, w_out=None):
+def attention(half, own, far, w_qkv, bias, scalars, sz, first=None, w_out=None):
     scale = 1.0 / math.sqrt(sz.head)
     last = w_out is not None
     steps = sz.groups // 2
@@ -421,7 +426,8 @@
         if last:
             (first_ref,) = take(1)
             out_refs = take(n_out)
-        qkv_ref, att_ref, w_ref = take(3)
+            take(2)
+        qkv_ref, w_ref, att_ref = take(3)
         if last:
             wo_ref, bo_ref, bf_ref = take(3)
         joined, spread = take(2)
@@ -500,18 +506,19 @@
     in_specs = [
         once(piece, fixed),
         once(piece, fixed),
-        pl.BlockSpec((sz.group,) + bias.shape[1:], lambda g, s: (half * steps + g, 0, 0)),
+        pl.BlockSpec((sz.group,) + bias.shape[1:], lambda g, s: (half * steps + g, 0, 0, 0)),
     ] + w_qkv.specs(3 * gcols, lambda g, s: g)
     out_specs = [
-        pl.BlockSpec((3, sz.rows, gcols), lambda g, s: (0, 0, g)),
+        pl.BlockSpec((3, sz.rows, gcols), lambda g, s: (0, 0, half * steps + g)),
+        pl.BlockSpec((width, 3 * gcols), lambda g, s: (0, half * steps + g)),
         pl.BlockSpec((sz.rows, gcols), lambda g, s: (0, g)),
-        pl.BlockSpec((width, 3 * gcols), lambda g, s: (0, g)),
     ]
     out_shape = [
-        jax.ShapeDtypeStruct((3, sz.rows, cols), BF16),
+        jax.ShapeDtypeStruct((3, sz.rows, width), BF16),
+        jax.ShapeDtypeStruct((width, 3 * width), BF16),
         jax.ShapeDtypeStruct((sz.rows, cols), BF16),
-        jax.ShapeDtypeStruct((width, 3 * cols), BF16),
     ]
+    aliases = {}
     scratch = [
         pltpu.VMEM((sz.rows, width), BF16),
         pltpu.VMEM((sz.group, sz.lens[0], sz.lens[0]), BF16),
@@ -532,7 +539,10 @@
         out_shape += [jax.ShapeDtypeStruct((width, width), BF16)]
         out_shape += [jax.ShapeDtypeStruct(piece, BF16)] * 2
         scratch += [pltpu.VMEM((sz.rows, cols), BF16), pltpu.VMEM((sz.rows, width), F32)]
-        args += [att_first, *out_args]
+        args += [first[2], *out_args]
+        aliases = {len(args): 0, len(args) + 1: 1}
+        in_specs += [pl.BlockSpec(memory_space=pl.ANY)] * 2
+        args += first[:2]
         flops += 2 * sz.rows * width * width
     return pl.pallas_call(
         kernel,
@@ -544,16 +554,16 @@
             scratch_shapes=scratch,
         ),
         out_shape=out_shape,
+        input_output_aliases=aliases,
         compiler_params=params(1),
         cost_estimate=cost(3 * flops, 16 * sz.rows * width),
         name="attention" + "_last" * last,
     )(*args)
 
 
-def attention_back(half, grad_own, grad_far, own, far, qkv, atts, w_qkv, w_out, bias_t, scalars, sz, shard, carry=None):
+def attention_back(grad_own, grad_far, own, far, qkv, atts, w_qkv, w_out, bias, scalars, sz, shard):
     scale = 1.0 / math.sqrt(sz.head)
-    last = carry is not None
-    steps = sz.groups // 2
+    steps = sz.groups
     direct = shard is not None
     outs = 2 if direct else 1
     gcols, width = sz.gcols, sz.width
@@ -564,22 +574,11 @@
     ):
         refs = list(refs)
         take = lambda count: [refs.pop(0) for _ in range(count)]
-        if last:
-            (carry_ref,) = take(1)
-        else:
-            att_refs = take(2)
+        att_refs = take(2)
         gw_refs = take(outs)
-        (fold_ref,) = take(1)
-        if last:
-            ho_ref, hf_ref = take(2)
-        else:
-            gwo_refs = gw_refs if direct else take(1)
-            (total,) = take(1)
-        grad, hidden_t, grad_att, parts, spread, pair_sum = take(6)
-        if last:
-            (total,) = take(1)
-        else:
-            (turned,) = take(1)
+        gwo_refs = gw_refs if direct else take(1)
+        fold_ref, ho_ref, hf_ref = take(3)
+        grad, hidden_t, grad_att, parts, spread, pair_sum, total, turned = take(8)
         step = pl.program_id(0)
 
         @pl.when(step == 0)
@@ -587,17 +586,14 @@
             join_frames(own_ref, far_ref, grad, sz)
             turn(grad[...], hidden_t, sc_ref[0], shard)
             join_frames(go_ref, gf_ref, grad, sz)
-            if last:
-                total[...] = carry_ref[...]
-            else:
-                total[...] = jnp.zeros_like(total)
-                for n, a_ref in enumerate(att_refs):
-                    turn(a_ref[...], turned, sc_ref[0], shard, n * a_ref.shape[1])
+            total[...] = jnp.zeros_like(total)
+            for n, a_ref in enumerate(att_refs):
+                turn(a_ref[...], turned, sc_ref[0], shard, n * a_ref.shape[1])
 
         grad_att[...] = dot_nt(grad[...], wo_ref[...]).astype(BF16)
         full = sz.lens[0]
         for head in range(sz.group):
-            spread_bias(bias_ref, head, spread.at[head], sz)
+            spread_bias(bias_ref, head, spread.at[head], sz, True)
             pair_sum[head] = jnp.zeros((full, full), F32)
 
         def one_micro(m, carry):
@@ -646,13 +642,11 @@
             rows = slice(n * quarter, (n + 1) * quarter)
             give(gw_refs, n // 2, n % 2 * quarter, dot_nn(hidden_t[rows, :], parts[...]))
         total[...] += dot_nt(parts[...], w_ref[...])
-        if not last:
-            columns = pl.ds(pl.multiple_of(step * 2 * gcols, 2 * gcols), 2 * gcols)
-            for n in range(4):
-                rows = slice(n * quarter, (n + 1) * quarter)
-                value = dot_nn(turned[rows, :], grad[:, columns])
-                give(gwo_refs, n // 2, n % 2 * quarter, value, 3 * gcols if direct else 0)
-            return
+        columns = pl.ds(pl.multiple_of(step * gcols, gcols), gcols)
+        for n in range(4):
+            rows = slice(n * quarter, (n + 1) * quarter)
+            value = dot_nn(turned[rows, :], grad[:, columns])
+            give(gwo_refs, n // 2, n % 2 * quarter, value, 3 * gcols if direct else 0)
 
         @pl.when(step == steps - 1)
         def _():
@@ -666,7 +660,7 @@
     fixed = lambda g, s: (0, 0, 0, 0)
     flat = lambda g, s: (0, 0)
     cols = width // 2
-    block_bias = (sz.group,) + bias_t.shape[1:]
+    fold = (sz.frame, (2 * sz.frames - 1) * sz.frame)
     in_specs = [
         once(piece, fixed),
         once(piece, fixed),
@@ -674,15 +668,21 @@
         once(piece, fixed),
         pl.BlockSpec((3, sz.rows, gcols), lambda g, s: (0, 0, g)),
         pl.BlockSpec((width, 3 * gcols), lambda g, s: (0, g)),
-        pl.BlockSpec((gcols, width), lambda g, s: (half * steps + g, 0)),
-        pl.BlockSpec(block_bias, lambda g, s: (half * steps + g, 0, 0)),
+        pl.BlockSpec((gcols, width), lambda g, s: (g, 0)),
+        pl.BlockSpec((sz.group,) + bias.shape[1:], lambda g, s: (g, 0, 0, 0)),
     ]
     along = lambda g, s: g
-    wide = 3 * gcols if last or not direct else 5 * gcols
+    wide = 4 * gcols if direct else 3 * gcols
     out_specs = grad_specs(direct, shard, width, wide, along)
-    out_specs += [pl.BlockSpec(block_bias, lambda g, s: (g, 0, 0))]
+    if not direct:
+        out_specs += grad_specs(direct, shard, width, gcols, along)
+    out_specs += [pl.BlockSpec((sz.group,) + fold, lambda g, s: (g, 0, 0))]
+    out_specs += [pl.BlockSpec(piece, fixed)] * 2
     out_shape = grad_shapes(direct, shard, width, steps * wide)
-    out_shape += [jax.ShapeDtypeStruct((HEADS // 2,) + bias_t.shape[1:], F32)]
+    if not direct:
+        out_shape += grad_shapes(direct, shard, width, width)
+    out_shape += [jax.ShapeDtypeStruct((HEADS,) + fold, F32)]
+    out_shape += [jax.ShapeDtypeStruct(piece, BF16)] * 2
     scratch = [
         pltpu.VMEM((sz.rows, width), BF16),
         pltpu.VMEM((width, sz.rows), BF16),
@@ -691,24 +691,11 @@
         pltpu.VMEM((sz.group, sz.lens[0], sz.lens[0]), BF16),
         pltpu.VMEM((sz.group, sz.lens[0], sz.lens[0]), F32),
     ]
-    args = [scalars, grad_own, grad_far, own, far, qkv, w_qkv, w_out, bias_t]
-    flops = 14 * sz.rows * width * cols + 10 * sz.rows * sz.lens[0] * cols
-    if last:
-        in_specs += [once((sz.rows, width), flat)]
-        out_specs += [pl.BlockSpec(piece, fixed)] * 2
-        out_shape += [jax.ShapeDtypeStruct(piece, BF16)] * 2
-        scratch += [pltpu.VMEM((sz.rows, width), F32)]
-        args += [carry]
-    else:
-        in_specs += [once((sz.rows, cols), flat)] * 2
-        if not direct:
-            out_specs += grad_specs(direct, shard, width, 2 * gcols, along)
-            out_shape += grad_shapes(direct, shard, width, width)
-        out_specs += [once((sz.rows, width), flat)]
-        out_shape += [jax.ShapeDtypeStruct((sz.rows, width), F32)]
-        scratch += [pltpu.VMEM((width, sz.rows), BF16)]
-        args += list(atts)
-        flops += 2 * sz.rows * width * width
+    args = [scalars, grad_own, grad_far, own, far, qkv, w_qkv, w_out, bias]
+    flops = 16 * sz.rows * width * width + 10 * sz.rows * sz.lens[0] * width
+    in_specs += [once((sz.rows, cols), flat)] * 2
+    scratch += [pltpu.VMEM((sz.rows, width), F32), pltpu.VMEM((width, sz.rows), BF16)]
+    args += list(atts)
     return pl.pallas_call(
         kernel,
         grid_spec=pltpu.PrefetchScalarGridSpec(
@@ -721,7 +708,7 @@
         out_shape=out_shape,
         compiler_params=params(1),
         cost_estimate=cost(3 * flops, 24 * sz.rows * width),
-        name="attention_back" + "_last" * last,
+        name="attention_back",
     )(*args)
 
 
@@ -742,7 +729,7 @@
     rows, width = sz.rows, sz.width
     quarter = width // 4
     n_up = len(weights[0].arrays)
-    copied = n_up == 4
+    copied = n_up > 1
 
     def kernel(sc_ref, h_ref, g_ref, bu_ref, *refs):
         refs = list(refs)
@@ -893,13 +880,10 @@
 
 
 def bias_blocks(table, bucket, places, sz):
-    steps = 2 * sz.frames - 1
     by_offset = dot_tn(table, bucket_onehot(bucket, table.shape[0])).astype(BF16)
-    by_offset = by_offset.reshape(HEADS, steps, -1)
-    shape = (HEADS, sz.frame, steps * sz.frame)
-    forward = jnp.einsum("hkj,jpq->hpkq", by_offset[:, ::-1], places, preferred_element_type=F32)
-    backward = jnp.einsum("hkj,jpq->hqkp", by_offset, places, preferred_element_type=F32)
-    return forward.astype(BF16).reshape(shape), backward.astype(BF16).reshape(shape)
+    by_offset = by_offset.reshape(HEADS * (2 * sz.frames - 1), -1)
+    blocks = dot_nn(by_offset, places.reshape(places.shape[0], -1)).astype(BF16)
+    return blocks.reshape(HEADS, -1, sz.frame, sz.frame)
 
 
 def split_low(value):
@@ -969,19 +953,24 @@
         return dot_nn(pick, parts).astype(BF16)
 
 
-def cut_rows(parts):
+def cut_rows(parts, widths):
     rows, columns = parts[0].shape
     half = rows // 2
 
     def kernel(*refs):
-        ins, outs = refs[:-2], refs[-2:]
+        ins, outs = refs[: len(parts)], refs[len(parts) :]
         for n, ref in enumerate(ins):
-            for k, out in enumerate(outs):
-                out[n] = ref[k * half : (k + 1) * half]
+            low = 0
+            for k, size in enumerate(widths):
+                for side in range(2):
+                    outs[2 * k + side][n] = ref[side * half : (side + 1) * half, low : low + size]
+                low += size
 
     return pl.pallas_call(
         kernel,
-        out_shape=[jax.ShapeDtypeStruct((len(parts), half, columns), BF16)] * 2,
+        out_shape=[
+            jax.ShapeDtypeStruct((len(parts), half, size), BF16) for size in widths for _ in range(2)
+        ],
         compiler_params=pltpu.CompilerParams(vmem_limit_bytes=VMEM_LIMIT),
         cost_estimate=cost(0, 4 * len(parts) * rows * columns),
         name="cut_rows",
@@ -989,14 +978,24 @@
 
 
 class Gather:
-    def __init__(self, net, shard):
+    def __init__(self, net, halves):
         self.net = net
-        self.got = [net.from_z(shard, k) for k in range(1, net.deep)]
-        self.shard = shard
-        self.halves = None
-
-    def along_z(self):
-        self.halves = cut_rows([self.shard] + list(self.got))
+        self.halves = list(halves)
+        self.got = []
+
+    @staticmethod
+    def along_z(net, shards):
+        both = jnp.concatenate(shards, axis=1)
+        return Gather.cut(net, both, Gather.send_z(net, both), [v.shape[1] for v in shards])
+
+    @staticmethod
+    def send_z(net, shard):
+        return [net.from_z(shard, k) for k in range(1, net.deep)]
+
+    @staticmethod
+    def cut(net, shard, got, widths):
+        made = cut_rows([shard] + list(got), widths)
+        return [Gather(net, made[2 * n : 2 * n + 2]) for n in range(len(widths))]
 
     def start(self, first):
         net = self.net
@@ -1011,10 +1010,12 @@
 
     def core(self):
         net = self.net
+        self.halves = [v for pair in zip(self.halves, self.got) for v in pair]
         self.got = [net.swap(v, net.CORE) for v in self.halves]
 
     def pieces(self):
-        return Pieces([self.halves[0], self.got[0], self.halves[1], self.got[1]])
+        near, far = self.halves, self.got
+        return Pieces([*near[:2], *far[:2], *near[2:], *far[2:]])
 
 
 def add_bf16(one, two):
@@ -1048,18 +1049,19 @@
                         at = near * 2 + other if half == 0 else other * 2 + near
                         outs[2 * half + role][0, other] = add_bf16(keep[0, at, span], got[0, at, span])
 
-        block = (1,) + self.keep[0].shape[1:]
-        out = (2, cut, self.columns)
+        spans = 1
+        block = (1,) + self.keep[0].shape[1:3] + (self.columns // spans,)
+        out = (2, cut, self.columns // spans)
         made = pl.pallas_call(
             kernel,
             grid_spec=pltpu.PrefetchScalarGridSpec(
                 num_scalar_prefetch=1,
-                grid=(net.deep,),
-                in_specs=[pl.BlockSpec(block, lambda z, s: (z, 0, 0, 0))] * 2,
-                out_specs=[pl.BlockSpec((1,) + out, lambda z, s: (z, 0, 0, 0))] * 4,
+                grid=(net.deep, spans),
+                in_specs=[pl.BlockSpec(block, lambda z, n, s: (z, 0, 0, n))] * 2,
+                out_specs=[pl.BlockSpec((1,) + out, lambda z, n, s: (z, 0, 0, n))] * 4,
             ),
-            out_shape=[jax.ShapeDtypeStruct((net.deep,) + out, BF16)] * 4,
-            compiler_params=params(1),
+            out_shape=[jax.ShapeDtypeStruct((net.deep, 2, cut, self.columns), BF16)] * 4,
+            compiler_params=params(2),
             cost_estimate=cost(0, 6 * self.keep[0].size),
             name="add_cores",
         )(self.bits, *self.keep, *self.got)
@@ -1080,25 +1082,17 @@
         self.keep = [made[0], made[2]]
         self.got = [net.swap(made[1], net.X), net.swap(made[3], net.Y)]
 
-    def fourth(self, *joined):
+    def fourth(self):
         net, rows, cut = self.net, self.rows, self.rows // 2
-        group = (self,) + joined
-        widths = [v.columns for v in group]
-
-        def kernel(sc_ref, *refs):
-            ins, outs = refs[: 4 * len(group)], refs[4 * len(group) :]
+
+        def kernel(sc_ref, k0, k1, g0, g1, *outs):
             for away, out in enumerate(outs):
                 at = (sc_ref[2] + net.deep - away) % net.deep
-                low = 0
-                for n, size in enumerate(widths):
-                    k0, k1, g0, g1 = ins[4 * n : 4 * n + 4]
-                    out[:cut, low : low + size] = add_bf16(k0[at], g0[at])
-                    out[cut:, low : low + size] = add_bf16(k1[at], g1[at])
-                    low += size
-
-        out = jax.ShapeDtypeStruct((rows, sum(widths)), BF16)
-        args = [v for one in group for v in (*one.keep, *one.got)]
-        made = self.call(kernel, args, [out] * net.deep, "add_third")
+                out[:cut] = add_bf16(k0[at], g0[at])
+                out[cut:] = add_bf16(k1[at], g1[at])
+
+        out = jax.ShapeDtypeStruct((rows, self.columns), BF16)
+        made = self.call(kernel, [*self.keep, *self.got], [out] * net.deep, "add_third")
         self.keep = [made[0]]
         self.got = [net.from_z(made[k], k) for k in range(1, net.deep)]
 
@@ -1141,8 +1135,10 @@
     width = sz.width
     core = lax.axis_index("win") % 2
     swap = [(n, n ^ 1) for n in range(lax.axis_size("win"))]
-    flags = [core] + [lengths[n, 0] for n in range(sz.micro)]
-    scalars = jnp.stack(flags + [index % 8, index // 8])
+    place_in = jnp.arange(3 + sz.micro, dtype=jnp.int32)
+    scalars = jnp.where(place_in == 0, core, jnp.where(place_in == 1 + sz.micro, index % 8, index // 8))
+    for n in range(sz.micro):
+        scalars = jnp.where(place_in == 1 + n, lengths[n, 0], scalars)
     strip = (sz.micro, 2, 2, sz.frames, sz.half, width)
     tok = tokens.reshape(strip)
     cot = cotangent.reshape(strip)
@@ -1174,7 +1170,6 @@
     mod = mod.reshape(sz.micro, 6, width)
 
     cols = width // 2
-    half_groups = sz.groups // 2
     by_group = w_qkv.reshape(rows, 3, sz.groups, sz.gcols).transpose(0, 2, 1, 3)
     by_group = by_group.reshape(rows, 2, 3 * cols)
     shard_q = [by_group[:, n] for n in range(2)]
@@ -1216,25 +1211,24 @@
         packs = [
             shard_q[0],
             jnp.concatenate([shard_q[1], w_out], axis=1),
+            pack_inner(shard_u[1], shard_d[1]),
             pack_inner(shard_u[0], shard_d[0]),
-            pack_inner(shard_u[1], shard_d[1]),
         ]
         rest_q = gather(packs[1])
-        one = Gather(net, packs[0])
-        one.along_z()
+        rest = gather(tie(packs[2], early))
+        (one,) = Gather.along_z(net, [packs[0]])
+        small = net.gather_pairs(tie(early[:, :, n_cond:], *notes))
         one.halves = tie2(one.halves, [mod_part])
         one.start(True)
         one.join()
         one.halves = tie2(one.halves, notes[:1])
         one.start(False)
-        one.join()
-        one.halves = tie2(one.halves, notes[1:])
+        three_pack = tie(packs[3], notes[0])
+        three_got = tie2(Gather.send_z(net, three_pack), one.got)
+        (three,) = Gather.cut(net, three_pack, three_got, [packs[3].shape[1]])
         one.core()
-        small = net.gather_pairs(tie(early[:, :, n_cond:], *notes))
-        three = Gather(net, tie(packs[2], *notes))
         full_q = [one.pieces(), Pieces([rest_q])]
         full_out = full_q[1]
-        rest = gather(tie(packs[3], early))
     else:
         full_q = [Pieces([gather(v)]) for v in shard_q]
         full_out = Pieces([gather(w_out)])
@@ -1246,31 +1240,34 @@
     full_bdown = small[:, n_up : n_up + n_down].astype(F32).reshape(1, width)
     table = small[:, n_up + n_down : n_small].reshape(-1, HEADS)
     places = offset_onehot(core, sz)
-    bias, bias_t = lax.optimization_barrier(bias_blocks(table, bucket, places, sz))
-
+    bias = bias_blocks(table, bucket, places, sz)
+
+    if net.direct:
+        mod = tie(mod, bias, *three.halves)
     own, send = first_norm(tok, mod, scalars, sz)
     far = lax.ppermute(send, "win", swap)
     if net.direct:
-        three.along_z()
         three.start(True)
-        far = tie(far, *three.halves)
-    qkv_0, att_0, wide_0 = attention(0, own, far, full_q[0], bias, scalars, sz)
-    if net.direct:
-        three.tie(att_0)
+    first = attention(0, own, far, full_q[0], bias, scalars, sz)
+    if net.direct:
+        three.tie(first[2])
         three.join()
         three.start(False)
-        att_0 = tie(att_0, *three.halves)
-    qkv_1, att_1, wide_1, wide_out, branch_own, branch_send = attention(
-        1, own, far, full_q[1], bias, scalars, sz, att_0, full_out
+        first = tie2(first, three.halves)
+    qkv, wide, att_1, wide_out, branch_own, branch_send = attention(
+        1, own, far, full_q[1], bias, scalars, sz, first, full_out
     )
+    if net.direct:
+        three.tie(branch_own)
+        branch_send = tie(branch_send, *three.got)
     branch_far = lax.ppermute(branch_send, "win", swap)
     hidden_two, grad_mlp = second_norm(tok, cot, branch_own, branch_far, mod, scalars, sz)
     flat = (sz.rows, width)
     both = (2, sz.micro, sz.used, sz.half, width)
     hidden_two, grad_mlp = hidden_two.reshape(flat), grad_mlp.reshape(flat)
     if net.direct:
-        three.tie(branch_own)
-        three.join()
+        three.tie(branch_far)
+        three.halves = tie2(three.halves, [branch_far])
         three.core()
         full_i = [[three.pieces()], [Pieces([rest])]]
     mlps = []
@@ -1294,55 +1291,47 @@
         second.tie(grad_own)
         second.second()
         grad_own = tie(grad_own, *second.keep)
-    shard = rows if net.direct else None
-    *g_0, carry = attention_back(
-        0, grad_own, grad_far, own, far, qkv_0, (att_0, att_1), wide_0, wide_out, bias_t,
-        scalars, sz, shard,
+    *g_att, fold, hid_own, hid_send = attention_back(
+        grad_own, grad_far, own, far, qkv, (first[2], att_1), wide, wide_out, bias, scalars, sz,
+        rows if net.direct else None,
     )
     if net.direct:
-        second.tie(carry)
+        second.tie(hid_own)
+        g_att = tie2(g_att, second.got)
+        hid_send = tie(hid_send, *second.got)
+        heads = Scatter(net, g_att)
+        hid_far = lax.ppermute(hid_send, "win", swap)
         second.third()
-        g_0 = lax.optimization_barrier((*g_0, *second.keep))[: len(g_0)]
-        heads_0 = Scatter(net, g_0[:2])
-        heads_0.second()
-        carry = tie(carry, *heads_0.keep)
-        fold_0 = g_0[2]
-    else:
-        fold_0 = g_0[1]
-    *g_1, fold_1, hid_own, hid_send = attention_back(
-        1, grad_own, grad_far, own, far, qkv_1, None, wide_1, wide_out, bias_t, scalars, sz,
-        shard, carry,
-    )
-    if net.direct:
-        second.tie(hid_own)
-        second.fourth()
-        heads_0.tie(hid_own)
-        heads_0.third()
-        g_1 = tie2(g_1, second.keep + heads_0.keep)
-        hid_send = tie(hid_send, *second.keep, *heads_0.keep)
-        heads_1 = Scatter(net, g_1)
-        hid_far = lax.ppermute(hid_send, "win", swap)
-        heads_1.second()
-        hid_far = tie(hid_far, *heads_1.keep)
+        heads.tie(*second.keep)
+        heads.second()
+        hid_far = tie(hid_far, r_first, *heads.keep)
     else:
         hid_far = lax.ppermute(hid_send, "win", swap)
     grad_in, sums_one = last_norm(tok, cot, grad_mid, hid_own, hid_far, mod, scalars, sz)
     if net.direct:
-        heads_1.tie(sums_one)
-        heads_1.third()
-        sums_one = tie(sums_one, *heads_1.keep)
+        second.tie(sums_one)
+        second.fourth()
+        sums_one, fold = lax.optimization_barrier((sums_one, fold, *second.keep))[:2]
 
     grad_mod = jnp.concatenate(
         [sums_one, sums_two[:, 3:4], sums_two[:, 0:3]], axis=1
     ).reshape(sz.micro, 6 * width)
-    by_offset = jnp.concatenate([offset_grad(fold, places, sz) for fold in (fold_0, fold_1)])
-    g_table = table_grad(by_offset, bucket, table.shape[0]).reshape(devices, -1)
+    g_table = table_grad(offset_grad(fold, places, sz), bucket, table.shape[0]).reshape(devices, -1)
+    if net.direct:
+        heads.tie(g_table)
+        heads.third()
+        second.tie(*heads.keep)
+        r_second = second.total()
+        g_table = tie(g_table, r_second)
     g_bup = inner_back([v[2] for v in mlps]).reshape(devices, -1)
     g_bdown = mlps[0][3].reshape(devices, -1)
     g_small = jnp.concatenate([g_bup, g_bdown, g_table], axis=1)
     if net.direct:
         every = jnp.concatenate([grad_mod.reshape(-1), g_small.reshape(-1)])
-        every = net.gather_clips(net.swap_sum(net.swap_sum(every, net.CORE), net.X))
+        every = net.swap_sum(net.swap_sum(every, net.CORE), net.X)
+        heads.tie(every)
+        heads.fourth()
+        every = net.gather_clips(tie(every, *heads.keep))
         mod_all = every[:, :, : grad_mod.size]
         g_small = jnp.sum(every[:, :, grad_mod.size :], axis=(0, 1)).reshape(g_small.shape)
         g_small = lax.dynamic_index_in_dim(g_small, index, 0, keepdims=False)
@@ -1358,22 +1347,19 @@
         jnp.sum(mod_all, axis=0), index * ada_b.shape[0], ada_b.shape[0]
     )
     if net.direct:
-        heads_1.fourth(heads_0)
-        r_u, r_d = zip(unpack_inner(r_first), unpack_inner(second.total()))
-        mine = heads_1.total()
-        r_q = [mine[:, 3 * cols :].reshape(rows, half_groups, -1), mine[:, : 3 * cols]]
-        r_out = r_q[0][:, :, 3 * sz.gcols :].reshape(rows, width)
-        r_q[0] = r_q[0][:, :, : 3 * sz.gcols]
+        r_u, r_d = zip(unpack_inner(r_first), unpack_inner(r_second))
+        mine = heads.total().reshape(rows, sz.groups, -1)
+        r_qkv = mine[:, :, : 3 * sz.gcols]
+        r_out = mine[:, :, 3 * sz.gcols :].reshape(rows, width)
     else:
         scatter = lambda v: lax.psum_scatter(
             v.astype(F32), axes, scatter_dimension=0, tiled=True
         )
         r_u = [scatter(v[-2]) for v in mlps]
         r_d = [scatter(v[-1]) for v in mlps]
-        r_q, r_out = [scatter(g_0[0]), scatter(g_1[0])], scatter(g_0[2])
+        r_qkv, r_out = scatter(g_att[0]), scatter(g_att[1])
     r_up = inner_back(r_u)
     r_down = jnp.concatenate(r_d)
-    r_qkv = jnp.stack([v.reshape(rows, half_groups, 3, sz.gcols) for v in r_q], axis=1)
     r_qkv = r_qkv.reshape(rows, sz.groups, 3, sz.gcols).transpose(0, 2, 1, 3)
     r_qkv = r_qkv.reshape(rows, 3 * width)
     return (

time: 546 us -> 479 us (0.88)
  waiting for transfers between devices: 94.4 us -> 51.1 us
  local copies, waits for them, and re-layouts: 49.3 us -> 38.1 us
    ppermute x36 -> x35, waiting for transfers between devices: 58.8 us -> 34.5 us  [swap(): lax.ppermute(value, self.AXES, [(n, n ^ which) for n in range(self.count)])]
    ppermute x21, waiting for transfers between devices: 30.7 us -> 13.4 us  [from_z(): lax.ppermute(value, self.AXES, [(n, move(n)) for n in range(self.count)])]
    another operation x8 -> x4, other arithmetic: 11.9 us -> 2.13 us  [join(): self.halves = [jnp.stack(pair) for pair in zip(self.halves, self.got)]]
    pallas_call x3 -> x2, Pallas kernels: 16.3 us -> 13.6 us  [second(): pl.pallas_call(kernel, grid_spec=pltpu.PrefetchScalarGridSpec(num_scalar_...]
    pallas_call x5 -> x4, Pallas kernels: 18.1 us -> 15.8 us  [call(): pl.pallas_call(kernel, grid_spec=pltpu.PrefetchScalarGridSpec(num_scalar_...]
    pallas_call x2 -> x1, Pallas kernels: 63 us -> 61.5 us  [attention_back(): pl.pallas_call(kernel, grid_spec=pltpu.PrefetchScalarGridSpec(num_scalar_...]
    unnamed x115 -> x126, local copies, waits for them, and re-layouts: 11.5 us -> 10.6 us
    ppermute x36 -> x35, starting transfers between devices: 40.3 us -> 39.5 us  [swap(): lax.ppermute(value, self.AXES, [(n, n ^ which) for n in range(self.count)])]
  transfers between devices with their start and end apart: 64 -> 63, of which waited for: 17 -> 14; matrix products, arithmetic and copies ran while one was open for 13% -> 11% of each run, Pallas kernels for 40% -> 54%
where the time goes in v3:
time: 479 us; the launch traced here: 473 us
  Pallas kernels  257 us (54%)
  starting transfers between devices  81.8 us (17%)
  waiting for transfers between devices  51.1 us (11%)
  local copies, waits for them, and re-layouts  38.1 us (8%)
  other arithmetic  18.1 us (4%)
  between operations  15.5 us (3%)
  matrix products  11 us (2%)
    pallas_call x2, Pallas kernels, mlp(): pl.pallas_call(kernel, grid_spec=pltpu.PrefetchScalarGridSpec(num_scalar_...  82.6 us
    pallas_call x1, Pallas kernels, attention_back(): pl.pallas_call(kernel, grid_spec=pltpu.PrefetchScalarGridSpec(num_scalar_...  61.5 us
    pallas_call x2, Pallas kernels, attention(): pl.pallas_call(kernel, grid_spec=pltpu.PrefetchScalarGridSpec(num_scalar_...  44.7 us
    ppermute x21, starting transfers between devices, from_z(): lax.ppermute(value, self.AXES, [(n, move(n)) for n in range(self.count)])  41.1 us
    ppermute x35, starting transfers between devices, swap(): lax.ppermute(value, self.AXES, [(n, n ^ which) for n in range(self.count)])  39.5 us
    ppermute x35, waiting for transfers between devices, swap(): lax.ppermute(value, self.AXES, [(n, n ^ which) for n in range(self.count)])  34.5 us
    pallas_call x4, Pallas kernels, call(): pl.pallas_call(kernel, grid_spec=pltpu.PrefetchScalarGridSpec(num_scalar_...  15.8 us
    pallas_call x1, Pallas kernels, after_mlp(): pl.pallas_call(kernel, grid_spec=pltpu.PrefetchScalarGridSpec(num_scalar_...  15.1 us
  transfers between devices with their start and end apart: 63, of which 14 were waited for; matrix products, arithmetic and copies ran while one was open for 11% of the time, Pallas kernels for 54%

profile of v3, /device:TPU:0, one launch (start us, length us, event | category | flops | bytes accessed | tf_op | source)
XLA Modules:
  0.0 472.6 jit_solution(11703725437491931685)
XLA Ops:
  34.0 4.1 collective-permute-done.4
  40.4 3.8 collective-permute-start.5
  74.5 8.8 %collective-permute-done.21.refs_5_ = bf16[2,4,16,1536]{3,2,1,0:T(8,128)(2,1)} collective-permute-done((bf16[2,4,16,1536]{3,2,1,0:T(8,128)(2,1)S(1)}, bf16[2,4,16,1536]{3,2,1,0:T(8,128)(2,1)}, u32[]{:S(2)}, u32[]{:S(2)}) %collective-permute-start.21) | collective-permute-done | bytes 393248 | tf_op jit(solution)/shard_map/ppermute | solution.py:923
  85.5 4.7 first_norm.1
  97.8 20.0 %attention.1 = (bf16[3,1152,1024]{2,1,0:T(8,128)(2,1)}, bf16[1024,3072]{1,0:T(8,128)(2,1)}, bf16[1152,512]{1,0:T(8,128)(2,1)}) custom-call(s32[5]{0:T(128)} %compare_select_fusion.7.sc_ref, bf16[2,9,32,1024]{3,2,1,0:T(8,128)(2,1)} %get-tuple-element.135.own_ref, bf16[2,9,32,1024]{3,2,1,0:T(8,128)(2,1)} %copy-done.49, ...), custom_call_target="tpu_custom_call" | custom-call | flops 13136560128 | bytes 18874368 | tf_op jit(solution)/shard_map/attention/pallas_call | solution.py:547
  118.9 4.2 collective-permute-start.29
  123.1 24.7 %attention_last.1 = (bf16[3,1152,1024]{2,1,0:T(8,128)(2,1)}, bf16[1024,3072]{1,0:T(8,128)(2,1)}, bf16[1152,512]{1,0:T(8,128)(2,1)}, bf16[1024,1024]{1,0:T(8,128)...) custom-call(s32[5]{0:T(128)} %compare_select_fusion.7.sc_ref, ...), custom_call_target="tpu_custom_call", output_to_operand_aliasing={{0}: (8, {}), {1}: (9, {})} | custom-call | flops 20384317440 | bytes 18874368 | tf_op jit(solution)/shard_map/attention_last/pallas_call | solution.py:547
  156.8 7.1 %second_norm.1 = (bf16[2,2,9,32,1024]{4,3,2,1,0:T(8,128)(2,1)}, bf16[2,2,9,32,1024]{4,3,2,1,0:T(8,128)(2,1)}) custom-call(s32[5]{0:T(128)} %compare_select_fusion.7.sc_ref, bf16[2,2,2,5,32,1024]{5,4,3,2,1,0:T(8,128)(2,1)} %bitcast.165, bf16[2,2,2,5,32,1024]{5,4,3,2,1,0:T(8,128)(2,1)} %bitcast.168, bf16[2,9,32,1024]{3,2,1,0:T(8,128)(2,1)} %get-tuple-element.145.bo_ref, ...), custom_call_target="tpu_custom_call" | custom-call | tf_op jit(solution)/shard_map/second_norm/pallas_call | solution.py:147
  163.9 41.2 %mlp.2 = (f32[1152,1024]{1,0:T(8,128)}, f32[1152,1024]{1,0:T(8,128)}, f32[1,2048]{1,0:T(1,128)}, f32[1,1024]{1,0:T(1,128)}, bf16[1024,4096]{1,0:T(8,128)(2,1)}) custom-call(s32[5]{0:T(128)} %compare_select_fusion.7.sc_ref, bf16[1152,1024]{1,0:T(8,128)(2,1)} %bitcast.230, bf16[1152,1024]{1,0:T(8,128)(2,1)} %bitcast.232, f32[1,2048]{1,0:T(1,128)} %squeeze.49.bu_ref, ...), custom_call_target="tpu_custom_call" | custom-call | flops 33822867456 | bytes 18874368 | tf_op jit(solution)/shard_map/mlp/pallas_call | solution.py:852
  205.2 41.5 %mlp.3 = (f32[1152,1024]{1,0:T(8,128)}, f32[1152,1024]{1,0:T(8,128)}, f32[1,2048]{1,0:T(1,128)}, bf16[16,32,4096]{2,1,0:T(8,128)(2,1)}, bf16[16,32,4096]{2,1,0:T(8,128)(2,1)}) custom-call(s32[5]{0:T(128)} %compare_select_fusion.7.sc_ref, bf16[1152,1024]{1,0:T(8,128)(2,1)} %bitcast.231, bf16[1152,1024]{1,0:T(8,128)(2,1)} %bitcast.233, ...), custom_call_target="tpu_custom_call" | custom-call | flops 33822867456 | bytes 18874368 | tf_op jit(solution)/shard_map/mlp/pallas_call | solution.py:852
  247.4 15.1 %after_mlp.1 = (bf16[2,2,2,5,32,1024]{5,4,3,2,1,0:T(8,128)(2,1)}, f32[2,2,9,32,1024]{4,3,2,1,0:T(8,128)}, bf16[2,9,32,1024]{3,2,1,0:T(8,128)(2,1)}, bf16[2,9,32,1024]{3,2,1,0:T(8,128)(2,1)}, f32[2,4,1024]{2,1,0:T(4,128)}) custom-call(s32[5]{0:T(128)} %compare_select_fusion.7.sc_ref, bf16[2,2,2,5,32,1024]{5,4,3,2,1,0:T(8,128)(2,1)} %bitcast.166, ...), custom_call_target="tpu_custom_call" | custom-call | tf_op jit(solution)/shard_map/after_mlp/pallas_call | solution.py:209
  263.5 7.0 %add_cores.2 = (bf16[4,2,16,4096]{3,2,1,0:T(8,128)(2,1)}, bf16[4,2,16,4096]{3,2,1,0:T(8,128)(2,1)}, bf16[4,2,16,4096]{3,2,1,0:T(8,128)(2,1)}, bf16[4,2,16,4096]{3,2,1,0:T(8,128)(2,1)}) custom-call(s32[3]{0:T(128)} %pad_add_fusion.sc_ref, bf16[4,4,32,4096]{3,2,1,0:T(8,128)(2,1)} %bitcast.180, bf16[4,4,32,4096]{3,2,1,0:T(8,128)(2,1)} %collective-permute-done.36.got), custom_call_target="tpu_custom_call" | custom-call | bytes 12582912 | tf_op jit(solution)/shard_map/add_cores/pallas_call | solution.py:1055
  270.6 5.3 %collective-permute-start.38 = (bf16[4,2,16,4096]{3,2,1,0:T(8,128)(2,1)}, bf16[4,2,16,4096]{3,2,1,0:T(8,128)(2,1)S(1)}, u32[]{:S(2)}, u32[]{:S(2)}) collective-permute-start(bf16[4,2,16,4096]{3,2,1,0:T(8,128)(2,1)} %get-tuple-element.179), channel_id=1, source_target_pairs={{0,4},{1,5},{2,6},{3,7},{4,0},{5,1},{6,2},{7,3},{8,12},{9,13},{10,... | collective-permute-start | bytes 3145736 | tf_op jit(solution)/shard_map/ppermute | solution.py:923
  278.0 61.5 %attention_back.1 = (bf16[16,32,4096]{2,1,0:T(8,128)(2,1)}, bf16[16,32,4096]{2,1,0:T(8,128)(2,1)}, f32[16,64,576]{2,1,0:T(8,128)}, bf16[2,9,32,1024]{3,2,1,0:T(8,128)(2,1)}, bf16[2,9,32,1024]{3,2,1,0:T(8,128)(2,1)}) custom-call(s32[5]{0:T(128)} %compare_select_fusion.7.sc_ref, bf16[2,9,32,1024]{3,2,1,0:T(8,128)(2,1)} %get-tuple-element.171.go_ref, ...), custom_call_target="tpu_custom_call" | custom-call | flops 69306679296 | bytes 28311552 | tf_op jit(solution)/shard_map/attention_back/pallas_call | solution.py:699
  340.9 4.6 add_second.2
  346.5 7.4 %collective-permute-start.43 = (bf16[4,16,4096]{2,1,0:T(8,128)(2,1)}, bf16[4,16,4096]{2,1,0:T(8,128)(2,1)}, u32[]{:S(2)}, u32[]{:S(2)}) collective-permute-start(bf16[4,16,4096]{2,1,0:T(8,128)(2,1)} %get-tuple-element.199), channel_id=1, source_target_pairs={{0,4},{1,5},{2,6},{3,7},{4,0},{5,1},{6,2},{7,3},{8,12},{9,13},{10,... | collective-permute-start | bytes 1572872 | tf_op jit(solution)/shard_map/ppermute | solution.py:923
  359.0 6.5 %add_cores.3 = (bf16[4,2,16,4096]{3,2,1,0:T(8,128)(2,1)}, bf16[4,2,16,4096]{3,2,1,0:T(8,128)(2,1)}, bf16[4,2,16,4096]{3,2,1,0:T(8,128)(2,1)}, bf16[4,2,16,4096]{3,2,1,0:T(8,128)(2,1)}) custom-call(s32[3]{0:T(128)} %pad_add_fusion.sc_ref, bf16[4,4,32,4096]{3,2,1,0:T(8,128)(2,1)} %bitcast.181, bf16[4,4,32,4096]{3,2,1,0:T(8,128)(2,1)} %collective-permute-done.41.got), custom_call_target="tpu_custom_call" | custom-call | bytes 12582912 | tf_op jit(solution)/shard_map/add_cores/pallas_call | solution.py:1055
  367.7 8.0 %last_norm.1 = (bf16[2,2,2,5,32,1024]{5,4,3,2,1,0:T(8,128)(2,1)}, f32[2,2,1024]{2,1,0:T(2,128)}) custom-call(s32[5]{0:T(128)} %compare_select_fusion.7.sc_ref, bf16[2,2,2,5,32,1024]{5,4,3,2,1,0:T(8,128)(2,1)} %bitcast.167, bf16[2,2,2,5,32,1024]{5,4,3,2,1,0:T(8,128)(2,1)} %bitcast.170, f32[2,2,9,32,1024]{4,3,2,1,0:T(8,128)} %get-tuple-element.164.gm_ref, ...), custom_call_target="tpu_custom_call" | custom-call | tf_op jit(solution)/shard_map/last_norm/pallas_call | solution.py:272
  381.9 3.7 copy.214
  385.6 5.1 %subtract_convert_fusion = (bf16[16,64,9,64]{1,3,2,0:T(8,128)(2,1)S(1)}, bf16[16,64,9,64]{1,3,2,0:T(8,128)(2,1)S(1)}) fusion(f32[16,64,9,64]{1,3,2,0:T(8,128)} %bitcast.171), kind=kLoop, calls=%fused_computation.2 | loop fusion | flops 2359296 | bytes 4718592 | tf_op jit(solution)/shard_map/convert_element_type | solution.py:891
  400.7 4.6 add_second.3
  415.4 4.7 collective-permute-done.50
  431.8 11.8 %collective-permute-start.59 = (bf16[32,4096]{1,0:T(8,128)(2,1)}, bf16[32,4096]{1,0:T(8,128)(2,1)S(1)}, u32[]{:S(2)}, u32[]{:S(2)}) collective-permute-start(bf16[32,4096]{1,0:T(8,128)(2,1)} %get-tuple-element.230), channel_id=1, source_target_pairs={{0,8},{1,9},{2,10},{3,11},{4,12},{5,13},{6,14},{7,15},{8,16},{9,17... | collective-permute-start | bytes 786440 | tf_op jit(solution)/shard_map/ppermute | solution.py:927
  444.6 12.9 %collective-permute-done.58 = bf16[32,4096]{1,0:T(8,128)(2,1)S(1)} collective-permute-done((bf16[32,4096]{1,0:T(8,128)(2,1)}, bf16[32,4096]{1,0:T(8,128)(2,1)S(1)}, u32[]{:S(2)}, u32[]{:S(2)}) %collective-permute-start.58) | collective-permute-done | bytes 262176 | tf_op jit(solution)/shard_map/ppermute | solution.py:927
  (391 shorter events, 138.7 us)
Async XLA Ops:
  7.3 115.9 %all-gather.3.cloned.1.call-start = ((), (), s32[]{:S(2)}) async-start(), calls=%async_computation.1 | async-start | bytes 5406720 | tf_op jit(solution)/shard_map/all_gather | solution.py:1209
  9.8 195.4 %all-gather.5.cloned.1.call-start = ((), (), s32[]{:S(2)}) async-start(), calls=%async_computation.2 | async-start | bytes 8650752 | tf_op jit(solution)/shard_map/all_gather | solution.py:1209
  17.1 23.3 %collective-permute-start.17 = (bf16[32,1536]{1,0:T(8,128)(2,1)S(1)}, bf16[32,1536]{1,0:T(8,128)(2,1)S(1)}, u32[]{:S(2)}, u32[]{:S(2)}) collective-permute-start(bf16[32,1536]{1,0:T(8,128)(2,1)S(1)} %bitcast.205), channel_id=1, source_target_pairs={{0,8},{1,9},{2,10},{3,11},{4,12},{5,13},{6,14},{7,15},{8,16},{9,17... | collective-permute-start | bytes 294920 | tf_op jit(solution)/shard_map/ppermute | solution.py:927
  17.8 26.4 %collective-permute-start.16 = (bf16[32,1536]{1,0:T(8,128)(2,1)S(1)}, bf16[32,1536]{1,0:T(8,128)(2,1)S(1)}, u32[]{:S(2)}, u32[]{:S(2)}) collective-permute-start(bf16[32,1536]{1,0:T(8,128)(2,1)S(1)} %bitcast.206), channel_id=1, source_target_pairs={{0,16},{1,17},{2,18},{3,19},{4,20},{5,21},{6,22},{7,23},{8,24},{9,... | collective-permute-start | bytes 294920 | tf_op jit(solution)/shard_map/ppermute | solution.py:927
  20.6 346.0 %reduce-scatter.2.cloned.1.call-start = ((), (), s32[]{:S(2)}) async-start(), calls=%async_computation.3 | async-start | bytes 8650752 | tf_op jit(solution)/shard_map/reduce_scatter | solution.py:1281
  50.3 21.9 %collective-permute-start.14 = (bf16[32,4096]{1,0:T(8,128)(2,1)S(1)}, bf16[32,4096]{1,0:T(8,128)(2,1)S(1)}, u32[]{:S(2)}, u32[]{:S(2)}) collective-permute-start(bf16[32,4096]{1,0:T(8,128)(2,1)S(1)} %copy.234.refs_0_), channel_id=1, source_target_pairs={{0,8},{1,9},{2,10},{3,11},{4,12},{5,13},{6,14},{7,15},{8,16},{9,17... | collective-permute-start | bytes 786440 | tf_op jit(solution)/shard_map/ppermute | solution.py:927
  50.3 21.9 %collective-permute-start.13 = (bf16[32,4096]{1,0:T(8,128)(2,1)S(1)}, bf16[32,4096]{1,0:T(8,128)(2,1)S(1)}, u32[]{:S(2)}, u32[]{:S(2)}) collective-permute-start(bf16[32,4096]{1,0:T(8,128)(2,1)S(1)} %copy.234.refs_0_), channel_id=1, source_target_pairs={{0,16},{1,17},{2,18},{3,19},{4,20},{5,21},{6,22},{7,23},{8,24},{9,... | collective-permute-start | bytes 786440 | tf_op jit(solution)/shard_map/ppermute | solution.py:927
  93.5 24.4 %collective-permute-start.27 = (bf16[4,16,4096]{2,1,0:T(8,128)(2,1)S(1)}, bf16[4,16,4096]{2,1,0:T(8,128)(2,1)S(1)}, u32[]{:S(2)}, u32[]{:S(2)}) collective-permute-start(bf16[4,16,4096]{2,1,0:T(8,128)(2,1)S(1)} %copy-done.12), channel_id=1, source_target_pairs={{0,2},{1,3},{2,0},{3,1},{4,6},{5,7},{6,4},{7,5},{8,10},{9,11},{10,... | collective-permute-start | bytes 1572872 | tf_op jit(solution)/shard_map/ppermute | solution.py:923
  95.5 22.4 %collective-permute-start.28 = (bf16[4,16,4096]{2,1,0:T(8,128)(2,1)S(1)}, bf16[4,16,4096]{2,1,0:T(8,128)(2,1)S(1)}, u32[]{:S(2)}, u32[]{:S(2)}) collective-permute-start(bf16[4,16,4096]{2,1,0:T(8,128)(2,1)S(1)} %copy-done.13), channel_id=1, source_target_pairs={{0,4},{1,5},{2,6},{3,7},{4,0},{5,1},{6,2},{7,3},{8,12},{9,13},{10,... | collective-permute-start | bytes 1572872 | tf_op jit(solution)/shard_map/ppermute | solution.py:923
  118.0 33.1 %collective-permute-start.30 = (bf16[2,4,16,4096]{3,2,1,0:T(8,128)(2,1)S(1)}, bf16[2,4,16,4096]{3,2,1,0:T(8,128)(2,1)}, u32[]{:S(2)}, u32[]{:S(2)}) collective-permute-start(bf16[2,4,16,4096]{3,2,1,0:T(8,128)(2,1)S(1)} %pad_maximum_fusion.2.refs_4_), channel_id=1, source_target_pairs={{0,2},{1,3},{2,0},{3,1},{4,6},{5,7},{6,4},{7,5},{8,10},{9,11},{10,... | collective-permute-start | bytes 3145736 | tf_op jit(solution)/shard_map/ppermute | solution.py:923
  118.9 32.1 %collective-permute-start.29 = (bf16[2,4,16,4096]{3,2,1,0:T(8,128)(2,1)S(1)}, bf16[2,4,16,4096]{3,2,1,0:T(8,128)(2,1)}, u32[]{:S(2)}, u32[]{:S(2)}) collective-permute-start(bf16[2,4,16,4096]{3,2,1,0:T(8,128)(2,1)S(1)} %pad_maximum_fusion.1.refs_0_), channel_id=1, source_target_pairs={{0,4},{1,5},{2,6},{3,7},{4,0},{5,1},{6,2},{7,3},{8,12},{9,13},{10,... | collective-permute-start | bytes 3145736 | tf_op jit(solution)/shard_map/ppermute | solution.py:923
  270.6 69.0 %collective-permute-start.38 = (bf16[4,2,16,4096]{3,2,1,0:T(8,128)(2,1)}, bf16[4,2,16,4096]{3,2,1,0:T(8,128)(2,1)S(1)}, u32[]{:S(2)}, u32[]{:S(2)}) collective-permute-start(bf16[4,2,16,4096]{3,2,1,0:T(8,128)(2,1)} %get-tuple-element.179), channel_id=1, source_target_pairs={{0,4},{1,5},{2,6},{3,7},{4,0},{5,1},{6,2},{7,3},{8,12},{9,13},{10,... | collective-permute-start | bytes 3145736 | tf_op jit(solution)/shard_map/ppermute | solution.py:923
  275.9 63.7 %collective-permute-start.39 = (bf16[4,2,16,4096]{3,2,1,0:T(8,128)(2,1)}, bf16[4,2,16,4096]{3,2,1,0:T(8,128)(2,1)S(1)}, u32[]{:S(2)}, u32[]{:S(2)}) collective-permute-start(bf16[4,2,16,4096]{3,2,1,0:T(8,128)(2,1)} %get-tuple-element.180), channel_id=1, source_target_pairs={{0,2},{1,3},{2,0},{3,1},{4,6},{5,7},{6,4},{7,5},{8,10},{9,11},{10,... | collective-permute-start | bytes 3145736 | tf_op jit(solution)/shard_map/ppermute | solution.py:923
  339.6 19.4 %collective-permute-start.41 = (bf16[4,4,32,4096]{3,2,1,0:T(8,128)(2,1)}, bf16[4,4,32,4096]{3,2,1,0:T(8,128)(2,1)}, u32[]{:S(2)}, u32[]{:S(2)}) collective-permute-start(bf16[4,4,32,4096]{3,2,1,0:T(8,128)(2,1)} %bitcast.227), channel_id=1, source_target_pairs={{0,1},{1,0},{2,3},{3,2},{4,5},{5,4},{6,7},{7,6},{8,9},{9,8},{10,11... | collective-permute-start | bytes 12582920 | tf_op jit(solution)/shard_map/ppermute | solution.py:923
  339.7 27.0 %collective-permute-start.40 = (bf16[2,9,32,1024]{3,2,1,0:T(8,128)(2,1)}, bf16[2,9,32,1024]{3,2,1,0:T(8,128)(2,1)S(1)}, u32[]{:S(2)}, u32[]{:S(2)}) collective-permute-start(bf16[2,9,32,1024]{3,2,1,0:T(8,128)(2,1)} %get-tuple-element.183), channel_id=1, source_target_pairs={{0,1},{1,0},{2,3},{3,2},{4,5},{5,4},{6,7},{7,6},{8,9},{9,8},{10,11... | collective-permute-start | bytes 3538952 | tf_op jit(solution)/shard_map/ppermute | solution.py:1303
  345.5 30.2 %collective-permute-start.42 = (bf16[4,16,4096]{2,1,0:T(8,128)(2,1)}, bf16[4,16,4096]{2,1,0:T(8,128)(2,1)S(1)}, u32[]{:S(2)}, u32[]{:S(2)}) collective-permute-start(bf16[4,16,4096]{2,1,0:T(8,128)(2,1)} %get-tuple-element.198), channel_id=1, source_target_pairs={{0,2},{1,3},{2,0},{3,1},{4,6},{5,7},{6,4},{7,5},{8,10},{9,11},{10,... | collective-permute-start | bytes 1572872 | tf_op jit(solution)/shard_map/ppermute | solution.py:923
  346.5 29.3 %collective-permute-start.43 = (bf16[4,16,4096]{2,1,0:T(8,128)(2,1)}, bf16[4,16,4096]{2,1,0:T(8,128)(2,1)}, u32[]{:S(2)}, u32[]{:S(2)}) collective-permute-start(bf16[4,16,4096]{2,1,0:T(8,128)(2,1)} %get-tuple-element.199), channel_id=1, source_target_pairs={{0,4},{1,5},{2,6},{3,7},{4,0},{5,1},{6,2},{7,3},{8,12},{9,13},{10,... | collective-permute-start | bytes 1572872 | tf_op jit(solution)/shard_map/ppermute | solution.py:923
  365.6 35.2 %collective-permute-start.47 = (bf16[4,2,16,4096]{3,2,1,0:T(8,128)(2,1)}, bf16[4,2,16,4096]{3,2,1,0:T(8,128)(2,1)}, u32[]{:S(2)}, u32[]{:S(2)}) collective-permute-start(bf16[4,2,16,4096]{3,2,1,0:T(8,128)(2,1)} %get-tuple-element.212), channel_id=1, source_target_pairs={{0,4},{1,5},{2,6},{3,7},{4,0},{5,1},{6,2},{7,3},{8,12},{9,13},{10,... | collective-permute-start | bytes 3145736 | tf_op jit(solution)/shard_map/ppermute | solution.py:923
  365.6 35.2 %collective-permute-start.48 = (bf16[4,2,16,4096]{3,2,1,0:T(8,128)(2,1)}, bf16[4,2,16,4096]{3,2,1,0:T(8,128)(2,1)}, u32[]{:S(2)}, u32[]{:S(2)}) collective-permute-start(bf16[4,2,16,4096]{3,2,1,0:T(8,128)(2,1)} %get-tuple-element.213), channel_id=1, source_target_pairs={{0,2},{1,3},{2,0},{3,1},{4,6},{5,7},{6,4},{7,5},{8,10},{9,11},{10,... | collective-permute-start | bytes 3145736 | tf_op jit(solution)/shard_map/ppermute | solution.py:923
  379.8 28.4 %collective-permute-start.44 = (bf16[32,4096]{1,0:T(8,128)(2,1)}, bf16[32,4096]{1,0:T(8,128)(2,1)}, u32[]{:S(2)}, u32[]{:S(2)}) collective-permute-start(bf16[32,4096]{1,0:T(8,128)(2,1)} %get-tuple-element.209), channel_id=1, source_target_pairs={{0,24},{1,25},{2,26},{3,27},{4,28},{5,29},{6,30},{7,31},{8,0},{9,1... | collective-permute-start | bytes 786440 | tf_op jit(solution)/shard_map/ppermute | solution.py:927
  379.8 28.4 %collective-permute-start.45 = (bf16[32,4096]{1,0:T(8,128)(2,1)}, bf16[32,4096]{1,0:T(8,128)(2,1)}, u32[]{:S(2)}, u32[]{:S(2)}) collective-permute-start(bf16[32,4096]{1,0:T(8,128)(2,1)} %get-tuple-element.210), channel_id=1, source_target_pairs={{0,16},{1,17},{2,18},{3,19},{4,20},{5,21},{6,22},{7,23},{8,24},{9,... | collective-permute-start | bytes 786440 | tf_op jit(solution)/shard_map/ppermute | solution.py:927
  379.8 28.4 %collective-permute-start.46 = (bf16[32,4096]{1,0:T(8,128)(2,1)}, bf16[32,4096]{1,0:T(8,128)(2,1)}, u32[]{:S(2)}, u32[]{:S(2)}) collective-permute-start(bf16[32,4096]{1,0:T(8,128)(2,1)} %get-tuple-element.211), channel_id=1, source_target_pairs={{0,8},{1,9},{2,10},{3,11},{4,12},{5,13},{6,14},{7,15},{8,16},{9,17... | collective-permute-start | bytes 786440 | tf_op jit(solution)/shard_map/ppermute | solution.py:927
  430.9 26.7 %collective-permute-start.58 = (bf16[32,4096]{1,0:T(8,128)(2,1)}, bf16[32,4096]{1,0:T(8,128)(2,1)S(1)}, u32[]{:S(2)}, u32[]{:S(2)}) collective-permute-start(bf16[32,4096]{1,0:T(8,128)(2,1)} %get-tuple-element.229), channel_id=1, source_target_pairs={{0,16},{1,17},{2,18},{3,19},{4,20},{5,21},{6,22},{7,23},{8,24},{9,... | collective-permute-start | bytes 786440 | tf_op jit(solution)/shard_map/ppermute | solution.py:927
  431.8 25.8 %collective-permute-start.59 = (bf16[32,4096]{1,0:T(8,128)(2,1)}, bf16[32,4096]{1,0:T(8,128)(2,1)S(1)}, u32[]{:S(2)}, u32[]{:S(2)}) collective-permute-start(bf16[32,4096]{1,0:T(8,128)(2,1)} %get-tuple-element.230), channel_id=1, source_target_pairs={{0,8},{1,9},{2,10},{3,11},{4,12},{5,13},{6,14},{7,15},{8,16},{9,17... | collective-permute-start | bytes 786440 | tf_op jit(solution)/shard_map/ppermute | solution.py:927
  (96 other events, 918.8 us)
Sparse Core Ops, SparseCore 0:
  11.0 85.2 all-gather.2
  99.1 83.8 all-gather.4
  205.2 152.1 reduce-scatter.1

commit v4 on v3

--- a/solution.py
+++ b/solution.py
@@ -74,8 +74,18 @@
         self.groups = HEADS // self.group
 
 
-def frame_rows(value):
-    return value.reshape(-1, value.shape[-1])
+def each_frame(body, sz):
+    for tw in range(2):
+
+        def step(t, carry, tw=tw):
+            body(tw, t, tw * sz.frames + t)
+            return carry
+
+        lax.fori_loop(0, sz.frames - tw, step, 0, unroll=True)
+
+
+def fold_rows(value):
+    return jnp.sum(value.reshape(-1, 8, value.shape[-1]), axis=0)
 
 
 def first_norm(tok, mod, core, sz):
@@ -84,14 +94,12 @@
         scale = 1.0 + mod_ref[0, 1:2, :]
         for slot, out_ref in enumerate((own_ref, far_ref)):
             column = sc_ref[0] ^ slot
-            for tw in range(2):
-                count = sz.frames - tw
-                rows = frame_rows(x_ref[0, tw, column, :count].astype(F32))
-                normed, _ = normalize(rows)
-                hidden = (normed * scale + shift).astype(BF16)
-                out_ref[0, tw * sz.frames : tw * sz.frames + count] = hidden.reshape(
-                    count, sz.half, sz.width
-                )
+
+            def one(tw, t, f, column=column, out_ref=out_ref):
+                normed, _ = normalize(x_ref[0, tw, column, t].astype(F32))
+                out_ref[0, f] = (normed * scale + shift).astype(BF16)
+
+            each_frame(one, sz)
 
     strip = (1, 2, 2, sz.frames, sz.half, sz.width)
     piece = (1, sz.used, sz.half, sz.width)
@@ -113,11 +121,6 @@
     )(core, tok, mod)
 
 
-def valid_rows(tw, count, length, sz):
-    frame = tw * sz.frames + lax.broadcasted_iota(jnp.int32, (count * sz.half, 1), 0) // sz.half
-    return (frame < length).astype(F32)
-
-
 def second_norm(tok, cot, branch_own, branch_far, mod, scalars, sz):
     def kernel(sc_ref, x_ref, c_ref, bo_ref, bf_ref, mod_ref, h_ref, g_ref):
         length = sc_ref[1 + pl.program_id(0)]
@@ -127,18 +130,15 @@
         gate2 = mod_ref[0, 5:6, :]
         for slot, b_ref in enumerate((bo_ref, bf_ref)):
             column = sc_ref[0] ^ slot
-            for tw in range(2):
-                count = sz.frames - tw
-                span = slice(tw * sz.frames, tw * sz.frames + count)
-                rows = frame_rows(x_ref[0, tw, column, :count].astype(F32))
-                branch = frame_rows(b_ref[0, span].astype(F32))
-                normed, _ = normalize(rows + gate1 * branch)
-                h_ref[slot, 0, span] = (
-                    (normed * scale + shift).astype(BF16).reshape(count, sz.half, sz.width)
-                )
-                grad = frame_rows(c_ref[0, tw, column, :count].astype(F32))
-                grad = grad * valid_rows(tw, count, length, sz) * gate2
-                g_ref[slot, 0, span] = grad.astype(BF16).reshape(count, sz.half, sz.width)
+
+            def one(tw, t, f, slot=slot, column=column, b_ref=b_ref):
+                rows = x_ref[0, tw, column, t].astype(F32) + gate1 * b_ref[0, f].astype(F32)
+                normed, _ = normalize(rows)
+                h_ref[slot, 0, f] = (normed * scale + shift).astype(BF16)
+                valid = (f < length).astype(F32)
+                g_ref[slot, 0, f] = (c_ref[0, tw, column, t].astype(F32) * (valid * gate2)).astype(BF16)
+
+            each_frame(one, sz)
 
     strip = (1, 2, 2, sz.frames, sz.half, sz.width)
     piece = (1, sz.used, sz.half, sz.width)
@@ -167,37 +167,35 @@
 def after_mlp(tok, cot, branch_own, branch_far, mlps, grads, mod, b_down, scalars, sz):
     def kernel(
         sc_ref, x_ref, c_ref, bo_ref, bf_ref, y0_ref, y1_ref, t0_ref, t1_ref, mod_ref, bd_ref,
-        out_ref, gm_ref, go_ref, gf_ref, sum_ref,
+        out_ref, gm_ref, go_ref, gf_ref, sum_ref, sums,
     ):
         length = sc_ref[1 + pl.program_id(0)]
         gate1 = mod_ref[0, 2:3, :]
         scale = 1.0 + mod_ref[0, 4:5, :]
         gate2 = mod_ref[0, 5:6, :]
-        sums = [jnp.zeros((1, sz.width), F32) for _ in range(4)]
+        sums[...] = jnp.zeros_like(sums)
         for slot, (b_ref, g_ref) in enumerate(((bo_ref, go_ref), (bf_ref, gf_ref))):
             column = sc_ref[0] ^ slot
-            for tw in range(2):
-                count = sz.frames - tw
-                span = slice(tw * sz.frames, tw * sz.frames + count)
-                shape = (count, sz.half, sz.width)
-                valid = valid_rows(tw, count, length, sz)
-                branch = frame_rows(b_ref[0, span].astype(F32))
-                middle = frame_rows(x_ref[0, tw, column, :count].astype(F32)) + gate1 * branch
+
+            def one(tw, t, f, slot=slot, column=column, b_ref=b_ref, g_ref=g_ref):
+                valid = (f < length).astype(F32)
+                branch = b_ref[0, f].astype(F32)
+                middle = x_ref[0, tw, column, t].astype(F32) + gate1 * branch
                 normed, inv = normalize(middle)
-                y = frame_rows(y0_ref[slot, 0, span] + y1_ref[slot, 0, span]) + bd_ref[0:1, :]
-                grad = frame_rows(c_ref[0, tw, column, :count].astype(F32))
-                out_ref[0, tw, column, :count] = (
-                    (middle + valid * gate2 * y).astype(BF16).reshape(shape)
-                )
-                two = frame_rows(t0_ref[slot, 0, span] + t1_ref[slot, 0, span])
+                y = y0_ref[slot, 0, f] + y1_ref[slot, 0, f] + bd_ref[0:1, :]
+                grad = c_ref[0, tw, column, t].astype(F32)
+                out_ref[0, tw, column, t] = (middle + valid * gate2 * y).astype(BF16)
+                two = t0_ref[slot, 0, f] + t1_ref[slot, 0, f]
                 gm = grad + norm_back(two * scale, normed, inv)
-                gm_ref[slot, 0, span] = gm.reshape(shape)
-                g_ref[0, span] = (valid * (gm * gate1)).astype(BF16).reshape(shape)
+                gm_ref[slot, 0, f] = gm
+                g_ref[0, f] = (valid * (gm * gate1)).astype(BF16)
                 for n, term in enumerate((two, two * normed, grad * valid * y, gm * branch)):
-                    sums[n] = sums[n] + jnp.sum(term, axis=0, keepdims=True)
+                    sums[n] += fold_rows(term)
+
+            each_frame(one, sz)
             out_ref[0, 1, column, sz.frames - 1] = x_ref[0, 1, column, sz.frames - 1]
         for n in range(4):
-            sum_ref[0, n : n + 1, :] = sums[n]
+            sum_ref[0, n : n + 1, :] = jnp.sum(sums[n], axis=0, keepdims=True)
 
     strip = (1, 2, 2, sz.frames, sz.half, sz.width)
     piece = (1, sz.used, sz.half, sz.width)
@@ -230,6 +228,7 @@
                 pl.BlockSpec(piece, at_piece),
                 pl.BlockSpec((1, 4, sz.width), lambda m, s: (m, 0, 0)),
             ],
+            scratch_shapes=[pltpu.VMEM((4, 8, sz.width), F32)],
         ),
         out_shape=[
             jax.ShapeDtypeStruct(tok.shape, BF16),
@@ -244,26 +243,25 @@
 
 
 def last_norm(tok, cot, grad_mid, grad_own, grad_far, mod, scalars, sz):
-    def kernel(sc_ref, x_ref, c_ref, gm_ref, go_ref, gf_ref, mod_ref, out_ref, sum_ref):
+    def kernel(sc_ref, x_ref, c_ref, gm_ref, go_ref, gf_ref, mod_ref, out_ref, sum_ref, sums):
         scale = 1.0 + mod_ref[0, 1:2, :]
-        sums = [jnp.zeros((1, sz.width), F32) for _ in range(2)]
+        sums[...] = jnp.zeros_like(sums)
         for slot, g_ref in enumerate((go_ref, gf_ref)):
             column = sc_ref[0] ^ slot
-            for tw in range(2):
-                count = sz.frames - tw
-                span = slice(tw * sz.frames, tw * sz.frames + count)
-                normed, inv = normalize(frame_rows(x_ref[0, tw, column, :count].astype(F32)))
-                one = frame_rows(g_ref[0, span].astype(F32))
-                grad = frame_rows(gm_ref[slot, 0, span]) + norm_back(one * scale, normed, inv)
-                out_ref[0, tw, column, :count] = grad.astype(BF16).reshape(
-                    count, sz.half, sz.width
-                )
-                for n, term in enumerate((one, one * normed)):
-                    sums[n] = sums[n] + jnp.sum(term, axis=0, keepdims=True)
+
+            def one(tw, t, f, slot=slot, column=column, g_ref=g_ref):
+                normed, inv = normalize(x_ref[0, tw, column, t].astype(F32))
+                grad = g_ref[0, f].astype(F32)
+                total = gm_ref[slot, 0, f] + norm_back(grad * scale, normed, inv)
+                out_ref[0, tw, column, t] = total.astype(BF16)
+                sums[0] += fold_rows(grad)
+                sums[1] += fold_rows(grad * normed)
+
+            each_frame(one, sz)
         for slot in range(2):
             out_ref[0, 1, slot, sz.frames - 1] = c_ref[0, 0, slot, 0]
         for n in range(2):
-            sum_ref[0, n : n + 1, :] = sums[n]
+            sum_ref[0, n : n + 1, :] = jnp.sum(sums[n], axis=0, keepdims=True)
 
     strip = (1, 2, 2, sz.frames, sz.half, sz.width)
     tail = (1, 1, 2, 1, sz.half, sz.width)
@@ -286,6 +284,7 @@
                 pl.BlockSpec(strip, lambda m, s: (m, 0, 0, 0, 0, 0)),
                 pl.BlockSpec((1, 2, sz.width), lambda m, s: (m, 0, 0)),
             ],
+            scratch_shapes=[pltpu.VMEM((2, 8, sz.width), F32)],
         ),
         out_shape=[
             jax.ShapeDtypeStruct(tok.shape, BF16),
@@ -579,6 +578,7 @@
         gwo_refs = gw_refs if direct else take(1)
         fold_ref, ho_ref, hf_ref = take(3)
         grad, hidden_t, grad_att, parts, spread, pair_sum, total, turned = take(8)
+        (folded,) = take(1)
         step = pl.program_id(0)
 
         @pl.when(step == 0)
@@ -632,12 +632,11 @@
 
         lax.fori_loop(0, sz.micro, one_micro, 0)
         for head in range(sz.group):
-            fold_ref[head] = jnp.zeros(fold_ref.shape[1:], F32)
+            folded[...] = jnp.zeros_like(folded)
             for t in range(sz.frames):
                 low = (sz.frames - 1 - t) * sz.frame
-                fold_ref[head, :, low : low + full] += pair_sum[
-                    head, t * sz.frame : (t + 1) * sz.frame, :
-                ]
+                folded[:, low : low + full] += pair_sum[head, t * sz.frame : (t + 1) * sz.frame, :]
+            fold_ref[head] = folded[...].astype(BF16)
         for n in range(4):
             rows = slice(n * quarter, (n + 1) * quarter)
             give(gw_refs, n // 2, n % 2 * quarter, dot_nn(hidden_t[rows, :], parts[...]))
@@ -681,7 +680,7 @@
     out_shape = grad_shapes(direct, shard, width, steps * wide)
     if not direct:
         out_shape += grad_shapes(direct, shard, width, width)
-    out_shape += [jax.ShapeDtypeStruct((HEADS,) + fold, F32)]
+    out_shape += [jax.ShapeDtypeStruct((HEADS,) + fold, BF16)]
     out_shape += [jax.ShapeDtypeStruct(piece, BF16)] * 2
     scratch = [
         pltpu.VMEM((sz.rows, width), BF16),
@@ -695,6 +694,7 @@
     flops = 16 * sz.rows * width * width + 10 * sz.rows * sz.lens[0] * width
     in_specs += [once((sz.rows, cols), flat)] * 2
     scratch += [pltpu.VMEM((sz.rows, width), F32), pltpu.VMEM((width, sz.rows), BF16)]
+    scratch += [pltpu.VMEM(fold, F32)]
     args += list(atts)
     return pl.pallas_call(
         kernel,
@@ -894,10 +894,8 @@
 def offset_grad(fold, places, sz):
     steps = 2 * sz.frames - 1
     fold = fold.reshape(-1, sz.frame, steps, sz.frame)
-    return sum(
-        jnp.einsum("hqkp,jpq->hkj", part, places, preferred_element_type=F32)
-        for part in split_low(fold)
-    ).reshape(fold.shape[0], -1)
+    made = jnp.einsum("hqkp,jpq->hkj", fold, places, preferred_element_type=F32)
+    return made.reshape(fold.shape[0], -1)
 
 
 def table_grad(by_offset, bucket, buckets):
@@ -941,6 +939,22 @@
         got = [self.from_z(kept[self.deep - k], k) for k in range(1, self.deep)]
         notes.append(got[-1])
         return kept[0] + sum(got)
+
+    def share(self, value, count, scatter):
+        deep = self.deep
+        got = self.swap(value, self.Y)
+        clips = jnp.stack([value[:count], got[:count]])
+        rest = (value[count:] + got[count:]).reshape(deep, -1)
+        pick = lambda at: lax.dynamic_index_in_dim(rest, at % deep, 0, keepdims=False)
+        sends = [
+            jnp.concatenate([clips.reshape(-1), pick(self.z + deep - k)]).astype(BF16)
+            for k in range(1, deep)
+        ]
+        sends = tie2(sends, scatter.got[:1])
+        got = [self.from_z(send, k).astype(F32) for k, send in enumerate(sends, 1)]
+        clips = jnp.stack([clips] + [v[: 2 * count].reshape(2, count) for v in got])
+        rest = (pick(self.z) + sum(v[2 * count :] for v in got)).reshape(8, -1)
+        return clips, lax.dynamic_index_in_dim(rest, self.index % 8, 0, keepdims=False)
 
     def gather_pairs(self, value):
         parts = value
@@ -1098,6 +1112,23 @@
 
     def total(self):
         return self.keep[0].astype(F32) + sum(v.astype(F32) for v in self.got)
+
+    def total_heads(self, sz):
+        size = sz.gcols
+
+        def kernel(sc_ref, own, g0, g1, g2, qkv_ref, out_ref):
+            for g in range(sz.groups):
+                for n in range(4):
+                    low = (4 * g + n) * size
+                    total = sum(v[:, low : low + size].astype(F32) for v in (own, g0, g1, g2))
+                    if n < 3:
+                        low = n * sz.width + g * size
+                        qkv_ref[:, low : low + size] = total
+                    else:
+                        out_ref[:, g * size : (g + 1) * size] = total
+
+        outs = [jax.ShapeDtypeStruct((self.rows, k * sz.width), F32) for k in (3, 1)]
+        return self.call(kernel, [*self.keep, *self.got], outs, "total_heads")
 
     def call(self, kernel, args, outs, name):
         return pl.pallas_call(
@@ -1331,10 +1362,7 @@
         every = net.swap_sum(net.swap_sum(every, net.CORE), net.X)
         heads.tie(every)
         heads.fourth()
-        every = net.gather_clips(tie(every, *heads.keep))
-        mod_all = every[:, :, : grad_mod.size]
-        g_small = jnp.sum(every[:, :, grad_mod.size :], axis=(0, 1)).reshape(g_small.shape)
-        g_small = lax.dynamic_index_in_dim(g_small, index, 0, keepdims=False)
+        mod_all, g_small = net.share(tie(every, *heads.keep), grad_mod.size, heads)
     else:
         mod_all = lax.all_gather(lax.psum(grad_mod, "win"), "clip", axis=0)
         g_small = lax.psum_scatter(g_small, axes, scatter_dimension=0, tiled=False)
@@ -1348,9 +1376,7 @@
     )
     if net.direct:
         r_u, r_d = zip(unpack_inner(r_first), unpack_inner(r_second))
-        mine = heads.total().reshape(rows, sz.groups, -1)
-        r_qkv = mine[:, :, : 3 * sz.gcols]
-        r_out = mine[:, :, 3 * sz.gcols :].reshape(rows, width)
+        r_qkv, r_out = heads.total_heads(sz)
     else:
         scatter = lambda v: lax.psum_scatter(
             v.astype(F32), axes, scatter_dimension=0, tiled=True
@@ -1358,10 +1384,10 @@
         r_u = [scatter(v[-2]) for v in mlps]
         r_d = [scatter(v[-1]) for v in mlps]
         r_qkv, r_out = scatter(g_att[0]), scatter(g_att[1])
+        r_qkv = r_qkv.reshape(rows, sz.groups, 3, sz.gcols).transpose(0, 2, 1, 3)
+        r_qkv = r_qkv.reshape(rows, 3 * width)
     r_up = inner_back(r_u)
     r_down = jnp.concatenate(r_d)
-    r_qkv = r_qkv.reshape(rows, sz.groups, 3, sz.gcols).transpose(0, 2, 1, 3)
-    r_qkv = r_qkv.reshape(rows, 3 * width)
     return (
         output.reshape(tokens.shape), grad_in.reshape(tokens.shape), grad_ada_w, grad_ada_b,
         r_qkv, r_out, r_up, g_small[:n_up], r_down, g_small[n_up : n_up + n_down],

time: 479 us -> 466 us (0.973)
  starting transfers between devices: 81.8 us -> 65.6 us
  Pallas kernels: 257 us -> 271 us
  other arithmetic: 18.1 us -> 12.1 us
    ppermute x35, starting transfers between devices: 39.5 us -> 21.9 us  [swap(): lax.ppermute(value, self.AXES, [(n, n ^ which) for n in range(self.count)])]
    pallas_call x1, Pallas kernels: 61.5 us -> 69 us  [attention_back(): pl.pallas_call(kernel, grid_spec=pltpu.PrefetchScalarGridSpec(num_scalar_...]
    convert_element_type x1 -> x3, other arithmetic: 5.09 us -> 0.03 us  [share(): got = [self.from_z(send, k).astype(F32) for k, send in enumerate(sends, 1)]]
    pallas_call x4 -> x5, Pallas kernels: 15.8 us -> 18.5 us  [call(): pl.pallas_call(kernel, grid_spec=pltpu.PrefetchScalarGridSpec(num_scalar_...]
    unnamed x126 -> x127, local copies, waits for them, and re-layouts: 10.6 us -> 11.3 us
  transfers between devices with their start and end apart: 63 -> 63, of which waited for: 14 -> 15; matrix products, arithmetic and copies ran while one was open for 11% -> 8% of each run, Pallas kernels for 54% -> 58%
where the time goes in v4:
time: 466 us; the launch traced here: 460 us
  Pallas kernels  271 us (58%)
  starting transfers between devices  65.6 us (14%)
  waiting for transfers between devices  53.2 us (11%)
  local copies, waits for them, and re-layouts  35.8 us (8%)
  between operations  15.6 us (3%)
  other arithmetic  12.1 us (3%)
  matrix products  6.28 us (1%)
    pallas_call x2, Pallas kernels, mlp(): pl.pallas_call(kernel, grid_spec=pltpu.PrefetchScalarGridSpec(num_scalar_...  82.8 us
    pallas_call x1, Pallas kernels, attention_back(): pl.pallas_call(kernel, grid_spec=pltpu.PrefetchScalarGridSpec(num_scalar_...  69 us
    pallas_call x2, Pallas kernels, attention(): pl.pallas_call(kernel, grid_spec=pltpu.PrefetchScalarGridSpec(num_scalar_...  49.4 us
    ppermute x21, starting transfers between devices, from_z(): lax.ppermute(value, self.AXES, [(n, move(n)) for n in range(self.count)])  42.8 us
    ppermute x35, waiting for transfers between devices, swap(): lax.ppermute(value, self.AXES, [(n, n ^ which) for n in range(self.count)])  36.6 us
    ppermute x35, starting transfers between devices, swap(): lax.ppermute(value, self.AXES, [(n, n ^ which) for n in range(self.count)])  21.9 us
    pallas_call x5, Pallas kernels, call(): pl.pallas_call(kernel, grid_spec=pltpu.PrefetchScalarGridSpec(num_scalar_...  18.5 us
    pallas_call x1, Pallas kernels, after_mlp(): pl.pallas_call(kernel, grid_spec=pltpu.PrefetchScalarGridSpec(num_scalar_...  15 us
  transfers between devices with their start and end apart: 63, of which 15 were waited for; matrix products, arithmetic and copies ran while one was open for 8% of the time, Pallas kernels for 58%

profile of v4, /device:TPU:0, one launch (start us, length us, event | category | flops | bytes accessed | tf_op | source)
XLA Modules:
  0.0 460.1 jit_solution(1841924447748549037)
XLA Ops:
  34.0 4.1 collective-permute-done.4
  40.4 3.8 collective-permute-start.5
  68.0 3.5 reshape.413.bias_ref
  74.4 8.8 %collective-permute-done.21.refs_5_ = bf16[2,4,16,1536]{3,2,1,0:T(8,128)(2,1)} collective-permute-done((bf16[2,4,16,1536]{3,2,1,0:T(8,128)(2,1)S(1)}, bf16[2,4,16,1536]{3,2,1,0:T(8,128)(2,1)}, u32[]{:S(2)}, u32[]{:S(2)}) %collective-permute-start.21) | collective-permute-done | bytes 393248 | tf_op jit(solution)/shard_map/ppermute | solution.py:921
  85.5 4.7 %first_norm.1 = (bf16[2,9,32,1024]{3,2,1,0:T(8,128)(2,1)}, bf16[2,9,32,1024]{3,2,1,0:T(8,128)(2,1)}) custom-call(s32[5]{0:T(128)} %compare_select_fusion.7.sc_ref, bf16[2,2,2,5,32,1024]{5,4,3,2,1,0:T(8,128)(2,1)} %bitcast.152, f32[2,6,1024]{2,1,0:T(8,128)} %reshape.409.mod_ref), custom_call_target="tpu_custom_call" | custom-call | tf_op jit(solution)/shard_map/first_norm/pallas_call | solution.py:107
  98.0 22.3 %attention.1 = (bf16[3,1152,1024]{2,1,0:T(8,128)(2,1)}, bf16[1024,3072]{1,0:T(8,128)(2,1)}, bf16[1152,512]{1,0:T(8,128)(2,1)}) custom-call(s32[5]{0:T(128)} %compare_select_fusion.7.sc_ref, bf16[2,9,32,1024]{3,2,1,0:T(8,128)(2,1)} %get-tuple-element.140.own_ref, bf16[2,9,32,1024]{3,2,1,0:T(8,128)(2,1)} %copy-done.50, ...), custom_call_target="tpu_custom_call" | custom-call | flops 13136560128 | bytes 18874368 | tf_op jit(solution)/shard_map/attention/pallas_call | solution.py:546
  121.5 27.1 %attention_last.1 = (bf16[3,1152,1024]{2,1,0:T(8,128)(2,1)}, bf16[1024,3072]{1,0:T(8,128)(2,1)}, bf16[1152,512]{1,0:T(8,128)(2,1)}, bf16[1024,1024]{1,0:T(8,128)...) custom-call(s32[5]{0:T(128)} %compare_select_fusion.7.sc_ref, ...), custom_call_target="tpu_custom_call", output_to_operand_aliasing={{0}: (8, {}), {1}: (9, {})} | custom-call | flops 20384317440 | bytes 18874368 | tf_op jit(solution)/shard_map/attention_last/pallas_call | solution.py:546
  148.6 4.7 %collective-permute-done.30.refs_5_ = bf16[2,4,16,4096]{3,2,1,0:T(8,128)(2,1)} collective-permute-done((bf16[2,4,16,4096]{3,2,1,0:T(8,128)(2,1)S(1)}, bf16[2,4,16,4096]{3,2,1,0:T(8,128)(2,1)}, u32[]{:S(2)}, u32[]{:S(2)}) %collective-permute-start.30) | collective-permute-done | bytes 1048608 | tf_op jit(solution)/shard_map/ppermute | solution.py:921
  153.3 4.4 collective-permute-done.31.bf_ref
  160.4 6.7 %second_norm.1 = (bf16[2,2,9,32,1024]{4,3,2,1,0:T(8,128)(2,1)}, bf16[2,2,9,32,1024]{4,3,2,1,0:T(8,128)(2,1)}) custom-call(s32[5]{0:T(128)} %compare_select_fusion.7.sc_ref, bf16[2,2,2,5,32,1024]{5,4,3,2,1,0:T(8,128)(2,1)} %bitcast.153, bf16[2,2,2,5,32,1024]{5,4,3,2,1,0:T(8,128)(2,1)} %bitcast.156, bf16[2,9,32,1024]{3,2,1,0:T(8,128)(2,1)} %get-tuple-element.150.bo_ref, ...), custom_call_target="tpu_custom_call" | custom-call | tf_op jit(solution)/shard_map/second_norm/pallas_call | solution.py:147
  167.1 41.1 %mlp.2 = (f32[1152,1024]{1,0:T(8,128)}, f32[1152,1024]{1,0:T(8,128)}, f32[1,2048]{1,0:T(1,128)}, f32[1,1024]{1,0:T(1,128)}, bf16[1024,4096]{1,0:T(8,128)(2,1)}) custom-call(s32[5]{0:T(128)} %compare_select_fusion.7.sc_ref, bf16[1152,1024]{1,0:T(8,128)(2,1)} %bitcast.216, bf16[1152,1024]{1,0:T(8,128)(2,1)} %bitcast.218, f32[1,2048]{1,0:T(1,128)} %squeeze.65.bu_ref, ...), custom_call_target="tpu_custom_call" | custom-call | flops 33822867456 | bytes 18874368 | tf_op jit(solution)/shard_map/mlp/pallas_call | solution.py:852
  208.3 41.7 %mlp.3 = (f32[1152,1024]{1,0:T(8,128)}, f32[1152,1024]{1,0:T(8,128)}, f32[1,2048]{1,0:T(1,128)}, bf16[16,32,4096]{2,1,0:T(8,128)(2,1)}, bf16[16,32,4096]{2,1,0:T(8,128)(2,1)}) custom-call(s32[5]{0:T(128)} %compare_select_fusion.7.sc_ref, bf16[1152,1024]{1,0:T(8,128)(2,1)} %bitcast.217, bf16[1152,1024]{1,0:T(8,128)(2,1)} %bitcast.219, ...), custom_call_target="tpu_custom_call" | custom-call | flops 33822867456 | bytes 18874368 | tf_op jit(solution)/shard_map/mlp/pallas_call | solution.py:852
  250.8 15.0 %after_mlp.1 = (bf16[2,2,2,5,32,1024]{5,4,3,2,1,0:T(8,128)(2,1)}, f32[2,2,9,32,1024]{4,3,2,1,0:T(8,128)}, bf16[2,9,32,1024]{3,2,1,0:T(8,128)(2,1)}, bf16[2,9,32,1024]{3,2,1,0:T(8,128)(2,1)}, f32[2,4,1024]{2,1,0:T(4,128)}) custom-call(s32[5]{0:T(128)} %compare_select_fusion.7.sc_ref, bf16[2,2,2,5,32,1024]{5,4,3,2,1,0:T(8,128)(2,1)} %bitcast.154, ...), custom_call_target="tpu_custom_call" | custom-call | tf_op jit(solution)/shard_map/after_mlp/pallas_call | solution.py:207
  266.7 7.0 %add_cores.2 = (bf16[4,2,16,4096]{3,2,1,0:T(8,128)(2,1)}, bf16[4,2,16,4096]{3,2,1,0:T(8,128)(2,1)}, bf16[4,2,16,4096]{3,2,1,0:T(8,128)(2,1)}, bf16[4,2,16,4096]{3,2,1,0:T(8,128)(2,1)}) custom-call(s32[3]{0:T(128)} %pad_add_fusion.sc_ref, bf16[4,4,32,4096]{3,2,1,0:T(8,128)(2,1)} %bitcast.168, bf16[4,4,32,4096]{3,2,1,0:T(8,128)(2,1)} %collective-permute-done.36.got), custom_call_target="tpu_custom_call" | custom-call | bytes 12582912 | tf_op jit(solution)/shard_map/add_cores/pallas_call | solution.py:1069
  275.7 69.0 %attention_back.1 = (bf16[16,32,4096]{2,1,0:T(8,128)(2,1)}, bf16[16,32,4096]{2,1,0:T(8,128)(2,1)}, bf16[16,64,576]{2,1,0:T(8,128)(2,1)}, bf16[2,9,32,1024]{3,2,1,0:T(8,128)(2,1)}, bf16[2,9,32,1024]{3,2,1,0:T(8,128)(2,1)}) custom-call(s32[5]{0:T(128)} %compare_select_fusion.7.sc_ref, bf16[2,9,32,1024]{3,2,1,0:T(8,128)(2,1)} %get-tuple-element.176.go_ref, ...), custom_call_target="tpu_custom_call" | custom-call | flops 69306679296 | bytes 28311552 | tf_op jit(solution)/shard_map/attention_back/pallas_call | solution.py:699
  346.1 4.6 add_second.2
  355.6 6.6 %add_cores.3 = (bf16[4,2,16,4096]{3,2,1,0:T(8,128)(2,1)}, bf16[4,2,16,4096]{3,2,1,0:T(8,128)(2,1)}, bf16[4,2,16,4096]{3,2,1,0:T(8,128)(2,1)}, bf16[4,2,16,4096]{3,2,1,0:T(8,128)(2,1)}) custom-call(s32[3]{0:T(128)} %pad_add_fusion.sc_ref, bf16[4,4,32,4096]{3,2,1,0:T(8,128)(2,1)} %bitcast.167, bf16[4,4,32,4096]{3,2,1,0:T(8,128)(2,1)} %collective-permute-done.41.got), custom_call_target="tpu_custom_call" | custom-call | bytes 12582912 | tf_op jit(solution)/shard_map/add_cores/pallas_call | solution.py:1069
  366.1 7.9 %last_norm.1 = (bf16[2,2,2,5,32,1024]{5,4,3,2,1,0:T(8,128)(2,1)}, f32[2,2,1024]{2,1,0:T(2,128)}) custom-call(s32[5]{0:T(128)} %compare_select_fusion.7.sc_ref, bf16[2,2,2,5,32,1024]{5,4,3,2,1,0:T(8,128)(2,1)} %bitcast.155, bf16[2,2,2,5,32,1024]{5,4,3,2,1,0:T(8,128)(2,1)} %bitcast.158, f32[2,2,9,32,1024]{4,3,2,1,0:T(8,128)} %get-tuple-element.169.gm_ref, ...), custom_call_target="tpu_custom_call" | custom-call | tf_op jit(solution)/shard_map/last_norm/pallas_call | solution.py:270
  380.3 4.3 copy.214
  389.8 4.5 add_second.3
  405.1 3.7 collective-permute-done.50
  423.5 4.2 collective-permute-start.55
  427.7 9.6 %collective-permute-start.56 = (bf16[27904]{0:T(1024)(128)(2,1)S(1)}, bf16[27904]{0:T(1024)(128)(2,1)S(1)}, u32[]{:S(2)}, u32[]{:S(2)}) collective-permute-start(bf16[27904]{0:T(1024)(128)(2,1)S(1)} %get-tuple-element.235), channel_id=1, source_target_pairs={{0,16},{1,17},{2,18},{3,19},{4,20},{5,21},{6,22},{7,23},{8,24},{9,... | collective-permute-start | bytes 167432 | tf_op jit(solution)/shard_map/ppermute | solution.py:925
  437.5 6.9 %collective-permute-done.58.g1 = bf16[32,4096]{1,0:T(8,128)(2,1)S(1)} collective-permute-done((bf16[32,4096]{1,0:T(8,128)(2,1)}, bf16[32,4096]{1,0:T(8,128)(2,1)S(1)}, u32[]{:S(2)}, u32[]{:S(2)}) %collective-permute-start.58) | collective-permute-done | bytes 262176 | tf_op jit(solution)/shard_map/ppermute | solution.py:925
  (401 shorter events, 128.4 us)
Async XLA Ops:
  7.3 114.2 %all-gather.3.cloned.1.call-start = ((), (), s32[]{:S(2)}) async-start(), calls=%async_computation.1 | async-start | bytes 5406720 | tf_op jit(solution)/shard_map/all_gather | solution.py:1240
  9.8 198.5 %all-gather.5.cloned.1.call-start = ((), (), s32[]{:S(2)}) async-start(), calls=%async_computation.2 | async-start | bytes 8650752 | tf_op jit(solution)/shard_map/all_gather | solution.py:1240
  17.1 23.3 %collective-permute-start.17 = (bf16[32,1536]{1,0:T(8,128)(2,1)S(1)}, bf16[32,1536]{1,0:T(8,128)(2,1)S(1)}, u32[]{:S(2)}, u32[]{:S(2)}) collective-permute-start(bf16[32,1536]{1,0:T(8,128)(2,1)S(1)} %bitcast.194), channel_id=1, source_target_pairs={{0,8},{1,9},{2,10},{3,11},{4,12},{5,13},{6,14},{7,15},{8,16},{9,17... | collective-permute-start | bytes 294920 | tf_op jit(solution)/shard_map/ppermute | solution.py:925
  17.8 26.4 %collective-permute-start.16 = (bf16[32,1536]{1,0:T(8,128)(2,1)S(1)}, bf16[32,1536]{1,0:T(8,128)(2,1)S(1)}, u32[]{:S(2)}, u32[]{:S(2)}) collective-permute-start(bf16[32,1536]{1,0:T(8,128)(2,1)S(1)} %bitcast.195), channel_id=1, source_target_pairs={{0,16},{1,17},{2,18},{3,19},{4,20},{5,21},{6,22},{7,23},{8,24},{9,... | collective-permute-start | bytes 294920 | tf_op jit(solution)/shard_map/ppermute | solution.py:925
  20.6 344.5 %reduce-scatter.2.cloned.1.call-start = ((), (), s32[]{:S(2)}) async-start(), calls=%async_computation.3 | async-start | bytes 8650752 | tf_op jit(solution)/shard_map/reduce_scatter | solution.py:1312
  50.4 21.8 %collective-permute-start.14 = (bf16[32,4096]{1,0:T(8,128)(2,1)S(1)}, bf16[32,4096]{1,0:T(8,128)(2,1)S(1)}, u32[]{:S(2)}, u32[]{:S(2)}) collective-permute-start(bf16[32,4096]{1,0:T(8,128)(2,1)S(1)} %copy.212.refs_0_), channel_id=1, source_target_pairs={{0,8},{1,9},{2,10},{3,11},{4,12},{5,13},{6,14},{7,15},{8,16},{9,17... | collective-permute-start | bytes 786440 | tf_op jit(solution)/shard_map/ppermute | solution.py:925
  50.4 21.8 %collective-permute-start.13 = (bf16[32,4096]{1,0:T(8,128)(2,1)S(1)}, bf16[32,4096]{1,0:T(8,128)(2,1)S(1)}, u32[]{:S(2)}, u32[]{:S(2)}) collective-permute-start(bf16[32,4096]{1,0:T(8,128)(2,1)S(1)} %copy.212.refs_0_), channel_id=1, source_target_pairs={{0,16},{1,17},{2,18},{3,19},{4,20},{5,21},{6,22},{7,23},{8,24},{9,... | collective-permute-start | bytes 786440 | tf_op jit(solution)/shard_map/ppermute | solution.py:925
  93.9 26.4 %collective-permute-start.27 = (bf16[4,16,4096]{2,1,0:T(8,128)(2,1)S(1)}, bf16[4,16,4096]{2,1,0:T(8,128)(2,1)S(1)}, u32[]{:S(2)}, u32[]{:S(2)}) collective-permute-start(bf16[4,16,4096]{2,1,0:T(8,128)(2,1)S(1)} %copy-done.12), channel_id=1, source_target_pairs={{0,2},{1,3},{2,0},{3,1},{4,6},{5,7},{6,4},{7,5},{8,10},{9,11},{10,... | collective-permute-start | bytes 1572872 | tf_op jit(solution)/shard_map/ppermute | solution.py:921
  95.5 24.7 %collective-permute-start.28 = (bf16[4,16,4096]{2,1,0:T(8,128)(2,1)S(1)}, bf16[4,16,4096]{2,1,0:T(8,128)(2,1)S(1)}, u32[]{:S(2)}, u32[]{:S(2)}) collective-permute-start(bf16[4,16,4096]{2,1,0:T(8,128)(2,1)S(1)} %copy-done.13), channel_id=1, source_target_pairs={{0,4},{1,5},{2,6},{3,7},{4,0},{5,1},{6,2},{7,3},{8,12},{9,13},{10,... | collective-permute-start | bytes 1572872 | tf_op jit(solution)/shard_map/ppermute | solution.py:921
  120.4 32.9 %collective-permute-start.30 = (bf16[2,4,16,4096]{3,2,1,0:T(8,128)(2,1)S(1)}, bf16[2,4,16,4096]{3,2,1,0:T(8,128)(2,1)}, u32[]{:S(2)}, u32[]{:S(2)}) collective-permute-start(bf16[2,4,16,4096]{3,2,1,0:T(8,128)(2,1)S(1)} %pad_maximum_fusion.2.refs_4_), channel_id=1, source_target_pairs={{0,2},{1,3},{2,0},{3,1},{4,6},{5,7},{6,4},{7,5},{8,10},{9,11},{10,... | collective-permute-start | bytes 3145736 | tf_op jit(solution)/shard_map/ppermute | solution.py:921
  121.4 31.9 %collective-permute-start.29 = (bf16[2,4,16,4096]{3,2,1,0:T(8,128)(2,1)S(1)}, bf16[2,4,16,4096]{3,2,1,0:T(8,128)(2,1)}, u32[]{:S(2)}, u32[]{:S(2)}) collective-permute-start(bf16[2,4,16,4096]{3,2,1,0:T(8,128)(2,1)S(1)} %pad_maximum_fusion.1.refs_0_), channel_id=1, source_target_pairs={{0,4},{1,5},{2,6},{3,7},{4,0},{5,1},{6,2},{7,3},{8,12},{9,13},{10,... | collective-permute-start | bytes 3145736 | tf_op jit(solution)/shard_map/ppermute | solution.py:921
  273.7 71.0 %collective-permute-start.38 = (bf16[4,2,16,4096]{3,2,1,0:T(8,128)(2,1)}, bf16[4,2,16,4096]{3,2,1,0:T(8,128)(2,1)S(1)}, u32[]{:S(2)}, u32[]{:S(2)}) collective-permute-start(bf16[4,2,16,4096]{3,2,1,0:T(8,128)(2,1)} %get-tuple-element.184), channel_id=1, source_target_pairs={{0,4},{1,5},{2,6},{3,7},{4,0},{5,1},{6,2},{7,3},{8,12},{9,13},{10,... | collective-permute-start | bytes 3145736 | tf_op jit(solution)/shard_map/ppermute | solution.py:921
  273.7 71.0 %collective-permute-start.39 = (bf16[4,2,16,4096]{3,2,1,0:T(8,128)(2,1)}, bf16[4,2,16,4096]{3,2,1,0:T(8,128)(2,1)S(1)}, u32[]{:S(2)}, u32[]{:S(2)}) collective-permute-start(bf16[4,2,16,4096]{3,2,1,0:T(8,128)(2,1)} %get-tuple-element.185), channel_id=1, source_target_pairs={{0,2},{1,3},{2,0},{3,1},{4,6},{5,7},{6,4},{7,5},{8,10},{9,11},{10,... | collective-permute-start | bytes 3145736 | tf_op jit(solution)/shard_map/ppermute | solution.py:921
  344.9 20.2 %collective-permute-start.40 = (bf16[2,9,32,1024]{3,2,1,0:T(8,128)(2,1)}, bf16[2,9,32,1024]{3,2,1,0:T(8,128)(2,1)S(1)}, u32[]{:S(2)}, u32[]{:S(2)}) collective-permute-start(bf16[2,9,32,1024]{3,2,1,0:T(8,128)(2,1)} %get-tuple-element.188), channel_id=1, source_target_pairs={{0,1},{1,0},{2,3},{3,2},{4,5},{5,4},{6,7},{7,6},{8,9},{9,8},{10,11... | collective-permute-start | bytes 3538952 | tf_op jit(solution)/shard_map/ppermute | solution.py:1334
  350.7 23.3 %collective-permute-start.42 = (bf16[4,16,4096]{2,1,0:T(8,128)(2,1)}, bf16[4,16,4096]{2,1,0:T(8,128)(2,1)S(1)}, u32[]{:S(2)}, u32[]{:S(2)}) collective-permute-start(bf16[4,16,4096]{2,1,0:T(8,128)(2,1)} %get-tuple-element.203), channel_id=1, source_target_pairs={{0,2},{1,3},{2,0},{3,1},{4,6},{5,7},{6,4},{7,5},{8,10},{9,11},{10,... | collective-permute-start | bytes 1572872 | tf_op jit(solution)/shard_map/ppermute | solution.py:921
  351.8 22.2 %collective-permute-start.43 = (bf16[4,16,4096]{2,1,0:T(8,128)(2,1)}, bf16[4,16,4096]{2,1,0:T(8,128)(2,1)S(1)}, u32[]{:S(2)}, u32[]{:S(2)}) collective-permute-start(bf16[4,16,4096]{2,1,0:T(8,128)(2,1)} %get-tuple-element.204), channel_id=1, source_target_pairs={{0,4},{1,5},{2,6},{3,7},{4,0},{5,1},{6,2},{7,3},{8,12},{9,13},{10,... | collective-permute-start | bytes 1572872 | tf_op jit(solution)/shard_map/ppermute | solution.py:921
  362.2 27.6 %collective-permute-start.47 = (bf16[4,2,16,4096]{3,2,1,0:T(8,128)(2,1)}, bf16[4,2,16,4096]{3,2,1,0:T(8,128)(2,1)}, u32[]{:S(2)}, u32[]{:S(2)}) collective-permute-start(bf16[4,2,16,4096]{3,2,1,0:T(8,128)(2,1)} %get-tuple-element.217), channel_id=1, source_target_pairs={{0,4},{1,5},{2,6},{3,7},{4,0},{5,1},{6,2},{7,3},{8,12},{9,13},{10,... | collective-permute-start | bytes 3145736 | tf_op jit(solution)/shard_map/ppermute | solution.py:921
  364.2 25.6 %collective-permute-start.48 = (bf16[4,2,16,4096]{3,2,1,0:T(8,128)(2,1)}, bf16[4,2,16,4096]{3,2,1,0:T(8,128)(2,1)}, u32[]{:S(2)}, u32[]{:S(2)}) collective-permute-start(bf16[4,2,16,4096]{3,2,1,0:T(8,128)(2,1)} %get-tuple-element.218), channel_id=1, source_target_pairs={{0,2},{1,3},{2,0},{3,1},{4,6},{5,7},{6,4},{7,5},{8,10},{9,11},{10,... | collective-permute-start | bytes 3145736 | tf_op jit(solution)/shard_map/ppermute | solution.py:921
  378.3 19.4 %collective-permute-start.45 = (bf16[32,4096]{1,0:T(8,128)(2,1)}, bf16[32,4096]{1,0:T(8,128)(2,1)}, u32[]{:S(2)}, u32[]{:S(2)}) collective-permute-start(bf16[32,4096]{1,0:T(8,128)(2,1)} %get-tuple-element.215), channel_id=1, source_target_pairs={{0,16},{1,17},{2,18},{3,19},{4,20},{5,21},{6,22},{7,23},{8,24},{9,... | collective-permute-start | bytes 786440 | tf_op jit(solution)/shard_map/ppermute | solution.py:925
  378.3 19.4 %collective-permute-start.46 = (bf16[32,4096]{1,0:T(8,128)(2,1)}, bf16[32,4096]{1,0:T(8,128)(2,1)}, u32[]{:S(2)}, u32[]{:S(2)}) collective-permute-start(bf16[32,4096]{1,0:T(8,128)(2,1)} %get-tuple-element.216), channel_id=1, source_target_pairs={{0,8},{1,9},{2,10},{3,11},{4,12},{5,13},{6,14},{7,15},{8,16},{9,17... | collective-permute-start | bytes 786440 | tf_op jit(solution)/shard_map/ppermute | solution.py:925
  416.4 28.0 %collective-permute-start.58 = (bf16[32,4096]{1,0:T(8,128)(2,1)}, bf16[32,4096]{1,0:T(8,128)(2,1)S(1)}, u32[]{:S(2)}, u32[]{:S(2)}) collective-permute-start(bf16[32,4096]{1,0:T(8,128)(2,1)} %get-tuple-element.237), channel_id=1, source_target_pairs={{0,16},{1,17},{2,18},{3,19},{4,20},{5,21},{6,22},{7,23},{8,24},{9,... | collective-permute-start | bytes 786440 | tf_op jit(solution)/shard_map/ppermute | solution.py:925
  418.2 26.2 %collective-permute-start.59 = (bf16[32,4096]{1,0:T(8,128)(2,1)}, bf16[32,4096]{1,0:T(8,128)(2,1)S(1)}, u32[]{:S(2)}, u32[]{:S(2)}) collective-permute-start(bf16[32,4096]{1,0:T(8,128)(2,1)} %get-tuple-element.238), channel_id=1, source_target_pairs={{0,8},{1,9},{2,10},{3,11},{4,12},{5,13},{6,14},{7,15},{8,16},{9,17... | collective-permute-start | bytes 786440 | tf_op jit(solution)/shard_map/ppermute | solution.py:925
  423.5 25.2 %collective-permute-start.55 = (bf16[27904]{0:T(1024)(128)(2,1)S(1)}, bf16[27904]{0:T(1024)(128)(2,1)S(1)}, u32[]{:S(2)}, u32[]{:S(2)}) collective-permute-start(bf16[27904]{0:T(1024)(128)(2,1)S(1)} %get-tuple-element.234), channel_id=1, source_target_pairs={{0,24},{1,25},{2,26},{3,27},{4,28},{5,29},{6,30},{7,31},{8,0},{9,1... | collective-permute-start | bytes 167432 | tf_op jit(solution)/shard_map/ppermute | solution.py:925
  427.7 20.9 %collective-permute-start.56 = (bf16[27904]{0:T(1024)(128)(2,1)S(1)}, bf16[27904]{0:T(1024)(128)(2,1)S(1)}, u32[]{:S(2)}, u32[]{:S(2)}) collective-permute-start(bf16[27904]{0:T(1024)(128)(2,1)S(1)} %get-tuple-element.235), channel_id=1, source_target_pairs={{0,16},{1,17},{2,18},{3,19},{4,20},{5,21},{6,22},{7,23},{8,24},{9,... | collective-permute-start | bytes 167432 | tf_op jit(solution)/shard_map/ppermute | solution.py:925
  (97 other events, 849.2 us)
Sparse Core Ops, SparseCore 0:
  11.0 85.6 all-gather.2
  99.5 83.4 all-gather.4
  208.4 148.7 reduce-scatter.1

commit v5 on v4

--- a/solution.py
+++ b/solution.py
@@ -1335,12 +1335,12 @@
         second.third()
         heads.tie(*second.keep)
         heads.second()
-        hid_far = tie(hid_far, r_first, *heads.keep)
+        hid_far = tie(hid_far, *heads.keep)
     else:
         hid_far = lax.ppermute(hid_send, "win", swap)
     grad_in, sums_one = last_norm(tok, cot, grad_mid, hid_own, hid_far, mod, scalars, sz)
     if net.direct:
-        second.tie(sums_one)
+        second.tie(sums_one, r_first)
         second.fourth()
         sums_one, fold = lax.optimization_barrier((sums_one, fold, *second.keep))[:2]
 

time: 466 us -> 464 us (level)
  starting transfers between devices: 65.6 us -> 77.9 us
  Pallas kernels: 271 us -> 259 us
    ppermute x21, starting transfers between devices: 42.8 us -> 50.3 us  [from_z(): lax.ppermute(value, self.AXES, [(n, move(n)) for n in range(self.count)])]
    pallas_call x1, Pallas kernels: 69 us -> 61.7 us  [attention_back(): pl.pallas_call(kernel, grid_spec=pltpu.PrefetchScalarGridSpec(num_scalar_...]
    pallas_call x2, Pallas kernels: 49.4 us -> 44.6 us  [attention(): pl.pallas_call(kernel, grid_spec=pltpu.PrefetchScalarGridSpec(num_scalar_...]
  transfers between devices with their start and end apart: 63 -> 63, of which waited for: 15 -> 15; matrix products, arithmetic and copies ran while one was open for 8% -> 8% of each run, Pallas kernels for 58% -> 56%
where the time goes in v5:
time: 464 us; the launch traced here: 461 us
  Pallas kernels  259 us (56%)
  starting transfers between devices  77.9 us (17%)
  waiting for transfers between devices  54.9 us (12%)
  local copies, waits for them, and re-layouts  34.8 us (7%)
  between operations  15.6 us (3%)
  other arithmetic  12.1 us (3%)
  matrix products  6.27 us (1%)
    pallas_call x2, Pallas kernels, mlp(): pl.pallas_call(kernel, grid_spec=pltpu.PrefetchScalarGridSpec(num_scalar_...  82.6 us
    pallas_call x1, Pallas kernels, attention_back(): pl.pallas_call(kernel, grid_spec=pltpu.PrefetchScalarGridSpec(num_scalar_...  61.7 us
    ppermute x21, starting transfers between devices, from_z(): lax.ppermute(value, self.AXES, [(n, move(n)) for n in range(self.count)])  50.3 us
    pallas_call x2, Pallas kernels, attention(): pl.pallas_call(kernel, grid_spec=pltpu.PrefetchScalarGridSpec(num_scalar_...  44.6 us
    ppermute x35, waiting for transfers between devices, swap(): lax.ppermute(value, self.AXES, [(n, n ^ which) for n in range(self.count)])  35.8 us
    ppermute x35, starting transfers between devices, swap(): lax.ppermute(value, self.AXES, [(n, n ^ which) for n in range(self.count)])  26.5 us
    pallas_call x5, Pallas kernels, call(): pl.pallas_call(kernel, grid_spec=pltpu.PrefetchScalarGridSpec(num_scalar_...  18.5 us
    ppermute x21, waiting for transfers between devices, from_z(): lax.ppermute(value, self.AXES, [(n, move(n)) for n in range(self.count)])  15.9 us
  transfers between devices with their start and end apart: 63, of which 15 were waited for; matrix products, arithmetic and copies ran while one was open for 8% of the time, Pallas kernels for 56%

profile of v5, /device:TPU:0, one launch (start us, length us, event | category | flops | bytes accessed | tf_op | source)
XLA Modules:
  0.0 460.7 jit_solution(11170268093028282576)
XLA Ops:
  34.0 4.1 collective-permute-done.4
  40.4 3.8 collective-permute-start.5
  74.4 8.8 %collective-permute-done.21.refs_5_ = bf16[2,4,16,1536]{3,2,1,0:T(8,128)(2,1)} collective-permute-done((bf16[2,4,16,1536]{3,2,1,0:T(8,128)(2,1)S(1)}, bf16[2,4,16,1536]{3,2,1,0:T(8,128)(2,1)}, u32[]{:S(2)}, u32[]{:S(2)}) %collective-permute-start.21) | collective-permute-done | bytes 393248 | tf_op jit(solution)/shard_map/ppermute | solution.py:921
  85.5 4.7 %first_norm.1 = (bf16[2,9,32,1024]{3,2,1,0:T(8,128)(2,1)}, bf16[2,9,32,1024]{3,2,1,0:T(8,128)(2,1)}) custom-call(s32[5]{0:T(128)} %compare_select_fusion.7.sc_ref, bf16[2,2,2,5,32,1024]{5,4,3,2,1,0:T(8,128)(2,1)} %bitcast.152, f32[2,6,1024]{2,1,0:T(8,128)} %reshape.409.mod_ref), custom_call_target="tpu_custom_call" | custom-call | tf_op jit(solution)/shard_map/first_norm/pallas_call | solution.py:107
  98.0 20.0 %attention.1 = (bf16[3,1152,1024]{2,1,0:T(8,128)(2,1)}, bf16[1024,3072]{1,0:T(8,128)(2,1)}, bf16[1152,512]{1,0:T(8,128)(2,1)}) custom-call(s32[5]{0:T(128)} %compare_select_fusion.7.sc_ref, bf16[2,9,32,1024]{3,2,1,0:T(8,128)(2,1)} %get-tuple-element.140.own_ref, bf16[2,9,32,1024]{3,2,1,0:T(8,128)(2,1)} %copy-done.50, ...), custom_call_target="tpu_custom_call" | custom-call | flops 13136560128 | bytes 18874368 | tf_op jit(solution)/shard_map/attention/pallas_call | solution.py:546
  120.2 24.6 %attention_last.1 = (bf16[3,1152,1024]{2,1,0:T(8,128)(2,1)}, bf16[1024,3072]{1,0:T(8,128)(2,1)}, bf16[1152,512]{1,0:T(8,128)(2,1)}, bf16[1024,1024]{1,0:T(8,128)...) custom-call(s32[5]{0:T(128)} %compare_select_fusion.7.sc_ref, ...), custom_call_target="tpu_custom_call", output_to_operand_aliasing={{0}: (8, {}), {1}: (9, {})} | custom-call | flops 20384317440 | bytes 18874368 | tf_op jit(solution)/shard_map/attention_last/pallas_call | solution.py:546
  144.9 6.1 %collective-permute-done.30.refs_5_ = bf16[2,4,16,4096]{3,2,1,0:T(8,128)(2,1)} collective-permute-done((bf16[2,4,16,4096]{3,2,1,0:T(8,128)(2,1)S(1)}, bf16[2,4,16,4096]{3,2,1,0:T(8,128)(2,1)}, u32[]{:S(2)}, u32[]{:S(2)}) %collective-permute-start.30) | collective-permute-done | bytes 1048608 | tf_op jit(solution)/shard_map/ppermute | solution.py:921
  156.7 6.7 %second_norm.1 = (bf16[2,2,9,32,1024]{4,3,2,1,0:T(8,128)(2,1)}, bf16[2,2,9,32,1024]{4,3,2,1,0:T(8,128)(2,1)}) custom-call(s32[5]{0:T(128)} %compare_select_fusion.7.sc_ref, bf16[2,2,2,5,32,1024]{5,4,3,2,1,0:T(8,128)(2,1)} %bitcast.153, bf16[2,2,2,5,32,1024]{5,4,3,2,1,0:T(8,128)(2,1)} %bitcast.156, bf16[2,9,32,1024]{3,2,1,0:T(8,128)(2,1)} %get-tuple-element.150.bo_ref, ...), custom_call_target="tpu_custom_call" | custom-call | tf_op jit(solution)/shard_map/second_norm/pallas_call | solution.py:147
  163.5 41.1 %mlp.2 = (f32[1152,1024]{1,0:T(8,128)}, f32[1152,1024]{1,0:T(8,128)}, f32[1,2048]{1,0:T(1,128)}, f32[1,1024]{1,0:T(1,128)}, bf16[1024,4096]{1,0:T(8,128)(2,1)}) custom-call(s32[5]{0:T(128)} %compare_select_fusion.7.sc_ref, bf16[1152,1024]{1,0:T(8,128)(2,1)} %bitcast.216, bf16[1152,1024]{1,0:T(8,128)(2,1)} %bitcast.218, f32[1,2048]{1,0:T(1,128)} %squeeze.65.bu_ref, ...), custom_call_target="tpu_custom_call" | custom-call | flops 33822867456 | bytes 18874368 | tf_op jit(solution)/shard_map/mlp/pallas_call | solution.py:852
  204.6 41.5 %mlp.3 = (f32[1152,1024]{1,0:T(8,128)}, f32[1152,1024]{1,0:T(8,128)}, f32[1,2048]{1,0:T(1,128)}, bf16[16,32,4096]{2,1,0:T(8,128)(2,1)}, bf16[16,32,4096]{2,1,0:T(8,128)(2,1)}) custom-call(s32[5]{0:T(128)} %compare_select_fusion.7.sc_ref, bf16[1152,1024]{1,0:T(8,128)(2,1)} %bitcast.217, bf16[1152,1024]{1,0:T(8,128)(2,1)} %bitcast.219, ...), custom_call_target="tpu_custom_call" | custom-call | flops 33822867456 | bytes 18874368 | tf_op jit(solution)/shard_map/mlp/pallas_call | solution.py:852
  247.0 14.9 %after_mlp.1 = (bf16[2,2,2,5,32,1024]{5,4,3,2,1,0:T(8,128)(2,1)}, f32[2,2,9,32,1024]{4,3,2,1,0:T(8,128)}, bf16[2,9,32,1024]{3,2,1,0:T(8,128)(2,1)}, bf16[2,9,32,1024]{3,2,1,0:T(8,128)(2,1)}, f32[2,4,1024]{2,1,0:T(4,128)}) custom-call(s32[5]{0:T(128)} %compare_select_fusion.7.sc_ref, bf16[2,2,2,5,32,1024]{5,4,3,2,1,0:T(8,128)(2,1)} %bitcast.154, ...), custom_call_target="tpu_custom_call" | custom-call | tf_op jit(solution)/shard_map/after_mlp/pallas_call | solution.py:207
  263.0 7.0 %add_cores.2 = (bf16[4,2,16,4096]{3,2,1,0:T(8,128)(2,1)}, bf16[4,2,16,4096]{3,2,1,0:T(8,128)(2,1)}, bf16[4,2,16,4096]{3,2,1,0:T(8,128)(2,1)}, bf16[4,2,16,4096]{3,2,1,0:T(8,128)(2,1)}) custom-call(s32[3]{0:T(128)} %pad_add_fusion.sc_ref, bf16[4,4,32,4096]{3,2,1,0:T(8,128)(2,1)} %bitcast.168, bf16[4,4,32,4096]{3,2,1,0:T(8,128)(2,1)} %collective-permute-done.36.got), custom_call_target="tpu_custom_call" | custom-call | bytes 12582912 | tf_op jit(solution)/shard_map/add_cores/pallas_call | solution.py:1069
  273.2 61.7 %attention_back.1 = (bf16[16,32,4096]{2,1,0:T(8,128)(2,1)}, bf16[16,32,4096]{2,1,0:T(8,128)(2,1)}, bf16[16,64,576]{2,1,0:T(8,128)(2,1)}, bf16[2,9,32,1024]{3,2,1,0:T(8,128)(2,1)}, bf16[2,9,32,1024]{3,2,1,0:T(8,128)(2,1)}) custom-call(s32[5]{0:T(128)} %compare_select_fusion.7.sc_ref, bf16[2,9,32,1024]{3,2,1,0:T(8,128)(2,1)} %get-tuple-element.176.go_ref, ...), custom_call_target="tpu_custom_call" | custom-call | flops 69306679296 | bytes 28311552 | tf_op jit(solution)/shard_map/attention_back/pallas_call | solution.py:699
  336.3 4.6 add_second.2
  346.5 6.6 %add_cores.3 = (bf16[4,2,16,4096]{3,2,1,0:T(8,128)(2,1)}, bf16[4,2,16,4096]{3,2,1,0:T(8,128)(2,1)}, bf16[4,2,16,4096]{3,2,1,0:T(8,128)(2,1)}, bf16[4,2,16,4096]{3,2,1,0:T(8,128)(2,1)}) custom-call(s32[3]{0:T(128)} %pad_add_fusion.sc_ref, bf16[4,4,32,4096]{3,2,1,0:T(8,128)(2,1)} %bitcast.167, bf16[4,4,32,4096]{3,2,1,0:T(8,128)(2,1)} %collective-permute-done.41.got), custom_call_target="tpu_custom_call" | custom-call | bytes 12582912 | tf_op jit(solution)/shard_map/add_cores/pallas_call | solution.py:1069
  355.4 7.9 %last_norm.1 = (bf16[2,2,2,5,32,1024]{5,4,3,2,1,0:T(8,128)(2,1)}, f32[2,2,1024]{2,1,0:T(2,128)}) custom-call(s32[5]{0:T(128)} %compare_select_fusion.7.sc_ref, bf16[2,2,2,5,32,1024]{5,4,3,2,1,0:T(8,128)(2,1)} %bitcast.155, bf16[2,2,2,5,32,1024]{5,4,3,2,1,0:T(8,128)(2,1)} %bitcast.158, f32[2,2,9,32,1024]{4,3,2,1,0:T(8,128)} %get-tuple-element.169.gm_ref, ...), custom_call_target="tpu_custom_call" | custom-call | tf_op jit(solution)/shard_map/last_norm/pallas_call | solution.py:270
  367.5 10.1 %collective-permute-start.44 = (bf16[32,4096]{1,0:T(8,128)(2,1)}, bf16[32,4096]{1,0:T(8,128)(2,1)}, u32[]{:S(2)}, u32[]{:S(2)}) collective-permute-start(bf16[32,4096]{1,0:T(8,128)(2,1)} %get-tuple-element.214), channel_id=1, source_target_pairs={{0,24},{1,25},{2,26},{3,27},{4,28},{5,29},{6,30},{7,31},{8,0},{9,1... | collective-permute-start | bytes 786440 | tf_op jit(solution)/shard_map/ppermute | solution.py:925
  380.8 4.3 copy.214
  390.3 4.5 add_second.3
  396.9 4.6 %collective-permute-done.45 = bf16[32,4096]{1,0:T(8,128)(2,1)} collective-permute-done((bf16[32,4096]{1,0:T(8,128)(2,1)}, bf16[32,4096]{1,0:T(8,128)(2,1)}, u32[]{:S(2)}, u32[]{:S(2)}) %collective-permute-start.45) | collective-permute-done | bytes 262176 | tf_op jit(solution)/shard_map/ppermute | solution.py:925
  421.1 4.3 collective-permute-done.54.g0
  425.4 3.6 collective-permute-start.55
  429.0 8.9 %collective-permute-start.56 = (bf16[27904]{0:T(1024)(128)(2,1)S(1)}, bf16[27904]{0:T(1024)(128)(2,1)S(1)}, u32[]{:S(2)}, u32[]{:S(2)}) collective-permute-start(bf16[27904]{0:T(1024)(128)(2,1)S(1)} %get-tuple-element.235), channel_id=1, source_target_pairs={{0,16},{1,17},{2,18},{3,19},{4,20},{5,21},{6,22},{7,23},{8,24},{9,... | collective-permute-start | bytes 167432 | tf_op jit(solution)/shard_map/ppermute | solution.py:925
  438.1 6.9 %collective-permute-done.58.g1 = bf16[32,4096]{1,0:T(8,128)(2,1)S(1)} collective-permute-done((bf16[32,4096]{1,0:T(8,128)(2,1)}, bf16[32,4096]{1,0:T(8,128)(2,1)S(1)}, u32[]{:S(2)}, u32[]{:S(2)}) %collective-permute-start.58) | collective-permute-done | bytes 262176 | tf_op jit(solution)/shard_map/ppermute | solution.py:925
  (401 shorter events, 133.7 us)
Async XLA Ops:
  7.3 113.0 %all-gather.3.cloned.1.call-start = ((), (), s32[]{:S(2)}) async-start(), calls=%async_computation.1 | async-start | bytes 5406720 | tf_op jit(solution)/shard_map/all_gather | solution.py:1240
  9.8 194.8 %all-gather.5.cloned.1.call-start = ((), (), s32[]{:S(2)}) async-start(), calls=%async_computation.2 | async-start | bytes 8650752 | tf_op jit(solution)/shard_map/all_gather | solution.py:1240
  17.1 23.3 %collective-permute-start.17 = (bf16[32,1536]{1,0:T(8,128)(2,1)S(1)}, bf16[32,1536]{1,0:T(8,128)(2,1)S(1)}, u32[]{:S(2)}, u32[]{:S(2)}) collective-permute-start(bf16[32,1536]{1,0:T(8,128)(2,1)S(1)} %bitcast.194), channel_id=1, source_target_pairs={{0,8},{1,9},{2,10},{3,11},{4,12},{5,13},{6,14},{7,15},{8,16},{9,17... | collective-permute-start | bytes 294920 | tf_op jit(solution)/shard_map/ppermute | solution.py:925
  17.8 26.4 %collective-permute-start.16 = (bf16[32,1536]{1,0:T(8,128)(2,1)S(1)}, bf16[32,1536]{1,0:T(8,128)(2,1)S(1)}, u32[]{:S(2)}, u32[]{:S(2)}) collective-permute-start(bf16[32,1536]{1,0:T(8,128)(2,1)S(1)} %bitcast.195), channel_id=1, source_target_pairs={{0,16},{1,17},{2,18},{3,19},{4,20},{5,21},{6,22},{7,23},{8,24},{9,... | collective-permute-start | bytes 294920 | tf_op jit(solution)/shard_map/ppermute | solution.py:925
  20.6 342.7 %reduce-scatter.2.cloned.1.call-start = ((), (), s32[]{:S(2)}) async-start(), calls=%async_computation.3 | async-start | bytes 8650752 | tf_op jit(solution)/shard_map/reduce_scatter | solution.py:1312
  50.4 21.8 %collective-permute-start.14 = (bf16[32,4096]{1,0:T(8,128)(2,1)S(1)}, bf16[32,4096]{1,0:T(8,128)(2,1)S(1)}, u32[]{:S(2)}, u32[]{:S(2)}) collective-permute-start(bf16[32,4096]{1,0:T(8,128)(2,1)S(1)} %copy.212.refs_0_), channel_id=1, source_target_pairs={{0,8},{1,9},{2,10},{3,11},{4,12},{5,13},{6,14},{7,15},{8,16},{9,17... | collective-permute-start | bytes 786440 | tf_op jit(solution)/shard_map/ppermute | solution.py:925
  50.4 21.8 %collective-permute-start.13 = (bf16[32,4096]{1,0:T(8,128)(2,1)S(1)}, bf16[32,4096]{1,0:T(8,128)(2,1)S(1)}, u32[]{:S(2)}, u32[]{:S(2)}) collective-permute-start(bf16[32,4096]{1,0:T(8,128)(2,1)S(1)} %copy.212.refs_0_), channel_id=1, source_target_pairs={{0,16},{1,17},{2,18},{3,19},{4,20},{5,21},{6,22},{7,23},{8,24},{9,... | collective-permute-start | bytes 786440 | tf_op jit(solution)/shard_map/ppermute | solution.py:925
  93.9 24.1 %collective-permute-start.27 = (bf16[4,16,4096]{2,1,0:T(8,128)(2,1)S(1)}, bf16[4,16,4096]{2,1,0:T(8,128)(2,1)S(1)}, u32[]{:S(2)}, u32[]{:S(2)}) collective-permute-start(bf16[4,16,4096]{2,1,0:T(8,128)(2,1)S(1)} %copy-done.12), channel_id=1, source_target_pairs={{0,2},{1,3},{2,0},{3,1},{4,6},{5,7},{6,4},{7,5},{8,10},{9,11},{10,... | collective-permute-start | bytes 1572872 | tf_op jit(solution)/shard_map/ppermute | solution.py:921
  95.5 22.4 %collective-permute-start.28 = (bf16[4,16,4096]{2,1,0:T(8,128)(2,1)S(1)}, bf16[4,16,4096]{2,1,0:T(8,128)(2,1)S(1)}, u32[]{:S(2)}, u32[]{:S(2)}) collective-permute-start(bf16[4,16,4096]{2,1,0:T(8,128)(2,1)S(1)} %copy-done.13), channel_id=1, source_target_pairs={{0,4},{1,5},{2,6},{3,7},{4,0},{5,1},{6,2},{7,3},{8,12},{9,13},{10,... | collective-permute-start | bytes 1572872 | tf_op jit(solution)/shard_map/ppermute | solution.py:921
  118.1 32.9 %collective-permute-start.30 = (bf16[2,4,16,4096]{3,2,1,0:T(8,128)(2,1)S(1)}, bf16[2,4,16,4096]{3,2,1,0:T(8,128)(2,1)}, u32[]{:S(2)}, u32[]{:S(2)}) collective-permute-start(bf16[2,4,16,4096]{3,2,1,0:T(8,128)(2,1)S(1)} %pad_maximum_fusion.2.refs_4_), channel_id=1, source_target_pairs={{0,2},{1,3},{2,0},{3,1},{4,6},{5,7},{6,4},{7,5},{8,10},{9,11},{10,... | collective-permute-start | bytes 3145736 | tf_op jit(solution)/shard_map/ppermute | solution.py:921
  119.1 31.9 %collective-permute-start.29 = (bf16[2,4,16,4096]{3,2,1,0:T(8,128)(2,1)S(1)}, bf16[2,4,16,4096]{3,2,1,0:T(8,128)(2,1)}, u32[]{:S(2)}, u32[]{:S(2)}) collective-permute-start(bf16[2,4,16,4096]{3,2,1,0:T(8,128)(2,1)S(1)} %pad_maximum_fusion.1.refs_0_), channel_id=1, source_target_pairs={{0,4},{1,5},{2,6},{3,7},{4,0},{5,1},{6,2},{7,3},{8,12},{9,13},{10,... | collective-permute-start | bytes 3145736 | tf_op jit(solution)/shard_map/ppermute | solution.py:921
  269.9 65.0 %collective-permute-start.38 = (bf16[4,2,16,4096]{3,2,1,0:T(8,128)(2,1)}, bf16[4,2,16,4096]{3,2,1,0:T(8,128)(2,1)S(1)}, u32[]{:S(2)}, u32[]{:S(2)}) collective-permute-start(bf16[4,2,16,4096]{3,2,1,0:T(8,128)(2,1)} %get-tuple-element.184), channel_id=1, source_target_pairs={{0,4},{1,5},{2,6},{3,7},{4,0},{5,1},{6,2},{7,3},{8,12},{9,13},{10,... | collective-permute-start | bytes 3145736 | tf_op jit(solution)/shard_map/ppermute | solution.py:921
  271.5 63.4 %collective-permute-start.39 = (bf16[4,2,16,4096]{3,2,1,0:T(8,128)(2,1)}, bf16[4,2,16,4096]{3,2,1,0:T(8,128)(2,1)S(1)}, u32[]{:S(2)}, u32[]{:S(2)}) collective-permute-start(bf16[4,2,16,4096]{3,2,1,0:T(8,128)(2,1)} %get-tuple-element.185), channel_id=1, source_target_pairs={{0,2},{1,3},{2,0},{3,1},{4,6},{5,7},{6,4},{7,5},{8,10},{9,11},{10,... | collective-permute-start | bytes 3145736 | tf_op jit(solution)/shard_map/ppermute | solution.py:921
  340.8 22.4 %collective-permute-start.42 = (bf16[4,16,4096]{2,1,0:T(8,128)(2,1)}, bf16[4,16,4096]{2,1,0:T(8,128)(2,1)S(1)}, u32[]{:S(2)}, u32[]{:S(2)}) collective-permute-start(bf16[4,16,4096]{2,1,0:T(8,128)(2,1)} %get-tuple-element.202), channel_id=1, source_target_pairs={{0,2},{1,3},{2,0},{3,1},{4,6},{5,7},{6,4},{7,5},{8,10},{9,11},{10,... | collective-permute-start | bytes 1572872 | tf_op jit(solution)/shard_map/ppermute | solution.py:921
  342.2 21.0 %collective-permute-start.43 = (bf16[4,16,4096]{2,1,0:T(8,128)(2,1)}, bf16[4,16,4096]{2,1,0:T(8,128)(2,1)S(1)}, u32[]{:S(2)}, u32[]{:S(2)}) collective-permute-start(bf16[4,16,4096]{2,1,0:T(8,128)(2,1)} %get-tuple-element.203), channel_id=1, source_target_pairs={{0,4},{1,5},{2,6},{3,7},{4,0},{5,1},{6,2},{7,3},{8,12},{9,13},{10,... | collective-permute-start | bytes 1572872 | tf_op jit(solution)/shard_map/ppermute | solution.py:921
  353.1 37.2 %collective-permute-start.47 = (bf16[4,2,16,4096]{3,2,1,0:T(8,128)(2,1)}, bf16[4,2,16,4096]{3,2,1,0:T(8,128)(2,1)}, u32[]{:S(2)}, u32[]{:S(2)}) collective-permute-start(bf16[4,2,16,4096]{3,2,1,0:T(8,128)(2,1)} %get-tuple-element.217), channel_id=1, source_target_pairs={{0,4},{1,5},{2,6},{3,7},{4,0},{5,1},{6,2},{7,3},{8,12},{9,13},{10,... | collective-permute-start | bytes 3145736 | tf_op jit(solution)/shard_map/ppermute | solution.py:921
  354.7 35.6 %collective-permute-start.48 = (bf16[4,2,16,4096]{3,2,1,0:T(8,128)(2,1)}, bf16[4,2,16,4096]{3,2,1,0:T(8,128)(2,1)}, u32[]{:S(2)}, u32[]{:S(2)}) collective-permute-start(bf16[4,2,16,4096]{3,2,1,0:T(8,128)(2,1)} %get-tuple-element.218), channel_id=1, source_target_pairs={{0,2},{1,3},{2,0},{3,1},{4,6},{5,7},{6,4},{7,5},{8,10},{9,11},{10,... | collective-permute-start | bytes 3145736 | tf_op jit(solution)/shard_map/ppermute | solution.py:921
  367.5 29.4 %collective-permute-start.44 = (bf16[32,4096]{1,0:T(8,128)(2,1)}, bf16[32,4096]{1,0:T(8,128)(2,1)}, u32[]{:S(2)}, u32[]{:S(2)}) collective-permute-start(bf16[32,4096]{1,0:T(8,128)(2,1)} %get-tuple-element.214), channel_id=1, source_target_pairs={{0,24},{1,25},{2,26},{3,27},{4,28},{5,29},{6,30},{7,31},{8,0},{9,1... | collective-permute-start | bytes 786440 | tf_op jit(solution)/shard_map/ppermute | solution.py:925
  377.6 23.9 %collective-permute-start.45 = (bf16[32,4096]{1,0:T(8,128)(2,1)}, bf16[32,4096]{1,0:T(8,128)(2,1)}, u32[]{:S(2)}, u32[]{:S(2)}) collective-permute-start(bf16[32,4096]{1,0:T(8,128)(2,1)} %get-tuple-element.215), channel_id=1, source_target_pairs={{0,16},{1,17},{2,18},{3,19},{4,20},{5,21},{6,22},{7,23},{8,24},{9,... | collective-permute-start | bytes 786440 | tf_op jit(solution)/shard_map/ppermute | solution.py:925
  378.7 22.8 %collective-permute-start.46 = (bf16[32,4096]{1,0:T(8,128)(2,1)}, bf16[32,4096]{1,0:T(8,128)(2,1)}, u32[]{:S(2)}, u32[]{:S(2)}) collective-permute-start(bf16[32,4096]{1,0:T(8,128)(2,1)} %get-tuple-element.216), channel_id=1, source_target_pairs={{0,8},{1,9},{2,10},{3,11},{4,12},{5,13},{6,14},{7,15},{8,16},{9,17... | collective-permute-start | bytes 786440 | tf_op jit(solution)/shard_map/ppermute | solution.py:925
  417.7 27.3 %collective-permute-start.58 = (bf16[32,4096]{1,0:T(8,128)(2,1)}, bf16[32,4096]{1,0:T(8,128)(2,1)S(1)}, u32[]{:S(2)}, u32[]{:S(2)}) collective-permute-start(bf16[32,4096]{1,0:T(8,128)(2,1)} %get-tuple-element.237), channel_id=1, source_target_pairs={{0,16},{1,17},{2,18},{3,19},{4,20},{5,21},{6,22},{7,23},{8,24},{9,... | collective-permute-start | bytes 786440 | tf_op jit(solution)/shard_map/ppermute | solution.py:925
  418.8 26.2 %collective-permute-start.59 = (bf16[32,4096]{1,0:T(8,128)(2,1)}, bf16[32,4096]{1,0:T(8,128)(2,1)S(1)}, u32[]{:S(2)}, u32[]{:S(2)}) collective-permute-start(bf16[32,4096]{1,0:T(8,128)(2,1)} %get-tuple-element.238), channel_id=1, source_target_pairs={{0,8},{1,9},{2,10},{3,11},{4,12},{5,13},{6,14},{7,15},{8,16},{9,17... | collective-permute-start | bytes 786440 | tf_op jit(solution)/shard_map/ppermute | solution.py:925
  425.4 23.8 %collective-permute-start.55 = (bf16[27904]{0:T(1024)(128)(2,1)S(1)}, bf16[27904]{0:T(1024)(128)(2,1)S(1)}, u32[]{:S(2)}, u32[]{:S(2)}) collective-permute-start(bf16[27904]{0:T(1024)(128)(2,1)S(1)} %get-tuple-element.234), channel_id=1, source_target_pairs={{0,24},{1,25},{2,26},{3,27},{4,28},{5,29},{6,30},{7,31},{8,0},{9,1... | collective-permute-start | bytes 167432 | tf_op jit(solution)/shard_map/ppermute | solution.py:925
  429.0 20.2 %collective-permute-start.56 = (bf16[27904]{0:T(1024)(128)(2,1)S(1)}, bf16[27904]{0:T(1024)(128)(2,1)S(1)}, u32[]{:S(2)}, u32[]{:S(2)}) collective-permute-start(bf16[27904]{0:T(1024)(128)(2,1)S(1)} %get-tuple-element.235), channel_id=1, source_target_pairs={{0,16},{1,17},{2,18},{3,19},{4,20},{5,21},{6,22},{7,23},{8,24},{9,... | collective-permute-start | bytes 167432 | tf_op jit(solution)/shard_map/ppermute | solution.py:925
  (97 other events, 860.2 us)
Sparse Core Ops, SparseCore 0:
  11.0 85.6 all-gather.2
  99.5 83.5 all-gather.4
  204.7 157.4 reduce-scatter.1

commit v6 on v5

--- a/solution.py
+++ b/solution.py
@@ -187,7 +187,7 @@
                 out_ref[0, tw, column, t] = (middle + valid * gate2 * y).astype(BF16)
                 two = t0_ref[slot, 0, f] + t1_ref[slot, 0, f]
                 gm = grad + norm_back(two * scale, normed, inv)
-                gm_ref[slot, 0, f] = gm
+                gm_ref[slot, 0, f] = gm.astype(BF16)
                 g_ref[0, f] = (valid * (gm * gate1)).astype(BF16)
                 for n, term in enumerate((two, two * normed, grad * valid * y, gm * branch)):
                     sums[n] += fold_rows(term)
@@ -232,7 +232,7 @@
         ),
         out_shape=[
             jax.ShapeDtypeStruct(tok.shape, BF16),
-            jax.ShapeDtypeStruct((2,) + full, F32),
+            jax.ShapeDtypeStruct((2,) + full, BF16),
             jax.ShapeDtypeStruct(full, BF16),
             jax.ShapeDtypeStruct(full, BF16),
             jax.ShapeDtypeStruct((sz.micro, 4, sz.width), F32),
@@ -252,7 +252,7 @@
             def one(tw, t, f, slot=slot, column=column, g_ref=g_ref):
                 normed, inv = normalize(x_ref[0, tw, column, t].astype(F32))
                 grad = g_ref[0, f].astype(F32)
-                total = gm_ref[slot, 0, f] + norm_back(grad * scale, normed, inv)
+                total = gm_ref[slot, 0, f].astype(F32) + norm_back(grad * scale, normed, inv)
                 out_ref[0, tw, column, t] = total.astype(BF16)
                 sums[0] += fold_rows(grad)
                 sums[1] += fold_rows(grad * normed)

time: 464 us -> 464 us (level)
  no operation moved by 1% of the time
where the time goes in v6:
time: 464 us; the launch traced here: 460 us
  Pallas kernels  259 us (56%)
  starting transfers between devices  75.7 us (16%)
  waiting for transfers between devices  56.7 us (12%)
  local copies, waits for them, and re-layouts  34.8 us (7%)
  between operations  15.6 us (3%)
  other arithmetic  12.1 us (3%)
  matrix products  6.27 us (1%)
    pallas_call x2, Pallas kernels, mlp(): pl.pallas_call(kernel, grid_spec=pltpu.PrefetchScalarGridSpec(num_scalar_...  82.6 us
    pallas_call x1, Pallas kernels, attention_back(): pl.pallas_call(kernel, grid_spec=pltpu.PrefetchScalarGridSpec(num_scalar_...  61.6 us
    ppermute x21, starting transfers between devices, from_z(): lax.ppermute(value, self.AXES, [(n, move(n)) for n in range(self.count)])  49.9 us
    pallas_call x2, Pallas kernels, attention(): pl.pallas_call(kernel, grid_spec=pltpu.PrefetchScalarGridSpec(num_scalar_...  44.6 us
    ppermute x35, waiting for transfers between devices, swap(): lax.ppermute(value, self.AXES, [(n, n ^ which) for n in range(self.count)])  37.4 us
    ppermute x35, starting transfers between devices, swap(): lax.ppermute(value, self.AXES, [(n, n ^ which) for n in range(self.count)])  24.7 us
    pallas_call x5, Pallas kernels, call(): pl.pallas_call(kernel, grid_spec=pltpu.PrefetchScalarGridSpec(num_scalar_...  18.5 us
    ppermute x21, waiting for transfers between devices, from_z(): lax.ppermute(value, self.AXES, [(n, move(n)) for n in range(self.count)])  16.1 us
  transfers between devices with their start and end apart: 63, of which 15 were waited for; matrix products, arithmetic and copies ran while one was open for 8% of the time, Pallas kernels for 56%

profile of v6, /device:TPU:0, one launch (start us, length us, event | category | flops | bytes accessed | tf_op | source)
XLA Modules:
  0.0 459.7 jit_solution(11672581707595630958)
XLA Ops:
  34.1 4.1 collective-permute-done.4
  40.4 3.8 collective-permute-start.5
  74.3 8.8 %collective-permute-done.21.refs_5_ = bf16[2,4,16,1536]{3,2,1,0:T(8,128)(2,1)} collective-permute-done((bf16[2,4,16,1536]{3,2,1,0:T(8,128)(2,1)S(1)}, bf16[2,4,16,1536]{3,2,1,0:T(8,128)(2,1)}, u32[]{:S(2)}, u32[]{:S(2)}) %collective-permute-start.21) | collective-permute-done | bytes 393248 | tf_op jit(solution)/shard_map/ppermute | solution.py:921
  85.4 4.7 %first_norm.1 = (bf16[2,9,32,1024]{3,2,1,0:T(8,128)(2,1)}, bf16[2,9,32,1024]{3,2,1,0:T(8,128)(2,1)}) custom-call(s32[5]{0:T(128)} %compare_select_fusion.7.sc_ref, bf16[2,2,2,5,32,1024]{5,4,3,2,1,0:T(8,128)(2,1)} %bitcast.152, f32[2,6,1024]{2,1,0:T(8,128)} %reshape.409.mod_ref), custom_call_target="tpu_custom_call" | custom-call | tf_op jit(solution)/shard_map/first_norm/pallas_call | solution.py:107
  98.8 20.0 %attention.1 = (bf16[3,1152,1024]{2,1,0:T(8,128)(2,1)}, bf16[1024,3072]{1,0:T(8,128)(2,1)}, bf16[1152,512]{1,0:T(8,128)(2,1)}) custom-call(s32[5]{0:T(128)} %compare_select_fusion.7.sc_ref, bf16[2,9,32,1024]{3,2,1,0:T(8,128)(2,1)} %get-tuple-element.140.own_ref, bf16[2,9,32,1024]{3,2,1,0:T(8,128)(2,1)} %copy-done.50, ...), custom_call_target="tpu_custom_call" | custom-call | flops 13136560128 | bytes 18874368 | tf_op jit(solution)/shard_map/attention/pallas_call | solution.py:546
  120.2 24.6 %attention_last.1 = (bf16[3,1152,1024]{2,1,0:T(8,128)(2,1)}, bf16[1024,3072]{1,0:T(8,128)(2,1)}, bf16[1152,512]{1,0:T(8,128)(2,1)}, bf16[1024,1024]{1,0:T(8,128)...) custom-call(s32[5]{0:T(128)} %compare_select_fusion.7.sc_ref, ...), custom_call_target="tpu_custom_call", output_to_operand_aliasing={{0}: (8, {}), {1}: (9, {})} | custom-call | flops 20384317440 | bytes 18874368 | tf_op jit(solution)/shard_map/attention_last/pallas_call | solution.py:546
  144.8 7.0 %collective-permute-done.30.refs_5_ = bf16[2,4,16,4096]{3,2,1,0:T(8,128)(2,1)} collective-permute-done((bf16[2,4,16,4096]{3,2,1,0:T(8,128)(2,1)S(1)}, bf16[2,4,16,4096]{3,2,1,0:T(8,128)(2,1)}, u32[]{:S(2)}, u32[]{:S(2)}) %collective-permute-start.30) | collective-permute-done | bytes 1048608 | tf_op jit(solution)/shard_map/ppermute | solution.py:921
  157.5 6.7 %second_norm.1 = (bf16[2,2,9,32,1024]{4,3,2,1,0:T(8,128)(2,1)}, bf16[2,2,9,32,1024]{4,3,2,1,0:T(8,128)(2,1)}) custom-call(s32[5]{0:T(128)} %compare_select_fusion.7.sc_ref, bf16[2,2,2,5,32,1024]{5,4,3,2,1,0:T(8,128)(2,1)} %bitcast.153, bf16[2,2,2,5,32,1024]{5,4,3,2,1,0:T(8,128)(2,1)} %bitcast.156, bf16[2,9,32,1024]{3,2,1,0:T(8,128)(2,1)} %get-tuple-element.150.bo_ref, ...), custom_call_target="tpu_custom_call" | custom-call | tf_op jit(solution)/shard_map/second_norm/pallas_call | solution.py:147
  164.2 41.2 %mlp.2 = (f32[1152,1024]{1,0:T(8,128)}, f32[1152,1024]{1,0:T(8,128)}, f32[1,2048]{1,0:T(1,128)}, f32[1,1024]{1,0:T(1,128)}, bf16[1024,4096]{1,0:T(8,128)(2,1)}) custom-call(s32[5]{0:T(128)} %compare_select_fusion.7.sc_ref, bf16[1152,1024]{1,0:T(8,128)(2,1)} %bitcast.216, bf16[1152,1024]{1,0:T(8,128)(2,1)} %bitcast.218, f32[1,2048]{1,0:T(1,128)} %squeeze.65.bu_ref, ...), custom_call_target="tpu_custom_call" | custom-call | flops 33822867456 | bytes 18874368 | tf_op jit(solution)/shard_map/mlp/pallas_call | solution.py:852
  205.5 41.5 %mlp.3 = (f32[1152,1024]{1,0:T(8,128)}, f32[1152,1024]{1,0:T(8,128)}, f32[1,2048]{1,0:T(1,128)}, bf16[16,32,4096]{2,1,0:T(8,128)(2,1)}, bf16[16,32,4096]{2,1,0:T(8,128)(2,1)}) custom-call(s32[5]{0:T(128)} %compare_select_fusion.7.sc_ref, bf16[1152,1024]{1,0:T(8,128)(2,1)} %bitcast.217, bf16[1152,1024]{1,0:T(8,128)(2,1)} %bitcast.219, ...), custom_call_target="tpu_custom_call" | custom-call | flops 33822867456 | bytes 18874368 | tf_op jit(solution)/shard_map/mlp/pallas_call | solution.py:852
  247.7 14.5 %after_mlp.1 = (bf16[2,2,2,5,32,1024]{5,4,3,2,1,0:T(8,128)(2,1)}, bf16[2,2,9,32,1024]{4,3,2,1,0:T(8,128)(2,1)}, bf16[2,9,32,1024]{3,2,1,0:T(8,128)(2,1)}, bf16[2,9,32,1024]{3,2,1,0:T(8,128)(2,1)}, f32[2,4,1024]{2,1,0:T(4,128)}) custom-call(s32[5]{0:T(128)} %compare_select_fusion.7.sc_ref, bf16[2,2,2,5,32,1024]{5,4,3,2,1,0:T(8,128)(2,1)} %bitcast.154, ...), custom_call_target="tpu_custom_call" | custom-call | tf_op jit(solution)/shard_map/after_mlp/pallas_call | solution.py:207
  263.3 7.0 %add_cores.2 = (bf16[4,2,16,4096]{3,2,1,0:T(8,128)(2,1)}, bf16[4,2,16,4096]{3,2,1,0:T(8,128)(2,1)}, bf16[4,2,16,4096]{3,2,1,0:T(8,128)(2,1)}, bf16[4,2,16,4096]{3,2,1,0:T(8,128)(2,1)}) custom-call(s32[3]{0:T(128)} %pad_add_fusion.sc_ref, bf16[4,4,32,4096]{3,2,1,0:T(8,128)(2,1)} %bitcast.168, bf16[4,4,32,4096]{3,2,1,0:T(8,128)(2,1)} %collective-permute-done.36.got), custom_call_target="tpu_custom_call" | custom-call | bytes 12582912 | tf_op jit(solution)/shard_map/add_cores/pallas_call | solution.py:1069
  272.8 61.6 %attention_back.1 = (bf16[16,32,4096]{2,1,0:T(8,128)(2,1)}, bf16[16,32,4096]{2,1,0:T(8,128)(2,1)}, bf16[16,64,576]{2,1,0:T(8,128)(2,1)}, bf16[2,9,32,1024]{3,2,1,0:T(8,128)(2,1)}, bf16[2,9,32,1024]{3,2,1,0:T(8,128)(2,1)}) custom-call(s32[5]{0:T(128)} %compare_select_fusion.7.sc_ref, bf16[2,9,32,1024]{3,2,1,0:T(8,128)(2,1)} %get-tuple-element.176.go_ref, ...), custom_call_target="tpu_custom_call" | custom-call | flops 69306679296 | bytes 28311552 | tf_op jit(solution)/shard_map/attention_back/pallas_call | solution.py:699
  335.9 4.6 add_second.2
  346.9 6.6 %add_cores.3 = (bf16[4,2,16,4096]{3,2,1,0:T(8,128)(2,1)}, bf16[4,2,16,4096]{3,2,1,0:T(8,128)(2,1)}, bf16[4,2,16,4096]{3,2,1,0:T(8,128)(2,1)}, bf16[4,2,16,4096]{3,2,1,0:T(8,128)(2,1)}) custom-call(s32[3]{0:T(128)} %pad_add_fusion.sc_ref, bf16[4,4,32,4096]{3,2,1,0:T(8,128)(2,1)} %bitcast.167, bf16[4,4,32,4096]{3,2,1,0:T(8,128)(2,1)} %collective-permute-done.41.got), custom_call_target="tpu_custom_call" | custom-call | bytes 12582912 | tf_op jit(solution)/shard_map/add_cores/pallas_call | solution.py:1069
  354.9 7.5 %last_norm.1 = (bf16[2,2,2,5,32,1024]{5,4,3,2,1,0:T(8,128)(2,1)}, f32[2,2,1024]{2,1,0:T(2,128)}) custom-call(s32[5]{0:T(128)} %compare_select_fusion.7.sc_ref, bf16[2,2,2,5,32,1024]{5,4,3,2,1,0:T(8,128)(2,1)} %bitcast.155, bf16[2,2,2,5,32,1024]{5,4,3,2,1,0:T(8,128)(2,1)} %bitcast.158, bf16[2,2,9,32,1024]{4,3,2,1,0:T(8,128)(2,1)} %get-tuple-element.169.gm_ref, ...), custom_call_target="tpu_custom_call" | custom-call | tf_op jit(solution)/shard_map/last_norm/pallas_call | solution.py:270
  366.7 9.9 %collective-permute-start.44 = (bf16[32,4096]{1,0:T(8,128)(2,1)}, bf16[32,4096]{1,0:T(8,128)(2,1)}, u32[]{:S(2)}, u32[]{:S(2)}) collective-permute-start(bf16[32,4096]{1,0:T(8,128)(2,1)} %get-tuple-element.214), channel_id=1, source_target_pairs={{0,24},{1,25},{2,26},{3,27},{4,28},{5,29},{6,30},{7,31},{8,0},{9,1... | collective-permute-start | bytes 786440 | tf_op jit(solution)/shard_map/ppermute | solution.py:925
  379.9 4.3 copy.214
  389.4 4.6 add_second.3
  396.0 4.6 %collective-permute-done.45 = bf16[32,4096]{1,0:T(8,128)(2,1)} collective-permute-done((bf16[32,4096]{1,0:T(8,128)(2,1)}, bf16[32,4096]{1,0:T(8,128)(2,1)}, u32[]{:S(2)}, u32[]{:S(2)}) %collective-permute-start.45) | collective-permute-done | bytes 262176 | tf_op jit(solution)/shard_map/ppermute | solution.py:925
  420.0 4.5 collective-permute-done.54.g0
  424.6 3.6 collective-permute-start.55
  428.1 8.7 %collective-permute-start.56 = (bf16[27904]{0:T(1024)(128)(2,1)S(1)}, bf16[27904]{0:T(1024)(128)(2,1)S(1)}, u32[]{:S(2)}, u32[]{:S(2)}) collective-permute-start(bf16[27904]{0:T(1024)(128)(2,1)S(1)} %get-tuple-element.235), channel_id=1, source_target_pairs={{0,16},{1,17},{2,18},{3,19},{4,20},{5,21},{6,22},{7,23},{8,24},{9,... | collective-permute-start | bytes 167432 | tf_op jit(solution)/shard_map/ppermute | solution.py:925
  437.1 6.9 %collective-permute-done.58.g1 = bf16[32,4096]{1,0:T(8,128)(2,1)S(1)} collective-permute-done((bf16[32,4096]{1,0:T(8,128)(2,1)}, bf16[32,4096]{1,0:T(8,128)(2,1)S(1)}, u32[]{:S(2)}, u32[]{:S(2)}) %collective-permute-start.58) | collective-permute-done | bytes 262176 | tf_op jit(solution)/shard_map/ppermute | solution.py:925
  (401 shorter events, 132.8 us)
Async XLA Ops:
  7.3 112.9 %all-gather.3.cloned.1.call-start = ((), (), s32[]{:S(2)}) async-start(), calls=%async_computation.1 | async-start | bytes 5406720 | tf_op jit(solution)/shard_map/all_gather | solution.py:1240
  9.8 195.7 %all-gather.5.cloned.1.call-start = ((), (), s32[]{:S(2)}) async-start(), calls=%async_computation.2 | async-start | bytes 8650752 | tf_op jit(solution)/shard_map/all_gather | solution.py:1240
  17.1 23.3 %collective-permute-start.17 = (bf16[32,1536]{1,0:T(8,128)(2,1)S(1)}, bf16[32,1536]{1,0:T(8,128)(2,1)S(1)}, u32[]{:S(2)}, u32[]{:S(2)}) collective-permute-start(bf16[32,1536]{1,0:T(8,128)(2,1)S(1)} %bitcast.194), channel_id=1, source_target_pairs={{0,8},{1,9},{2,10},{3,11},{4,12},{5,13},{6,14},{7,15},{8,16},{9,17... | collective-permute-start | bytes 294920 | tf_op jit(solution)/shard_map/ppermute | solution.py:925
  17.8 26.4 %collective-permute-start.16 = (bf16[32,1536]{1,0:T(8,128)(2,1)S(1)}, bf16[32,1536]{1,0:T(8,128)(2,1)S(1)}, u32[]{:S(2)}, u32[]{:S(2)}) collective-permute-start(bf16[32,1536]{1,0:T(8,128)(2,1)S(1)} %bitcast.195), channel_id=1, source_target_pairs={{0,16},{1,17},{2,18},{3,19},{4,20},{5,21},{6,22},{7,23},{8,24},{9,... | collective-permute-start | bytes 294920 | tf_op jit(solution)/shard_map/ppermute | solution.py:925
  20.6 341.9 %reduce-scatter.2.cloned.1.call-start = ((), (), s32[]{:S(2)}) async-start(), calls=%async_computation.3 | async-start | bytes 8650752 | tf_op jit(solution)/shard_map/reduce_scatter | solution.py:1312
  50.4 21.8 %collective-permute-start.14 = (bf16[32,4096]{1,0:T(8,128)(2,1)S(1)}, bf16[32,4096]{1,0:T(8,128)(2,1)S(1)}, u32[]{:S(2)}, u32[]{:S(2)}) collective-permute-start(bf16[32,4096]{1,0:T(8,128)(2,1)S(1)} %copy.212.refs_0_), channel_id=1, source_target_pairs={{0,8},{1,9},{2,10},{3,11},{4,12},{5,13},{6,14},{7,15},{8,16},{9,17... | collective-permute-start | bytes 786440 | tf_op jit(solution)/shard_map/ppermute | solution.py:925
  50.4 21.8 %collective-permute-start.13 = (bf16[32,4096]{1,0:T(8,128)(2,1)S(1)}, bf16[32,4096]{1,0:T(8,128)(2,1)S(1)}, u32[]{:S(2)}, u32[]{:S(2)}) collective-permute-start(bf16[32,4096]{1,0:T(8,128)(2,1)S(1)} %copy.212.refs_0_), channel_id=1, source_target_pairs={{0,16},{1,17},{2,18},{3,19},{4,20},{5,21},{6,22},{7,23},{8,24},{9,... | collective-permute-start | bytes 786440 | tf_op jit(solution)/shard_map/ppermute | solution.py:925
  94.3 24.6 %collective-permute-start.27 = (bf16[4,16,4096]{2,1,0:T(8,128)(2,1)S(1)}, bf16[4,16,4096]{2,1,0:T(8,128)(2,1)S(1)}, u32[]{:S(2)}, u32[]{:S(2)}) collective-permute-start(bf16[4,16,4096]{2,1,0:T(8,128)(2,1)S(1)} %copy-done.12), channel_id=1, source_target_pairs={{0,2},{1,3},{2,0},{3,1},{4,6},{5,7},{6,4},{7,5},{8,10},{9,11},{10,... | collective-permute-start | bytes 1572872 | tf_op jit(solution)/shard_map/ppermute | solution.py:921
  96.0 22.9 %collective-permute-start.28 = (bf16[4,16,4096]{2,1,0:T(8,128)(2,1)S(1)}, bf16[4,16,4096]{2,1,0:T(8,128)(2,1)S(1)}, u32[]{:S(2)}, u32[]{:S(2)}) collective-permute-start(bf16[4,16,4096]{2,1,0:T(8,128)(2,1)S(1)} %copy-done.13), channel_id=1, source_target_pairs={{0,4},{1,5},{2,6},{3,7},{4,0},{5,1},{6,2},{7,3},{8,12},{9,13},{10,... | collective-permute-start | bytes 1572872 | tf_op jit(solution)/shard_map/ppermute | solution.py:921
  119.0 32.8 %collective-permute-start.30 = (bf16[2,4,16,4096]{3,2,1,0:T(8,128)(2,1)S(1)}, bf16[2,4,16,4096]{3,2,1,0:T(8,128)(2,1)}, u32[]{:S(2)}, u32[]{:S(2)}) collective-permute-start(bf16[2,4,16,4096]{3,2,1,0:T(8,128)(2,1)S(1)} %pad_maximum_fusion.2.refs_4_), channel_id=1, source_target_pairs={{0,2},{1,3},{2,0},{3,1},{4,6},{5,7},{6,4},{7,5},{8,10},{9,11},{10,... | collective-permute-start | bytes 3145736 | tf_op jit(solution)/shard_map/ppermute | solution.py:921
  119.7 32.1 %collective-permute-start.29 = (bf16[2,4,16,4096]{3,2,1,0:T(8,128)(2,1)S(1)}, bf16[2,4,16,4096]{3,2,1,0:T(8,128)(2,1)}, u32[]{:S(2)}, u32[]{:S(2)}) collective-permute-start(bf16[2,4,16,4096]{3,2,1,0:T(8,128)(2,1)S(1)} %pad_maximum_fusion.1.refs_0_), channel_id=1, source_target_pairs={{0,4},{1,5},{2,6},{3,7},{4,0},{5,1},{6,2},{7,3},{8,12},{9,13},{10,... | collective-permute-start | bytes 3145736 | tf_op jit(solution)/shard_map/ppermute | solution.py:921
  270.4 64.2 %collective-permute-start.38 = (bf16[4,2,16,4096]{3,2,1,0:T(8,128)(2,1)}, bf16[4,2,16,4096]{3,2,1,0:T(8,128)(2,1)S(1)}, u32[]{:S(2)}, u32[]{:S(2)}) collective-permute-start(bf16[4,2,16,4096]{3,2,1,0:T(8,128)(2,1)} %get-tuple-element.184), channel_id=1, source_target_pairs={{0,4},{1,5},{2,6},{3,7},{4,0},{5,1},{6,2},{7,3},{8,12},{9,13},{10,... | collective-permute-start | bytes 3145736 | tf_op jit(solution)/shard_map/ppermute | solution.py:921
  270.9 63.7 %collective-permute-start.39 = (bf16[4,2,16,4096]{3,2,1,0:T(8,128)(2,1)}, bf16[4,2,16,4096]{3,2,1,0:T(8,128)(2,1)S(1)}, u32[]{:S(2)}, u32[]{:S(2)}) collective-permute-start(bf16[4,2,16,4096]{3,2,1,0:T(8,128)(2,1)} %get-tuple-element.185), channel_id=1, source_target_pairs={{0,2},{1,3},{2,0},{3,1},{4,6},{5,7},{6,4},{7,5},{8,10},{9,11},{10,... | collective-permute-start | bytes 3145736 | tf_op jit(solution)/shard_map/ppermute | solution.py:921
  340.4 22.0 %collective-permute-start.42 = (bf16[4,16,4096]{2,1,0:T(8,128)(2,1)}, bf16[4,16,4096]{2,1,0:T(8,128)(2,1)S(1)}, u32[]{:S(2)}, u32[]{:S(2)}) collective-permute-start(bf16[4,16,4096]{2,1,0:T(8,128)(2,1)} %get-tuple-element.202), channel_id=1, source_target_pairs={{0,2},{1,3},{2,0},{3,1},{4,6},{5,7},{6,4},{7,5},{8,10},{9,11},{10,... | collective-permute-start | bytes 1572872 | tf_op jit(solution)/shard_map/ppermute | solution.py:921
  341.6 20.9 %collective-permute-start.43 = (bf16[4,16,4096]{2,1,0:T(8,128)(2,1)}, bf16[4,16,4096]{2,1,0:T(8,128)(2,1)S(1)}, u32[]{:S(2)}, u32[]{:S(2)}) collective-permute-start(bf16[4,16,4096]{2,1,0:T(8,128)(2,1)} %get-tuple-element.203), channel_id=1, source_target_pairs={{0,4},{1,5},{2,6},{3,7},{4,0},{5,1},{6,2},{7,3},{8,12},{9,13},{10,... | collective-permute-start | bytes 1572872 | tf_op jit(solution)/shard_map/ppermute | solution.py:921
  353.5 35.9 %collective-permute-start.47 = (bf16[4,2,16,4096]{3,2,1,0:T(8,128)(2,1)}, bf16[4,2,16,4096]{3,2,1,0:T(8,128)(2,1)}, u32[]{:S(2)}, u32[]{:S(2)}) collective-permute-start(bf16[4,2,16,4096]{3,2,1,0:T(8,128)(2,1)} %get-tuple-element.217), channel_id=1, source_target_pairs={{0,4},{1,5},{2,6},{3,7},{4,0},{5,1},{6,2},{7,3},{8,12},{9,13},{10,... | collective-permute-start | bytes 3145736 | tf_op jit(solution)/shard_map/ppermute | solution.py:921
  354.0 35.3 %collective-permute-start.48 = (bf16[4,2,16,4096]{3,2,1,0:T(8,128)(2,1)}, bf16[4,2,16,4096]{3,2,1,0:T(8,128)(2,1)}, u32[]{:S(2)}, u32[]{:S(2)}) collective-permute-start(bf16[4,2,16,4096]{3,2,1,0:T(8,128)(2,1)} %get-tuple-element.218), channel_id=1, source_target_pairs={{0,2},{1,3},{2,0},{3,1},{4,6},{5,7},{6,4},{7,5},{8,10},{9,11},{10,... | collective-permute-start | bytes 3145736 | tf_op jit(solution)/shard_map/ppermute | solution.py:921
  366.7 29.3 %collective-permute-start.44 = (bf16[32,4096]{1,0:T(8,128)(2,1)}, bf16[32,4096]{1,0:T(8,128)(2,1)}, u32[]{:S(2)}, u32[]{:S(2)}) collective-permute-start(bf16[32,4096]{1,0:T(8,128)(2,1)} %get-tuple-element.214), channel_id=1, source_target_pairs={{0,24},{1,25},{2,26},{3,27},{4,28},{5,29},{6,30},{7,31},{8,0},{9,1... | collective-permute-start | bytes 786440 | tf_op jit(solution)/shard_map/ppermute | solution.py:925
  376.6 24.1 %collective-permute-start.45 = (bf16[32,4096]{1,0:T(8,128)(2,1)}, bf16[32,4096]{1,0:T(8,128)(2,1)}, u32[]{:S(2)}, u32[]{:S(2)}) collective-permute-start(bf16[32,4096]{1,0:T(8,128)(2,1)} %get-tuple-element.215), channel_id=1, source_target_pairs={{0,16},{1,17},{2,18},{3,19},{4,20},{5,21},{6,22},{7,23},{8,24},{9,... | collective-permute-start | bytes 786440 | tf_op jit(solution)/shard_map/ppermute | solution.py:925
  377.8 22.8 %collective-permute-start.46 = (bf16[32,4096]{1,0:T(8,128)(2,1)}, bf16[32,4096]{1,0:T(8,128)(2,1)}, u32[]{:S(2)}, u32[]{:S(2)}) collective-permute-start(bf16[32,4096]{1,0:T(8,128)(2,1)} %get-tuple-element.216), channel_id=1, source_target_pairs={{0,8},{1,9},{2,10},{3,11},{4,12},{5,13},{6,14},{7,15},{8,16},{9,17... | collective-permute-start | bytes 786440 | tf_op jit(solution)/shard_map/ppermute | solution.py:925
  416.8 27.2 %collective-permute-start.58 = (bf16[32,4096]{1,0:T(8,128)(2,1)}, bf16[32,4096]{1,0:T(8,128)(2,1)S(1)}, u32[]{:S(2)}, u32[]{:S(2)}) collective-permute-start(bf16[32,4096]{1,0:T(8,128)(2,1)} %get-tuple-element.237), channel_id=1, source_target_pairs={{0,16},{1,17},{2,18},{3,19},{4,20},{5,21},{6,22},{7,23},{8,24},{9,... | collective-permute-start | bytes 786440 | tf_op jit(solution)/shard_map/ppermute | solution.py:925
  417.8 26.2 %collective-permute-start.59 = (bf16[32,4096]{1,0:T(8,128)(2,1)}, bf16[32,4096]{1,0:T(8,128)(2,1)S(1)}, u32[]{:S(2)}, u32[]{:S(2)}) collective-permute-start(bf16[32,4096]{1,0:T(8,128)(2,1)} %get-tuple-element.238), channel_id=1, source_target_pairs={{0,8},{1,9},{2,10},{3,11},{4,12},{5,13},{6,14},{7,15},{8,16},{9,17... | collective-permute-start | bytes 786440 | tf_op jit(solution)/shard_map/ppermute | solution.py:925
  424.6 23.6 %collective-permute-start.55 = (bf16[27904]{0:T(1024)(128)(2,1)S(1)}, bf16[27904]{0:T(1024)(128)(2,1)S(1)}, u32[]{:S(2)}, u32[]{:S(2)}) collective-permute-start(bf16[27904]{0:T(1024)(128)(2,1)S(1)} %get-tuple-element.234), channel_id=1, source_target_pairs={{0,24},{1,25},{2,26},{3,27},{4,28},{5,29},{6,30},{7,31},{8,0},{9,1... | collective-permute-start | bytes 167432 | tf_op jit(solution)/shard_map/ppermute | solution.py:925
  428.1 20.0 %collective-permute-start.56 = (bf16[27904]{0:T(1024)(128)(2,1)S(1)}, bf16[27904]{0:T(1024)(128)(2,1)S(1)}, u32[]{:S(2)}, u32[]{:S(2)}) collective-permute-start(bf16[27904]{0:T(1024)(128)(2,1)S(1)} %get-tuple-element.235), channel_id=1, source_target_pairs={{0,16},{1,17},{2,18},{3,19},{4,20},{5,21},{6,22},{7,23},{8,24},{9,... | collective-permute-start | bytes 167432 | tf_op jit(solution)/shard_map/ppermute | solution.py:925
  (97 other events, 868.2 us)
Sparse Core Ops, SparseCore 0:
  11.0 85.6 all-gather.2
  99.5 83.5 all-gather.4
  205.6 156.2 reduce-scatter.1

commit v7 on v6

--- a/solution.py
+++ b/solution.py
@@ -886,11 +886,6 @@
     return blocks.reshape(HEADS, -1, sz.frame, sz.frame)
 
 
-def split_low(value):
-    high = value.astype(BF16)
-    return high, (value - high.astype(F32)).astype(BF16)
-
-
 def offset_grad(fold, places, sz):
     steps = 2 * sz.frames - 1
     fold = fold.reshape(-1, sz.frame, steps, sz.frame)
@@ -900,7 +895,7 @@
 
 def table_grad(by_offset, bucket, buckets):
     onehot = bucket_onehot(bucket, buckets)
-    return sum(dot_nt(onehot, part) for part in split_low(by_offset))
+    return dot_nt(onehot, by_offset.astype(BF16))
 
 
 class Net:

time: 464 us -> 466 us (level)
  Pallas kernels: 259 us -> 247 us
  starting transfers between devices: 75.7 us -> 85 us
    ppermute x35, starting transfers between devices: 24.7 us -> 35.6 us  [swap(): lax.ppermute(value, self.AXES, [(n, n ^ which) for n in range(self.count)])]
    pallas_call x1, Pallas kernels: 61.6 us -> 54.6 us  [attention_back(): pl.pallas_call(kernel, grid_spec=pltpu.PrefetchScalarGridSpec(num_scalar_...]
    unnamed x127 -> x123, local copies, waits for them, and re-layouts: 10.3 us -> 12.9 us
  transfers between devices with their start and end apart: 63 -> 63, of which waited for: 15 -> 16; matrix products, arithmetic and copies ran while one was open for 8% -> 8% of each run, Pallas kernels for 56% -> 53%
where the time goes in v7:
time: 466 us; the launch traced here: 464 us
  Pallas kernels  247 us (53%)
  starting transfers between devices  85 us (18%)
  waiting for transfers between devices  60.5 us (13%)
  local copies, waits for them, and re-layouts  37.3 us (8%)
  between operations  15.6 us (3%)
  other arithmetic  12.9 us (3%)
  matrix products  5.43 us (1%)
    pallas_call x2, Pallas kernels, mlp(): pl.pallas_call(kernel, grid_spec=pltpu.PrefetchScalarGridSpec(num_scalar_...  82.8 us
    pallas_call x1, Pallas kernels, attention_back(): pl.pallas_call(kernel, grid_spec=pltpu.PrefetchScalarGridSpec(num_scalar_...  54.6 us
    ppermute x21, starting transfers between devices, from_z(): lax.ppermute(value, self.AXES, [(n, move(n)) for n in range(self.count)])  48.4 us
    pallas_call x2, Pallas kernels, attention(): pl.pallas_call(kernel, grid_spec=pltpu.PrefetchScalarGridSpec(num_scalar_...  40.3 us
    ppermute x35, waiting for transfers between devices, swap(): lax.ppermute(value, self.AXES, [(n, n ^ which) for n in range(self.count)])  38.3 us
    ppermute x35, starting transfers between devices, swap(): lax.ppermute(value, self.AXES, [(n, n ^ which) for n in range(self.count)])  35.6 us
    ppermute x21, waiting for transfers between devices, from_z(): lax.ppermute(value, self.AXES, [(n, move(n)) for n in range(self.count)])  19.1 us
    pallas_call x5, Pallas kernels, call(): pl.pallas_call(kernel, grid_spec=pltpu.PrefetchScalarGridSpec(num_scalar_...  18.5 us
  transfers between devices with their start and end apart: 63, of which 16 were waited for; matrix products, arithmetic and copies ran while one was open for 8% of the time, Pallas kernels for 53%

profile of v7, /device:TPU:0, one launch (start us, length us, event | category | flops | bytes accessed | tf_op | source)
XLA Modules:
  0.0 464.1 jit_solution(16904588048031519446)
XLA Ops:
  34.1 4.1 collective-permute-done.4
  40.4 3.8 collective-permute-start.5
  74.5 8.8 %collective-permute-done.21.refs_5_ = bf16[2,4,16,1536]{3,2,1,0:T(8,128)(2,1)} collective-permute-done((bf16[2,4,16,1536]{3,2,1,0:T(8,128)(2,1)S(1)}, bf16[2,4,16,1536]{3,2,1,0:T(8,128)(2,1)}, u32[]{:S(2)}, u32[]{:S(2)}) %collective-permute-start.21) | collective-permute-done | bytes 393248 | tf_op jit(solution)/shard_map/ppermute | solution.py:916
  85.6 4.7 %first_norm.1 = (bf16[2,9,32,1024]{3,2,1,0:T(8,128)(2,1)}, bf16[2,9,32,1024]{3,2,1,0:T(8,128)(2,1)}) custom-call(s32[5]{0:T(128)} %compare_select_fusion.7.sc_ref, bf16[2,2,2,5,32,1024]{5,4,3,2,1,0:T(8,128)(2,1)} %bitcast.157, f32[2,6,1024]{2,1,0:T(8,128)} %reshape.408.mod_ref), custom_call_target="tpu_custom_call" | custom-call | tf_op jit(solution)/shard_map/first_norm/pallas_call | solution.py:107
  98.5 17.8 %attention.1 = (bf16[3,1152,1024]{2,1,0:T(8,128)(2,1)}, bf16[1024,3072]{1,0:T(8,128)(2,1)}, bf16[1152,512]{1,0:T(8,128)(2,1)}) custom-call(s32[5]{0:T(128)} %compare_select_fusion.7.sc_ref, bf16[2,9,32,1024]{3,2,1,0:T(8,128)(2,1)} %get-tuple-element.140.own_ref, bf16[2,9,32,1024]{3,2,1,0:T(8,128)(2,1)} %copy-done.48, ...), custom_call_target="tpu_custom_call" | custom-call | flops 13136560128 | bytes 18874368 | tf_op jit(solution)/shard_map/attention/pallas_call | solution.py:546
  120.5 22.6 %attention_last.1 = (bf16[3,1152,1024]{2,1,0:T(8,128)(2,1)}, bf16[1024,3072]{1,0:T(8,128)(2,1)}, bf16[1152,512]{1,0:T(8,128)(2,1)}, bf16[1024,1024]{1,0:T(8,128)...) custom-call(s32[5]{0:T(128)} %compare_select_fusion.7.sc_ref, ...), custom_call_target="tpu_custom_call", output_to_operand_aliasing={{0}: (8, {}), {1}: (9, {})} | custom-call | flops 20384317440 | bytes 18874368 | tf_op jit(solution)/shard_map/attention_last/pallas_call | solution.py:546
  143.0 6.1 %collective-permute-done.30.refs_5_ = bf16[2,4,16,4096]{3,2,1,0:T(8,128)(2,1)} collective-permute-done((bf16[2,4,16,4096]{3,2,1,0:T(8,128)(2,1)S(1)}, bf16[2,4,16,4096]{3,2,1,0:T(8,128)(2,1)}, u32[]{:S(2)}, u32[]{:S(2)}) %collective-permute-start.30) | collective-permute-done | bytes 1048608 | tf_op jit(solution)/shard_map/ppermute | solution.py:916
  154.9 6.7 %second_norm.1 = (bf16[2,2,9,32,1024]{4,3,2,1,0:T(8,128)(2,1)}, bf16[2,2,9,32,1024]{4,3,2,1,0:T(8,128)(2,1)}) custom-call(s32[5]{0:T(128)} %compare_select_fusion.7.sc_ref, bf16[2,2,2,5,32,1024]{5,4,3,2,1,0:T(8,128)(2,1)} %bitcast.158, bf16[2,2,2,5,32,1024]{5,4,3,2,1,0:T(8,128)(2,1)} %bitcast.161, bf16[2,9,32,1024]{3,2,1,0:T(8,128)(2,1)} %get-tuple-element.150.bo_ref, ...), custom_call_target="tpu_custom_call" | custom-call | tf_op jit(solution)/shard_map/second_norm/pallas_call | solution.py:147
  162.4 41.3 %mlp.2 = (f32[1152,1024]{1,0:T(8,128)}, f32[1152,1024]{1,0:T(8,128)}, f32[1,2048]{1,0:T(1,128)}, f32[1,1024]{1,0:T(1,128)}, bf16[1024,4096]{1,0:T(8,128)(2,1)}) custom-call(s32[5]{0:T(128)} %compare_select_fusion.7.sc_ref, bf16[1152,1024]{1,0:T(8,128)(2,1)} %bitcast.221, bf16[1152,1024]{1,0:T(8,128)(2,1)} %bitcast.223, f32[1,2048]{1,0:T(1,128)} %squeeze.65.bu_ref, ...), custom_call_target="tpu_custom_call" | custom-call | flops 33822867456 | bytes 18874368 | tf_op jit(solution)/shard_map/mlp/pallas_call | solution.py:852
  203.9 41.5 %mlp.3 = (f32[1152,1024]{1,0:T(8,128)}, f32[1152,1024]{1,0:T(8,128)}, f32[1,2048]{1,0:T(1,128)}, bf16[16,32,4096]{2,1,0:T(8,128)(2,1)}, bf16[16,32,4096]{2,1,0:T(8,128)(2,1)}) custom-call(s32[5]{0:T(128)} %compare_select_fusion.7.sc_ref, bf16[1152,1024]{1,0:T(8,128)(2,1)} %bitcast.222, bf16[1152,1024]{1,0:T(8,128)(2,1)} %bitcast.224, ...), custom_call_target="tpu_custom_call" | custom-call | flops 33822867456 | bytes 18874368 | tf_op jit(solution)/shard_map/mlp/pallas_call | solution.py:852
  246.1 14.6 %after_mlp.1 = (bf16[2,2,2,5,32,1024]{5,4,3,2,1,0:T(8,128)(2,1)}, bf16[2,2,9,32,1024]{4,3,2,1,0:T(8,128)(2,1)}, bf16[2,9,32,1024]{3,2,1,0:T(8,128)(2,1)}, bf16[2,9,32,1024]{3,2,1,0:T(8,128)(2,1)}, f32[2,4,1024]{2,1,0:T(4,128)}) custom-call(s32[5]{0:T(128)} %compare_select_fusion.7.sc_ref, bf16[2,2,2,5,32,1024]{5,4,3,2,1,0:T(8,128)(2,1)} %bitcast.159, ...), custom_call_target="tpu_custom_call" | custom-call | tf_op jit(solution)/shard_map/after_mlp/pallas_call | solution.py:207
  261.8 6.9 %add_cores.2 = (bf16[4,2,16,4096]{3,2,1,0:T(8,128)(2,1)}, bf16[4,2,16,4096]{3,2,1,0:T(8,128)(2,1)}, bf16[4,2,16,4096]{3,2,1,0:T(8,128)(2,1)}, bf16[4,2,16,4096]{3,2,1,0:T(8,128)(2,1)}) custom-call(s32[3]{0:T(128)} %pad_add_fusion.sc_ref, bf16[4,4,32,4096]{3,2,1,0:T(8,128)(2,1)} %bitcast.172, bf16[4,4,32,4096]{3,2,1,0:T(8,128)(2,1)} %collective-permute-done.36.got), custom_call_target="tpu_custom_call" | custom-call | bytes 12582912 | tf_op jit(solution)/shard_map/add_cores/pallas_call | solution.py:1064
  272.9 54.6 %attention_back.1 = (bf16[16,32,4096]{2,1,0:T(8,128)(2,1)}, bf16[16,32,4096]{2,1,0:T(8,128)(2,1)}, bf16[16,64,576]{2,1,0:T(8,128)(2,1)}, bf16[2,9,32,1024]{3,2,1,0:T(8,128)(2,1)}, bf16[2,9,32,1024]{3,2,1,0:T(8,128)(2,1)}) custom-call(s32[5]{0:T(128)} %compare_select_fusion.7.sc_ref, bf16[2,9,32,1024]{3,2,1,0:T(8,128)(2,1)} %get-tuple-element.176.go_ref, ...), custom_call_target="tpu_custom_call" | custom-call | flops 69306679296 | bytes 28311552 | tf_op jit(solution)/shard_map/attention_back/pallas_call | solution.py:699
  329.4 4.6 add_second.2
  335.5 7.4 %collective-permute-start.43 = (bf16[4,16,4096]{2,1,0:T(8,128)(2,1)}, bf16[4,16,4096]{2,1,0:T(8,128)(2,1)}, u32[]{:S(2)}, u32[]{:S(2)}) collective-permute-start(bf16[4,16,4096]{2,1,0:T(8,128)(2,1)} %get-tuple-element.203), channel_id=1, source_target_pairs={{0,4},{1,5},{2,6},{3,7},{4,0},{5,1},{6,2},{7,3},{8,12},{9,13},{10,... | collective-permute-start | bytes 1572872 | tf_op jit(solution)/shard_map/ppermute | solution.py:916
  344.9 6.8 %add_cores.3 = (bf16[4,2,16,4096]{3,2,1,0:T(8,128)(2,1)}, bf16[4,2,16,4096]{3,2,1,0:T(8,128)(2,1)}, bf16[4,2,16,4096]{3,2,1,0:T(8,128)(2,1)}, bf16[4,2,16,4096]{3,2,1,0:T(8,128)(2,1)}) custom-call(s32[3]{0:T(128)} %pad_add_fusion.sc_ref, bf16[4,4,32,4096]{3,2,1,0:T(8,128)(2,1)} %bitcast.173, bf16[4,4,32,4096]{3,2,1,0:T(8,128)(2,1)} %copy-done.3), custom_call_target="tpu_custom_call" | custom-call | bytes 12582912 | tf_op jit(solution)/shard_map/add_cores/pallas_call | solution.py:1064
  358.8 7.6 %last_norm.1 = (bf16[2,2,2,5,32,1024]{5,4,3,2,1,0:T(8,128)(2,1)}, f32[2,2,1024]{2,1,0:T(2,128)}) custom-call(s32[5]{0:T(128)} %compare_select_fusion.7.sc_ref, bf16[2,2,2,5,32,1024]{5,4,3,2,1,0:T(8,128)(2,1)} %bitcast.160, bf16[2,2,2,5,32,1024]{5,4,3,2,1,0:T(8,128)(2,1)} %bitcast.163, bf16[2,2,9,32,1024]{4,3,2,1,0:T(8,128)(2,1)} %get-tuple-element.169.gm_ref, ...), custom_call_target="tpu_custom_call" | custom-call | tf_op jit(solution)/shard_map/last_norm/pallas_call | solution.py:270
  369.7 11.0 %collective-permute-start.44 = (bf16[32,4096]{1,0:T(8,128)(2,1)}, bf16[32,4096]{1,0:T(8,128)(2,1)S(1)}, u32[]{:S(2)}, u32[]{:S(2)}) collective-permute-start(bf16[32,4096]{1,0:T(8,128)(2,1)} %get-tuple-element.214), channel_id=1, source_target_pairs={{0,24},{1,25},{2,26},{3,27},{4,28},{5,29},{6,30},{7,31},{8,0},{9,1... | collective-permute-start | bytes 786440 | tf_op jit(solution)/shard_map/ppermute | solution.py:920
  383.6 4.3 copy.215
  392.1 4.6 add_second.3
  398.7 6.4 %collective-permute-done.45 = bf16[32,4096]{1,0:T(8,128)(2,1)} collective-permute-done((bf16[32,4096]{1,0:T(8,128)(2,1)}, bf16[32,4096]{1,0:T(8,128)(2,1)}, u32[]{:S(2)}, u32[]{:S(2)}) %collective-permute-start.45) | collective-permute-done | bytes 262176 | tf_op jit(solution)/shard_map/ppermute | solution.py:920
  424.6 5.7 %collective-permute-done.54.g0 = bf16[32,4096]{1,0:T(8,128)(2,1)S(1)} collective-permute-done((bf16[32,4096]{1,0:T(8,128)(2,1)}, bf16[32,4096]{1,0:T(8,128)(2,1)S(1)}, u32[]{:S(2)}, u32[]{:S(2)}) %collective-permute-start.54) | collective-permute-done | bytes 262176 | tf_op jit(solution)/shard_map/ppermute | solution.py:920
  433.0 8.3 %collective-permute-start.56 = (bf16[27904]{0:T(1024)(128)(2,1)S(1)}, bf16[27904]{0:T(1024)(128)(2,1)S(1)}, u32[]{:S(2)}, u32[]{:S(2)}) collective-permute-start(bf16[27904]{0:T(1024)(128)(2,1)S(1)} %get-tuple-element.235), channel_id=1, source_target_pairs={{0,16},{1,17},{2,18},{3,19},{4,20},{5,21},{6,22},{7,23},{8,24},{9,... | collective-permute-start | bytes 167432 | tf_op jit(solution)/shard_map/ppermute | solution.py:920
  441.5 6.9 %collective-permute-done.58.g1 = bf16[32,4096]{1,0:T(8,128)(2,1)S(1)} collective-permute-done((bf16[32,4096]{1,0:T(8,128)(2,1)}, bf16[32,4096]{1,0:T(8,128)(2,1)S(1)}, u32[]{:S(2)}, u32[]{:S(2)}) %collective-permute-start.58) | collective-permute-done | bytes 262176 | tf_op jit(solution)/shard_map/ppermute | solution.py:920
  (395 shorter events, 141.7 us)
Async XLA Ops:
  7.3 113.2 %all-gather.3.cloned.1.call-start = ((), (), s32[]{:S(2)}) async-start(), calls=%async_computation.1 | async-start | bytes 5406720 | tf_op jit(solution)/shard_map/all_gather | solution.py:1235
  9.8 194.1 %all-gather.5.cloned.1.call-start = ((), (), s32[]{:S(2)}) async-start(), calls=%async_computation.2 | async-start | bytes 8650752 | tf_op jit(solution)/shard_map/all_gather | solution.py:1235
  17.1 23.3 %collective-permute-start.17 = (bf16[32,1536]{1,0:T(8,128)(2,1)S(1)}, bf16[32,1536]{1,0:T(8,128)(2,1)S(1)}, u32[]{:S(2)}, u32[]{:S(2)}) collective-permute-start(bf16[32,1536]{1,0:T(8,128)(2,1)S(1)} %bitcast.199), channel_id=1, source_target_pairs={{0,8},{1,9},{2,10},{3,11},{4,12},{5,13},{6,14},{7,15},{8,16},{9,17... | collective-permute-start | bytes 294920 | tf_op jit(solution)/shard_map/ppermute | solution.py:920
  17.8 26.5 %collective-permute-start.16 = (bf16[32,1536]{1,0:T(8,128)(2,1)S(1)}, bf16[32,1536]{1,0:T(8,128)(2,1)S(1)}, u32[]{:S(2)}, u32[]{:S(2)}) collective-permute-start(bf16[32,1536]{1,0:T(8,128)(2,1)S(1)} %bitcast.200), channel_id=1, source_target_pairs={{0,16},{1,17},{2,18},{3,19},{4,20},{5,21},{6,22},{7,23},{8,24},{9,... | collective-permute-start | bytes 294920 | tf_op jit(solution)/shard_map/ppermute | solution.py:920
  20.6 345.8 %reduce-scatter.2.cloned.1.call-start = ((), (), s32[]{:S(2)}) async-start(), calls=%async_computation.3 | async-start | bytes 8650752 | tf_op jit(solution)/shard_map/reduce_scatter | solution.py:1307
  50.4 22.0 %collective-permute-start.14 = (bf16[32,4096]{1,0:T(8,128)(2,1)S(1)}, bf16[32,4096]{1,0:T(8,128)(2,1)S(1)}, u32[]{:S(2)}, u32[]{:S(2)}) collective-permute-start(bf16[32,4096]{1,0:T(8,128)(2,1)S(1)} %copy.213.refs_0_), channel_id=1, source_target_pairs={{0,8},{1,9},{2,10},{3,11},{4,12},{5,13},{6,14},{7,15},{8,16},{9,17... | collective-permute-start | bytes 786440 | tf_op jit(solution)/shard_map/ppermute | solution.py:920
  50.4 21.9 %collective-permute-start.13 = (bf16[32,4096]{1,0:T(8,128)(2,1)S(1)}, bf16[32,4096]{1,0:T(8,128)(2,1)S(1)}, u32[]{:S(2)}, u32[]{:S(2)}) collective-permute-start(bf16[32,4096]{1,0:T(8,128)(2,1)S(1)} %copy.213.refs_0_), channel_id=1, source_target_pairs={{0,16},{1,17},{2,18},{3,19},{4,20},{5,21},{6,22},{7,23},{8,24},{9,... | collective-permute-start | bytes 786440 | tf_op jit(solution)/shard_map/ppermute | solution.py:920
  94.3 22.0 %collective-permute-start.27 = (bf16[4,16,4096]{2,1,0:T(8,128)(2,1)S(1)}, bf16[4,16,4096]{2,1,0:T(8,128)(2,1)S(1)}, u32[]{:S(2)}, u32[]{:S(2)}) collective-permute-start(bf16[4,16,4096]{2,1,0:T(8,128)(2,1)S(1)} %copy-done.11), channel_id=1, source_target_pairs={{0,2},{1,3},{2,0},{3,1},{4,6},{5,7},{6,4},{7,5},{8,10},{9,11},{10,... | collective-permute-start | bytes 1572872 | tf_op jit(solution)/shard_map/ppermute | solution.py:916
  95.9 20.3 %collective-permute-start.28 = (bf16[4,16,4096]{2,1,0:T(8,128)(2,1)S(1)}, bf16[4,16,4096]{2,1,0:T(8,128)(2,1)S(1)}, u32[]{:S(2)}, u32[]{:S(2)}) collective-permute-start(bf16[4,16,4096]{2,1,0:T(8,128)(2,1)S(1)} %copy-done.12), channel_id=1, source_target_pairs={{0,4},{1,5},{2,6},{3,7},{4,0},{5,1},{6,2},{7,3},{8,12},{9,13},{10,... | collective-permute-start | bytes 1572872 | tf_op jit(solution)/shard_map/ppermute | solution.py:916
  116.4 32.8 %collective-permute-start.30 = (bf16[2,4,16,4096]{3,2,1,0:T(8,128)(2,1)S(1)}, bf16[2,4,16,4096]{3,2,1,0:T(8,128)(2,1)}, u32[]{:S(2)}, u32[]{:S(2)}) collective-permute-start(bf16[2,4,16,4096]{3,2,1,0:T(8,128)(2,1)S(1)} %pad_maximum_fusion.2.refs_4_), channel_id=1, source_target_pairs={{0,2},{1,3},{2,0},{3,1},{4,6},{5,7},{6,4},{7,5},{8,10},{9,11},{10,... | collective-permute-start | bytes 3145736 | tf_op jit(solution)/shard_map/ppermute | solution.py:916
  117.2 31.9 %collective-permute-start.29 = (bf16[2,4,16,4096]{3,2,1,0:T(8,128)(2,1)S(1)}, bf16[2,4,16,4096]{3,2,1,0:T(8,128)(2,1)}, u32[]{:S(2)}, u32[]{:S(2)}) collective-permute-start(bf16[2,4,16,4096]{3,2,1,0:T(8,128)(2,1)S(1)} %pad_maximum_fusion.1.refs_0_), channel_id=1, source_target_pairs={{0,4},{1,5},{2,6},{3,7},{4,0},{5,1},{6,2},{7,3},{8,12},{9,13},{10,... | collective-permute-start | bytes 3145736 | tf_op jit(solution)/shard_map/ppermute | solution.py:916
  268.7 58.9 %collective-permute-start.38 = (bf16[4,2,16,4096]{3,2,1,0:T(8,128)(2,1)}, bf16[4,2,16,4096]{3,2,1,0:T(8,128)(2,1)S(1)}, u32[]{:S(2)}, u32[]{:S(2)}) collective-permute-start(bf16[4,2,16,4096]{3,2,1,0:T(8,128)(2,1)} %get-tuple-element.184), channel_id=1, source_target_pairs={{0,4},{1,5},{2,6},{3,7},{4,0},{5,1},{6,2},{7,3},{8,12},{9,13},{10,... | collective-permute-start | bytes 3145736 | tf_op jit(solution)/shard_map/ppermute | solution.py:916
  271.5 56.1 %collective-permute-start.39 = (bf16[4,2,16,4096]{3,2,1,0:T(8,128)(2,1)}, bf16[4,2,16,4096]{3,2,1,0:T(8,128)(2,1)S(1)}, u32[]{:S(2)}, u32[]{:S(2)}) collective-permute-start(bf16[4,2,16,4096]{3,2,1,0:T(8,128)(2,1)} %get-tuple-element.185), channel_id=1, source_target_pairs={{0,2},{1,3},{2,0},{3,1},{4,6},{5,7},{6,4},{7,5},{8,10},{9,11},{10,... | collective-permute-start | bytes 3145736 | tf_op jit(solution)/shard_map/ppermute | solution.py:916
  328.9 28.9 %collective-permute-start.40 = (bf16[2,9,32,1024]{3,2,1,0:T(8,128)(2,1)}, bf16[2,9,32,1024]{3,2,1,0:T(8,128)(2,1)S(1)}, u32[]{:S(2)}, u32[]{:S(2)}) collective-permute-start(bf16[2,9,32,1024]{3,2,1,0:T(8,128)(2,1)} %get-tuple-element.188), channel_id=1, source_target_pairs={{0,1},{1,0},{2,3},{3,2},{4,5},{5,4},{6,7},{7,6},{8,9},{9,8},{10,11... | collective-permute-start | bytes 3538952 | tf_op jit(solution)/shard_map/ppermute | solution.py:1329
  333.9 32.4 %collective-permute-start.42 = (bf16[4,16,4096]{2,1,0:T(8,128)(2,1)}, bf16[4,16,4096]{2,1,0:T(8,128)(2,1)}, u32[]{:S(2)}, u32[]{:S(2)}) collective-permute-start(bf16[4,16,4096]{2,1,0:T(8,128)(2,1)} %get-tuple-element.202), channel_id=1, source_target_pairs={{0,2},{1,3},{2,0},{3,1},{4,6},{5,7},{6,4},{7,5},{8,10},{9,11},{10,... | collective-permute-start | bytes 1572872 | tf_op jit(solution)/shard_map/ppermute | solution.py:916
  335.5 30.9 %collective-permute-start.43 = (bf16[4,16,4096]{2,1,0:T(8,128)(2,1)}, bf16[4,16,4096]{2,1,0:T(8,128)(2,1)}, u32[]{:S(2)}, u32[]{:S(2)}) collective-permute-start(bf16[4,16,4096]{2,1,0:T(8,128)(2,1)} %get-tuple-element.203), channel_id=1, source_target_pairs={{0,4},{1,5},{2,6},{3,7},{4,0},{5,1},{6,2},{7,3},{8,12},{9,13},{10,... | collective-permute-start | bytes 1572872 | tf_op jit(solution)/shard_map/ppermute | solution.py:916
  351.6 40.5 %collective-permute-start.47 = (bf16[4,2,16,4096]{3,2,1,0:T(8,128)(2,1)}, bf16[4,2,16,4096]{3,2,1,0:T(8,128)(2,1)}, u32[]{:S(2)}, u32[]{:S(2)}) collective-permute-start(bf16[4,2,16,4096]{3,2,1,0:T(8,128)(2,1)} %get-tuple-element.217), channel_id=1, source_target_pairs={{0,4},{1,5},{2,6},{3,7},{4,0},{5,1},{6,2},{7,3},{8,12},{9,13},{10,... | collective-permute-start | bytes 3145736 | tf_op jit(solution)/shard_map/ppermute | solution.py:916
  352.3 39.7 %collective-permute-start.48 = (bf16[4,2,16,4096]{3,2,1,0:T(8,128)(2,1)}, bf16[4,2,16,4096]{3,2,1,0:T(8,128)(2,1)}, u32[]{:S(2)}, u32[]{:S(2)}) collective-permute-start(bf16[4,2,16,4096]{3,2,1,0:T(8,128)(2,1)} %get-tuple-element.218), channel_id=1, source_target_pairs={{0,2},{1,3},{2,0},{3,1},{4,6},{5,7},{6,4},{7,5},{8,10},{9,11},{10,... | collective-permute-start | bytes 3145736 | tf_op jit(solution)/shard_map/ppermute | solution.py:916
  369.7 28.9 %collective-permute-start.44 = (bf16[32,4096]{1,0:T(8,128)(2,1)}, bf16[32,4096]{1,0:T(8,128)(2,1)S(1)}, u32[]{:S(2)}, u32[]{:S(2)}) collective-permute-start(bf16[32,4096]{1,0:T(8,128)(2,1)} %get-tuple-element.214), channel_id=1, source_target_pairs={{0,24},{1,25},{2,26},{3,27},{4,28},{5,29},{6,30},{7,31},{8,0},{9,1... | collective-permute-start | bytes 786440 | tf_op jit(solution)/shard_map/ppermute | solution.py:920
  380.7 24.3 %collective-permute-start.45 = (bf16[32,4096]{1,0:T(8,128)(2,1)}, bf16[32,4096]{1,0:T(8,128)(2,1)}, u32[]{:S(2)}, u32[]{:S(2)}) collective-permute-start(bf16[32,4096]{1,0:T(8,128)(2,1)} %get-tuple-element.215), channel_id=1, source_target_pairs={{0,16},{1,17},{2,18},{3,19},{4,20},{5,21},{6,22},{7,23},{8,24},{9,... | collective-permute-start | bytes 786440 | tf_op jit(solution)/shard_map/ppermute | solution.py:920
  381.6 23.5 %collective-permute-start.46 = (bf16[32,4096]{1,0:T(8,128)(2,1)}, bf16[32,4096]{1,0:T(8,128)(2,1)}, u32[]{:S(2)}, u32[]{:S(2)}) collective-permute-start(bf16[32,4096]{1,0:T(8,128)(2,1)} %get-tuple-element.216), channel_id=1, source_target_pairs={{0,8},{1,9},{2,10},{3,11},{4,12},{5,13},{6,14},{7,15},{8,16},{9,17... | collective-permute-start | bytes 786440 | tf_op jit(solution)/shard_map/ppermute | solution.py:920
  421.6 26.8 %collective-permute-start.58 = (bf16[32,4096]{1,0:T(8,128)(2,1)}, bf16[32,4096]{1,0:T(8,128)(2,1)S(1)}, u32[]{:S(2)}, u32[]{:S(2)}) collective-permute-start(bf16[32,4096]{1,0:T(8,128)(2,1)} %get-tuple-element.237), channel_id=1, source_target_pairs={{0,16},{1,17},{2,18},{3,19},{4,20},{5,21},{6,22},{7,23},{8,24},{9,... | collective-permute-start | bytes 786440 | tf_op jit(solution)/shard_map/ppermute | solution.py:920
  422.2 26.2 %collective-permute-start.59 = (bf16[32,4096]{1,0:T(8,128)(2,1)}, bf16[32,4096]{1,0:T(8,128)(2,1)S(1)}, u32[]{:S(2)}, u32[]{:S(2)}) collective-permute-start(bf16[32,4096]{1,0:T(8,128)(2,1)} %get-tuple-element.238), channel_id=1, source_target_pairs={{0,8},{1,9},{2,10},{3,11},{4,12},{5,13},{6,14},{7,15},{8,16},{9,17... | collective-permute-start | bytes 786440 | tf_op jit(solution)/shard_map/ppermute | solution.py:920
  430.4 22.3 %collective-permute-start.55 = (bf16[27904]{0:T(1024)(128)(2,1)S(1)}, bf16[27904]{0:T(1024)(128)(2,1)S(1)}, u32[]{:S(2)}, u32[]{:S(2)}) collective-permute-start(bf16[27904]{0:T(1024)(128)(2,1)S(1)} %get-tuple-element.234), channel_id=1, source_target_pairs={{0,24},{1,25},{2,26},{3,27},{4,28},{5,29},{6,30},{7,31},{8,0},{9,1... | collective-permute-start | bytes 167432 | tf_op jit(solution)/shard_map/ppermute | solution.py:920
  (95 other events, 872.1 us)
Sparse Core Ops, SparseCore 0:
  11.0 85.8 all-gather.2
  99.7 83.2 all-gather.4
  203.9 157.8 reduce-scatter.1
